TPU v7x, 256 devices: a whole 4x4x8 slice. The times are simulated.
256 devices in a mesh: stream: 64 (over z, x, y_hi), tm: 4 (over y_lo, core).
Axes of the slice: x: 4, y: 4 (y_hi: 2, y_lo: 2; y = y_hi * 2 + y_lo), z: 8, core: 2. Of those that a mesh axis runs over, the one named last changes fastest.
Arguments:
- raw: bfloat16 [4096, 4096], P('stream', 'tm'), may hold values from -400 to 400
- taps: float32 [65], replicated, may hold values from -0.75 to 0.75
Outputs:
- information: float32 [9, 4096, 4096], P(None, 'stream', 'tm')
- filtered: bfloat16 [4096, 4096], P('stream', 'tm')
All inputs are finite; a program needn't handle non-finite values.
Results may differ from a plain program's by a relative error of at most 0.0014.
Values may be sent and summed in bfloat16 or wider, within the bound.
No kernel may reach another device: no remote copies, remote signals or barrier semaphores. Data moves between devices by JAX's collectives and lax.ppermute only.
A program may use at most 256 MiB of HBM per device.

v0:
```python
import jax
import jax.numpy as jnp
import numpy as np
from jax import lax
from jax.experimental import pallas as pl
from jax.experimental.pallas import tpu as pltpu
from jax.sharding import Mesh, PartitionSpec as P

LAGS = 9
REACH = 4
HALF = 32
NT = (((1,), (1,)), ((), ()))
MB = 1 << 20


def filter_kernel(place, raw, taps, out, first, second, blocks, weights):
    parts, rows, bins = raw.shape
    per = bins // 128
    count = parts * per
    blocks[0] = jnp.zeros((rows, 128), jnp.bfloat16)
    blocks[count + 1] = jnp.zeros((rows, 128), jnp.bfloat16)
    for q in range(parts):
        for b in range(per):
            blocks[1 + q * per + b] = raw[q, :, b * 128 : (b + 1) * 128]
    line = jnp.broadcast_to(taps[...], (128, 384))
    band = pltpu.roll(line, 128 - HALF, axis=1, stride=1, stride_axis=0)
    high = band.astype(jnp.bfloat16)
    rest = band - high.astype(jnp.float32)
    middle = rest.astype(jnp.bfloat16)
    low = (rest - middle.astype(jnp.float32)).astype(jnp.bfloat16)
    weights[0:128] = high
    weights[128:256] = middle
    weights[256:384] = low
    group = 8
    for g in range(count // group):
        total = None
        for k in range(3):
            piece = blocks[g * group + k : g * group + k + group].reshape(group * rows, 128)
            term = lax.dot_general(
                piece, weights[:, k * 128 : (k + 1) * 128], NT, preferred_element_type=jnp.float32
            )
            total = term if total is None else total + term
        value = (total[:, 256:384] + total[:, 128:256]) + total[:, 0:128]
        value = value.astype(jnp.bfloat16)
        for b in range(group):
            n = g * group + b
            out[:, n * 128 : (n + 1) * 128] = value[b * rows : (b + 1) * rows]
    at = pl.multiple_of(place[0], 8)
    first[...] = out[pl.ds(at, 8), :]
    at = pl.multiple_of(place[1], 8)
    second[...] = out[pl.ds(at, 8), :]


def run_filter(place, raw, taps):
    parts, rows, bins = raw.shape
    vmem = pl.BlockSpec(memory_space=pltpu.VMEM)
    return pl.pallas_call(
        filter_kernel,
        in_specs=[pl.BlockSpec(memory_space=pltpu.SMEM), vmem, vmem],
        out_specs=[vmem, vmem, vmem],
        out_shape=[
            jax.ShapeDtypeStruct((rows, parts * bins), jnp.bfloat16),
            jax.ShapeDtypeStruct((8, parts * bins), jnp.bfloat16),
            jax.ShapeDtypeStruct((8, parts * bins), jnp.bfloat16),
        ],
        scratch_shapes=[
            pltpu.VMEM((parts * bins // 128 + 2, rows, 128), jnp.bfloat16),
            pltpu.VMEM((384, 384), jnp.bfloat16),
        ],
        compiler_params=pltpu.CompilerParams(vmem_limit_bytes=24 * MB),
        name="fir",
    )(place, raw, taps)


def lag_kernel(rows_ref, out, energy):
    value = rows_ref[0].astype(jnp.float32)
    bins = value.shape[1]
    energy[...] = jnp.broadcast_to(jnp.sum(value * value, axis=1, keepdims=True), energy.shape)
    at = lax.broadcasted_iota(jnp.int32, value.shape, 1)
    for lag in range(LAGS):
        step = lag - REACH
        if step == 0:
            moved = value
        else:
            moved = pltpu.roll(value, step % bins, axis=1)
            inside = at >= step if step > 0 else at < bins + step
            moved = jnp.where(inside, moved, 0.0)
        out[lag] = moved.astype(jnp.bfloat16)


def run_lags(rows):
    sides, count, bins = rows.shape
    per = count // 16
    return pl.pallas_call(
        lag_kernel,
        grid=(sides * per,),
        in_specs=[pl.BlockSpec((1, 16, bins), lambda i: (i // per, i % per, 0))],
        out_specs=[
            pl.BlockSpec((LAGS, 16, bins), lambda i: (0, i, 0)),
            pl.BlockSpec((16, 128), lambda i: (i, 0)),
        ],
        out_shape=[
            jax.ShapeDtypeStruct((LAGS, sides * count, bins), jnp.bfloat16),
            jax.ShapeDtypeStruct((sides * count, 128), jnp.float32),
        ],
        compiler_params=pltpu.CompilerParams(vmem_limit_bytes=24 * MB),
        cost_estimate=pl.CostEstimate(flops=10 * MB, bytes_accessed=12 * MB, transcendentals=0),
        name="lags",
    )(rows)


def moment_kernel(plan, slots, at, lagged, energy, *rest):
    units = rest[: len(plan)]
    own, other, columns, scale, sems = rest[len(plan) :]
    step = pl.program_id(0)
    count = lagged.shape[1]
    width = columns.shape[0] * columns.shape[1]

    @pl.when(step == 0)
    def _():
        copies = []
        for ref, (lead, start) in zip(units, plan):
            for k in range(lead):
                copies.append(
                    pltpu.make_async_copy(ref.at[k], columns.at[at[start + k]], sems.at[start + k])
                )
        for copy in copies:
            copy.start()
        for copy in copies:
            copy.wait()
        for g in range(width // 128):
            block = columns[g * 16 : (g + 1) * 16].astype(jnp.float32).reshape(128, -1)
            total = jnp.sum(block * block, axis=1, keepdims=True)
            root = 0.8 / jnp.sqrt(total + 1e-05)
            scale[:, g * 128 : (g + 1) * 128] = jnp.transpose(jnp.broadcast_to(root, (128, 128)))

    group = lagged.shape[0]
    bins = lagged.shape[2]
    left = lagged[...].reshape(group * count, bins)
    right = columns[...].reshape(width, bins)
    moments = lax.dot_general(left, right, NT, preferred_element_type=jnp.float32)
    rows = 1.0 / jnp.sqrt(energy[:, 0:1] + 1e-05)
    half = count // 2
    across = scale[0:1, :]
    for lag in range(group):
        for side, ref in enumerate((own, other)):
            lo = lag * count + side * half
            ratio = moments[lo : lo + half] * (rows[side * half : (side + 1) * half] * across)
            value = -0.5 * jnp.log(1.0 - ratio * ratio)
            ref[lag] = value.astype(ref.dtype)


def run_moments(at, lagged, energy, units):
    plan = []
    start = 0
    for unit in units:
        plan.append((unit.shape[0], start))
        start += unit.shape[0]
    slots = start
    lags, count, bins = lagged.shape
    width = slots * 8
    group = 3
    half = count // 2

    def body(*refs):
        moment_kernel(plan, slots, *refs)

    result = pl.BlockSpec((group, half, width), lambda i: (i, 0, 0))
    return pl.pallas_call(
        body,
        grid=(lags // group,),
        in_specs=[
            pl.BlockSpec(memory_space=pltpu.SMEM),
            pl.BlockSpec((group, count, bins), lambda i: (i, 0, 0)),
            pl.BlockSpec((count, 128), lambda i: (0, 0)),
        ]
        + [pl.BlockSpec(memory_space=pl.ANY)] * len(units),
        out_specs=[result, result],
        out_shape=[
            jax.ShapeDtypeStruct((lags, half, width), jnp.float32),
            jax.ShapeDtypeStruct((lags, half, width), jnp.float32),
        ],
        scratch_shapes=[
            pltpu.VMEM((slots, 8, bins), jnp.bfloat16),
            pltpu.VMEM((128, width), jnp.float32),
            pltpu.SemaphoreType.DMA((slots,)),
        ],
        compiler_params=pltpu.CompilerParams(vmem_limit_bytes=48 * MB),
        cost_estimate=pl.CostEstimate(
            flops=2 * lags * count * width * bins,
            bytes_accessed=2 * bins * (lags * count + width) + 4 * lags * count * width,
            transcendentals=lags * count * width,
        ),
        name="moments",
    )(at, lagged, energy, *units)


def join_kernel(place, own_a, got_a, own_b, got_b, out):
    low = place[0] == 0
    lane = lax.broadcasted_iota(jnp.int32, own_a.shape[1:2] + (128,), 1) < 64
    for half, (own, got) in enumerate(((own_a, got_a), (own_b, got_b))):
        for lag in range(own.shape[0]):
            for tile in range(own.shape[2] // 128):
                span = slice(tile * 128, (tile + 1) * 128)
                here = own[lag, :, span]
                there = got[lag, :, span].astype(jnp.float32)
                one = jnp.where(low, here, there)
                two = jnp.where(low, there, here)
                base = half * 512 + tile * 256
                out[lag, :, base : base + 128] = jnp.where(lane, one, pltpu.roll(two, 64, axis=1))
                out[lag, :, base + 128 : base + 256] = jnp.where(
                    lane, pltpu.roll(one, 64, axis=1), two
                )


def run_join(place, own_a, got_a, own_b, got_b):
    lags, rows, width = own_a.shape
    spec = pl.BlockSpec((3, rows, width), lambda i: (i, 0, 0))
    return pl.pallas_call(
        join_kernel,
        grid=(lags // 3,),
        in_specs=[pl.BlockSpec(memory_space=pltpu.SMEM)] + [spec] * 4,
        out_specs=pl.BlockSpec((3, rows, 4 * width), lambda i: (i, 0, 0)),
        out_shape=jax.ShapeDtypeStruct((lags, rows, 4 * width), jnp.float32),
        compiler_params=pltpu.CompilerParams(vmem_limit_bytes=32 * MB),
        name="join",
    )(place, own_a, got_a, own_b, got_b)


def around(value, axis, step):
    size = lax.axis_size(axis)
    return lax.ppermute(value, axis, [(i, (i + step) % size) for i in range(size)])


def spread(value, odd):
    pairs = []
    for z in range(8):
        for q in range(4):
            j = (z & 1) ^ odd
            pairs.append((z * 4 + q, (2 * q + j) * 4 + (z >> 1)))
    return lax.ppermute(value, ("z", "yl", "core"), pairs)


def shards(raw, taps):
    z = lax.axis_index("z")
    x = lax.axis_index("x")
    yh = lax.axis_index("yh")
    q = lax.axis_index(("yl", "core"))
    e = z % 2
    bins = raw.shape[1]
    everything = lax.all_gather(raw, ("yl", "core"), axis=0, tiled=False)
    line = jnp.pad(taps.reshape(1, -1), ((0, 0), (0, 384 - taps.shape[0])))
    place = jnp.stack([16 * q + 8 * e, 16 * q + 8 * (1 - e)]).astype(jnp.int32)
    full, first, second = run_filter(place, everything, line)
    one = spread(first, 0)
    two = spread(second, 1)
    unit_a = jnp.where(e == 0, one, two)[None]
    unit_b = jnp.where(e == 0, two, one)[None]
    near = [unit_a, around(unit_a, "x", 1), around(unit_a, "x", -1), around(unit_a, "x", 2)]
    x_of = [x, x - 1, x + 1, x + 2]
    base_a = jnp.concatenate(near, axis=0)
    units_a, at_a = [base_a], [xx % 4 * 8 + z for xx in x_of]
    up = down = base_a
    for step in (1, 2, 3):
        up = around(up, "z", 1)
        down = around(down, "z", -1)
        units_a += [up, down]
        at_a += [xx % 4 * 8 + (z - step) % 8 for xx in x_of]
        at_a += [xx % 4 * 8 + (z + step) % 8 for xx in x_of]
    units_a += [around(up[0:2], "z", 1), around(down[2:4], "z", -1)]
    at_a += [xx % 4 * 8 + (z + 4) % 8 for xx in x_of]
    up = down = unit_b
    near, z_of = [unit_b], [z]
    for step in (1, 2, 3):
        up = around(up, "z", 1)
        down = around(down, "z", -1)
        near += [up, down]
        z_of += [z - step, z + step]
    near.append(around(up, "z", 1))
    z_of.append(z + 4)
    base_b = jnp.concatenate(near, axis=0)
    units_b = [
        base_b,
        around(base_b, "x", 1),
        around(base_b, "x", -1),
        around(base_b[0:4], "x", 2),
        around(base_b[4:8], "x", -2),
    ]
    at_b = []
    for xx in (x, x - 1, x + 1, x + 2):
        at_b += [xx % 4 * 8 + zz % 8 for zz in z_of]
    partner = lax.ppermute(full, "yh", [(0, 1), (1, 0)])
    lagged, energy = run_lags(jnp.stack([full, partner]))
    own_a, send_a = run_moments(jnp.stack(at_a).astype(jnp.int32), lagged, energy, units_a)
    got_a = lax.ppermute(send_a, "yh", [(0, 1), (1, 0)])
    own_b, send_b = run_moments(jnp.stack(at_b).astype(jnp.int32), lagged, energy, units_b)
    got_b = lax.ppermute(send_b, "yh", [(0, 1), (1, 0)])
    information = run_join(yh.reshape(1).astype(jnp.int32), own_a, got_a, own_b, got_b)
    filtered = lax.dynamic_slice_in_dim(full, q * bins, bins, 1)
    return (information, filtered)


def solution(mesh):
    fine = Mesh(mesh.devices.reshape(8, 4, 2, 2, 2), ("z", "x", "yh", "yl", "core"))
    rows, bins = ("z", "x", "yh"), ("yl", "core")
    return jax.shard_map(
        shards,
        mesh=fine,
        in_specs=(P(rows, bins), P()),
        out_specs=(P(None, rows, bins), P(rows, bins)),
        check_vma=False,
    )
```

profile of v0, /device:TPU:8, one launch (start us, length us, event | category | flops | bytes accessed | tf_op | source)
XLA Modules:
  0.0 118.9 jit_solution(11562839611006522271)
XLA Ops:
  0.7 8.1 %all-gather = bf16[256,1024]{1,0:T(8,128)(2,1)S(1)} all-gather(bf16[64,1024]{1,0:T(8,128)(2,1)} %param.2), channel_id=2, replica_groups=mesh['z'=8,'x'=4,'yh'=2,'yl'=2,'core'=2] {'yl','core'}, dimensions={0}, use_global_device_ids=true | all-gather | bytes 655360 | tf_op jit(solution)/shard_map/all_gather | solution.py:251
  9.5 2.1 %fir.1 = (bf16[64,4096]{1,0:T(8,128)(2,1)S(1)}, bf16[8,4096]{1,0:T(8,128)(2,1)S(1)}, bf16[8,4096]{1,0:T(8,128)(2,1)S(1)}) custom-call(s32[2]{0:T(128)S(1)} %pad_add_fusion.place, bf16[4,64,1024]{2,1,0:T(8,128)(2,1)S(1)} %bitcast.48, f32[1,384]{1,0:T(1,128)S(1)} %pad.4.taps), custom_call_target="tpu_custom_call" | custom-call | tf_op jit(solution)/shard_map/fir/pallas_call | solution.py:57
  11.5 8.4 %collective-permute-start.1 = (bf16[8,4096]{1,0:T(8,128)(2,1)S(1)}, bf16[8,4096]{1,0:T(8,128)(2,1)S(1)}, u32[]{:S(2)}, u32[]{:S(2)}) collective-permute-start(bf16[8,4096]{1,0:T(8,128)(2,1)S(1)} %get-tuple-element.14), channel_id=1, source_target_pairs={{0,0},{1,64},{2,128},{3,192},{32,32},{33,96},{34,160},{35,224},{64... | collective-permute-start | bytes 196616 | tf_op jit(solution)/shard_map/ppermute | solution.py:241
  20.0 2.4 %collective-permute-start = (bf16[64,4096]{1,0:T(8,128)(2,1)S(1)}, bf16[64,4096]{1,0:T(8,128)(2,1)S(1)}, u32[]{:S(2)}, u32[]{:S(2)}) collective-permute-start(bf16[64,4096]{1,0:T(8,128)(2,1)S(1)} %get-tuple-element.11), channel_id=1, source_target_pairs={{0,4},{4,0},{1,5},{5,1},{2,6},{6,2},{3,7},{7,3},{8,12},{12,8},{9,1... | collective-permute-start | bytes 1572872 | tf_op jit(solution)/shard_map/ppermute | solution.py:292
  22.7 5.6 %collective-permute-done.2 = bf16[8,4096]{1,0:T(8,128)(2,1)S(1)} collective-permute-done((bf16[8,4096]{1,0:T(8,128)(2,1)S(1)}, bf16[8,4096]{1,0:T(8,128)(2,1)S(1)}, u32[]{:S(2)}, u32[]{:S(2)}) %collective-permute-start.2) | collective-permute-done | bytes 65568 | tf_op jit(solution)/shard_map/ppermute | solution.py:241
  28.3 1.6 %collective-permute-start.3 = (bf16[1,8,4096]{2,1,0:T(8,128)(2,1)S(1)}, bf16[1,8,4096]{2,1,0:T(8,128)(2,1)S(1)}, u32[]{:S(2)}, u32[]{:S(2)}) collective-permute-start(bf16[1,8,4096]{2,1,0:T(8,128)(2,1)S(1)} %select_bitcast_fusion.1), channel_id=1, source_target_pairs={{0,8},{8,16},{16,24},{24,0},{1,9},{9,17},{17,25},{25,1},{2,10},{10... | collective-permute-start | bytes 196616 | tf_op jit(solution)/shard_map/ppermute | solution.py:232
  29.9 1.7 %collective-permute-start.4 = (bf16[1,8,4096]{2,1,0:T(8,128)(2,1)S(1)}, bf16[1,8,4096]{2,1,0:T(8,128)(2,1)S(1)}, u32[]{:S(2)}, u32[]{:S(2)}) collective-permute-start(bf16[1,8,4096]{2,1,0:T(8,128)(2,1)S(1)} %select_bitcast_fusion.1), channel_id=1, source_target_pairs={{0,24},{8,0},{16,8},{24,16},{1,25},{9,1},{17,9},{25,17},{2,26},{10... | collective-permute-start | bytes 196616 | tf_op jit(solution)/shard_map/ppermute | solution.py:232
  31.6 1.8 %collective-permute-start.5 = (bf16[1,8,4096]{2,1,0:T(8,128)(2,1)S(1)}, bf16[1,8,4096]{2,1,0:T(8,128)(2,1)S(1)}, u32[]{:S(2)}, u32[]{:S(2)}) collective-permute-start(bf16[1,8,4096]{2,1,0:T(8,128)(2,1)S(1)} %select_bitcast_fusion.1), channel_id=1, source_target_pairs={{0,16},{8,24},{16,0},{24,8},{1,17},{9,25},{17,1},{25,9},{2,18},{10... | collective-permute-start | bytes 196616 | tf_op jit(solution)/shard_map/ppermute | solution.py:232
  33.5 1.8 %collective-permute-start.15 = (bf16[1,8,4096]{2,1,0:T(8,128)(2,1)S(1)}, bf16[1,8,4096]{2,1,0:T(8,128)(2,1)S(1)}, u32[]{:S(2)}, u32[]{:S(2)}) collective-permute-start(bf16[1,8,4096]{2,1,0:T(8,128)(2,1)S(1)} %get-tuple-element.21), channel_id=1, source_target_pairs={{0,32},{32,64},{64,96},{96,128},{128,160},{160,192},{192,224},{224... | collective-permute-start | bytes 196616 | tf_op jit(solution)/shard_map/ppermute | solution.py:232
  35.3 1.5 %collective-permute-start.16 = (bf16[1,8,4096]{2,1,0:T(8,128)(2,1)S(1)}, bf16[1,8,4096]{2,1,0:T(8,128)(2,1)S(1)}, u32[]{:S(2)}, u32[]{:S(2)}) collective-permute-start(bf16[1,8,4096]{2,1,0:T(8,128)(2,1)S(1)} %get-tuple-element.21), channel_id=1, source_target_pairs={{0,224},{32,0},{64,32},{96,64},{128,96},{160,128},{192,160},{224,1... | collective-permute-start | bytes 196616 | tf_op jit(solution)/shard_map/ppermute | solution.py:232
  37.4 1.8 %collective-permute-start.6 = (bf16[4,8,4096]{2,1,0:T(8,128)(2,1)S(1)}, bf16[4,8,4096]{2,1,0:T(8,128)(2,1)S(1)}, u32[]{:S(2)}, u32[]{:S(2)}) collective-permute-start(bf16[4,8,4096]{2,1,0:T(8,128)(2,1)S(1)} %pad_maximum_fusion.1.refs_3_), channel_id=1, source_target_pairs={{0,32},{32,64},{64,96},{96,128},{128,160},{160,192},{192,224},{224... | collective-permute-start | bytes 786440 | tf_op jit(solution)/shard_map/ppermute | solution.py:232
  39.2 1.5 %collective-permute-start.7 = (bf16[4,8,4096]{2,1,0:T(8,128)(2,1)S(1)}, bf16[4,8,4096]{2,1,0:T(8,128)(2,1)S(1)}, u32[]{:S(2)}, u32[]{:S(2)}) collective-permute-start(bf16[4,8,4096]{2,1,0:T(8,128)(2,1)S(1)} %pad_maximum_fusion.1.refs_3_), channel_id=1, source_target_pairs={{0,224},{32,0},{64,32},{96,64},{128,96},{160,128},{192,160},{224,1... | collective-permute-start | bytes 786440 | tf_op jit(solution)/shard_map/ppermute | solution.py:232
  41.3 2.8 %collective-permute-start.18 = (bf16[1,8,4096]{2,1,0:T(8,128)(2,1)S(1)}, bf16[1,8,4096]{2,1,0:T(8,128)(2,1)S(1)}, u32[]{:S(2)}, u32[]{:S(2)}) collective-permute-start(bf16[1,8,4096]{2,1,0:T(8,128)(2,1)S(1)} %collective-permute-done.16), channel_id=1, source_target_pairs={{0,224},{32,0},{64,32},{96,64},{128,96},{160,128},{192,160},{224,1... | collective-permute-start | bytes 196616 | tf_op jit(solution)/shard_map/ppermute | solution.py:232
  44.1 2.4 %collective-permute-done.17 = bf16[1,8,4096]{2,1,0:T(8,128)(2,1)S(1)} collective-permute-done((bf16[1,8,4096]{2,1,0:T(8,128)(2,1)S(1)}, bf16[1,8,4096]{2,1,0:T(8,128)(2,1)S(1)}, u32[]{:S(2)}, u32[]{:S(2)}) %collective-permute-start.17) | collective-permute-done | bytes 65568 | tf_op jit(solution)/shard_map/ppermute | solution.py:232
  46.6 3.3 %collective-permute-start.20 = (bf16[1,8,4096]{2,1,0:T(8,128)(2,1)S(1)}, bf16[1,8,4096]{2,1,0:T(8,128)(2,1)S(1)}, u32[]{:S(2)}, u32[]{:S(2)}) collective-permute-start(bf16[1,8,4096]{2,1,0:T(8,128)(2,1)S(1)} %collective-permute-done.18), channel_id=1, source_target_pairs={{0,224},{32,0},{64,32},{96,64},{128,96},{160,128},{192,160},{224,1... | collective-permute-start | bytes 196616 | tf_op jit(solution)/shard_map/ppermute | solution.py:232
  49.9 2.7 %collective-permute-done.19 = bf16[1,8,4096]{2,1,0:T(8,128)(2,1)S(1)} collective-permute-done((bf16[1,8,4096]{2,1,0:T(8,128)(2,1)S(1)}, bf16[1,8,4096]{2,1,0:T(8,128)(2,1)S(1)}, u32[]{:S(2)}, u32[]{:S(2)}) %collective-permute-start.19) | collective-permute-done | bytes 65568 | tf_op jit(solution)/shard_map/ppermute | solution.py:232
  52.9 5.2 %collective-permute-done.21 = bf16[1,8,4096]{2,1,0:T(8,128)(2,1)S(1)} collective-permute-done((bf16[1,8,4096]{2,1,0:T(8,128)(2,1)S(1)}, bf16[1,8,4096]{2,1,0:T(8,128)(2,1)S(1)}, u32[]{:S(2)}, u32[]{:S(2)}) %collective-permute-start.21) | collective-permute-done | bytes 65568 | tf_op jit(solution)/shard_map/ppermute | solution.py:232
  58.1 3.2 %collective-permute-start.23 = (bf16[8,8,4096]{2,1,0:T(8,128)(2,1)S(1)}, bf16[8,8,4096]{2,1,0:T(8,128)(2,1)S(1)}, u32[]{:S(2)}, u32[]{:S(2)}) collective-permute-start(bf16[8,8,4096]{2,1,0:T(8,128)(2,1)S(1)} %constant_dynamic-update-slice_fusion.refs_3_), channel_id=1, source_target_pairs={{0,24},{8,0},{16,8},{24,16},{1,25},{9,1},{17,9},{25,17},{2,26},{10... | collective-permute-start | bytes 1572872 | tf_op jit(solution)/shard_map/ppermute | solution.py:232
  61.3 2.1 %collective-permute-done.8.refs_6_ = bf16[4,8,4096]{2,1,0:T(8,128)(2,1)S(1)} collective-permute-done((bf16[4,8,4096]{2,1,0:T(8,128)(2,1)S(1)}, bf16[4,8,4096]{2,1,0:T(8,128)(2,1)S(1)}, u32[]{:S(2)}, u32[]{:S(2)}) %collective-permute-start.8) | collective-permute-done | bytes 262176 | tf_op jit(solution)/shard_map/ppermute | solution.py:232
  63.5 2.2 %collective-permute-start.24 = (bf16[4,8,4096]{2,1,0:T(8,128)(2,1)S(1)}, bf16[4,8,4096]{2,1,0:T(8,128)(2,1)S(1)}, u32[]{:S(2)}, u32[]{:S(2)}) collective-permute-start(bf16[4,8,4096]{2,1,0:T(8,128)(2,1)S(1)} %pad_maximum_fusion.2), channel_id=1, source_target_pairs={{0,16},{8,24},{16,0},{24,8},{1,17},{9,25},{17,1},{25,9},{2,18},{10... | collective-permute-start | bytes 786440 | tf_op jit(solution)/shard_map/ppermute | solution.py:232
  65.7 3.3 %collective-permute-done.9.refs_7_ = bf16[4,8,4096]{2,1,0:T(8,128)(2,1)S(1)} collective-permute-done((bf16[4,8,4096]{2,1,0:T(8,128)(2,1)S(1)}, bf16[4,8,4096]{2,1,0:T(8,128)(2,1)S(1)}, u32[]{:S(2)}, u32[]{:S(2)}) %collective-permute-start.9) | collective-permute-done | bytes 262176 | tf_op jit(solution)/shard_map/ppermute | solution.py:232
  68.9 2.0 %collective-permute-done.10.refs_8_ = bf16[4,8,4096]{2,1,0:T(8,128)(2,1)S(1)} collective-permute-done((bf16[4,8,4096]{2,1,0:T(8,128)(2,1)S(1)}, bf16[4,8,4096]{2,1,0:T(8,128)(2,1)S(1)}, u32[]{:S(2)}, u32[]{:S(2)}) %collective-permute-start.10) | collective-permute-done | bytes 262176 | tf_op jit(solution)/shard_map/ppermute | solution.py:232
  71.1 3.6 %lags.1 = (bf16[9,128,4096]{2,1,0:T(8,128)(2,1)S(1)}, f32[128,128]{1,0:T(8,128)S(1)}) custom-call(bf16[2,64,4096]{2,1,0:T(8,128)(2,1)S(1)} %pad_maximum_fusion.rows_ref), custom_call_target="tpu_custom_call" | custom-call | flops 10485760 | bytes 12582912 | tf_op jit(solution)/shard_map/lags/pallas_call | solution.py:94
  74.7 3.7 %copy-done = bf16[9,128,4096]{2,1,0:T(8,128)(2,1)} copy-done((bf16[9,128,4096]{2,1,0:T(8,128)(2,1)}, bf16[9,128,4096]{2,1,0:T(8,128)(2,1)S(1)}, u32[]{:S(2)}) %copy-start) | copy-done | bytes 9437208
  78.8 1.7 %collective-permute-start.12 = (bf16[2,8,4096]{2,1,0:T(8,128)(2,1)S(1)}, bf16[2,8,4096]{2,1,0:T(8,128)(2,1)S(1)}, u32[]{:S(2)}, u32[]{:S(2)}) collective-permute-start(bf16[2,8,4096]{2,1,0:T(8,128)(2,1)S(1)} %slice.12), channel_id=1, source_target_pairs={{0,32},{32,64},{64,96},{96,128},{128,160},{160,192},{192,224},{224... | collective-permute-start | bytes 393224 | tf_op jit(solution)/shard_map/ppermute | solution.py:232
  80.5 1.6 %collective-permute-start.13 = (bf16[2,8,4096]{2,1,0:T(8,128)(2,1)S(1)}, bf16[2,8,4096]{2,1,0:T(8,128)(2,1)S(1)}, u32[]{:S(2)}, u32[]{:S(2)}) collective-permute-start(bf16[2,8,4096]{2,1,0:T(8,128)(2,1)S(1)} %slice.13), channel_id=1, source_target_pairs={{0,224},{32,0},{64,32},{96,64},{128,96},{160,128},{192,160},{224,1... | collective-permute-start | bytes 393224 | tf_op jit(solution)/shard_map/ppermute | solution.py:232
  82.1 9.9 %moments.3 = (f32[9,64,256]{2,1,0:T(8,128)S(1)}, f32[9,64,256]{2,1,0:T(8,128)S(1)}) custom-call(s32[32]{0:T(128)S(1)} %stack.203.refs_0_, bf16[9,128,4096]{2,1,0:T(8,128)(2,1)} %copy-done, f32[128,128]{1,0:T(8,128)S(1)} %get-tuple-element.13.refs_2_, bf16[8,8,4096]{2,1,0:T(8,128)(2,1)S(1)} %constant_dynamic-update-slice_fusion.refs_3_, ...), custom_call_target="tpu_custom_call" | custom-call | flops 2415919104 | bytes 12713984 | tf_op jit(solution)/shard_map/moments/pallas_call | solution.py:169
  92.0 2.4 %collective-permute-start.26 = (f32[9,64,256]{2,1,0:T(8,128)S(1)}, f32[9,64,256]{2,1,0:T(8,128)S(1)}, u32[]{:S(2)}, u32[]{:S(2)}) collective-permute-start(f32[9,64,256]{2,1,0:T(8,128)S(1)} %get-tuple-element.19), channel_id=1, source_target_pairs={{0,4},{4,0},{1,5},{5,1},{2,6},{6,2},{3,7},{7,3},{8,12},{12,8},{9,1... | collective-permute-start | bytes 1769480 | tf_op jit(solution)/shard_map/ppermute | solution.py:297
  94.3 10.6 %moments.2 = (f32[9,64,256]{2,1,0:T(8,128)S(1)}, f32[9,64,256]{2,1,0:T(8,128)}) custom-call(s32[32]{0:T(128)S(1)} %stack.192.refs_0_, bf16[9,128,4096]{2,1,0:T(8,128)(2,1)} %copy-done, f32[128,128]{1,0:T(8,128)S(1)} %get-tuple-element.13.refs_2_, bf16[4,8,4096]{2,1,0:T(8,128)(2,1)S(1)} %pad_maximum_fusion.1.refs_3_, ...), custom_call_target="tpu_custom_call" | custom-call | flops 2415919104 | bytes 12713984 | tf_op jit(solution)/shard_map/moments/pallas_call | solution.py:169
  104.9 1.3 %collective-permute-start.14 = (f32[9,64,256]{2,1,0:T(8,128)}, f32[9,64,256]{2,1,0:T(8,128)S(1)}, u32[]{:S(2)}, u32[]{:S(2)}) collective-permute-start(f32[9,64,256]{2,1,0:T(8,128)} %get-tuple-element.17), channel_id=1, source_target_pairs={{0,4},{4,0},{1,5},{5,1},{2,6},{6,2},{3,7},{7,3},{8,12},{12,8},{9,1... | collective-permute-start | bytes 1769480 | tf_op jit(solution)/shard_map/ppermute | solution.py:295
  106.9 9.7 %collective-permute-done.14.got_a = f32[9,64,256]{2,1,0:T(8,128)S(1)} collective-permute-done((f32[9,64,256]{2,1,0:T(8,128)}, f32[9,64,256]{2,1,0:T(8,128)S(1)}, u32[]{:S(2)}, u32[]{:S(2)}) %collective-permute-start.14) | collective-permute-done | bytes 589856 | tf_op jit(solution)/shard_map/ppermute | solution.py:295
  116.6 2.3 %join.1 = f32[9,64,1024]{2,1,0:T(8,128)} custom-call(s32[1]{0:T(128)} %bitcast.place, f32[9,64,256]{2,1,0:T(8,128)S(1)} %get-tuple-element.16.own_a, f32[9,64,256]{2,1,0:T(8,128)S(1)} %collective-permute-done.14.got_a, f32[9,64,256]{2,1,0:T(8,128)S(1)} %get-tuple-element.18.own_b, f32[9,64,256]{2,1,0:T(8,128)S(1)} %collective-permute-done.26.got_b), custom_call_target="tpu_custom_call" | custom-call | tf_op jit(solution)/shard_map/join/pallas_call | solution.py:219
  (50 shorter events, 3.9 us)
Async XLA Ops:
  11.5 11.1 %collective-permute-start.1 = (bf16[8,4096]{1,0:T(8,128)(2,1)S(1)}, bf16[8,4096]{1,0:T(8,128)(2,1)S(1)}, u32[]{:S(2)}, u32[]{:S(2)}) collective-permute-start(bf16[8,4096]{1,0:T(8,128)(2,1)S(1)} %get-tuple-element.14), channel_id=1, source_target_pairs={{0,0},{1,64},{2,128},{3,192},{32,32},{33,96},{34,160},{35,224},{64... | collective-permute-start | bytes 196616 | tf_op jit(solution)/shard_map/ppermute | solution.py:241
  19.9 8.4 %collective-permute-start.2 = (bf16[8,4096]{1,0:T(8,128)(2,1)S(1)}, bf16[8,4096]{1,0:T(8,128)(2,1)S(1)}, u32[]{:S(2)}, u32[]{:S(2)}) collective-permute-start(bf16[8,4096]{1,0:T(8,128)(2,1)S(1)} %get-tuple-element.15), channel_id=1, source_target_pairs={{0,32},{1,96},{2,160},{3,224},{32,0},{33,64},{34,128},{35,192},{64... | collective-permute-start | bytes 196616 | tf_op jit(solution)/shard_map/ppermute | solution.py:241
  20.0 43.4 %collective-permute-start = (bf16[64,4096]{1,0:T(8,128)(2,1)S(1)}, bf16[64,4096]{1,0:T(8,128)(2,1)S(1)}, u32[]{:S(2)}, u32[]{:S(2)}) collective-permute-start(bf16[64,4096]{1,0:T(8,128)(2,1)S(1)} %get-tuple-element.11), channel_id=1, source_target_pairs={{0,4},{4,0},{1,5},{5,1},{2,6},{6,2},{3,7},{7,3},{8,12},{12,8},{9,1... | collective-permute-start | bytes 1572872 | tf_op jit(solution)/shard_map/ppermute | solution.py:292
  28.3 7.0 %collective-permute-start.3 = (bf16[1,8,4096]{2,1,0:T(8,128)(2,1)S(1)}, bf16[1,8,4096]{2,1,0:T(8,128)(2,1)S(1)}, u32[]{:S(2)}, u32[]{:S(2)}) collective-permute-start(bf16[1,8,4096]{2,1,0:T(8,128)(2,1)S(1)} %select_bitcast_fusion.1), channel_id=1, source_target_pairs={{0,8},{8,16},{16,24},{24,0},{1,9},{9,17},{17,25},{25,1},{2,10},{10... | collective-permute-start | bytes 196616 | tf_op jit(solution)/shard_map/ppermute | solution.py:232
  29.9 6.9 %collective-permute-start.4 = (bf16[1,8,4096]{2,1,0:T(8,128)(2,1)S(1)}, bf16[1,8,4096]{2,1,0:T(8,128)(2,1)S(1)}, u32[]{:S(2)}, u32[]{:S(2)}) collective-permute-start(bf16[1,8,4096]{2,1,0:T(8,128)(2,1)S(1)} %select_bitcast_fusion.1), channel_id=1, source_target_pairs={{0,24},{8,0},{16,8},{24,16},{1,25},{9,1},{17,9},{25,17},{2,26},{10... | collective-permute-start | bytes 196616 | tf_op jit(solution)/shard_map/ppermute | solution.py:232
  31.6 5.8 %collective-permute-start.5 = (bf16[1,8,4096]{2,1,0:T(8,128)(2,1)S(1)}, bf16[1,8,4096]{2,1,0:T(8,128)(2,1)S(1)}, u32[]{:S(2)}, u32[]{:S(2)}) collective-permute-start(bf16[1,8,4096]{2,1,0:T(8,128)(2,1)S(1)} %select_bitcast_fusion.1), channel_id=1, source_target_pairs={{0,16},{8,24},{16,0},{24,8},{1,17},{9,25},{17,1},{25,9},{2,18},{10... | collective-permute-start | bytes 196616 | tf_op jit(solution)/shard_map/ppermute | solution.py:232
  33.5 7.3 %collective-permute-start.15 = (bf16[1,8,4096]{2,1,0:T(8,128)(2,1)S(1)}, bf16[1,8,4096]{2,1,0:T(8,128)(2,1)S(1)}, u32[]{:S(2)}, u32[]{:S(2)}) collective-permute-start(bf16[1,8,4096]{2,1,0:T(8,128)(2,1)S(1)} %get-tuple-element.21), channel_id=1, source_target_pairs={{0,32},{32,64},{64,96},{96,128},{128,160},{160,192},{192,224},{224... | collective-permute-start | bytes 196616 | tf_op jit(solution)/shard_map/ppermute | solution.py:232
  35.3 6.0 %collective-permute-start.16 = (bf16[1,8,4096]{2,1,0:T(8,128)(2,1)S(1)}, bf16[1,8,4096]{2,1,0:T(8,128)(2,1)S(1)}, u32[]{:S(2)}, u32[]{:S(2)}) collective-permute-start(bf16[1,8,4096]{2,1,0:T(8,128)(2,1)S(1)} %get-tuple-element.21), channel_id=1, source_target_pairs={{0,224},{32,0},{64,32},{96,64},{128,96},{160,128},{192,160},{224,1... | collective-permute-start | bytes 196616 | tf_op jit(solution)/shard_map/ppermute | solution.py:232
  37.4 15.2 %collective-permute-start.6 = (bf16[4,8,4096]{2,1,0:T(8,128)(2,1)S(1)}, bf16[4,8,4096]{2,1,0:T(8,128)(2,1)S(1)}, u32[]{:S(2)}, u32[]{:S(2)}) collective-permute-start(bf16[4,8,4096]{2,1,0:T(8,128)(2,1)S(1)} %pad_maximum_fusion.1.refs_3_), channel_id=1, source_target_pairs={{0,32},{32,64},{64,96},{96,128},{128,160},{160,192},{192,224},{224... | collective-permute-start | bytes 786440 | tf_op jit(solution)/shard_map/ppermute | solution.py:232
  39.2 22.1 %collective-permute-start.7 = (bf16[4,8,4096]{2,1,0:T(8,128)(2,1)S(1)}, bf16[4,8,4096]{2,1,0:T(8,128)(2,1)S(1)}, u32[]{:S(2)}, u32[]{:S(2)}) collective-permute-start(bf16[4,8,4096]{2,1,0:T(8,128)(2,1)S(1)} %pad_maximum_fusion.1.refs_3_), channel_id=1, source_target_pairs={{0,224},{32,0},{64,32},{96,64},{128,96},{160,128},{192,160},{224,1... | collective-permute-start | bytes 786440 | tf_op jit(solution)/shard_map/ppermute | solution.py:232
  40.7 5.7 %collective-permute-start.17 = (bf16[1,8,4096]{2,1,0:T(8,128)(2,1)S(1)}, bf16[1,8,4096]{2,1,0:T(8,128)(2,1)S(1)}, u32[]{:S(2)}, u32[]{:S(2)}) collective-permute-start(bf16[1,8,4096]{2,1,0:T(8,128)(2,1)S(1)} %collective-permute-done.15), channel_id=1, source_target_pairs={{0,32},{32,64},{64,96},{96,128},{128,160},{160,192},{192,224},{224... | collective-permute-start | bytes 196616 | tf_op jit(solution)/shard_map/ppermute | solution.py:232
  41.3 5.3 %collective-permute-start.18 = (bf16[1,8,4096]{2,1,0:T(8,128)(2,1)S(1)}, bf16[1,8,4096]{2,1,0:T(8,128)(2,1)S(1)}, u32[]{:S(2)}, u32[]{:S(2)}) collective-permute-start(bf16[1,8,4096]{2,1,0:T(8,128)(2,1)S(1)} %collective-permute-done.16), channel_id=1, source_target_pairs={{0,224},{32,0},{64,32},{96,64},{128,96},{160,128},{192,160},{224,1... | collective-permute-start | bytes 196616 | tf_op jit(solution)/shard_map/ppermute | solution.py:232
  46.5 6.1 %collective-permute-start.19 = (bf16[1,8,4096]{2,1,0:T(8,128)(2,1)S(1)}, bf16[1,8,4096]{2,1,0:T(8,128)(2,1)S(1)}, u32[]{:S(2)}, u32[]{:S(2)}) collective-permute-start(bf16[1,8,4096]{2,1,0:T(8,128)(2,1)S(1)} %collective-permute-done.17), channel_id=1, source_target_pairs={{0,32},{32,64},{64,96},{96,128},{128,160},{160,192},{192,224},{224... | collective-permute-start | bytes 196616 | tf_op jit(solution)/shard_map/ppermute | solution.py:232
  46.6 6.1 %collective-permute-start.20 = (bf16[1,8,4096]{2,1,0:T(8,128)(2,1)S(1)}, bf16[1,8,4096]{2,1,0:T(8,128)(2,1)S(1)}, u32[]{:S(2)}, u32[]{:S(2)}) collective-permute-start(bf16[1,8,4096]{2,1,0:T(8,128)(2,1)S(1)} %collective-permute-done.18), channel_id=1, source_target_pairs={{0,224},{32,0},{64,32},{96,64},{128,96},{160,128},{192,160},{224,1... | collective-permute-start | bytes 196616 | tf_op jit(solution)/shard_map/ppermute | solution.py:232
  52.6 5.5 %collective-permute-start.21 = (bf16[1,8,4096]{2,1,0:T(8,128)(2,1)S(1)}, bf16[1,8,4096]{2,1,0:T(8,128)(2,1)S(1)}, u32[]{:S(2)}, u32[]{:S(2)}) collective-permute-start(bf16[1,8,4096]{2,1,0:T(8,128)(2,1)S(1)} %collective-permute-done.19), channel_id=1, source_target_pairs={{0,32},{32,64},{64,96},{96,128},{128,160},{160,192},{192,224},{224... | collective-permute-start | bytes 196616 | tf_op jit(solution)/shard_map/ppermute | solution.py:232
  52.7 10.7 %collective-permute-start.8 = (bf16[4,8,4096]{2,1,0:T(8,128)(2,1)S(1)}, bf16[4,8,4096]{2,1,0:T(8,128)(2,1)S(1)}, u32[]{:S(2)}, u32[]{:S(2)}) collective-permute-start(bf16[4,8,4096]{2,1,0:T(8,128)(2,1)S(1)} %collective-permute-done.6.refs_4_), channel_id=1, source_target_pairs={{0,32},{32,64},{64,96},{96,128},{128,160},{160,192},{192,224},{224... | collective-permute-start | bytes 786440 | tf_op jit(solution)/shard_map/ppermute | solution.py:232
  58.1 24.0 %collective-permute-start.22 = (bf16[8,8,4096]{2,1,0:T(8,128)(2,1)S(1)}, bf16[8,8,4096]{2,1,0:T(8,128)(2,1)S(1)}, u32[]{:S(2)}, u32[]{:S(2)}) collective-permute-start(bf16[8,8,4096]{2,1,0:T(8,128)(2,1)S(1)} %constant_dynamic-update-slice_fusion.refs_3_), channel_id=1, source_target_pairs={{0,8},{8,16},{16,24},{24,0},{1,9},{9,17},{17,25},{25,1},{2,10},{10... | collective-permute-start | bytes 1572872 | tf_op jit(solution)/shard_map/ppermute | solution.py:232
  58.1 24.0 %collective-permute-start.23 = (bf16[8,8,4096]{2,1,0:T(8,128)(2,1)S(1)}, bf16[8,8,4096]{2,1,0:T(8,128)(2,1)S(1)}, u32[]{:S(2)}, u32[]{:S(2)}) collective-permute-start(bf16[8,8,4096]{2,1,0:T(8,128)(2,1)S(1)} %constant_dynamic-update-slice_fusion.refs_3_), channel_id=1, source_target_pairs={{0,24},{8,0},{16,8},{24,16},{1,25},{9,1},{17,9},{25,17},{2,26},{10... | collective-permute-start | bytes 1572872 | tf_op jit(solution)/shard_map/ppermute | solution.py:232
  61.3 7.6 %collective-permute-start.9 = (bf16[4,8,4096]{2,1,0:T(8,128)(2,1)S(1)}, bf16[4,8,4096]{2,1,0:T(8,128)(2,1)S(1)}, u32[]{:S(2)}, u32[]{:S(2)}) collective-permute-start(bf16[4,8,4096]{2,1,0:T(8,128)(2,1)S(1)} %collective-permute-done.7.refs_5_), channel_id=1, source_target_pairs={{0,224},{32,0},{64,32},{96,64},{128,96},{160,128},{192,160},{224,1... | collective-permute-start | bytes 786440 | tf_op jit(solution)/shard_map/ppermute | solution.py:232
  63.4 7.6 %collective-permute-start.10 = (bf16[4,8,4096]{2,1,0:T(8,128)(2,1)S(1)}, bf16[4,8,4096]{2,1,0:T(8,128)(2,1)S(1)}, u32[]{:S(2)}, u32[]{:S(2)}) collective-permute-start(bf16[4,8,4096]{2,1,0:T(8,128)(2,1)S(1)} %collective-permute-done.8.refs_6_), channel_id=1, source_target_pairs={{0,32},{32,64},{64,96},{96,128},{128,160},{160,192},{192,224},{224... | collective-permute-start | bytes 786440 | tf_op jit(solution)/shard_map/ppermute | solution.py:232
  63.5 17.1 %collective-permute-start.24 = (bf16[4,8,4096]{2,1,0:T(8,128)(2,1)S(1)}, bf16[4,8,4096]{2,1,0:T(8,128)(2,1)S(1)}, u32[]{:S(2)}, u32[]{:S(2)}) collective-permute-start(bf16[4,8,4096]{2,1,0:T(8,128)(2,1)S(1)} %pad_maximum_fusion.2), channel_id=1, source_target_pairs={{0,16},{8,24},{16,0},{24,8},{1,17},{9,25},{17,1},{25,9},{2,18},{10... | collective-permute-start | bytes 786440 | tf_op jit(solution)/shard_map/ppermute | solution.py:232
  68.9 13.2 %collective-permute-start.25 = (bf16[4,8,4096]{2,1,0:T(8,128)(2,1)S(1)}, bf16[4,8,4096]{2,1,0:T(8,128)(2,1)S(1)}, u32[]{:S(2)}, u32[]{:S(2)}) collective-permute-start(bf16[4,8,4096]{2,1,0:T(8,128)(2,1)S(1)} %pad_maximum_fusion.3), channel_id=1, source_target_pairs={{0,16},{8,24},{16,0},{24,8},{1,17},{9,25},{17,1},{25,9},{2,18},{10... | collective-permute-start | bytes 786440 | tf_op jit(solution)/shard_map/ppermute | solution.py:232
  71.0 7.8 %collective-permute-start.11 = (bf16[4,8,4096]{2,1,0:T(8,128)(2,1)S(1)}, bf16[4,8,4096]{2,1,0:T(8,128)(2,1)S(1)}, u32[]{:S(2)}, u32[]{:S(2)}) collective-permute-start(bf16[4,8,4096]{2,1,0:T(8,128)(2,1)S(1)} %collective-permute-done.9.refs_7_), channel_id=1, source_target_pairs={{0,224},{32,0},{64,32},{96,64},{128,96},{160,128},{192,160},{224,1... | collective-permute-start | bytes 786440 | tf_op jit(solution)/shard_map/ppermute | solution.py:232
  74.7 3.7 %copy-start = (bf16[9,128,4096]{2,1,0:T(8,128)(2,1)}, bf16[9,128,4096]{2,1,0:T(8,128)(2,1)S(1)}, u32[]{:S(2)}) copy-start(bf16[9,128,4096]{2,1,0:T(8,128)(2,1)S(1)} %get-tuple-element.12.refs_1_) | copy-start | bytes 28311556
  78.8 15.6 %collective-permute-start.12 = (bf16[2,8,4096]{2,1,0:T(8,128)(2,1)S(1)}, bf16[2,8,4096]{2,1,0:T(8,128)(2,1)S(1)}, u32[]{:S(2)}, u32[]{:S(2)}) collective-permute-start(bf16[2,8,4096]{2,1,0:T(8,128)(2,1)S(1)} %slice.12), channel_id=1, source_target_pairs={{0,32},{32,64},{64,96},{96,128},{128,160},{160,192},{192,224},{224... | collective-permute-start | bytes 393224 | tf_op jit(solution)/shard_map/ppermute | solution.py:232
  80.5 13.8 %collective-permute-start.13 = (bf16[2,8,4096]{2,1,0:T(8,128)(2,1)S(1)}, bf16[2,8,4096]{2,1,0:T(8,128)(2,1)S(1)}, u32[]{:S(2)}, u32[]{:S(2)}) collective-permute-start(bf16[2,8,4096]{2,1,0:T(8,128)(2,1)S(1)} %slice.13), channel_id=1, source_target_pairs={{0,224},{32,0},{64,32},{96,64},{128,96},{160,128},{192,160},{224,1... | collective-permute-start | bytes 393224 | tf_op jit(solution)/shard_map/ppermute | solution.py:232
  92.0 15.0 %collective-permute-start.26 = (f32[9,64,256]{2,1,0:T(8,128)S(1)}, f32[9,64,256]{2,1,0:T(8,128)S(1)}, u32[]{:S(2)}, u32[]{:S(2)}) collective-permute-start(f32[9,64,256]{2,1,0:T(8,128)S(1)} %get-tuple-element.19), channel_id=1, source_target_pairs={{0,4},{4,0},{1,5},{5,1},{2,6},{6,2},{3,7},{7,3},{8,12},{12,8},{9,1... | collective-permute-start | bytes 1769480 | tf_op jit(solution)/shard_map/ppermute | solution.py:297
  104.9 11.7 %collective-permute-start.14 = (f32[9,64,256]{2,1,0:T(8,128)}, f32[9,64,256]{2,1,0:T(8,128)S(1)}, u32[]{:S(2)}, u32[]{:S(2)}) collective-permute-start(f32[9,64,256]{2,1,0:T(8,128)} %get-tuple-element.17), channel_id=1, source_target_pairs={{0,4},{4,0},{1,5},{5,1},{2,6},{6,2},{3,7},{7,3},{8,12},{12,8},{9,1... | collective-permute-start | bytes 1769480 | tf_op jit(solution)/shard_map/ppermute | solution.py:295
where the time goes:
time: 119 us
  starting transfers between devices  42 us (35%)
  waiting for transfers between devices  34 us (29%)
  Pallas kernels  28.4 us (24%)
  blocking collectives  8.08 us (7%)
  local copies, waits for them, and re-layouts  5.26 us (4%)
    ppermute x22, starting transfers between devices, around(): lax.ppermute(value, axis, [(i, (i + step) % size) for i in range(size)])  27.4 us
    pallas_call x2, Pallas kernels, run_moments(): pl.pallas_call(body, grid=(lags // group,), in_specs=[pl.BlockSpec(memory...  20.4 us
    ppermute x22, waiting for transfers between devices, around(): lax.ppermute(value, axis, [(i, (i + step) % size) for i in range(size)])  18.7 us
    ppermute x1, waiting for transfers between devices, shards(): got_a = lax.ppermute(send_a, 'yh', [(0, 1), (1, 0)])  9.68 us
    ppermute x2, starting transfers between devices, spread(): return lax.ppermute(value, ('z', 'yl', 'core'), pairs)  8.47 us
    all_gather x1, blocking collectives, shards(): everything = lax.all_gather(raw, ('yl', 'core'), axis=0, tiled=False)  8.08 us
    ppermute x2, waiting for transfers between devices, spread(): return lax.ppermute(value, ('z', 'yl', 'core'), pairs)  5.65 us
    unnamed x8, local copies, waits for them, and re-layouts  3.69 us
  transfers between devices with their start and end apart: 27, of which 10 were waited for; matrix products, arithmetic and copies ran while one was open for 1% of the time, Pallas kernels for 20%

commit v1 on v0

v1 whole, which is shorter than its diff:
```python
import jax
import jax.numpy as jnp
import numpy as np
from jax import lax
from jax.experimental import pallas as pl
from jax.experimental.pallas import tpu as pltpu
from jax.sharding import Mesh, PartitionSpec as P

LAGS = 9
REACH = 4
HALF = 32
NT = (((1,), (1,)), ((), ()))
MB = 1 << 20
SENT = jnp.float16
SCALE = 65536.0
SWAP = [(0, 1), (1, 0)]


def filter_kernel(place, raw, taps, out, first, second, mine, blocks, weights, line):
    parts, rows, bins = raw.shape
    per = bins // 128
    count = parts * per
    blocks[0] = jnp.zeros((rows, 128), jnp.bfloat16)
    blocks[count + 1] = jnp.zeros((rows, 128), jnp.bfloat16)
    for q in range(parts):
        for b in range(per):
            blocks[1 + q * per + b] = raw[q, :, b * 128 : (b + 1) * 128]
    line[...] = jnp.zeros(line.shape, jnp.float32)
    line[0:1, 0 : taps.shape[1]] = taps[...]
    wide = jnp.broadcast_to(line[0:1, :], (128, 384))
    band = pltpu.roll(wide, 128 - HALF, axis=1, stride=1, stride_axis=0)
    high = band.astype(jnp.bfloat16)
    rest = band - high.astype(jnp.float32)
    middle = rest.astype(jnp.bfloat16)
    low = (rest - middle.astype(jnp.float32)).astype(jnp.bfloat16)
    weights[0:128] = high
    weights[128:256] = middle
    weights[256:384] = low
    group = 8
    for g in range(count // group):
        total = None
        for k in range(3):
            piece = blocks[g * group + k : g * group + k + group].reshape(group * rows, 128)
            term = lax.dot_general(
                piece, weights[:, k * 128 : (k + 1) * 128], NT, preferred_element_type=jnp.float32
            )
            total = term if total is None else total + term
        value = (total[:, 256:384] + total[:, 128:256]) + total[:, 0:128]
        value = value.astype(jnp.bfloat16)
        for b in range(group):
            n = g * group + b
            out[:, n * 128 : (n + 1) * 128] = value[b * rows : (b + 1) * rows]
    at = pl.multiple_of(place[0], 8)
    first[...] = out[pl.ds(at, 8), :]
    at = pl.multiple_of(place[1], 8)
    second[...] = out[pl.ds(at, 8), :]
    at = pl.multiple_of(place[2], 128)
    mine[...] = out[:, pl.ds(at, bins)]


def run_filter(place, raw, taps):
    parts, rows, bins = raw.shape
    vmem = pl.BlockSpec(memory_space=pltpu.VMEM)
    return pl.pallas_call(
        filter_kernel,
        in_specs=[pl.BlockSpec(memory_space=pltpu.SMEM), vmem, vmem],
        out_specs=[vmem, vmem, vmem, vmem],
        out_shape=[
            jax.ShapeDtypeStruct((rows, parts * bins), jnp.bfloat16),
            jax.ShapeDtypeStruct((8, parts * bins), jnp.bfloat16),
            jax.ShapeDtypeStruct((8, parts * bins), jnp.bfloat16),
            jax.ShapeDtypeStruct((rows, bins), jnp.bfloat16),
        ],
        scratch_shapes=[
            pltpu.VMEM((parts * bins // 128 + 2, rows, 128), jnp.bfloat16),
            pltpu.VMEM((384, 384), jnp.bfloat16),
            pltpu.VMEM((8, 384), jnp.float32),
        ],
        compiler_params=pltpu.CompilerParams(vmem_limit_bytes=8 * MB),
        name="fir",
    )(place, raw, taps)


def lag_kernel(rows_ref, out, energy):
    bins = rows_ref.shape[1]
    at = lax.broadcasted_iota(jnp.int32, (16, bins), 1)
    for part in range(rows_ref.shape[0] // 16):
        span = slice(part * 16, (part + 1) * 16)
        value = rows_ref[span].astype(jnp.float32)
        total = jnp.sum(value * value, axis=1, keepdims=True)
        energy[span] = jnp.broadcast_to(total, (16, 128))
        for lag in range(LAGS):
            step = lag - REACH
            if step == 0:
                moved = value
            else:
                moved = pltpu.roll(value, step % bins, axis=1)
                inside = at >= step if step > 0 else at < bins + step
                moved = jnp.where(inside, moved, 0.0)
            out[lag, span] = moved.astype(jnp.bfloat16)


def run_lags(rows):
    count, bins = rows.shape
    vmem = pl.BlockSpec(memory_space=pltpu.VMEM)
    return pl.pallas_call(
        lag_kernel,
        in_specs=[vmem],
        out_specs=[vmem, vmem],
        out_shape=[
            jax.ShapeDtypeStruct((LAGS, count, bins), jnp.bfloat16),
            jax.ShapeDtypeStruct((count, 128), jnp.float32),
        ],
        compiler_params=pltpu.CompilerParams(vmem_limit_bytes=8 * MB),
        cost_estimate=pl.CostEstimate(flops=10 * MB, bytes_accessed=6 * MB, transcendentals=0),
        name="lags",
    )(rows)


def weigh(lagged, energy, columns, across, emit):
    lags, count, bins = lagged.shape
    left = lagged[...].reshape(lags * count, bins)
    right = columns[...].reshape(-1, bins)
    moments = lax.dot_general(left, right, NT, preferred_element_type=jnp.float32)
    norms = (1.0 / jnp.sqrt(energy[:, 0:1] + 1e-05)) * across
    for lag in range(lags):
        ratio = moments[lag * count : (lag + 1) * count] * norms
        emit(lag, -0.5 * jnp.log(1.0 - ratio * ratio))


def partner_kernel(steps, place, lagged, energy, *rest):
    units = rest[: len(steps)]
    send, columns, scale, sems = rest[len(steps) :]
    width = columns.shape[0] * columns.shape[1]
    z = place[3]
    x = place[4]
    copies = []
    for ref, moves in zip(units, steps):
        for k, (x_step, z_step) in enumerate(moves):
            slot = ((x + x_step) & 3) * 8 + ((z + z_step) & 7)
            copies.append(pltpu.make_async_copy(ref.at[k], columns.at[slot], sems.at[len(copies)]))
    for copy in copies:
        copy.start()
    for copy in copies:
        copy.wait()
    for g in range(width // 128):
        block = columns[g * 16 : (g + 1) * 16].astype(jnp.float32).reshape(128, -1)
        total = jnp.sum(block * block, axis=1, keepdims=True)
        root = 0.8 / jnp.sqrt(total + 1e-05)
        root = jnp.transpose(jnp.broadcast_to(root, (128, 128)))
        scale[:, g * 128 : (g + 1) * 128] = root[0:8]

    def emit(lag, value):
        send[lag] = value * SCALE

    weigh(lagged, energy, columns, scale[0:1, :], emit)


def run_partner(place, lagged, energy, units, steps):
    slots = sum(len(moves) for moves in steps)
    lags, count, bins = lagged.shape
    width = slots * 8

    def body(*refs):
        partner_kernel(steps, *refs)

    vmem = pl.BlockSpec(memory_space=pltpu.VMEM)
    return pl.pallas_call(
        body,
        in_specs=[pl.BlockSpec(memory_space=pltpu.SMEM), vmem, vmem]
        + [pl.BlockSpec(memory_space=pl.ANY)] * len(units),
        out_specs=[vmem, vmem, vmem],
        out_shape=[
            jax.ShapeDtypeStruct((lags, count, width), jnp.float32),
            jax.ShapeDtypeStruct((slots, 8, bins), jnp.bfloat16),
            jax.ShapeDtypeStruct((8, width), jnp.float32),
        ],
        scratch_shapes=[pltpu.SemaphoreType.DMA((slots,))],
        compiler_params=pltpu.CompilerParams(vmem_limit_bytes=8 * MB),
        cost_estimate=pl.CostEstimate(
            flops=2 * lags * count * width * bins,
            bytes_accessed=2 * bins * width,
            transcendentals=lags * count * width,
        ),
        name="partner",
    )(place, lagged, energy, *units)


def own_kernel(lagged, energy, columns_a, scale_a, columns_b, scale_b, out_a, out_b):
    for columns, scale, out in ((columns_a, scale_a, out_a), (columns_b, scale_b, out_b)):

        def emit(lag, value):
            out[lag] = value

        weigh(lagged, energy, columns, scale[0:1, :], emit)


def run_own(lagged, energy, columns_a, scale_a, columns_b, scale_b):
    lags, count, bins = lagged.shape
    width = scale_a.shape[1]
    vmem = pl.BlockSpec(memory_space=pltpu.VMEM)
    shape = jax.ShapeDtypeStruct((lags, count, width), jnp.float32)
    return pl.pallas_call(
        own_kernel,
        in_specs=[vmem] * 6,
        out_specs=[vmem, vmem],
        out_shape=[shape, shape],
        compiler_params=pltpu.CompilerParams(vmem_limit_bytes=8 * MB),
        cost_estimate=pl.CostEstimate(
            flops=4 * lags * count * width * bins,
            bytes_accessed=4 * lags * count * width,
            transcendentals=2 * lags * count * width,
        ),
        name="own",
    )(lagged, energy, columns_a, scale_a, columns_b, scale_b)


def join_kernel(place, own_a, got_a, own_b, got_b, out):
    low = place[5] == 0
    lane = lax.broadcasted_iota(jnp.int32, own_a.shape[1:2] + (128,), 1) < 64
    for half, (own, got) in enumerate(((own_a, got_a), (own_b, got_b))):
        for lag in range(own.shape[0]):
            for tile in range(own.shape[2] // 128):
                span = slice(tile * 128, (tile + 1) * 128)
                here = own[lag, :, span]
                there = got[lag, :, span] * (1.0 / SCALE)
                one = jnp.where(low, here, there)
                two = jnp.where(low, there, here)
                base = half * 512 + tile * 256
                out[lag, :, base : base + 128] = jnp.where(lane, one, pltpu.roll(two, 64, axis=1))
                out[lag, :, base + 128 : base + 256] = jnp.where(
                    lane, pltpu.roll(one, 64, axis=1), two
                )


def run_join(place, own_a, got_a, own_b, got_b):
    lags, rows, width = own_a.shape
    spec = pl.BlockSpec((3, rows, width), lambda i: (i, 0, 0))
    return pl.pallas_call(
        join_kernel,
        grid=(lags // 3,),
        in_specs=[pl.BlockSpec(memory_space=pltpu.SMEM)] + [spec] * 4,
        out_specs=pl.BlockSpec((3, rows, 4 * width), lambda i: (i, 0, 0)),
        out_shape=jax.ShapeDtypeStruct((lags, rows, 4 * width), jnp.float32),
        compiler_params=pltpu.CompilerParams(vmem_limit_bytes=8 * MB),
        name="join",
    )(place, own_a, got_a, own_b, got_b)


def around(value, axis, step):
    size = lax.axis_size(axis)
    return lax.ppermute(value, axis, [(i, (i + step) % size) for i in range(size)])


def swap_half(value):
    return lax.ppermute(value.astype(SENT), "yh", SWAP).astype(jnp.float32)


def spread(value, odd):
    pairs = []
    for z in range(8):
        for q in range(4):
            j = (z & 1) ^ odd
            pairs.append((z * 4 + q, (2 * q + j) * 4 + (z >> 1)))
    return lax.ppermute(value, ("z", "yl", "core"), pairs)


def shards(raw, taps):
    z = lax.axis_index("z")
    x = lax.axis_index("x")
    yh = lax.axis_index("yh")
    q = lax.axis_index(("yl", "core"))
    e = z % 2
    bins = raw.shape[1]
    everything = lax.all_gather(raw, ("yl", "core"), axis=0, tiled=False)
    place = [16 * q + 8 * e, 16 * q + 8 * (1 - e), q * bins, z, x, yh]
    place = jnp.stack(place).astype(jnp.int32)
    full, first, second, mine = run_filter(place, everything, taps.reshape(1, -1))
    one = spread(first, 0)
    two = spread(second, 1)
    unit_a = jnp.where(e == 0, one, two)[None]
    unit_b = jnp.where(e == 0, two, one)[None]
    x_steps = (0, -1, 1, 2)
    near = [unit_a, around(unit_a, "x", 1), around(unit_a, "x", -1), around(unit_a, "x", 2)]
    base_a = jnp.concatenate(near, axis=0)
    units_a, steps_a = [base_a], [[(k, 0) for k in x_steps]]
    up = down = base_a
    for step in (1, 2, 3):
        up = around(up, "z", 1)
        down = around(down, "z", -1)
        units_a += [up, down]
        steps_a += [[(k, -step) for k in x_steps], [(k, step) for k in x_steps]]
    units_a += [around(up[0:2], "z", 1), around(down[2:4], "z", -1)]
    steps_a += [[(k, 4) for k in x_steps[0:2]], [(k, 4) for k in x_steps[2:4]]]
    up = down = unit_b
    near, z_steps = [unit_b], [0]
    for step in (1, 2, 3):
        up = around(up, "z", 1)
        down = around(down, "z", -1)
        near += [up, down]
        z_steps += [-step, step]
    near.append(around(up, "z", 1))
    z_steps.append(4)
    base_b = jnp.concatenate(near, axis=0)
    units_b = [
        base_b,
        around(base_b, "x", 1),
        around(base_b, "x", -1),
        around(base_b[0:4], "x", 2),
        around(base_b[4:8], "x", -2),
    ]
    steps_b = [[(k, d) for d in z_steps] for k in (0, -1, 1)]
    steps_b += [[(2, d) for d in z_steps[0:4]], [(2, d) for d in z_steps[4:8]]]
    partner = lax.ppermute(full, "yh", SWAP)
    lagged, energy = run_lags(full)
    far_lagged, far_energy = run_lags(partner)
    send_a, columns_a, scale_a = run_partner(place, far_lagged, far_energy, units_a, steps_a)
    got_a = swap_half(send_a)
    send_b, columns_b, scale_b = run_partner(place, far_lagged, far_energy, units_b, steps_b)
    got_b = swap_half(send_b)
    own_a, own_b = run_own(lagged, energy, columns_a, scale_a, columns_b, scale_b)
    information = run_join(place, own_a, got_a, own_b, got_b)
    return (information, mine)


def solution(mesh):
    fine = Mesh(mesh.devices.reshape(8, 4, 2, 2, 2), ("z", "x", "yh", "yl", "core"))
    rows, bins = ("z", "x", "yh"), ("yl", "core")
    return jax.shard_map(
        shards,
        mesh=fine,
        in_specs=(P(rows, bins), P()),
        out_specs=(P(None, rows, bins), P(rows, bins)),
        check_vma=False,
    )
```

time: 119 us -> 121 us (1.017)
  the two profiles are of different devices: /device:TPU:8 before, /device:TPU:2 now
where the time goes in v1:
time: 121 us
  starting transfers between devices  49.1 us (41%)
  waiting for transfers between devices  39.9 us (33%)
  Pallas kernels  22.3 us (18%)
  blocking collectives  7.47 us (6%)
    ppermute x22, starting transfers between devices, around(): lax.ppermute(value, axis, [(i, (i + step) % size) for i in range(size)])  39.6 us
    ppermute x22, waiting for transfers between devices, around(): lax.ppermute(value, axis, [(i, (i + step) % size) for i in range(size)])  36.4 us
    pallas_call x2, Pallas kernels, run_partner(): pl.pallas_call(body, in_specs=[pl.BlockSpec(memory_space=pltpu.SMEM), vme...  11.4 us
    all_gather x1, blocking collectives, shards(): everything = lax.all_gather(raw, ('yl', 'core'), axis=0, tiled=False)  7.47 us
    ppermute x2, starting transfers between devices, swap_half(): return lax.ppermute(value.astype(SENT), 'yh', SWAP).astype(jnp.float32)  3.92 us
    ppermute x2, waiting for transfers between devices, swap_half(): return lax.ppermute(value.astype(SENT), 'yh', SWAP).astype(jnp.float32)  3.54 us
    ppermute x1, starting transfers between devices, shards(): partner = lax.ppermute(full, 'yh', SWAP)  2.9 us
    pallas_call x1, Pallas kernels, run_join(): pl.pallas_call(join_kernel, grid=(lags // 3,), in_specs=[pl.BlockSpec(mem...  2.89 us
  transfers between devices with their start and end apart: 27, of which 8 were waited for; matrix products, arithmetic and copies ran while one was open for 0% of the time, Pallas kernels for 14%

profile of v1, /device:TPU:2, one launch (start us, length us, event | category | flops | bytes accessed | tf_op | source)
XLA Modules:
  0.0 120.8 jit_solution(18372022147893209120)
XLA Ops:
  0.7 7.5 %all-gather = bf16[256,1024]{1,0:T(8,128)(2,1)S(1)} all-gather(bf16[64,1024]{1,0:T(8,128)(2,1)} %param.2), channel_id=2, replica_groups=mesh['z'=8,'x'=4,'yh'=2,'yl'=2,'core'=2] {'yl','core'}, dimensions={0}, use_global_device_ids=true | all-gather | bytes 655360 | tf_op jit(solution)/shard_map/all_gather | solution.py:275
  8.9 2.7 %fir.1 = (bf16[64,4096]{1,0:T(8,128)(2,1)S(1)}, bf16[8,4096]{1,0:T(8,128)(2,1)S(1)}, bf16[8,4096]{1,0:T(8,128)(2,1)S(1)}, bf16[64,1024]{1,0:T(8,128)(2,1)}) custom-call(s32[6]{0:T(128)S(1)} %stack.27.place.refs_0_, bf16[4,64,1024]{2,1,0:T(8,128)(2,1)S(1)} %bitcast.13, f32[1,65]{1,0:T(1,128)S(1)} %bitcast.14), custom_call_target="tpu_custom_call" | custom-call | tf_op jit(solution)/shard_map/fir/pallas_call | solution.py:64
  12.3 2.0 %collective-permute-start.2 = (bf16[8,4096]{1,0:T(8,128)(2,1)S(1)}, bf16[8,4096]{1,0:T(8,128)(2,1)S(1)}, u32[]{:S(2)}, u32[]{:S(2)}) collective-permute-start(bf16[8,4096]{1,0:T(8,128)(2,1)S(1)} %get-tuple-element.24), channel_id=1, source_target_pairs={{0,32},{1,96},{2,160},{3,224},{32,0},{33,64},{34,128},{35,192},{64... | collective-permute-start | bytes 196616 | tf_op jit(solution)/shard_map/ppermute | solution.py:265
  14.3 2.9 %collective-permute-start = (bf16[64,4096]{1,0:T(8,128)(2,1)S(1)}, bf16[64,4096]{1,0:T(8,128)(2,1)S(1)}, u32[]{:S(2)}, u32[]{:S(2)}) collective-permute-start(bf16[64,4096]{1,0:T(8,128)(2,1)S(1)} %get-tuple-element.18.rows_ref), channel_id=1, source_target_pairs={{0,4},{4,0},{1,5},{5,1},{2,6},{6,2},{3,7},{7,3},{8,12},{12,8},{9,1... | collective-permute-start | bytes 1572872 | tf_op jit(solution)/shard_map/ppermute | solution.py:314
  17.2 2.2 %collective-permute-start.5 = (bf16[1,8,4096]{2,1,0:T(8,128)(2,1)S(1)}, bf16[1,8,4096]{2,1,0:T(8,128)(2,1)S(1)}, u32[]{:S(2)}, u32[]{:S(2)}) collective-permute-start(bf16[1,8,4096]{2,1,0:T(8,128)(2,1)S(1)} %select_bitcast_fusion.1), channel_id=1, source_target_pairs={{0,16},{8,24},{16,0},{24,8},{1,17},{9,25},{17,1},{25,9},{2,18},{10... | collective-permute-start | bytes 196616 | tf_op jit(solution)/shard_map/ppermute | solution.py:252
  19.4 1.4 %collective-permute-start.4 = (bf16[1,8,4096]{2,1,0:T(8,128)(2,1)S(1)}, bf16[1,8,4096]{2,1,0:T(8,128)(2,1)S(1)}, u32[]{:S(2)}, u32[]{:S(2)}) collective-permute-start(bf16[1,8,4096]{2,1,0:T(8,128)(2,1)S(1)} %select_bitcast_fusion.1), channel_id=1, source_target_pairs={{0,24},{8,0},{16,8},{24,16},{1,25},{9,1},{17,9},{25,17},{2,26},{10... | collective-permute-start | bytes 196616 | tf_op jit(solution)/shard_map/ppermute | solution.py:252
  21.4 13.4 %collective-permute-start.15 = (bf16[1,8,4096]{2,1,0:T(8,128)(2,1)S(1)}, bf16[1,8,4096]{2,1,0:T(8,128)(2,1)S(1)}, u32[]{:S(2)}, u32[]{:S(2)}) collective-permute-start(bf16[1,8,4096]{2,1,0:T(8,128)(2,1)S(1)} %get-tuple-element.35), channel_id=1, source_target_pairs={{0,224},{32,0},{64,32},{96,64},{128,96},{160,128},{192,160},{224,1... | collective-permute-start | bytes 196616 | tf_op jit(solution)/shard_map/ppermute | solution.py:252
  34.9 3.6 %collective-permute-start.7 = (bf16[4,8,4096]{2,1,0:T(8,128)(2,1)S(1)}, bf16[4,8,4096]{2,1,0:T(8,128)(2,1)S(1)}, u32[]{:S(2)}, u32[]{:S(2)}) collective-permute-start(bf16[4,8,4096]{2,1,0:T(8,128)(2,1)S(1)} %pad_maximum_fusion.refs_3_), channel_id=1, source_target_pairs={{0,224},{32,0},{64,32},{96,64},{128,96},{160,128},{192,160},{224,1... | collective-permute-start | bytes 786440 | tf_op jit(solution)/shard_map/ppermute | solution.py:252
  38.6 3.2 %collective-permute-start.17 = (bf16[1,8,4096]{2,1,0:T(8,128)(2,1)S(1)}, bf16[1,8,4096]{2,1,0:T(8,128)(2,1)S(1)}, u32[]{:S(2)}, u32[]{:S(2)}) collective-permute-start(bf16[1,8,4096]{2,1,0:T(8,128)(2,1)S(1)} %collective-permute-done.15), channel_id=1, source_target_pairs={{0,224},{32,0},{64,32},{96,64},{128,96},{160,128},{192,160},{224,1... | collective-permute-start | bytes 196616 | tf_op jit(solution)/shard_map/ppermute | solution.py:252
  41.8 5.5 %collective-permute-done.16 = bf16[1,8,4096]{2,1,0:T(8,128)(2,1)S(1)} collective-permute-done((bf16[1,8,4096]{2,1,0:T(8,128)(2,1)S(1)}, bf16[1,8,4096]{2,1,0:T(8,128)(2,1)S(1)}, u32[]{:S(2)}, u32[]{:S(2)}) %collective-permute-start.16) | collective-permute-done | bytes 65568 | tf_op jit(solution)/shard_map/ppermute | solution.py:252
  47.4 2.5 %collective-permute-start.23 = (bf16[4,8,4096]{2,1,0:T(8,128)(2,1)S(1)}, bf16[4,8,4096]{2,1,0:T(8,128)(2,1)S(1)}, u32[]{:S(2)}, u32[]{:S(2)}) collective-permute-start(bf16[4,8,4096]{2,1,0:T(8,128)(2,1)S(1)} %pad_maximum_fusion.1), channel_id=1, source_target_pairs={{0,16},{8,24},{16,0},{24,8},{1,17},{9,25},{17,1},{25,9},{2,18},{10... | collective-permute-start | bytes 786440 | tf_op jit(solution)/shard_map/ppermute | solution.py:252
  50.0 5.4 %collective-permute-done.18 = bf16[1,8,4096]{2,1,0:T(8,128)(2,1)S(1)} collective-permute-done((bf16[1,8,4096]{2,1,0:T(8,128)(2,1)S(1)}, bf16[1,8,4096]{2,1,0:T(8,128)(2,1)S(1)}, u32[]{:S(2)}, u32[]{:S(2)}) %collective-permute-start.18) | collective-permute-done | bytes 65568 | tf_op jit(solution)/shard_map/ppermute | solution.py:252
  55.5 4.9 %collective-permute-done.19 = bf16[1,8,4096]{2,1,0:T(8,128)(2,1)S(1)} collective-permute-done((bf16[1,8,4096]{2,1,0:T(8,128)(2,1)S(1)}, bf16[1,8,4096]{2,1,0:T(8,128)(2,1)S(1)}, u32[]{:S(2)}, u32[]{:S(2)}) %collective-permute-start.19) | collective-permute-done | bytes 65568 | tf_op jit(solution)/shard_map/ppermute | solution.py:252
  60.4 3.2 %collective-permute-start.9 = (bf16[4,8,4096]{2,1,0:T(8,128)(2,1)S(1)}, bf16[4,8,4096]{2,1,0:T(8,128)(2,1)S(1)}, u32[]{:S(2)}, u32[]{:S(2)}) collective-permute-start(bf16[4,8,4096]{2,1,0:T(8,128)(2,1)S(1)} %collective-permute-done.7.refs_5_), channel_id=1, source_target_pairs={{0,224},{32,0},{64,32},{96,64},{128,96},{160,128},{192,160},{224,1... | collective-permute-start | bytes 786440 | tf_op jit(solution)/shard_map/ppermute | solution.py:252
  63.8 6.1 %collective-permute-done.9.refs_7_ = bf16[4,8,4096]{2,1,0:T(8,128)(2,1)S(1)} collective-permute-done((bf16[4,8,4096]{2,1,0:T(8,128)(2,1)S(1)}, bf16[4,8,4096]{2,1,0:T(8,128)(2,1)S(1)}, u32[]{:S(2)}, u32[]{:S(2)}) %collective-permute-start.9) | collective-permute-done | bytes 262176 | tf_op jit(solution)/shard_map/ppermute | solution.py:252
  69.8 3.7 %collective-permute-start.11 = (bf16[4,8,4096]{2,1,0:T(8,128)(2,1)S(1)}, bf16[4,8,4096]{2,1,0:T(8,128)(2,1)S(1)}, u32[]{:S(2)}, u32[]{:S(2)}) collective-permute-start(bf16[4,8,4096]{2,1,0:T(8,128)(2,1)S(1)} %collective-permute-done.9.refs_7_), channel_id=1, source_target_pairs={{0,224},{32,0},{64,32},{96,64},{128,96},{160,128},{192,160},{224,1... | collective-permute-start | bytes 786440 | tf_op jit(solution)/shard_map/ppermute | solution.py:252
  73.5 1.0 collective-permute-start.22
  74.6 1.1 collective-permute-start.21
  75.6 1.8 %collective-permute-done.11.refs_9_ = bf16[4,8,4096]{2,1,0:T(8,128)(2,1)S(1)} collective-permute-done((bf16[4,8,4096]{2,1,0:T(8,128)(2,1)S(1)}, bf16[4,8,4096]{2,1,0:T(8,128)(2,1)S(1)}, u32[]{:S(2)}, u32[]{:S(2)}) %collective-permute-start.11) | collective-permute-done | bytes 262176 | tf_op jit(solution)/shard_map/ppermute | solution.py:252
  77.5 9.4 %collective-permute-done.10.refs_8_ = bf16[4,8,4096]{2,1,0:T(8,128)(2,1)S(1)} collective-permute-done((bf16[4,8,4096]{2,1,0:T(8,128)(2,1)S(1)}, bf16[4,8,4096]{2,1,0:T(8,128)(2,1)S(1)}, u32[]{:S(2)}, u32[]{:S(2)}) %collective-permute-start.10) | collective-permute-done | bytes 262176 | tf_op jit(solution)/shard_map/ppermute | solution.py:252
  86.9 1.2 %collective-permute-start.24 = (bf16[4,8,4096]{2,1,0:T(8,128)(2,1)S(1)}, bf16[4,8,4096]{2,1,0:T(8,128)(2,1)S(1)}, u32[]{:S(2)}, u32[]{:S(2)}) collective-permute-start(bf16[4,8,4096]{2,1,0:T(8,128)(2,1)S(1)} %pad_maximum_fusion.2), channel_id=1, source_target_pairs={{0,16},{8,24},{16,0},{24,8},{1,17},{9,25},{17,1},{25,9},{2,18},{10... | collective-permute-start | bytes 786440 | tf_op jit(solution)/shard_map/ppermute | solution.py:252
  88.1 0.9 collective-permute-start.13
  89.1 1.2 collective-permute-start.12
  90.2 1.3 %lags.3 = (bf16[9,64,4096]{2,1,0:T(8,128)(2,1)S(1)}, f32[64,128]{1,0:T(8,128)S(1)}) custom-call(bf16[64,4096]{1,0:T(8,128)(2,1)S(1)} %collective-permute-done.rows_ref), custom_call_target="tpu_custom_call" | custom-call | flops 10485760 | bytes 6291456 | tf_op jit(solution)/shard_map/lags/pallas_call | solution.py:106
  91.5 3.2 %collective-permute-done.24.refs_7_ = bf16[4,8,4096]{2,1,0:T(8,128)(2,1)S(1)} collective-permute-done((bf16[4,8,4096]{2,1,0:T(8,128)(2,1)S(1)}, bf16[4,8,4096]{2,1,0:T(8,128)(2,1)S(1)}, u32[]{:S(2)}, u32[]{:S(2)}) %collective-permute-start.24) | collective-permute-done | bytes 262176 | tf_op jit(solution)/shard_map/ppermute | solution.py:252
  94.7 5.7 %partner.3 = (f32[9,64,256]{2,1,0:T(8,128)S(1)}, bf16[32,8,4096]{2,1,0:T(8,128)(2,1)S(1)}, f32[8,256]{1,0:T(8,128)S(1)}) custom-call(s32[6]{0:T(128)S(1)} %stack.27.place.refs_0_, bf16[9,64,4096]{2,1,0:T(8,128)(2,1)S(1)} %get-tuple-element.21.refs_1_, f32[64,128]{1,0:T(8,128)S(1)} %get-tuple-element.22.refs_2_, ...), custom_call_target="tpu_custom_call" | custom-call | flops 1207959552 | bytes 2097152 | tf_op jit(solution)/shard_map/partner/pallas_call | solution.py:168
  100.5 3.2 %collective-permute-start.26 = (f16[9,64,256]{2,1,0:T(8,128)(2,1)S(1)}, f16[9,64,256]{2,1,0:T(8,128)(2,1)S(1)}, u32[]{:S(2)}, u32[]{:S(2)}) collective-permute-start(f16[9,64,256]{2,1,0:T(8,128)(2,1)S(1)} %convert_element_type.14), channel_id=1, source_target_pairs={{0,4},{4,0},{1,5},{5,1},{2,6},{6,2},{3,7},{7,3},{8,12},{12,8},{9,1... | collective-permute-start | bytes 884744 | tf_op jit(solution)/shard_map/ppermute | solution.py:256
  103.7 5.8 %partner.2 = (f32[9,64,256]{2,1,0:T(8,128)S(1)}, bf16[32,8,4096]{2,1,0:T(8,128)(2,1)S(1)}, f32[8,256]{1,0:T(8,128)S(1)}) custom-call(s32[6]{0:T(128)S(1)} %stack.27.place.refs_0_, bf16[9,64,4096]{2,1,0:T(8,128)(2,1)S(1)} %get-tuple-element.21.refs_1_, f32[64,128]{1,0:T(8,128)S(1)} %get-tuple-element.22.refs_2_, ...), custom_call_target="tpu_custom_call" | custom-call | flops 1207959552 | bytes 2097152 | tf_op jit(solution)/shard_map/partner/pallas_call | solution.py:168
  110.2 1.3 %lags.2 = (bf16[9,64,4096]{2,1,0:T(8,128)(2,1)S(1)}, f32[64,128]{1,0:T(8,128)S(1)}) custom-call(bf16[64,4096]{1,0:T(8,128)(2,1)S(1)} %get-tuple-element.18.rows_ref), custom_call_target="tpu_custom_call" | custom-call | flops 10485760 | bytes 6291456 | tf_op jit(solution)/shard_map/lags/pallas_call | solution.py:106
  111.5 2.7 %own.1 = (f32[9,64,256]{2,1,0:T(8,128)S(1)}, f32[9,64,256]{2,1,0:T(8,128)S(1)}) custom-call(bf16[9,64,4096]{2,1,0:T(8,128)(2,1)S(1)} %get-tuple-element.19.lagged, f32[64,128]{1,0:T(8,128)S(1)} %get-tuple-element.20.energy, bf16[32,8,4096]{2,1,0:T(8,128)(2,1)S(1)} %get-tuple-element.25.columns_a, f32[8,256]{1,0:T(8,128)S(1)} %get-tuple-element.26.scale_a, ...), custom_call_target="tpu_custom_call" | custom-call | flops 2415919104 | bytes 589824 | tf_op jit(solution)/shard_map/own/pallas_call | solution.py:203
  114.3 3.5 %collective-permute-done.25 = f16[9,64,256]{2,1,0:T(8,128)(2,1)S(1)} collective-permute-done((f16[9,64,256]{2,1,0:T(8,128)(2,1)S(1)}, f16[9,64,256]{2,1,0:T(8,128)(2,1)S(1)}, u32[]{:S(2)}, u32[]{:S(2)}) %collective-permute-start.25) | collective-permute-done | bytes 294944 | tf_op jit(solution)/shard_map/ppermute | solution.py:256
  117.9 2.9 %join.1 = f32[9,64,1024]{2,1,0:T(8,128)} custom-call(s32[6]{0:T(128)S(1)} %stack.27.place.refs_0_, f32[9,64,256]{2,1,0:T(8,128)S(1)} %get-tuple-element.29.own_a, f32[9,64,256]{2,1,0:T(8,128)S(1)} %convert_element_type.13.got_a, f32[9,64,256]{2,1,0:T(8,128)S(1)} %get-tuple-element.31.own_b, f32[9,64,256]{2,1,0:T(8,128)S(1)} %convert_element_type.15.got_b), custom_call_target="tpu_custom_call" | custom-call | tf_op jit(solution)/shard_map/join/pallas_call | solution.py:239
  (51 shorter events, 3.3 us)
Async XLA Ops:
  8.2 0.7 copy-start
  11.6 5.6 %collective-permute-start.1 = (bf16[8,4096]{1,0:T(8,128)(2,1)S(1)}, bf16[8,4096]{1,0:T(8,128)(2,1)S(1)}, u32[]{:S(2)}, u32[]{:S(2)}) collective-permute-start(bf16[8,4096]{1,0:T(8,128)(2,1)S(1)} %get-tuple-element.23), channel_id=1, source_target_pairs={{0,0},{1,64},{2,128},{3,192},{32,32},{33,96},{34,160},{35,224},{64... | collective-permute-start | bytes 196616 | tf_op jit(solution)/shard_map/ppermute | solution.py:265
  12.3 4.9 %collective-permute-start.2 = (bf16[8,4096]{1,0:T(8,128)(2,1)S(1)}, bf16[8,4096]{1,0:T(8,128)(2,1)S(1)}, u32[]{:S(2)}, u32[]{:S(2)}) collective-permute-start(bf16[8,4096]{1,0:T(8,128)(2,1)S(1)} %get-tuple-element.24), channel_id=1, source_target_pairs={{0,32},{1,96},{2,160},{3,224},{32,0},{33,64},{34,128},{35,192},{64... | collective-permute-start | bytes 196616 | tf_op jit(solution)/shard_map/ppermute | solution.py:265
  14.3 74.8 %collective-permute-start = (bf16[64,4096]{1,0:T(8,128)(2,1)S(1)}, bf16[64,4096]{1,0:T(8,128)(2,1)S(1)}, u32[]{:S(2)}, u32[]{:S(2)}) collective-permute-start(bf16[64,4096]{1,0:T(8,128)(2,1)S(1)} %get-tuple-element.18.rows_ref), channel_id=1, source_target_pairs={{0,4},{4,0},{1,5},{5,1},{2,6},{6,2},{3,7},{7,3},{8,12},{12,8},{9,1... | collective-permute-start | bytes 1572872 | tf_op jit(solution)/shard_map/ppermute | solution.py:314
  17.2 17.7 %collective-permute-start.5 = (bf16[1,8,4096]{2,1,0:T(8,128)(2,1)S(1)}, bf16[1,8,4096]{2,1,0:T(8,128)(2,1)S(1)}, u32[]{:S(2)}, u32[]{:S(2)}) collective-permute-start(bf16[1,8,4096]{2,1,0:T(8,128)(2,1)S(1)} %select_bitcast_fusion.1), channel_id=1, source_target_pairs={{0,16},{8,24},{16,0},{24,8},{1,17},{9,25},{17,1},{25,9},{2,18},{10... | collective-permute-start | bytes 196616 | tf_op jit(solution)/shard_map/ppermute | solution.py:252
  19.4 15.5 %collective-permute-start.4 = (bf16[1,8,4096]{2,1,0:T(8,128)(2,1)S(1)}, bf16[1,8,4096]{2,1,0:T(8,128)(2,1)S(1)}, u32[]{:S(2)}, u32[]{:S(2)}) collective-permute-start(bf16[1,8,4096]{2,1,0:T(8,128)(2,1)S(1)} %select_bitcast_fusion.1), channel_id=1, source_target_pairs={{0,24},{8,0},{16,8},{24,16},{1,25},{9,1},{17,9},{25,17},{2,26},{10... | collective-permute-start | bytes 196616 | tf_op jit(solution)/shard_map/ppermute | solution.py:252
  20.8 14.0 %collective-permute-start.3 = (bf16[1,8,4096]{2,1,0:T(8,128)(2,1)S(1)}, bf16[1,8,4096]{2,1,0:T(8,128)(2,1)S(1)}, u32[]{:S(2)}, u32[]{:S(2)}) collective-permute-start(bf16[1,8,4096]{2,1,0:T(8,128)(2,1)S(1)} %select_bitcast_fusion.1), channel_id=1, source_target_pairs={{0,8},{8,16},{16,24},{24,0},{1,9},{9,17},{17,25},{25,1},{2,10},{10... | collective-permute-start | bytes 196616 | tf_op jit(solution)/shard_map/ppermute | solution.py:252
  21.4 17.1 %collective-permute-start.15 = (bf16[1,8,4096]{2,1,0:T(8,128)(2,1)S(1)}, bf16[1,8,4096]{2,1,0:T(8,128)(2,1)S(1)}, u32[]{:S(2)}, u32[]{:S(2)}) collective-permute-start(bf16[1,8,4096]{2,1,0:T(8,128)(2,1)S(1)} %get-tuple-element.35), channel_id=1, source_target_pairs={{0,224},{32,0},{64,32},{96,64},{128,96},{160,128},{192,160},{224,1... | collective-permute-start | bytes 196616 | tf_op jit(solution)/shard_map/ppermute | solution.py:252
  34.9 6.9 %collective-permute-start.14 = (bf16[1,8,4096]{2,1,0:T(8,128)(2,1)S(1)}, bf16[1,8,4096]{2,1,0:T(8,128)(2,1)S(1)}, u32[]{:S(2)}, u32[]{:S(2)}) collective-permute-start(bf16[1,8,4096]{2,1,0:T(8,128)(2,1)S(1)} %get-tuple-element.35), channel_id=1, source_target_pairs={{0,32},{32,64},{64,96},{96,128},{128,160},{160,192},{192,224},{224... | collective-permute-start | bytes 196616 | tf_op jit(solution)/shard_map/ppermute | solution.py:252
  34.9 25.5 %collective-permute-start.7 = (bf16[4,8,4096]{2,1,0:T(8,128)(2,1)S(1)}, bf16[4,8,4096]{2,1,0:T(8,128)(2,1)S(1)}, u32[]{:S(2)}, u32[]{:S(2)}) collective-permute-start(bf16[4,8,4096]{2,1,0:T(8,128)(2,1)S(1)} %pad_maximum_fusion.refs_3_), channel_id=1, source_target_pairs={{0,224},{32,0},{64,32},{96,64},{128,96},{160,128},{192,160},{224,1... | collective-permute-start | bytes 786440 | tf_op jit(solution)/shard_map/ppermute | solution.py:252
  38.5 25.1 %collective-permute-start.6 = (bf16[4,8,4096]{2,1,0:T(8,128)(2,1)S(1)}, bf16[4,8,4096]{2,1,0:T(8,128)(2,1)S(1)}, u32[]{:S(2)}, u32[]{:S(2)}) collective-permute-start(bf16[4,8,4096]{2,1,0:T(8,128)(2,1)S(1)} %pad_maximum_fusion.refs_3_), channel_id=1, source_target_pairs={{0,32},{32,64},{64,96},{96,128},{128,160},{160,192},{192,224},{224... | collective-permute-start | bytes 786440 | tf_op jit(solution)/shard_map/ppermute | solution.py:252
  38.6 11.4 %collective-permute-start.17 = (bf16[1,8,4096]{2,1,0:T(8,128)(2,1)S(1)}, bf16[1,8,4096]{2,1,0:T(8,128)(2,1)S(1)}, u32[]{:S(2)}, u32[]{:S(2)}) collective-permute-start(bf16[1,8,4096]{2,1,0:T(8,128)(2,1)S(1)} %collective-permute-done.15), channel_id=1, source_target_pairs={{0,224},{32,0},{64,32},{96,64},{128,96},{160,128},{192,160},{224,1... | collective-permute-start | bytes 196616 | tf_op jit(solution)/shard_map/ppermute | solution.py:252
  41.8 5.6 %collective-permute-start.16 = (bf16[1,8,4096]{2,1,0:T(8,128)(2,1)S(1)}, bf16[1,8,4096]{2,1,0:T(8,128)(2,1)S(1)}, u32[]{:S(2)}, u32[]{:S(2)}) collective-permute-start(bf16[1,8,4096]{2,1,0:T(8,128)(2,1)S(1)} %collective-permute-done.14), channel_id=1, source_target_pairs={{0,32},{32,64},{64,96},{96,128},{128,160},{160,192},{192,224},{224... | collective-permute-start | bytes 196616 | tf_op jit(solution)/shard_map/ppermute | solution.py:252
  47.4 40.7 %collective-permute-start.23 = (bf16[4,8,4096]{2,1,0:T(8,128)(2,1)S(1)}, bf16[4,8,4096]{2,1,0:T(8,128)(2,1)S(1)}, u32[]{:S(2)}, u32[]{:S(2)}) collective-permute-start(bf16[4,8,4096]{2,1,0:T(8,128)(2,1)S(1)} %pad_maximum_fusion.1), channel_id=1, source_target_pairs={{0,16},{8,24},{16,0},{24,8},{1,17},{9,25},{17,1},{25,9},{2,18},{10... | collective-permute-start | bytes 786440 | tf_op jit(solution)/shard_map/ppermute | solution.py:252
  49.9 5.6 %collective-permute-start.18 = (bf16[1,8,4096]{2,1,0:T(8,128)(2,1)S(1)}, bf16[1,8,4096]{2,1,0:T(8,128)(2,1)S(1)}, u32[]{:S(2)}, u32[]{:S(2)}) collective-permute-start(bf16[1,8,4096]{2,1,0:T(8,128)(2,1)S(1)} %collective-permute-done.16), channel_id=1, source_target_pairs={{0,32},{32,64},{64,96},{96,128},{128,160},{160,192},{192,224},{224... | collective-permute-start | bytes 196616 | tf_op jit(solution)/shard_map/ppermute | solution.py:252
  55.5 4.9 %collective-permute-start.19 = (bf16[1,8,4096]{2,1,0:T(8,128)(2,1)S(1)}, bf16[1,8,4096]{2,1,0:T(8,128)(2,1)S(1)}, u32[]{:S(2)}, u32[]{:S(2)}) collective-permute-start(bf16[1,8,4096]{2,1,0:T(8,128)(2,1)S(1)} %collective-permute-done.17), channel_id=1, source_target_pairs={{0,224},{32,0},{64,32},{96,64},{128,96},{160,128},{192,160},{224,1... | collective-permute-start | bytes 196616 | tf_op jit(solution)/shard_map/ppermute | solution.py:252
  60.4 13.1 %collective-permute-start.20 = (bf16[1,8,4096]{2,1,0:T(8,128)(2,1)S(1)}, bf16[1,8,4096]{2,1,0:T(8,128)(2,1)S(1)}, u32[]{:S(2)}, u32[]{:S(2)}) collective-permute-start(bf16[1,8,4096]{2,1,0:T(8,128)(2,1)S(1)} %collective-permute-done.18), channel_id=1, source_target_pairs={{0,32},{32,64},{64,96},{96,128},{128,160},{160,192},{192,224},{224... | collective-permute-start | bytes 196616 | tf_op jit(solution)/shard_map/ppermute | solution.py:252
  60.4 9.4 %collective-permute-start.9 = (bf16[4,8,4096]{2,1,0:T(8,128)(2,1)S(1)}, bf16[4,8,4096]{2,1,0:T(8,128)(2,1)S(1)}, u32[]{:S(2)}, u32[]{:S(2)}) collective-permute-start(bf16[4,8,4096]{2,1,0:T(8,128)(2,1)S(1)} %collective-permute-done.7.refs_5_), channel_id=1, source_target_pairs={{0,224},{32,0},{64,32},{96,64},{128,96},{160,128},{192,160},{224,1... | collective-permute-start | bytes 786440 | tf_op jit(solution)/shard_map/ppermute | solution.py:252
  63.7 10.9 %collective-permute-start.8 = (bf16[4,8,4096]{2,1,0:T(8,128)(2,1)S(1)}, bf16[4,8,4096]{2,1,0:T(8,128)(2,1)S(1)}, u32[]{:S(2)}, u32[]{:S(2)}) collective-permute-start(bf16[4,8,4096]{2,1,0:T(8,128)(2,1)S(1)} %collective-permute-done.6.refs_4_), channel_id=1, source_target_pairs={{0,32},{32,64},{64,96},{96,128},{128,160},{160,192},{192,224},{224... | collective-permute-start | bytes 786440 | tf_op jit(solution)/shard_map/ppermute | solution.py:252
  69.8 7.6 %collective-permute-start.11 = (bf16[4,8,4096]{2,1,0:T(8,128)(2,1)S(1)}, bf16[4,8,4096]{2,1,0:T(8,128)(2,1)S(1)}, u32[]{:S(2)}, u32[]{:S(2)}) collective-permute-start(bf16[4,8,4096]{2,1,0:T(8,128)(2,1)S(1)} %collective-permute-done.9.refs_7_), channel_id=1, source_target_pairs={{0,224},{32,0},{64,32},{96,64},{128,96},{160,128},{192,160},{224,1... | collective-permute-start | bytes 786440 | tf_op jit(solution)/shard_map/ppermute | solution.py:252
  73.5 21.2 %collective-permute-start.22 = (bf16[8,8,4096]{2,1,0:T(8,128)(2,1)S(1)}, bf16[8,8,4096]{2,1,0:T(8,128)(2,1)S(1)}, u32[]{:S(2)}, u32[]{:S(2)}) collective-permute-start(bf16[8,8,4096]{2,1,0:T(8,128)(2,1)S(1)} %constant_dynamic-update-slice_fusion.refs_3_), channel_id=1, source_target_pairs={{0,24},{8,0},{16,8},{24,16},{1,25},{9,1},{17,9},{25,17},{2,26},{10... | collective-permute-start | bytes 1572872 | tf_op jit(solution)/shard_map/ppermute | solution.py:252
  74.6 20.2 %collective-permute-start.21 = (bf16[8,8,4096]{2,1,0:T(8,128)(2,1)S(1)}, bf16[8,8,4096]{2,1,0:T(8,128)(2,1)S(1)}, u32[]{:S(2)}, u32[]{:S(2)}) collective-permute-start(bf16[8,8,4096]{2,1,0:T(8,128)(2,1)S(1)} %constant_dynamic-update-slice_fusion.refs_3_), channel_id=1, source_target_pairs={{0,8},{8,16},{16,24},{24,0},{1,9},{9,17},{17,25},{25,1},{2,10},{10... | collective-permute-start | bytes 1572872 | tf_op jit(solution)/shard_map/ppermute | solution.py:252
  77.4 9.4 %collective-permute-start.10 = (bf16[4,8,4096]{2,1,0:T(8,128)(2,1)S(1)}, bf16[4,8,4096]{2,1,0:T(8,128)(2,1)S(1)}, u32[]{:S(2)}, u32[]{:S(2)}) collective-permute-start(bf16[4,8,4096]{2,1,0:T(8,128)(2,1)S(1)} %collective-permute-done.8.refs_6_), channel_id=1, source_target_pairs={{0,32},{32,64},{64,96},{96,128},{128,160},{160,192},{192,224},{224... | collective-permute-start | bytes 786440 | tf_op jit(solution)/shard_map/ppermute | solution.py:252
  86.9 7.9 %collective-permute-start.24 = (bf16[4,8,4096]{2,1,0:T(8,128)(2,1)S(1)}, bf16[4,8,4096]{2,1,0:T(8,128)(2,1)S(1)}, u32[]{:S(2)}, u32[]{:S(2)}) collective-permute-start(bf16[4,8,4096]{2,1,0:T(8,128)(2,1)S(1)} %pad_maximum_fusion.2), channel_id=1, source_target_pairs={{0,16},{8,24},{16,0},{24,8},{1,17},{9,25},{17,1},{25,9},{2,18},{10... | collective-permute-start | bytes 786440 | tf_op jit(solution)/shard_map/ppermute | solution.py:252
  88.1 15.5 %collective-permute-start.13 = (bf16[2,8,4096]{2,1,0:T(8,128)(2,1)S(1)}, bf16[2,8,4096]{2,1,0:T(8,128)(2,1)S(1)}, u32[]{:S(2)}, u32[]{:S(2)}) collective-permute-start(bf16[2,8,4096]{2,1,0:T(8,128)(2,1)S(1)} %slice.13), channel_id=1, source_target_pairs={{0,224},{32,0},{64,32},{96,64},{128,96},{160,128},{192,160},{224,1... | collective-permute-start | bytes 393224 | tf_op jit(solution)/shard_map/ppermute | solution.py:252
  89.1 14.6 %collective-permute-start.12 = (bf16[2,8,4096]{2,1,0:T(8,128)(2,1)S(1)}, bf16[2,8,4096]{2,1,0:T(8,128)(2,1)S(1)}, u32[]{:S(2)}, u32[]{:S(2)}) collective-permute-start(bf16[2,8,4096]{2,1,0:T(8,128)(2,1)S(1)} %slice.12), channel_id=1, source_target_pairs={{0,32},{32,64},{64,96},{96,128},{128,160},{160,192},{192,224},{224... | collective-permute-start | bytes 393224 | tf_op jit(solution)/shard_map/ppermute | solution.py:252
  100.5 13.7 %collective-permute-start.26 = (f16[9,64,256]{2,1,0:T(8,128)(2,1)S(1)}, f16[9,64,256]{2,1,0:T(8,128)(2,1)S(1)}, u32[]{:S(2)}, u32[]{:S(2)}) collective-permute-start(f16[9,64,256]{2,1,0:T(8,128)(2,1)S(1)} %convert_element_type.14), channel_id=1, source_target_pairs={{0,4},{4,0},{1,5},{5,1},{2,6},{6,2},{3,7},{7,3},{8,12},{12,8},{9,1... | collective-permute-start | bytes 884744 | tf_op jit(solution)/shard_map/ppermute | solution.py:256
  109.5 8.3 %collective-permute-start.25 = (f16[9,64,256]{2,1,0:T(8,128)(2,1)S(1)}, f16[9,64,256]{2,1,0:T(8,128)(2,1)S(1)}, u32[]{:S(2)}, u32[]{:S(2)}) collective-permute-start(f16[9,64,256]{2,1,0:T(8,128)(2,1)S(1)} %convert_element_type.12), channel_id=1, source_target_pairs={{0,4},{4,0},{1,5},{5,1},{2,6},{6,2},{3,7},{7,3},{8,12},{12,8},{9,1... | collective-permute-start | bytes 884744 | tf_op jit(solution)/shard_map/ppermute | solution.py:256

commit v2 on v1

--- a/solution.py
+++ b/solution.py
@@ -13,7 +13,6 @@
 MB = 1 << 20
 SENT = jnp.float16
 SCALE = 65536.0
-SWAP = [(0, 1), (1, 0)]
 
 
 def filter_kernel(place, raw, taps, out, first, second, mine, blocks, weights, line):
@@ -117,10 +116,9 @@
     )(rows)
 
 
-def weigh(lagged, energy, columns, across, emit):
+def weigh(lagged, energy, right, across, emit):
     lags, count, bins = lagged.shape
     left = lagged[...].reshape(lags * count, bins)
-    right = columns[...].reshape(-1, bins)
     moments = lax.dot_general(left, right, NT, preferred_element_type=jnp.float32)
     norms = (1.0 / jnp.sqrt(energy[:, 0:1] + 1e-05)) * across
     for lag in range(lags):
@@ -128,71 +126,77 @@
         emit(lag, -0.5 * jnp.log(1.0 - ratio * ratio))
 
 
-def partner_kernel(steps, place, lagged, energy, *rest):
+def partner_kernel(steps, place, far_y, energy_y, far_x, energy_x, far_xy, energy_xy, *rest):
     units = rest[: len(steps)]
-    send, columns, scale, sems = rest[len(steps) :]
+    send_y, send_x, send_xy, columns, scale = rest[len(steps) :]
+    z = place[3]
+    for ref, moves in zip(units, steps):
+        for k, (pair, z_step) in enumerate(moves):
+            columns[pair * 8 + ((z + z_step) & 7)] = ref[k]
     width = columns.shape[0] * columns.shape[1]
-    z = place[3]
-    x = place[4]
-    copies = []
-    for ref, moves in zip(units, steps):
-        for k, (x_step, z_step) in enumerate(moves):
-            slot = ((x + x_step) & 3) * 8 + ((z + z_step) & 7)
-            copies.append(pltpu.make_async_copy(ref.at[k], columns.at[slot], sems.at[len(copies)]))
-    for copy in copies:
-        copy.start()
-    for copy in copies:
-        copy.wait()
     for g in range(width // 128):
         block = columns[g * 16 : (g + 1) * 16].astype(jnp.float32).reshape(128, -1)
         total = jnp.sum(block * block, axis=1, keepdims=True)
         root = 0.8 / jnp.sqrt(total + 1e-05)
         root = jnp.transpose(jnp.broadcast_to(root, (128, 128)))
         scale[:, g * 128 : (g + 1) * 128] = root[0:8]
-
-    def emit(lag, value):
-        send[lag] = value * SCALE
-
-    weigh(lagged, energy, columns, scale[0:1, :], emit)
-
-
-def run_partner(place, lagged, energy, units, steps):
+    right = columns[...].reshape(width, -1)
+    across = scale[0:1, :]
+    for lagged, energy, send in (
+        (far_xy, energy_xy, send_xy),
+        (far_x, energy_x, send_x),
+        (far_y, energy_y, send_y),
+    ):
+
+        def emit(lag, value):
+            send[lag] = value * SCALE
+
+        weigh(lagged, energy, right, across, emit)
+
+
+def run_partner(place, rows, units, steps):
     slots = sum(len(moves) for moves in steps)
-    lags, count, bins = lagged.shape
+    lags, count, bins = rows[0].shape
     width = slots * 8
 
     def body(*refs):
         partner_kernel(steps, *refs)
 
     vmem = pl.BlockSpec(memory_space=pltpu.VMEM)
+    result = jax.ShapeDtypeStruct((lags, count, width), jnp.float32)
     return pl.pallas_call(
         body,
-        in_specs=[pl.BlockSpec(memory_space=pltpu.SMEM), vmem, vmem]
-        + [pl.BlockSpec(memory_space=pl.ANY)] * len(units),
-        out_specs=[vmem, vmem, vmem],
+        in_specs=[pl.BlockSpec(memory_space=pltpu.SMEM)] + [vmem] * (len(rows) + len(units)),
+        out_specs=[vmem] * 5,
         out_shape=[
-            jax.ShapeDtypeStruct((lags, count, width), jnp.float32),
+            result,
+            result,
+            result,
             jax.ShapeDtypeStruct((slots, 8, bins), jnp.bfloat16),
             jax.ShapeDtypeStruct((8, width), jnp.float32),
         ],
-        scratch_shapes=[pltpu.SemaphoreType.DMA((slots,))],
         compiler_params=pltpu.CompilerParams(vmem_limit_bytes=8 * MB),
         cost_estimate=pl.CostEstimate(
-            flops=2 * lags * count * width * bins,
+            flops=6 * lags * count * width * bins,
             bytes_accessed=2 * bins * width,
-            transcendentals=lags * count * width,
+            transcendentals=3 * lags * count * width,
         ),
         name="partner",
-    )(place, lagged, energy, *units)
+    )(place, *rows, *units)
 
 
 def own_kernel(lagged, energy, columns_a, scale_a, columns_b, scale_b, out_a, out_b):
-    for columns, scale, out in ((columns_a, scale_a, out_a), (columns_b, scale_b, out_b)):
-
-        def emit(lag, value):
-            out[lag] = value
-
-        weigh(lagged, energy, columns, scale[0:1, :], emit)
+    bins = lagged.shape[2]
+    width = scale_a.shape[1]
+    right = [columns[...].reshape(width, bins) for columns in (columns_a, columns_b)]
+    right = jnp.concatenate(right, axis=0)
+    across = jnp.concatenate([scale_a[0:1, :], scale_b[0:1, :]], axis=1)
+
+    def emit(lag, value):
+        out_a[lag] = value[:, :width]
+        out_b[lag] = value[:, width:]
+
+    weigh(lagged, energy, right, across, emit)
 
 
 def run_own(lagged, energy, columns_a, scale_a, columns_b, scale_b):
@@ -215,36 +219,39 @@
     )(lagged, energy, columns_a, scale_a, columns_b, scale_b)
 
 
-def join_kernel(place, own_a, got_a, own_b, got_b, out):
+def join_kernel(place, *refs):
+    out = refs[-1]
+    x = place[4]
     low = place[5] == 0
-    lane = lax.broadcasted_iota(jnp.int32, own_a.shape[1:2] + (128,), 1) < 64
-    for half, (own, got) in enumerate(((own_a, got_a), (own_b, got_b))):
-        for lag in range(own.shape[0]):
-            for tile in range(own.shape[2] // 128):
-                span = slice(tile * 128, (tile + 1) * 128)
-                here = own[lag, :, span]
-                there = got[lag, :, span] * (1.0 / SCALE)
+    rows = out.shape[1]
+    lane = lax.broadcasted_iota(jnp.int32, (rows, 128), 1) < 64
+    for half in range(2):
+        for flip in range(2):
+            same, cross = refs[half * 4 + flip * 2], refs[half * 4 + flip * 2 + 1]
+            here_x = x ^ flip
+            for lag in range(out.shape[0]):
+                here = same[lag] * (1.0 / SCALE) if flip else same[lag]
+                there = cross[lag] * (1.0 / SCALE)
                 one = jnp.where(low, here, there)
                 two = jnp.where(low, there, here)
-                base = half * 512 + tile * 256
-                out[lag, :, base : base + 128] = jnp.where(lane, one, pltpu.roll(two, 64, axis=1))
-                out[lag, :, base + 128 : base + 256] = jnp.where(
-                    lane, pltpu.roll(one, 64, axis=1), two
-                )
-
-
-def run_join(place, own_a, got_a, own_b, got_b):
-    lags, rows, width = own_a.shape
+                at = pl.multiple_of((half * 4 + here_x) * 128, 128)
+                out[lag, :, pl.ds(at, 128)] = jnp.where(lane, one, pltpu.roll(two, 64, axis=1))
+                at = pl.multiple_of((half * 4 + (here_x ^ 2)) * 128, 128)
+                out[lag, :, pl.ds(at, 128)] = jnp.where(lane, pltpu.roll(one, 64, axis=1), two)
+
+
+def run_join(place, quarters):
+    lags, rows, width = quarters[0].shape
     spec = pl.BlockSpec((3, rows, width), lambda i: (i, 0, 0))
     return pl.pallas_call(
         join_kernel,
         grid=(lags // 3,),
-        in_specs=[pl.BlockSpec(memory_space=pltpu.SMEM)] + [spec] * 4,
-        out_specs=pl.BlockSpec((3, rows, 4 * width), lambda i: (i, 0, 0)),
-        out_shape=jax.ShapeDtypeStruct((lags, rows, 4 * width), jnp.float32),
+        in_specs=[pl.BlockSpec(memory_space=pltpu.SMEM)] + [spec] * 8,
+        out_specs=pl.BlockSpec((3, rows, 8 * width), lambda i: (i, 0, 0)),
+        out_shape=jax.ShapeDtypeStruct((lags, rows, 8 * width), jnp.float32),
         compiler_params=pltpu.CompilerParams(vmem_limit_bytes=8 * MB),
         name="join",
-    )(place, own_a, got_a, own_b, got_b)
+    )(place, *quarters)
 
 
 def around(value, axis, step):
@@ -252,8 +259,20 @@
     return lax.ppermute(value, axis, [(i, (i + step) % size) for i in range(size)])
 
 
-def swap_half(value):
-    return lax.ppermute(value.astype(SENT), "yh", SWAP).astype(jnp.float32)
+def cross_y(value):
+    return lax.ppermute(value, "yh", [(0, 1), (1, 0)])
+
+
+def cross_x(value):
+    return lax.ppermute(value, "x", [(0, 1), (1, 0), (2, 3), (3, 2)])
+
+
+def cross_xy(value):
+    return lax.ppermute(value, ("x", "yh"), [(i, i ^ 3) for i in range(8)])
+
+
+def sent(move, value):
+    return move(value.astype(SENT)).astype(jnp.float32)
 
 
 def spread(value, odd):
@@ -263,6 +282,20 @@
             j = (z & 1) ^ odd
             pairs.append((z * 4 + q, (2 * q + j) * 4 + (z >> 1)))
     return lax.ppermute(value, ("z", "yl", "core"), pairs)
+
+
+def chain(unit):
+    base = jnp.concatenate([unit, around(unit, "x", 2)], axis=0)
+    units, steps = [base], [[(0, 0), (1, 0)]]
+    up = down = base
+    for step in (1, 2, 3):
+        up = around(up, "z", 1)
+        down = around(down, "z", -1)
+        units += [up, down]
+        steps += [[(0, -step), (1, -step)], [(0, step), (1, step)]]
+    units += [around(up[0:1], "z", 1), around(down[1:2], "z", -1)]
+    steps += [[(0, 4)], [(1, 4)]]
+    return units, steps
 
 
 def shards(raw, taps):
@@ -280,46 +313,22 @@
     two = spread(second, 1)
     unit_a = jnp.where(e == 0, one, two)[None]
     unit_b = jnp.where(e == 0, two, one)[None]
-    x_steps = (0, -1, 1, 2)
-    near = [unit_a, around(unit_a, "x", 1), around(unit_a, "x", -1), around(unit_a, "x", 2)]
-    base_a = jnp.concatenate(near, axis=0)
-    units_a, steps_a = [base_a], [[(k, 0) for k in x_steps]]
-    up = down = base_a
-    for step in (1, 2, 3):
-        up = around(up, "z", 1)
-        down = around(down, "z", -1)
-        units_a += [up, down]
-        steps_a += [[(k, -step) for k in x_steps], [(k, step) for k in x_steps]]
-    units_a += [around(up[0:2], "z", 1), around(down[2:4], "z", -1)]
-    steps_a += [[(k, 4) for k in x_steps[0:2]], [(k, 4) for k in x_steps[2:4]]]
-    up = down = unit_b
-    near, z_steps = [unit_b], [0]
-    for step in (1, 2, 3):
-        up = around(up, "z", 1)
-        down = around(down, "z", -1)
-        near += [up, down]
-        z_steps += [-step, step]
-    near.append(around(up, "z", 1))
-    z_steps.append(4)
-    base_b = jnp.concatenate(near, axis=0)
-    units_b = [
-        base_b,
-        around(base_b, "x", 1),
-        around(base_b, "x", -1),
-        around(base_b[0:4], "x", 2),
-        around(base_b[4:8], "x", -2),
-    ]
-    steps_b = [[(k, d) for d in z_steps] for k in (0, -1, 1)]
-    steps_b += [[(2, d) for d in z_steps[0:4]], [(2, d) for d in z_steps[4:8]]]
-    partner = lax.ppermute(full, "yh", SWAP)
+    units_a, steps_a = chain(unit_a)
+    units_b, steps_b = chain(unit_b)
+    row_y = cross_y(full)
+    row_x = cross_x(full)
+    row_xy = cross_x(row_y)
     lagged, energy = run_lags(full)
-    far_lagged, far_energy = run_lags(partner)
-    send_a, columns_a, scale_a = run_partner(place, far_lagged, far_energy, units_a, steps_a)
-    got_a = swap_half(send_a)
-    send_b, columns_b, scale_b = run_partner(place, far_lagged, far_energy, units_b, steps_b)
-    got_b = swap_half(send_b)
-    own_a, own_b = run_own(lagged, energy, columns_a, scale_a, columns_b, scale_b)
-    information = run_join(place, own_a, got_a, own_b, got_b)
+    rows = [*run_lags(row_y), *run_lags(row_x), *run_lags(row_xy)]
+    quarters = []
+    columns = []
+    for units, steps in ((units_a, steps_a), (units_b, steps_b)):
+        send_y, send_x, send_xy, *kept = run_partner(place, rows, units, steps)
+        got_xy = sent(cross_xy, send_xy)
+        quarters.append([sent(cross_y, send_y), sent(cross_x, send_x), got_xy])
+        columns += kept
+    own = run_own(lagged, energy, *columns)
+    information = run_join(place, [part for k in range(2) for part in (own[k], *quarters[k])])
     return (information, mine)
 
 

time: 121 us -> 104 us (0.86)
  waiting for transfers between devices: 39.9 us -> 15 us
  starting transfers between devices: 49.1 us -> 57.6 us
    ppermute x22 -> x18, waiting for transfers between devices: 36.4 us -> 9.56 us  [around(): lax.ppermute(value, axis, [(i, (i + step) % size) for i in range(size)])]
    ppermute x3 -> x9, starting transfers between devices: 6.82 us -> 15.5 us  [the longest x2 6.13 us: cross_xy(): return lax.ppermute(value, ('x', 'yh'), [(i, i ^ 3) for i in range(8)])]
    pallas_call x2 -> x4, Pallas kernels: 2.53 us -> 5.06 us  [run_lags(): pl.pallas_call(lag_kernel, in_specs=[vmem], out_specs=[vmem, vmem], out_s...]
    ppermute x2, waiting for transfers between devices: 0.01 us -> 2.35 us  [spread(): return lax.ppermute(value, ('z', 'yl', 'core'), pairs)]
    pallas_call x2, Pallas kernels: 11.4 us -> 9.32 us  [run_partner(): pl.pallas_call(body, in_specs=[pl.BlockSpec(memory_space=pltpu.SMEM)] + [...]
    pallas_call x1, Pallas kernels: 2.71 us -> 1.47 us  [run_own(): pl.pallas_call(own_kernel, in_specs=[vmem] * 6, out_specs=[vmem, vmem], o...]
    ppermute x3 -> x9, waiting for transfers between devices: 3.54 us -> 3.11 us  [the longest x3 2.28 us: cross_y(): return lax.ppermute(value, 'yh', [(0, 1), (1, 0)])]
    ppermute x22 -> x18, starting transfers between devices: 39.6 us -> 39.4 us  [around(): lax.ppermute(value, axis, [(i, (i + step) % size) for i in range(size)])]
  transfers between devices with their start and end apart: 27 -> 29, of which waited for: 8 -> 8; matrix products, arithmetic and copies ran while one was open for 0% -> 0% of each run, Pallas kernels for 14% -> 15%
where the time goes in v2:
time: 104 us
  starting transfers between devices  57.6 us (55%)
  Pallas kernels  21.5 us (21%)
  waiting for transfers between devices  15 us (14%)
  blocking collectives  7.47 us (7%)
    ppermute x18, starting transfers between devices, around(): lax.ppermute(value, axis, [(i, (i + step) % size) for i in range(size)])  39.4 us
    ppermute x18, waiting for transfers between devices, around(): lax.ppermute(value, axis, [(i, (i + step) % size) for i in range(size)])  9.56 us
    pallas_call x2, Pallas kernels, run_partner(): pl.pallas_call(body, in_specs=[pl.BlockSpec(memory_space=pltpu.SMEM)] + [...  9.32 us
    all_gather x1, blocking collectives, shards(): everything = lax.all_gather(raw, ('yl', 'core'), axis=0, tiled=False)  7.47 us
    ppermute x2, starting transfers between devices, cross_xy(): return lax.ppermute(value, ('x', 'yh'), [(i, i ^ 3) for i in range(8)])  6.13 us
    ppermute x4, starting transfers between devices, cross_x(): return lax.ppermute(value, 'x', [(0, 1), (1, 0), (2, 3), (3, 2)])  5.11 us
    pallas_call x4, Pallas kernels, run_lags(): pl.pallas_call(lag_kernel, in_specs=[vmem], out_specs=[vmem, vmem], out_s...  5.06 us
    ppermute x3, starting transfers between devices, cross_y(): return lax.ppermute(value, 'yh', [(0, 1), (1, 0)])  4.28 us
  transfers between devices with their start and end apart: 29, of which 8 were waited for; matrix products, arithmetic and copies ran while one was open for 0% of the time, Pallas kernels for 15%

profile of v2, /device:TPU:2, one launch (start us, length us, event | category | flops | bytes accessed | tf_op | source)
XLA Modules:
  0.0 103.5 jit_solution(4858016744104558263)
XLA Ops:
  0.7 7.5 %all-gather = bf16[256,1024]{1,0:T(8,128)(2,1)S(1)} all-gather(bf16[64,1024]{1,0:T(8,128)(2,1)} %param.2), channel_id=2, replica_groups=mesh['z'=8,'x'=4,'yh'=2,'yl'=2,'core'=2] {'yl','core'}, dimensions={0}, use_global_device_ids=true | all-gather | bytes 655360 | tf_op jit(solution)/shard_map/all_gather | solution.py:308
  8.9 2.7 %fir.1 = (bf16[64,4096]{1,0:T(8,128)(2,1)S(1)}, bf16[8,4096]{1,0:T(8,128)(2,1)S(1)}, bf16[8,4096]{1,0:T(8,128)(2,1)S(1)}, bf16[64,1024]{1,0:T(8,128)(2,1)}) custom-call(s32[6]{0:T(128)S(1)} %stack.27.place.refs_0_, bf16[4,64,1024]{2,1,0:T(8,128)(2,1)S(1)} %bitcast.12, f32[1,65]{1,0:T(1,128)S(1)} %bitcast.13), custom_call_target="tpu_custom_call" | custom-call | tf_op jit(solution)/shard_map/fir/pallas_call | solution.py:63
  12.3 2.0 %collective-permute-start.4 = (bf16[8,4096]{1,0:T(8,128)(2,1)S(1)}, bf16[8,4096]{1,0:T(8,128)(2,1)S(1)}, u32[]{:S(2)}, u32[]{:S(2)}) collective-permute-start(bf16[8,4096]{1,0:T(8,128)(2,1)S(1)} %get-tuple-element.36), channel_id=1, source_target_pairs={{0,32},{1,96},{2,160},{3,224},{32,0},{33,64},{34,128},{35,192},{64... | collective-permute-start | bytes 196616 | tf_op jit(solution)/shard_map/ppermute | solution.py:284
  14.3 2.3 %collective-permute-done.4 = bf16[8,4096]{1,0:T(8,128)(2,1)S(1)} collective-permute-done((bf16[8,4096]{1,0:T(8,128)(2,1)S(1)}, bf16[8,4096]{1,0:T(8,128)(2,1)S(1)}, u32[]{:S(2)}, u32[]{:S(2)}) %collective-permute-start.4) | collective-permute-done | bytes 65568 | tf_op jit(solution)/shard_map/ppermute | solution.py:284
  16.6 2.2 %collective-permute-start.5 = (bf16[1,8,4096]{2,1,0:T(8,128)(2,1)S(1)}, bf16[1,8,4096]{2,1,0:T(8,128)(2,1)S(1)}, u32[]{:S(2)}, u32[]{:S(2)}) collective-permute-start(bf16[1,8,4096]{2,1,0:T(8,128)(2,1)S(1)} %get-tuple-element.51), channel_id=1, source_target_pairs={{0,16},{8,24},{16,0},{24,8},{1,17},{9,25},{17,1},{25,9},{2,18},{10... | collective-permute-start | bytes 196616 | tf_op jit(solution)/shard_map/ppermute | solution.py:259
  18.8 2.9 %collective-permute-start = (bf16[64,4096]{1,0:T(8,128)(2,1)S(1)}, bf16[64,4096]{1,0:T(8,128)(2,1)S(1)}, u32[]{:S(2)}, u32[]{:S(2)}) collective-permute-start(bf16[64,4096]{1,0:T(8,128)(2,1)S(1)} %get-tuple-element.26.rows_ref), channel_id=1, source_target_pairs={{0,4},{4,0},{1,5},{5,1},{2,6},{6,2},{3,7},{7,3},{8,12},{12,8},{9,1... | collective-permute-start | bytes 1572872 | tf_op jit(solution)/shard_map/ppermute | solution.py:263
  21.7 1.4 %collective-permute-start.14 = (bf16[1,8,4096]{2,1,0:T(8,128)(2,1)S(1)}, bf16[1,8,4096]{2,1,0:T(8,128)(2,1)S(1)}, u32[]{:S(2)}, u32[]{:S(2)}) collective-permute-start(bf16[1,8,4096]{2,1,0:T(8,128)(2,1)S(1)} %get-tuple-element.50), channel_id=1, source_target_pairs={{0,16},{8,24},{16,0},{24,8},{1,17},{9,25},{17,1},{25,9},{2,18},{10... | collective-permute-start | bytes 196616 | tf_op jit(solution)/shard_map/ppermute | solution.py:259
  23.2 14.1 %collective-permute-start.7 = (bf16[2,8,4096]{2,1,0:T(8,128)(2,1)S(1)}, bf16[2,8,4096]{2,1,0:T(8,128)(2,1)S(1)}, u32[]{:S(2)}, u32[]{:S(2)}) collective-permute-start(bf16[2,8,4096]{2,1,0:T(8,128)(2,1)S(1)} %pad_maximum_fusion.refs_7_), channel_id=1, source_target_pairs={{0,224},{32,0},{64,32},{96,64},{128,96},{160,128},{192,160},{224,1... | collective-permute-start | bytes 393224 | tf_op jit(solution)/shard_map/ppermute | solution.py:259
  37.3 4.2 %collective-permute-start.16 = (bf16[2,8,4096]{2,1,0:T(8,128)(2,1)S(1)}, bf16[2,8,4096]{2,1,0:T(8,128)(2,1)S(1)}, u32[]{:S(2)}, u32[]{:S(2)}) collective-permute-start(bf16[2,8,4096]{2,1,0:T(8,128)(2,1)S(1)} %pad_maximum_fusion.1.refs_7_), channel_id=1, source_target_pairs={{0,224},{32,0},{64,32},{96,64},{128,96},{160,128},{192,160},{224,1... | collective-permute-start | bytes 393224 | tf_op jit(solution)/shard_map/ppermute | solution.py:259
  41.5 1.4 %collective-permute-start.1 = (bf16[64,4096]{1,0:T(8,128)(2,1)S(1)}, bf16[64,4096]{1,0:T(8,128)(2,1)S(1)}, u32[]{:S(2)}, u32[]{:S(2)}) collective-permute-start(bf16[64,4096]{1,0:T(8,128)(2,1)S(1)} %get-tuple-element.26.rows_ref), channel_id=1, source_target_pairs={{0,8},{8,0},{16,24},{24,16},{1,9},{9,1},{17,25},{25,17},{2,10},{10... | collective-permute-start | bytes 1572872 | tf_op jit(solution)/shard_map/ppermute | solution.py:267
  43.5 3.8 %collective-permute-start.9 = (bf16[2,8,4096]{2,1,0:T(8,128)(2,1)S(1)}, bf16[2,8,4096]{2,1,0:T(8,128)(2,1)S(1)}, u32[]{:S(2)}, u32[]{:S(2)}) collective-permute-start(bf16[2,8,4096]{2,1,0:T(8,128)(2,1)S(1)} %collective-permute-done.7.refs_9_), channel_id=1, source_target_pairs={{0,224},{32,0},{64,32},{96,64},{128,96},{160,128},{192,160},{224,1... | collective-permute-start | bytes 393224 | tf_op jit(solution)/shard_map/ppermute | solution.py:259
  47.4 2.9 %collective-permute-done.15.refs_8_ = bf16[2,8,4096]{2,1,0:T(8,128)(2,1)S(1)} collective-permute-done((bf16[2,8,4096]{2,1,0:T(8,128)(2,1)S(1)}, bf16[2,8,4096]{2,1,0:T(8,128)(2,1)S(1)}, u32[]{:S(2)}, u32[]{:S(2)}) %collective-permute-start.15) | collective-permute-done | bytes 131104 | tf_op jit(solution)/shard_map/ppermute | solution.py:259
  50.2 4.1 %collective-permute-start.18 = (bf16[2,8,4096]{2,1,0:T(8,128)(2,1)S(1)}, bf16[2,8,4096]{2,1,0:T(8,128)(2,1)S(1)}, u32[]{:S(2)}, u32[]{:S(2)}) collective-permute-start(bf16[2,8,4096]{2,1,0:T(8,128)(2,1)S(1)} %collective-permute-done.16.refs_9_), channel_id=1, source_target_pairs={{0,224},{32,0},{64,32},{96,64},{128,96},{160,128},{192,160},{224,1... | collective-permute-start | bytes 393224 | tf_op jit(solution)/shard_map/ppermute | solution.py:259
  54.3 3.2 %collective-permute-start.11 = (bf16[2,8,4096]{2,1,0:T(8,128)(2,1)S(1)}, bf16[2,8,4096]{2,1,0:T(8,128)(2,1)S(1)}, u32[]{:S(2)}, u32[]{:S(2)}) collective-permute-start(bf16[2,8,4096]{2,1,0:T(8,128)(2,1)S(1)} %collective-permute-done.9.refs_11_), channel_id=1, source_target_pairs={{0,224},{32,0},{64,32},{96,64},{128,96},{160,128},{192,160},{224,1... | collective-permute-start | bytes 393224 | tf_op jit(solution)/shard_map/ppermute | solution.py:259
  57.6 3.6 %collective-permute-done.17.refs_10_ = bf16[2,8,4096]{2,1,0:T(8,128)(2,1)S(1)} collective-permute-done((bf16[2,8,4096]{2,1,0:T(8,128)(2,1)S(1)}, bf16[2,8,4096]{2,1,0:T(8,128)(2,1)S(1)}, u32[]{:S(2)}, u32[]{:S(2)}) %collective-permute-start.17) | collective-permute-done | bytes 131104 | tf_op jit(solution)/shard_map/ppermute | solution.py:259
  61.6 1.7 %collective-permute-start.19 = (bf16[2,8,4096]{2,1,0:T(8,128)(2,1)S(1)}, bf16[2,8,4096]{2,1,0:T(8,128)(2,1)S(1)}, u32[]{:S(2)}, u32[]{:S(2)}) collective-permute-start(bf16[2,8,4096]{2,1,0:T(8,128)(2,1)S(1)} %collective-permute-done.17.refs_10_), channel_id=1, source_target_pairs={{0,32},{32,64},{64,96},{96,128},{128,160},{160,192},{192,224},{224... | collective-permute-start | bytes 393224 | tf_op jit(solution)/shard_map/ppermute | solution.py:259
  63.2 1.8 %collective-permute-done.10.refs_12_ = bf16[2,8,4096]{2,1,0:T(8,128)(2,1)S(1)} collective-permute-done((bf16[2,8,4096]{2,1,0:T(8,128)(2,1)S(1)}, bf16[2,8,4096]{2,1,0:T(8,128)(2,1)S(1)}, u32[]{:S(2)}, u32[]{:S(2)}) %collective-permute-start.10) | collective-permute-done | bytes 131104 | tf_op jit(solution)/shard_map/ppermute | solution.py:259
  65.1 2.0 %collective-permute-start.13 = (bf16[1,8,4096]{2,1,0:T(8,128)(2,1)S(1)}, bf16[1,8,4096]{2,1,0:T(8,128)(2,1)S(1)}, u32[]{:S(2)}, u32[]{:S(2)}) collective-permute-start(bf16[1,8,4096]{2,1,0:T(8,128)(2,1)S(1)} %slice.17), channel_id=1, source_target_pairs={{0,224},{32,0},{64,32},{96,64},{128,96},{160,128},{192,160},{224,1... | collective-permute-start | bytes 196616 | tf_op jit(solution)/shard_map/ppermute | solution.py:259
  68.4 2.1 %collective-permute-start.22 = (bf16[1,8,4096]{2,1,0:T(8,128)(2,1)S(1)}, bf16[1,8,4096]{2,1,0:T(8,128)(2,1)S(1)}, u32[]{:S(2)}, u32[]{:S(2)}) collective-permute-start(bf16[1,8,4096]{2,1,0:T(8,128)(2,1)S(1)} %slice.19), channel_id=1, source_target_pairs={{0,224},{32,0},{64,32},{96,64},{128,96},{160,128},{192,160},{224,1... | collective-permute-start | bytes 196616 | tf_op jit(solution)/shard_map/ppermute | solution.py:259
  70.5 1.3 %lags.5 = (bf16[9,64,4096]{2,1,0:T(8,128)(2,1)S(1)}, f32[64,128]{1,0:T(8,128)S(1)}) custom-call(bf16[64,4096]{1,0:T(8,128)(2,1)S(1)} %collective-permute-done.rows_ref), custom_call_target="tpu_custom_call" | custom-call | flops 10485760 | bytes 6291456 | tf_op jit(solution)/shard_map/lags/pallas_call | solution.py:105
  71.9 1.3 %lags.6 = (bf16[9,64,4096]{2,1,0:T(8,128)(2,1)S(1)}, f32[64,128]{1,0:T(8,128)S(1)}) custom-call(bf16[64,4096]{1,0:T(8,128)(2,1)S(1)} %collective-permute-done.1.rows_ref), custom_call_target="tpu_custom_call" | custom-call | flops 10485760 | bytes 6291456 | tf_op jit(solution)/shard_map/lags/pallas_call | solution.py:105
  73.2 1.3 %lags.7 = (bf16[9,64,4096]{2,1,0:T(8,128)(2,1)S(1)}, f32[64,128]{1,0:T(8,128)S(1)}) custom-call(bf16[64,4096]{1,0:T(8,128)(2,1)S(1)} %collective-permute-done.2.rows_ref), custom_call_target="tpu_custom_call" | custom-call | flops 10485760 | bytes 6291456 | tf_op jit(solution)/shard_map/lags/pallas_call | solution.py:105
  74.5 4.7 %partner.2 = (f32[9,64,128]{2,1,0:T(8,128)S(1)}, f32[9,64,128]{2,1,0:T(8,128)S(1)}, f32[9,64,128]{2,1,0:T(8,128)S(1)}, bf16[16,8,4096]{2,1,0:T(8,128)(2,1)S(1)}, f32[8,128]{1,0:T(8,128)S(1)}) custom-call(s32[6]{0:T(128)S(1)} %stack.27.place.refs_0_, bf16[9,64,4096]{2,1,0:T(8,128)(2,1)S(1)} %get-tuple-element.29.refs_1_, ...), custom_call_target="tpu_custom_call" | custom-call | flops 1811939328 | bytes 1048576 | tf_op jit(solution)/shard_map/partner/pallas_call | solution.py:167
  79.2 3.2 %collective-permute-start.25 = (f16[9,64,128]{2,1,0:T(8,128)(2,1)S(1)}, f16[9,64,128]{2,1,0:T(8,128)(2,1)S(1)}, u32[]{:S(2)}, u32[]{:S(2)}) collective-permute-start(f16[9,64,128]{2,1,0:T(8,128)(2,1)S(1)} %convert_element_type.40), channel_id=1, source_target_pairs={{0,12},{4,8},{8,4},{12,0},{16,28},{20,24},{24,20},{28,16},{1,13},{... | collective-permute-start | bytes 442376 | tf_op jit(solution)/shard_map/ppermute | solution.py:271
  82.4 4.6 %partner.3 = (f32[9,64,128]{2,1,0:T(8,128)S(1)}, f32[9,64,128]{2,1,0:T(8,128)S(1)}, f32[9,64,128]{2,1,0:T(8,128)S(1)}, bf16[16,8,4096]{2,1,0:T(8,128)(2,1)S(1)}, f32[8,128]{1,0:T(8,128)S(1)}) custom-call(s32[6]{0:T(128)S(1)} %stack.27.place.refs_0_, bf16[9,64,4096]{2,1,0:T(8,128)(2,1)S(1)} %get-tuple-element.29.refs_1_, ...), custom_call_target="tpu_custom_call" | custom-call | flops 1811939328 | bytes 1048576 | tf_op jit(solution)/shard_map/partner/pallas_call | solution.py:167
  87.2 1.5 %collective-permute-start.24 = (f16[9,64,128]{2,1,0:T(8,128)(2,1)S(1)}, f16[9,64,128]{2,1,0:T(8,128)(2,1)S(1)}, u32[]{:S(2)}, u32[]{:S(2)}) collective-permute-start(f16[9,64,128]{2,1,0:T(8,128)(2,1)S(1)} %convert_element_type.38), channel_id=1, source_target_pairs={{0,8},{8,0},{16,24},{24,16},{1,9},{9,1},{17,25},{25,17},{2,10},{10... | collective-permute-start | bytes 442376 | tf_op jit(solution)/shard_map/ppermute | solution.py:267
  89.5 2.9 %collective-permute-start.28 = (f16[9,64,128]{2,1,0:T(8,128)(2,1)S(1)}, f16[9,64,128]{2,1,0:T(8,128)(2,1)S(1)}, u32[]{:S(2)}, u32[]{:S(2)}) collective-permute-start(f16[9,64,128]{2,1,0:T(8,128)(2,1)S(1)} %convert_element_type.46), channel_id=1, source_target_pairs={{0,12},{4,8},{8,4},{12,0},{16,28},{20,24},{24,20},{28,16},{1,13},{... | collective-permute-start | bytes 442376 | tf_op jit(solution)/shard_map/ppermute | solution.py:271
  92.4 1.5 %collective-permute-start.27 = (f16[9,64,128]{2,1,0:T(8,128)(2,1)S(1)}, f16[9,64,128]{2,1,0:T(8,128)(2,1)S(1)}, u32[]{:S(2)}, u32[]{:S(2)}) collective-permute-start(f16[9,64,128]{2,1,0:T(8,128)(2,1)S(1)} %convert_element_type.44), channel_id=1, source_target_pairs={{0,8},{8,0},{16,24},{24,16},{1,9},{9,1},{17,25},{25,17},{2,10},{10... | collective-permute-start | bytes 442376 | tf_op jit(solution)/shard_map/ppermute | solution.py:267
  94.6 1.3 %lags.4 = (bf16[9,64,4096]{2,1,0:T(8,128)(2,1)S(1)}, f32[64,128]{1,0:T(8,128)S(1)}) custom-call(bf16[64,4096]{1,0:T(8,128)(2,1)S(1)} %get-tuple-element.26.rows_ref), custom_call_target="tpu_custom_call" | custom-call | flops 10485760 | bytes 6291456 | tf_op jit(solution)/shard_map/lags/pallas_call | solution.py:105
  95.9 1.5 %own.1 = (f32[9,64,128]{2,1,0:T(8,128)S(1)}, f32[9,64,128]{2,1,0:T(8,128)S(1)}) custom-call(bf16[9,64,4096]{2,1,0:T(8,128)(2,1)S(1)} %get-tuple-element.27.lagged, f32[64,128]{1,0:T(8,128)S(1)} %get-tuple-element.28.energy, bf16[16,8,4096]{2,1,0:T(8,128)(2,1)S(1)} %get-tuple-element.37.columns_a, f32[8,128]{1,0:T(8,128)S(1)} %get-tuple-element.38.scale_a, ...), custom_call_target="tpu_custom_call" | custom-call | flops 1207959552 | bytes 294912 | tf_op jit(solution)/shard_map/own/pallas_call | solution.py:207
  98.6 2.0 %collective-permute-done.26 = f16[9,64,128]{2,1,0:T(8,128)(2,1)S(1)} collective-permute-done((f16[9,64,128]{2,1,0:T(8,128)(2,1)S(1)}, f16[9,64,128]{2,1,0:T(8,128)(2,1)S(1)}, u32[]{:S(2)}, u32[]{:S(2)}) %collective-permute-start.26) | collective-permute-done | bytes 147488 | tf_op jit(solution)/shard_map/ppermute | solution.py:263
  100.6 2.9 %join.1 = f32[9,64,1024]{2,1,0:T(8,128)} custom-call(s32[6]{0:T(128)S(1)} %stack.27.place.refs_0_, f32[9,64,128]{2,1,0:T(8,128)S(1)} %get-tuple-element.41.refs_0_, f32[9,64,128]{2,1,0:T(8,128)S(1)} %convert_element_type.37.refs_1_, f32[9,64,128]{2,1,0:T(8,128)S(1)} %convert_element_type.39.refs_2_, f32[9,64,128]{2,1,0:T(8,128)S(1)} %convert_element_type.41.refs_3_, ...), custom_call_target="tpu_custom_call" | custom-call | tf_op jit(solution)/shard_map/join/pallas_call | solution.py:246
  (58 shorter events, 6.5 us)
Async XLA Ops:
  8.2 0.7 copy-start
  11.6 2.7 %collective-permute-start.3 = (bf16[8,4096]{1,0:T(8,128)(2,1)S(1)}, bf16[8,4096]{1,0:T(8,128)(2,1)S(1)}, u32[]{:S(2)}, u32[]{:S(2)}) collective-permute-start(bf16[8,4096]{1,0:T(8,128)(2,1)S(1)} %get-tuple-element.35), channel_id=1, source_target_pairs={{0,0},{1,64},{2,128},{3,192},{32,32},{33,96},{34,160},{35,224},{64... | collective-permute-start | bytes 196616 | tf_op jit(solution)/shard_map/ppermute | solution.py:284
  12.3 4.4 %collective-permute-start.4 = (bf16[8,4096]{1,0:T(8,128)(2,1)S(1)}, bf16[8,4096]{1,0:T(8,128)(2,1)S(1)}, u32[]{:S(2)}, u32[]{:S(2)}) collective-permute-start(bf16[8,4096]{1,0:T(8,128)(2,1)S(1)} %get-tuple-element.36), channel_id=1, source_target_pairs={{0,32},{1,96},{2,160},{3,224},{32,0},{33,64},{34,128},{35,192},{64... | collective-permute-start | bytes 196616 | tf_op jit(solution)/shard_map/ppermute | solution.py:284
  16.6 6.5 %collective-permute-start.5 = (bf16[1,8,4096]{2,1,0:T(8,128)(2,1)S(1)}, bf16[1,8,4096]{2,1,0:T(8,128)(2,1)S(1)}, u32[]{:S(2)}, u32[]{:S(2)}) collective-permute-start(bf16[1,8,4096]{2,1,0:T(8,128)(2,1)S(1)} %get-tuple-element.51), channel_id=1, source_target_pairs={{0,16},{8,24},{16,0},{24,8},{1,17},{9,25},{17,1},{25,9},{2,18},{10... | collective-permute-start | bytes 196616 | tf_op jit(solution)/shard_map/ppermute | solution.py:259
  18.8 24.1 %collective-permute-start = (bf16[64,4096]{1,0:T(8,128)(2,1)S(1)}, bf16[64,4096]{1,0:T(8,128)(2,1)S(1)}, u32[]{:S(2)}, u32[]{:S(2)}) collective-permute-start(bf16[64,4096]{1,0:T(8,128)(2,1)S(1)} %get-tuple-element.26.rows_ref), channel_id=1, source_target_pairs={{0,4},{4,0},{1,5},{5,1},{2,6},{6,2},{3,7},{7,3},{8,12},{12,8},{9,1... | collective-permute-start | bytes 1572872 | tf_op jit(solution)/shard_map/ppermute | solution.py:263
  21.7 15.5 %collective-permute-start.14 = (bf16[1,8,4096]{2,1,0:T(8,128)(2,1)S(1)}, bf16[1,8,4096]{2,1,0:T(8,128)(2,1)S(1)}, u32[]{:S(2)}, u32[]{:S(2)}) collective-permute-start(bf16[1,8,4096]{2,1,0:T(8,128)(2,1)S(1)} %get-tuple-element.50), channel_id=1, source_target_pairs={{0,16},{8,24},{16,0},{24,8},{1,17},{9,25},{17,1},{25,9},{2,18},{10... | collective-permute-start | bytes 196616 | tf_op jit(solution)/shard_map/ppermute | solution.py:259
  23.2 20.4 %collective-permute-start.7 = (bf16[2,8,4096]{2,1,0:T(8,128)(2,1)S(1)}, bf16[2,8,4096]{2,1,0:T(8,128)(2,1)S(1)}, u32[]{:S(2)}, u32[]{:S(2)}) collective-permute-start(bf16[2,8,4096]{2,1,0:T(8,128)(2,1)S(1)} %pad_maximum_fusion.refs_7_), channel_id=1, source_target_pairs={{0,224},{32,0},{64,32},{96,64},{128,96},{160,128},{192,160},{224,1... | collective-permute-start | bytes 393224 | tf_op jit(solution)/shard_map/ppermute | solution.py:259
  37.2 6.3 %collective-permute-start.6 = (bf16[2,8,4096]{2,1,0:T(8,128)(2,1)S(1)}, bf16[2,8,4096]{2,1,0:T(8,128)(2,1)S(1)}, u32[]{:S(2)}, u32[]{:S(2)}) collective-permute-start(bf16[2,8,4096]{2,1,0:T(8,128)(2,1)S(1)} %pad_maximum_fusion.refs_7_), channel_id=1, source_target_pairs={{0,32},{32,64},{64,96},{96,128},{128,160},{160,192},{192,224},{224... | collective-permute-start | bytes 393224 | tf_op jit(solution)/shard_map/ppermute | solution.py:259
  37.3 10.1 %collective-permute-start.16 = (bf16[2,8,4096]{2,1,0:T(8,128)(2,1)S(1)}, bf16[2,8,4096]{2,1,0:T(8,128)(2,1)S(1)}, u32[]{:S(2)}, u32[]{:S(2)}) collective-permute-start(bf16[2,8,4096]{2,1,0:T(8,128)(2,1)S(1)} %pad_maximum_fusion.1.refs_7_), channel_id=1, source_target_pairs={{0,224},{32,0},{64,32},{96,64},{128,96},{160,128},{192,160},{224,1... | collective-permute-start | bytes 393224 | tf_op jit(solution)/shard_map/ppermute | solution.py:259
  41.5 30.3 %collective-permute-start.1 = (bf16[64,4096]{1,0:T(8,128)(2,1)S(1)}, bf16[64,4096]{1,0:T(8,128)(2,1)S(1)}, u32[]{:S(2)}, u32[]{:S(2)}) collective-permute-start(bf16[64,4096]{1,0:T(8,128)(2,1)S(1)} %get-tuple-element.26.rows_ref), channel_id=1, source_target_pairs={{0,8},{8,0},{16,24},{24,16},{1,9},{9,1},{17,25},{25,17},{2,10},{10... | collective-permute-start | bytes 1572872 | tf_op jit(solution)/shard_map/ppermute | solution.py:267
  42.9 30.3 %collective-permute-start.2 = (bf16[64,4096]{1,0:T(8,128)(2,1)S(1)}, bf16[64,4096]{1,0:T(8,128)(2,1)S(1)}, u32[]{:S(2)}, u32[]{:S(2)}) collective-permute-start(bf16[64,4096]{1,0:T(8,128)(2,1)S(1)} %collective-permute-done.rows_ref), channel_id=1, source_target_pairs={{0,8},{8,0},{16,24},{24,16},{1,9},{9,1},{17,25},{25,17},{2,10},{10... | collective-permute-start | bytes 1572872 | tf_op jit(solution)/shard_map/ppermute | solution.py:267
  43.5 6.7 %collective-permute-start.15 = (bf16[2,8,4096]{2,1,0:T(8,128)(2,1)S(1)}, bf16[2,8,4096]{2,1,0:T(8,128)(2,1)S(1)}, u32[]{:S(2)}, u32[]{:S(2)}) collective-permute-start(bf16[2,8,4096]{2,1,0:T(8,128)(2,1)S(1)} %pad_maximum_fusion.1.refs_7_), channel_id=1, source_target_pairs={{0,32},{32,64},{64,96},{96,128},{128,160},{160,192},{192,224},{224... | collective-permute-start | bytes 393224 | tf_op jit(solution)/shard_map/ppermute | solution.py:259
  43.5 10.8 %collective-permute-start.9 = (bf16[2,8,4096]{2,1,0:T(8,128)(2,1)S(1)}, bf16[2,8,4096]{2,1,0:T(8,128)(2,1)S(1)}, u32[]{:S(2)}, u32[]{:S(2)}) collective-permute-start(bf16[2,8,4096]{2,1,0:T(8,128)(2,1)S(1)} %collective-permute-done.7.refs_9_), channel_id=1, source_target_pairs={{0,224},{32,0},{64,32},{96,64},{128,96},{160,128},{192,160},{224,1... | collective-permute-start | bytes 393224 | tf_op jit(solution)/shard_map/ppermute | solution.py:259
  47.4 7.0 %collective-permute-start.8 = (bf16[2,8,4096]{2,1,0:T(8,128)(2,1)S(1)}, bf16[2,8,4096]{2,1,0:T(8,128)(2,1)S(1)}, u32[]{:S(2)}, u32[]{:S(2)}) collective-permute-start(bf16[2,8,4096]{2,1,0:T(8,128)(2,1)S(1)} %collective-permute-done.6.refs_8_), channel_id=1, source_target_pairs={{0,32},{32,64},{64,96},{96,128},{128,160},{160,192},{192,224},{224... | collective-permute-start | bytes 393224 | tf_op jit(solution)/shard_map/ppermute | solution.py:259
  50.2 7.3 %collective-permute-start.18 = (bf16[2,8,4096]{2,1,0:T(8,128)(2,1)S(1)}, bf16[2,8,4096]{2,1,0:T(8,128)(2,1)S(1)}, u32[]{:S(2)}, u32[]{:S(2)}) collective-permute-start(bf16[2,8,4096]{2,1,0:T(8,128)(2,1)S(1)} %collective-permute-done.16.refs_9_), channel_id=1, source_target_pairs={{0,224},{32,0},{64,32},{96,64},{128,96},{160,128},{192,160},{224,1... | collective-permute-start | bytes 393224 | tf_op jit(solution)/shard_map/ppermute | solution.py:259
  54.3 6.9 %collective-permute-start.17 = (bf16[2,8,4096]{2,1,0:T(8,128)(2,1)S(1)}, bf16[2,8,4096]{2,1,0:T(8,128)(2,1)S(1)}, u32[]{:S(2)}, u32[]{:S(2)}) collective-permute-start(bf16[2,8,4096]{2,1,0:T(8,128)(2,1)S(1)} %collective-permute-done.15.refs_8_), channel_id=1, source_target_pairs={{0,32},{32,64},{64,96},{96,128},{128,160},{160,192},{192,224},{224... | collective-permute-start | bytes 393224 | tf_op jit(solution)/shard_map/ppermute | solution.py:259
  54.3 7.2 %collective-permute-start.11 = (bf16[2,8,4096]{2,1,0:T(8,128)(2,1)S(1)}, bf16[2,8,4096]{2,1,0:T(8,128)(2,1)S(1)}, u32[]{:S(2)}, u32[]{:S(2)}) collective-permute-start(bf16[2,8,4096]{2,1,0:T(8,128)(2,1)S(1)} %collective-permute-done.9.refs_11_), channel_id=1, source_target_pairs={{0,224},{32,0},{64,32},{96,64},{128,96},{160,128},{192,160},{224,1... | collective-permute-start | bytes 393224 | tf_op jit(solution)/shard_map/ppermute | solution.py:259
  57.6 7.5 %collective-permute-start.10 = (bf16[2,8,4096]{2,1,0:T(8,128)(2,1)S(1)}, bf16[2,8,4096]{2,1,0:T(8,128)(2,1)S(1)}, u32[]{:S(2)}, u32[]{:S(2)}) collective-permute-start(bf16[2,8,4096]{2,1,0:T(8,128)(2,1)S(1)} %collective-permute-done.8.refs_10_), channel_id=1, source_target_pairs={{0,32},{32,64},{64,96},{96,128},{128,160},{160,192},{192,224},{224... | collective-permute-start | bytes 393224 | tf_op jit(solution)/shard_map/ppermute | solution.py:259
  61.2 5.9 %collective-permute-start.20 = (bf16[2,8,4096]{2,1,0:T(8,128)(2,1)S(1)}, bf16[2,8,4096]{2,1,0:T(8,128)(2,1)S(1)}, u32[]{:S(2)}, u32[]{:S(2)}) collective-permute-start(bf16[2,8,4096]{2,1,0:T(8,128)(2,1)S(1)} %collective-permute-done.18.refs_11_), channel_id=1, source_target_pairs={{0,224},{32,0},{64,32},{96,64},{128,96},{160,128},{192,160},{224,1... | collective-permute-start | bytes 393224 | tf_op jit(solution)/shard_map/ppermute | solution.py:259
  61.6 6.9 %collective-permute-start.19 = (bf16[2,8,4096]{2,1,0:T(8,128)(2,1)S(1)}, bf16[2,8,4096]{2,1,0:T(8,128)(2,1)S(1)}, u32[]{:S(2)}, u32[]{:S(2)}) collective-permute-start(bf16[2,8,4096]{2,1,0:T(8,128)(2,1)S(1)} %collective-permute-done.17.refs_10_), channel_id=1, source_target_pairs={{0,32},{32,64},{64,96},{96,128},{128,160},{160,192},{192,224},{224... | collective-permute-start | bytes 393224 | tf_op jit(solution)/shard_map/ppermute | solution.py:259
  65.1 9.4 %collective-permute-start.13 = (bf16[1,8,4096]{2,1,0:T(8,128)(2,1)S(1)}, bf16[1,8,4096]{2,1,0:T(8,128)(2,1)S(1)}, u32[]{:S(2)}, u32[]{:S(2)}) collective-permute-start(bf16[1,8,4096]{2,1,0:T(8,128)(2,1)S(1)} %slice.17), channel_id=1, source_target_pairs={{0,224},{32,0},{64,32},{96,64},{128,96},{160,128},{192,160},{224,1... | collective-permute-start | bytes 196616 | tf_op jit(solution)/shard_map/ppermute | solution.py:259
  67.1 7.3 %collective-permute-start.12 = (bf16[1,8,4096]{2,1,0:T(8,128)(2,1)S(1)}, bf16[1,8,4096]{2,1,0:T(8,128)(2,1)S(1)}, u32[]{:S(2)}, u32[]{:S(2)}) collective-permute-start(bf16[1,8,4096]{2,1,0:T(8,128)(2,1)S(1)} %slice.16), channel_id=1, source_target_pairs={{0,32},{32,64},{64,96},{96,128},{128,160},{160,192},{192,224},{224... | collective-permute-start | bytes 196616 | tf_op jit(solution)/shard_map/ppermute | solution.py:259
  68.4 14.0 %collective-permute-start.22 = (bf16[1,8,4096]{2,1,0:T(8,128)(2,1)S(1)}, bf16[1,8,4096]{2,1,0:T(8,128)(2,1)S(1)}, u32[]{:S(2)}, u32[]{:S(2)}) collective-permute-start(bf16[1,8,4096]{2,1,0:T(8,128)(2,1)S(1)} %slice.19), channel_id=1, source_target_pairs={{0,224},{32,0},{64,32},{96,64},{128,96},{160,128},{192,160},{224,1... | collective-permute-start | bytes 196616 | tf_op jit(solution)/shard_map/ppermute | solution.py:259
  71.8 10.6 %collective-permute-start.21 = (bf16[1,8,4096]{2,1,0:T(8,128)(2,1)S(1)}, bf16[1,8,4096]{2,1,0:T(8,128)(2,1)S(1)}, u32[]{:S(2)}, u32[]{:S(2)}) collective-permute-start(bf16[1,8,4096]{2,1,0:T(8,128)(2,1)S(1)} %slice.18), channel_id=1, source_target_pairs={{0,32},{32,64},{64,96},{96,128},{128,160},{160,192},{192,224},{224... | collective-permute-start | bytes 196616 | tf_op jit(solution)/shard_map/ppermute | solution.py:259
  79.2 14.8 %collective-permute-start.25 = (f16[9,64,128]{2,1,0:T(8,128)(2,1)S(1)}, f16[9,64,128]{2,1,0:T(8,128)(2,1)S(1)}, u32[]{:S(2)}, u32[]{:S(2)}) collective-permute-start(f16[9,64,128]{2,1,0:T(8,128)(2,1)S(1)} %convert_element_type.40), channel_id=1, source_target_pairs={{0,12},{4,8},{8,4},{12,0},{16,28},{20,24},{24,20},{28,16},{1,13},{... | collective-permute-start | bytes 442376 | tf_op jit(solution)/shard_map/ppermute | solution.py:271
  87.2 10.2 %collective-permute-start.24 = (f16[9,64,128]{2,1,0:T(8,128)(2,1)S(1)}, f16[9,64,128]{2,1,0:T(8,128)(2,1)S(1)}, u32[]{:S(2)}, u32[]{:S(2)}) collective-permute-start(f16[9,64,128]{2,1,0:T(8,128)(2,1)S(1)} %convert_element_type.38), channel_id=1, source_target_pairs={{0,8},{8,0},{16,24},{24,16},{1,9},{9,1},{17,25},{25,17},{2,10},{10... | collective-permute-start | bytes 442376 | tf_op jit(solution)/shard_map/ppermute | solution.py:267
  88.8 8.9 %collective-permute-start.23 = (f16[9,64,128]{2,1,0:T(8,128)(2,1)S(1)}, f16[9,64,128]{2,1,0:T(8,128)(2,1)S(1)}, u32[]{:S(2)}, u32[]{:S(2)}) collective-permute-start(f16[9,64,128]{2,1,0:T(8,128)(2,1)S(1)} %convert_element_type.36), channel_id=1, source_target_pairs={{0,4},{4,0},{1,5},{5,1},{2,6},{6,2},{3,7},{7,3},{8,12},{12,8},{9,1... | collective-permute-start | bytes 442376 | tf_op jit(solution)/shard_map/ppermute | solution.py:263
  89.5 8.2 %collective-permute-start.28 = (f16[9,64,128]{2,1,0:T(8,128)(2,1)S(1)}, f16[9,64,128]{2,1,0:T(8,128)(2,1)S(1)}, u32[]{:S(2)}, u32[]{:S(2)}) collective-permute-start(f16[9,64,128]{2,1,0:T(8,128)(2,1)S(1)} %convert_element_type.46), channel_id=1, source_target_pairs={{0,12},{4,8},{8,4},{12,0},{16,28},{20,24},{24,20},{28,16},{1,13},{... | collective-permute-start | bytes 442376 | tf_op jit(solution)/shard_map/ppermute | solution.py:271
  92.4 6.1 %collective-permute-start.27 = (f16[9,64,128]{2,1,0:T(8,128)(2,1)S(1)}, f16[9,64,128]{2,1,0:T(8,128)(2,1)S(1)}, u32[]{:S(2)}, u32[]{:S(2)}) collective-permute-start(f16[9,64,128]{2,1,0:T(8,128)(2,1)S(1)} %convert_element_type.44), channel_id=1, source_target_pairs={{0,8},{8,0},{16,24},{24,16},{1,9},{9,1},{17,25},{25,17},{2,10},{10... | collective-permute-start | bytes 442376 | tf_op jit(solution)/shard_map/ppermute | solution.py:267
  94.0 6.6 %collective-permute-start.26 = (f16[9,64,128]{2,1,0:T(8,128)(2,1)S(1)}, f16[9,64,128]{2,1,0:T(8,128)(2,1)S(1)}, u32[]{:S(2)}, u32[]{:S(2)}) collective-permute-start(f16[9,64,128]{2,1,0:T(8,128)(2,1)S(1)} %convert_element_type.42), channel_id=1, source_target_pairs={{0,4},{4,0},{1,5},{5,1},{2,6},{6,2},{3,7},{7,3},{8,12},{12,8},{9,1... | collective-permute-start | bytes 442376 | tf_op jit(solution)/shard_map/ppermute | solution.py:263

commit v3 on v2

v3 whole, which is shorter than its diff:
```python
import jax
import jax.numpy as jnp
import numpy as np
from jax import lax
from jax.experimental import pallas as pl
from jax.experimental.pallas import tpu as pltpu
from jax.sharding import Mesh, PartitionSpec as P

LAGS = 9
REACH = 4
HALF = 32
NT = (((1,), (1,)), ((), ()))
MB = 1 << 20
SENT = jnp.float16
SCALE = 65536.0


def cut_kernel(place, raw, *outs):
    for k, out in enumerate(outs):
        at = pl.multiple_of(((place[0] + k) & 7) * 8, 8)
        out[...] = raw[pl.ds(at, 8), :]


def run_cut(place, raw):
    rows, bins = raw.shape
    vmem = pl.BlockSpec(memory_space=pltpu.VMEM)
    piece = jax.ShapeDtypeStruct((8, bins), raw.dtype)
    return pl.pallas_call(
        cut_kernel,
        in_specs=[pl.BlockSpec(memory_space=pltpu.SMEM), vmem],
        out_specs=[vmem] * (rows // 8),
        out_shape=[piece] * (rows // 8),
        compiler_params=pltpu.CompilerParams(vmem_limit_bytes=4 * MB),
        name="cut",
    )(place, raw)


def band(taps, line, weights):
    line[...] = jnp.zeros(line.shape, jnp.float32)
    line[0:1, 0 : taps.shape[1]] = taps[...]
    wide = jnp.broadcast_to(line[0:1, :], (128, 384))
    full = pltpu.roll(wide, 128 - HALF, axis=1, stride=1, stride_axis=0)
    high = full.astype(jnp.bfloat16)
    rest = full - high.astype(jnp.float32)
    middle = rest.astype(jnp.bfloat16)
    low = (rest - middle.astype(jnp.float32)).astype(jnp.bfloat16)
    weights[0:128] = high
    weights[128:256] = middle
    weights[256:384] = low


def filtered_blocks(window, weights):
    total = None
    for k in range(3):
        piece = window(k)
        piece = piece.reshape(piece.shape[0] * piece.shape[1], 128)
        term = lax.dot_general(
            piece, weights[:, k * 128 : (k + 1) * 128], NT, preferred_element_type=jnp.float32
        )
        total = term if total is None else total + term
    value = (total[:, 256:384] + total[:, 128:256]) + total[:, 0:128]
    return value.astype(jnp.bfloat16)


def piece_filter_kernel(place, taps, *refs):
    pieces = refs[:8]
    out, blocks, weights, line = refs[8:]
    per = pieces[0].shape[1] // 128
    count = 4 * per
    for e in range(2):
        blocks[e, 0] = jnp.zeros((8, 128), jnp.bfloat16)
        blocks[e, count + 1] = jnp.zeros((8, 128), jnp.bfloat16)
    for k, piece in enumerate(pieces):
        u = (place[1] - k) & 7
        for b in range(per):
            blocks[u >> 2, 1 + (u & 3) * per + b] = piece[:, b * 128 : (b + 1) * 128]
    band(taps, line, weights)
    for e in range(2):
        value = filtered_blocks(lambda k: blocks[e, k : k + count], weights)
        for n in range(count):
            out[e, :, n * 128 : (n + 1) * 128] = value[n * 8 : (n + 1) * 8]


def run_piece_filter(place, taps, pieces):
    bins = pieces[0].shape[1]
    vmem = pl.BlockSpec(memory_space=pltpu.VMEM)
    return pl.pallas_call(
        piece_filter_kernel,
        in_specs=[pl.BlockSpec(memory_space=pltpu.SMEM)] + [vmem] * 9,
        out_specs=vmem,
        out_shape=jax.ShapeDtypeStruct((2, 8, 4 * bins), jnp.bfloat16),
        scratch_shapes=[
            pltpu.VMEM((2, 4 * bins // 128 + 2, 8, 128), jnp.bfloat16),
            pltpu.VMEM((384, 384), jnp.bfloat16),
            pltpu.VMEM((8, 384), jnp.float32),
        ],
        compiler_params=pltpu.CompilerParams(vmem_limit_bytes=8 * MB),
        name="pieces",
    )(place, taps, *pieces)


def row_filter_kernel(place, taps, own, core, line_y, both, out, mine, blocks, weights, line):
    rows, bins = own.shape
    per = bins // 128
    count = 4 * per
    q = place[2]
    blocks[0] = jnp.zeros((rows, 128), jnp.bfloat16)
    blocks[count + 1] = jnp.zeros((rows, 128), jnp.bfloat16)
    for flip, part in enumerate((own, core, line_y, both)):
        for b in range(per):
            blocks[1 + (q ^ flip) * per + b] = part[:, b * 128 : (b + 1) * 128]
    band(taps, line, weights)
    group = 8
    for g in range(0, count, group):
        value = filtered_blocks(lambda k: blocks[g + k : g + k + group], weights)
        for b in range(group):
            n = g + b
            out[:, n * 128 : (n + 1) * 128] = value[b * rows : (b + 1) * rows]
    mine[...] = out[:, pl.ds(pl.multiple_of(q * bins, 128), bins)]


def run_row_filter(place, taps, parts):
    rows, bins = parts[0].shape
    vmem = pl.BlockSpec(memory_space=pltpu.VMEM)
    return pl.pallas_call(
        row_filter_kernel,
        in_specs=[pl.BlockSpec(memory_space=pltpu.SMEM)] + [vmem] * 5,
        out_specs=[vmem, vmem],
        out_shape=[
            jax.ShapeDtypeStruct((rows, 4 * bins), jnp.bfloat16),
            jax.ShapeDtypeStruct((rows, bins), jnp.bfloat16),
        ],
        scratch_shapes=[
            pltpu.VMEM((4 * bins // 128 + 2, rows, 128), jnp.bfloat16),
            pltpu.VMEM((384, 384), jnp.bfloat16),
            pltpu.VMEM((8, 384), jnp.float32),
        ],
        compiler_params=pltpu.CompilerParams(vmem_limit_bytes=8 * MB),
        cost_estimate=pl.CostEstimate(flops=1 << 30, bytes_accessed=4 * MB, transcendentals=0),
        name="rows",
    )(place, taps, *parts)


def lag_kernel(rows_ref, out, energy):
    bins = rows_ref.shape[1]
    at = lax.broadcasted_iota(jnp.int32, (16, bins), 1)
    for part in range(rows_ref.shape[0] // 16):
        span = slice(part * 16, (part + 1) * 16)
        value = rows_ref[span].astype(jnp.float32)
        total = jnp.sum(value * value, axis=1, keepdims=True)
        energy[span] = jnp.broadcast_to(total, (16, 128))
        for lag in range(LAGS):
            step = lag - REACH
            if step == 0:
                moved = value
            else:
                moved = pltpu.roll(value, step % bins, axis=1)
                inside = at >= step if step > 0 else at < bins + step
                moved = jnp.where(inside, moved, 0.0)
            out[lag, span] = moved.astype(jnp.bfloat16)


def run_lags(rows):
    count, bins = rows.shape
    vmem = pl.BlockSpec(memory_space=pltpu.VMEM)
    return pl.pallas_call(
        lag_kernel,
        in_specs=[vmem],
        out_specs=[vmem, vmem],
        out_shape=[
            jax.ShapeDtypeStruct((LAGS, count, bins), jnp.bfloat16),
            jax.ShapeDtypeStruct((count, 128), jnp.float32),
        ],
        compiler_params=pltpu.CompilerParams(vmem_limit_bytes=8 * MB),
        cost_estimate=pl.CostEstimate(flops=10 * MB, bytes_accessed=6 * MB, transcendentals=0),
        name="lags",
    )(rows)


def weigh(lagged, energy, right, across, emit):
    lags, count, bins = lagged.shape
    left = lagged[...].reshape(lags * count, bins)
    moments = lax.dot_general(left, right, NT, preferred_element_type=jnp.float32)
    norms = (1.0 / jnp.sqrt(energy[:, 0:1] + 1e-05)) * across
    for lag in range(lags):
        ratio = moments[lag * count : (lag + 1) * count] * norms
        emit(lag, -0.5 * jnp.log(1.0 - ratio * ratio))


def columns_kernel(steps, place, *refs):
    units = refs[: len(steps)]
    columns, scale = refs[len(steps) :]
    z = place[1]
    for ref, moves in zip(units, steps):
        for k, (part, z_step) in enumerate(moves):
            columns[part * 8 + ((z + z_step) & 7)] = ref[k]
    width = columns.shape[0] * columns.shape[1]
    for g in range(width // 128):
        block = columns[g * 16 : (g + 1) * 16].astype(jnp.float32).reshape(128, -1)
        total = jnp.sum(block * block, axis=1, keepdims=True)
        root = 0.8 / jnp.sqrt(total + 1e-05)
        root = jnp.transpose(jnp.broadcast_to(root, (128, 128)))
        scale[:, g * 128 : (g + 1) * 128] = root[0:8]


def run_columns(place, units, steps):
    slots = sum(len(moves) for moves in steps)
    bins = units[0].shape[2]

    def body(*refs):
        columns_kernel(steps, *refs)

    vmem = pl.BlockSpec(memory_space=pltpu.VMEM)
    return pl.pallas_call(
        body,
        in_specs=[pl.BlockSpec(memory_space=pltpu.SMEM)] + [vmem] * len(units),
        out_specs=[vmem, vmem],
        out_shape=[
            jax.ShapeDtypeStruct((slots, 8, bins), jnp.bfloat16),
            jax.ShapeDtypeStruct((8, slots * 8), jnp.float32),
        ],
        compiler_params=pltpu.CompilerParams(vmem_limit_bytes=8 * MB),
        cost_estimate=pl.CostEstimate(flops=8 * MB, bytes_accessed=4 * MB, transcendentals=0),
        name="columns",
    )(place, *units)


def weigh_kernel(factor, lagged, energy, columns, scale, out):
    lags, count, bins = lagged.shape
    left = lagged[...].reshape(lags * count, bins)
    right = columns[...].reshape(-1, bins)
    moments = lax.dot_general(left, right, NT, preferred_element_type=jnp.float32)
    norms = (1.0 / jnp.sqrt(energy[:, 0:1] + 1e-05)) * scale[0:1, :]
    for lag in range(lags):
        ratio = moments[lag * count : (lag + 1) * count] * norms
        value = -0.5 * jnp.log(1.0 - ratio * ratio)
        out[lag] = value if factor == 1 else value * factor


def run_weigh(rows, columns, scale, factor):
    lagged, energy = rows
    lags, count, bins = lagged.shape
    width = scale.shape[1]

    def body(*refs):
        weigh_kernel(factor, *refs)

    vmem = pl.BlockSpec(memory_space=pltpu.VMEM)
    return pl.pallas_call(
        body,
        in_specs=[vmem] * 4,
        out_specs=vmem,
        out_shape=jax.ShapeDtypeStruct((lags, count, width), jnp.float32),
        compiler_params=pltpu.CompilerParams(vmem_limit_bytes=8 * MB),
        cost_estimate=pl.CostEstimate(
            flops=2 * lags * count * width * bins,
            bytes_accessed=4 * lags * count * width,
            transcendentals=lags * count * width,
        ),
        name="weigh",
    )(lagged, energy, columns, scale)


def join_kernel(place, own, got_y, got_x, got_xy, out):
    low = place[4] == 0
    rows = out.shape[1]
    lane = lax.broadcasted_iota(jnp.int32, (rows, 128), 1) < 64
    for half in range(2):
        span = slice(half * 128, (half + 1) * 128)
        for flip, (same, cross) in enumerate(((own, got_y), (got_x, got_xy))):
            here_x = place[3] ^ flip
            for lag in range(out.shape[0]):
                here = same[lag, :, span] * (1.0 / SCALE) if flip else same[lag, :, span]
                there = cross[lag, :, span] * (1.0 / SCALE)
                one = jnp.where(low, here, there)
                two = jnp.where(low, there, here)
                at = pl.multiple_of((half * 4 + here_x) * 128, 128)
                out[lag, :, pl.ds(at, 128)] = jnp.where(lane, one, pltpu.roll(two, 64, axis=1))
                at = pl.multiple_of((half * 4 + (here_x ^ 2)) * 128, 128)
                out[lag, :, pl.ds(at, 128)] = jnp.where(lane, pltpu.roll(one, 64, axis=1), two)


def run_join(place, *quarters):
    lags, rows, width = quarters[0].shape
    spec = pl.BlockSpec((3, rows, width), lambda i: (i, 0, 0))
    return pl.pallas_call(
        join_kernel,
        grid=(lags // 3,),
        in_specs=[pl.BlockSpec(memory_space=pltpu.SMEM)] + [spec] * 4,
        out_specs=pl.BlockSpec((3, rows, 4 * width), lambda i: (i, 0, 0)),
        out_shape=jax.ShapeDtypeStruct((lags, rows, 4 * width), jnp.float32),
        compiler_params=pltpu.CompilerParams(vmem_limit_bytes=8 * MB),
        name="join",
    )(place, *quarters)


def around(value, axis, step):
    size = lax.axis_size(axis)
    return lax.ppermute(value, axis, [(i, (i + step) % size) for i in range(size)])


def cross_y(value):
    return lax.ppermute(value, "yh", [(0, 1), (1, 0)])


def cross_x(value):
    return lax.ppermute(value, "x", [(0, 1), (1, 0), (2, 3), (3, 2)])


def cross_xy(value):
    return lax.ppermute(value, ("x", "yh"), [(i, i ^ 3) for i in range(8)])


def sent(move, value):
    return move(value.astype(SENT)).astype(jnp.float32)


def spread(value, k):
    pairs = []
    for z in range(8):
        for q in range(4):
            pairs.append((z * 4 + q, ((4 * (z & 1) + q + k) & 7) * 4 + (z >> 1)))
    return lax.ppermute(value, ("z", "yl", "core"), pairs)


def flipped(value, flip):
    return lax.ppermute(value, ("yl", "core"), [(i, i ^ flip) for i in range(4)])


def after(value, *others):
    return lax.optimization_barrier((value, *others))[0]


def shards(raw, taps):
    z = lax.axis_index("z")
    x = lax.axis_index("x")
    yh = lax.axis_index("yh")
    q = lax.axis_index(("yl", "core"))
    place = jnp.stack([4 * (z % 2) + q, z, q, x, yh]).astype(jnp.int32)
    taps = taps.reshape(1, -1)
    pieces = [spread(piece, k) for k, piece in enumerate(run_cut(place, raw))]
    parts = [raw] + [flipped(raw, flip) for flip in (1, 2, 3)]
    unit = run_piece_filter(place, taps, pieces)
    base = jnp.concatenate([unit, around(unit, "x", 2)], axis=0)
    units, steps = [base], [[(0, 0), (2, 0), (1, 0), (3, 0)]]
    order = [part for part, _ in steps[0]]
    first = (around(base, "z", 1), around(base, "z", -1))
    second = (around(first[0], "z", 1), around(first[1], "z", -1))
    full, mine = run_row_filter(place, taps, [after(raw, unit)] + parts[1:])
    row_y = cross_y(full)
    row_x = cross_x(full)
    row_xy = cross_x(after(row_y, *first))
    own = run_lags(after(full, *first))
    ready = after(second, own)
    third = (around(ready[0], "z", 1), around(ready[1], "z", -1))
    far_y = run_lags(after(row_y, *second))
    ready = after(third, far_y)
    units += [*first, *second, *third, around(ready[0][0:2], "z", 1), around(ready[1][2:4], "z", -1)]
    for step in (1, 2, 3):
        steps += [[(part, -step) for part in order], [(part, step) for part in order]]
    steps += [[(part, 4) for part in order[0:2]], [(part, 4) for part in order[2:4]]]
    far_x = run_lags(after(row_x, *third))
    far_xy = run_lags(row_xy)
    columns, scale = run_columns(place, units, steps)
    got_xy = sent(cross_xy, run_weigh(far_xy, columns, scale, SCALE))
    got_x = sent(cross_x, run_weigh(far_x, columns, scale, SCALE))
    got_y = sent(cross_y, run_weigh(far_y, columns, scale, SCALE))
    information = run_join(place, run_weigh(own, columns, scale, 1), got_y, got_x, got_xy)
    return (information, mine)


def solution(mesh):
    fine = Mesh(mesh.devices.reshape(8, 4, 2, 2, 2), ("z", "x", "yh", "yl", "core"))
    rows, bins = ("z", "x", "yh"), ("yl", "core")
    return jax.shard_map(
        shards,
        mesh=fine,
        in_specs=(P(rows, bins), P()),
        out_specs=(P(None, rows, bins), P(rows, bins)),
        check_vma=False,
    )
```

time: 104 us -> 112 us (1.077)
  starting transfers between devices: 57.6 us -> 67.8 us
  blocking collectives: 7.47 us -> 0 us
  waiting for transfers between devices: 15 us -> 19.2 us
  local copies, waits for them, and re-layouts: 0.76 us -> 3.22 us
  Pallas kernels: 21.5 us -> 19.5 us
    ppermute x2 -> x8, starting transfers between devices: 2.66 us -> 32.8 us  [spread(): return lax.ppermute(value, ('z', 'yl', 'core'), pairs)]
    ppermute x18 -> x9, starting transfers between devices: 39.4 us -> 15.4 us  [around(): lax.ppermute(value, axis, [(i, (i + step) % size) for i in range(size)])]
    ppermute x0 -> x3, starting transfers between devices: none -> 8.33 us  [flipped(): lax.ppermute(value, ('yl', 'core'), [(i, i ^ flip) for i in range(4)])]
    all_gather x1 -> x0, blocking collectives: 7.47 us -> none  [shards(): everything = lax.all_gather(raw, ('yl', 'core'), axis=0, tiled=False)]
    ppermute x2 -> x1, waiting for transfers between devices: 0.01 us -> 6.32 us  [cross_xy(): return lax.ppermute(value, ('x', 'yh'), [(i, i ^ 3) for i in range(8)])]
    ppermute x0 -> x3, waiting for transfers between devices: none -> 3.5 us  [flipped(): lax.ppermute(value, ('yl', 'core'), [(i, i ^ flip) for i in range(4)])]
    ppermute x2 -> x1, starting transfers between devices: 6.13 us -> 3.32 us  [cross_xy(): return lax.ppermute(value, ('x', 'yh'), [(i, i ^ 3) for i in range(8)])]
    unnamed x2 -> x8, local copies, waits for them, and re-layouts: 0.66 us -> 3.12 us
  transfers between devices with their start and end apart: 29 -> 26, of which waited for: 8 -> 7; matrix products, arithmetic and copies ran while one was open for 0% -> 0% of each run, Pallas kernels for 15% -> 13%
where the time goes in v3:
time: 112 us; the launch traced here: 111 us
  starting transfers between devices  67.8 us (61%)
  Pallas kernels  19.5 us (17%)
  waiting for transfers between devices  19.2 us (17%)
  local copies, waits for them, and re-layouts  3.22 us (3%)
    ppermute x8, starting transfers between devices, spread(): return lax.ppermute(value, ('z', 'yl', 'core'), pairs)  32.8 us
    ppermute x9, starting transfers between devices, around(): lax.ppermute(value, axis, [(i, (i + step) % size) for i in range(size)])  15.4 us
    ppermute x3, starting transfers between devices, flipped(): lax.ppermute(value, ('yl', 'core'), [(i, i ^ flip) for i in range(4)])  8.33 us
    ppermute x9, waiting for transfers between devices, around(): lax.ppermute(value, axis, [(i, (i + step) % size) for i in range(size)])  7.73 us
    ppermute x1, waiting for transfers between devices, cross_xy(): return lax.ppermute(value, ('x', 'yh'), [(i, i ^ 3) for i in range(8)])  6.32 us
    pallas_call x4, Pallas kernels, run_weigh(): pl.pallas_call(body, in_specs=[vmem] * 4, out_specs=vmem, out_shape=jax.S...  5.74 us
    pallas_call x4, Pallas kernels, run_lags(): pl.pallas_call(lag_kernel, in_specs=[vmem], out_specs=[vmem, vmem], out_s...  5.05 us
    ppermute x3, starting transfers between devices, cross_x(): return lax.ppermute(value, 'x', [(0, 1), (1, 0), (2, 3), (3, 2)])  4.4 us
  transfers between devices with their start and end apart: 26, of which 7 were waited for; matrix products, arithmetic and copies ran while one was open for 0% of the time, Pallas kernels for 13%

profile of v3, /device:TPU:2, one launch (start us, length us, event | category | flops | bytes accessed | tf_op | source)
XLA Modules:
  0.0 111.0 jit_solution(8030792758931637479)
XLA Ops:
  2.9 10.9 %collective-permute-start.1 = (bf16[8,1024]{1,0:T(8,128)(2,1)S(1)}, bf16[8,1024]{1,0:T(8,128)(2,1)S(1)}, u32[]{:S(2)}, u32[]{:S(2)}) collective-permute-start(bf16[8,1024]{1,0:T(8,128)(2,1)S(1)} %get-tuple-element.32), channel_id=1, source_target_pairs={{0,32},{1,64},{2,96},{3,128},{32,160},{33,192},{34,224},{35,0},{64... | collective-permute-start | bytes 49160 | tf_op jit(solution)/shard_map/ppermute | solution.py:323
  13.8 3.5 %collective-permute-start.2 = (bf16[8,1024]{1,0:T(8,128)(2,1)S(1)}, bf16[8,1024]{1,0:T(8,128)(2,1)S(1)}, u32[]{:S(2)}, u32[]{:S(2)}) collective-permute-start(bf16[8,1024]{1,0:T(8,128)(2,1)S(1)} %get-tuple-element.33), channel_id=1, source_target_pairs={{0,64},{1,96},{2,128},{3,160},{32,192},{33,224},{34,0},{35,32},{64... | collective-permute-start | bytes 49160 | tf_op jit(solution)/shard_map/ppermute | solution.py:323
  17.3 3.4 %collective-permute-start.3 = (bf16[8,1024]{1,0:T(8,128)(2,1)S(1)}, bf16[8,1024]{1,0:T(8,128)(2,1)S(1)}, u32[]{:S(2)}, u32[]{:S(2)}) collective-permute-start(bf16[8,1024]{1,0:T(8,128)(2,1)S(1)} %get-tuple-element.34), channel_id=1, source_target_pairs={{0,96},{1,128},{2,160},{3,192},{32,224},{33,0},{34,32},{35,64},{64... | collective-permute-start | bytes 49160 | tf_op jit(solution)/shard_map/ppermute | solution.py:323
  20.8 3.5 %collective-permute-start.4 = (bf16[8,1024]{1,0:T(8,128)(2,1)S(1)}, bf16[8,1024]{1,0:T(8,128)(2,1)S(1)}, u32[]{:S(2)}, u32[]{:S(2)}) collective-permute-start(bf16[8,1024]{1,0:T(8,128)(2,1)S(1)} %get-tuple-element.35), channel_id=1, source_target_pairs={{0,128},{1,160},{2,192},{3,224},{32,0},{33,32},{34,64},{35,96},{64... | collective-permute-start | bytes 49160 | tf_op jit(solution)/shard_map/ppermute | solution.py:323
  24.3 6.8 %collective-permute-start.5 = (bf16[8,1024]{1,0:T(8,128)(2,1)S(1)}, bf16[8,1024]{1,0:T(8,128)(2,1)S(1)}, u32[]{:S(2)}, u32[]{:S(2)}) collective-permute-start(bf16[8,1024]{1,0:T(8,128)(2,1)S(1)} %get-tuple-element.36), channel_id=1, source_target_pairs={{0,160},{1,192},{2,224},{3,0},{32,32},{33,64},{34,96},{35,128},{64... | collective-permute-start | bytes 49160 | tf_op jit(solution)/shard_map/ppermute | solution.py:323
  31.1 1.9 %collective-permute-start.6 = (bf16[8,1024]{1,0:T(8,128)(2,1)S(1)}, bf16[8,1024]{1,0:T(8,128)(2,1)S(1)}, u32[]{:S(2)}, u32[]{:S(2)}) collective-permute-start(bf16[8,1024]{1,0:T(8,128)(2,1)S(1)} %get-tuple-element.37), channel_id=1, source_target_pairs={{0,192},{1,224},{2,0},{3,32},{32,64},{33,96},{34,128},{35,160},{64... | collective-permute-start | bytes 49160 | tf_op jit(solution)/shard_map/ppermute | solution.py:323
  33.0 2.0 %collective-permute-start.7 = (bf16[8,1024]{1,0:T(8,128)(2,1)S(1)}, bf16[8,1024]{1,0:T(8,128)(2,1)S(1)}, u32[]{:S(2)}, u32[]{:S(2)}) collective-permute-start(bf16[8,1024]{1,0:T(8,128)(2,1)S(1)} %get-tuple-element.38), channel_id=1, source_target_pairs={{0,224},{1,0},{2,32},{3,64},{32,96},{33,128},{34,160},{35,192},{64... | collective-permute-start | bytes 49160 | tf_op jit(solution)/shard_map/ppermute | solution.py:323
  35.1 1.6 %collective-permute-done.6.refs_6_ = bf16[8,1024]{1,0:T(8,128)(2,1)S(1)} collective-permute-done((bf16[8,1024]{1,0:T(8,128)(2,1)S(1)}, bf16[8,1024]{1,0:T(8,128)(2,1)S(1)}, u32[]{:S(2)}, u32[]{:S(2)}) %collective-permute-start.6) | collective-permute-done | bytes 16416 | tf_op jit(solution)/shard_map/ppermute | solution.py:323
  38.5 2.2 %collective-permute-start.11 = (bf16[2,8,4096]{2,1,0:T(8,128)(2,1)S(1)}, bf16[2,8,4096]{2,1,0:T(8,128)(2,1)S(1)}, u32[]{:S(2)}, u32[]{:S(2)}) collective-permute-start(bf16[2,8,4096]{2,1,0:T(8,128)(2,1)S(1)} %pieces.1), channel_id=1, source_target_pairs={{0,16},{8,24},{16,0},{24,8},{1,17},{9,25},{17,1},{25,9},{2,18},{10... | collective-permute-start | bytes 393224 | tf_op jit(solution)/shard_map/ppermute | solution.py:299
  41.0 7.9 %collective-permute-start.9 = (bf16[64,1024]{1,0:T(8,128)(2,1)}, bf16[64,1024]{1,0:T(8,128)(2,1)S(1)}, u32[]{:S(2)}, u32[]{:S(2)}) collective-permute-start(bf16[64,1024]{1,0:T(8,128)(2,1)} %own), channel_id=1, source_target_pairs={{0,2},{1,3},{2,0},{3,1},{4,6},{5,7},{6,4},{7,5},{8,10},{9,11},{10,... | collective-permute-start | bytes 393224 | tf_op jit(solution)/shard_map/ppermute | solution.py:327
  49.6 2.8 %collective-permute-start.13 = (bf16[4,8,4096]{2,1,0:T(8,128)(2,1)S(1)}, bf16[4,8,4096]{2,1,0:T(8,128)(2,1)S(1)}, u32[]{:S(2)}, u32[]{:S(2)}) collective-permute-start(bf16[4,8,4096]{2,1,0:T(8,128)(2,1)S(1)} %pad_maximum_fusion.refs_1_), channel_id=1, source_target_pairs={{0,224},{32,0},{64,32},{96,64},{128,96},{160,128},{192,160},{224,1... | collective-permute-start | bytes 786440 | tf_op jit(solution)/shard_map/ppermute | solution.py:299
  53.5 2.4 %collective-permute-done.10.both = bf16[64,1024]{1,0:T(8,128)(2,1)S(1)} collective-permute-done((bf16[64,1024]{1,0:T(8,128)(2,1)}, bf16[64,1024]{1,0:T(8,128)(2,1)S(1)}, u32[]{:S(2)}, u32[]{:S(2)}) %collective-permute-start.10) | collective-permute-done | bytes 131104 | tf_op jit(solution)/shard_map/ppermute | solution.py:327
  57.5 2.7 %rows.1 = (bf16[64,4096]{1,0:T(8,128)(2,1)S(1)}, bf16[64,1024]{1,0:T(8,128)(2,1)}) custom-call(s32[5]{0:T(128)S(1)} %stack.23.place.refs_0_, f32[1,65]{1,0:T(1,128)S(1)} %bitcast.7, bf16[64,1024]{1,0:T(8,128)(2,1)S(1)} %copy-done.1, bf16[64,1024]{1,0:T(8,128)(2,1)S(1)} %collective-permute-done.8.core, bf16[64,1024]{1,0:T(8,128)(2,1)S(1)} %collective-permute-done.9.line_y, ...), custom_call_target="tpu_custom_call" | custom-call | flops 1073741824 | bytes 4194304 | tf_op jit(solution)/shard_map/rows/pallas_call | solution.py:125
  60.2 3.2 %collective-permute-start.18 = (bf16[64,4096]{1,0:T(8,128)(2,1)S(1)}, bf16[64,4096]{1,0:T(8,128)(2,1)S(1)}, u32[]{:S(2)}, u32[]{:S(2)}) collective-permute-start(bf16[64,4096]{1,0:T(8,128)(2,1)S(1)} %get-tuple-element.41.rows_ref), channel_id=1, source_target_pairs={{0,4},{4,0},{1,5},{5,1},{2,6},{6,2},{3,7},{7,3},{8,12},{12,8},{9,1... | collective-permute-start | bytes 1572872 | tf_op jit(solution)/shard_map/ppermute | solution.py:303
  63.4 3.2 %collective-permute-start.15 = (bf16[4,8,4096]{2,1,0:T(8,128)(2,1)S(1)}, bf16[4,8,4096]{2,1,0:T(8,128)(2,1)S(1)}, u32[]{:S(2)}, u32[]{:S(2)}) collective-permute-start(bf16[4,8,4096]{2,1,0:T(8,128)(2,1)S(1)} %collective-permute-done.13.refs_3_), channel_id=1, source_target_pairs={{0,224},{32,0},{64,32},{96,64},{128,96},{160,128},{192,160},{224,1... | collective-permute-start | bytes 786440 | tf_op jit(solution)/shard_map/ppermute | solution.py:299
  66.7 1.4 %collective-permute-start.22 = (bf16[64,4096]{1,0:T(8,128)(2,1)S(1)}, bf16[64,4096]{1,0:T(8,128)(2,1)S(1)}, u32[]{:S(2)}, u32[]{:S(2)}) collective-permute-start(bf16[64,4096]{1,0:T(8,128)(2,1)S(1)} %get-tuple-element.41.rows_ref), channel_id=1, source_target_pairs={{0,8},{8,0},{16,24},{24,16},{1,9},{9,1},{17,25},{25,17},{2,10},{10... | collective-permute-start | bytes 1572872 | tf_op jit(solution)/shard_map/ppermute | solution.py:307
  69.4 3.5 %collective-permute-done.14.refs_4_ = bf16[4,8,4096]{2,1,0:T(8,128)(2,1)S(1)} collective-permute-done((bf16[4,8,4096]{2,1,0:T(8,128)(2,1)S(1)}, bf16[4,8,4096]{2,1,0:T(8,128)(2,1)S(1)}, u32[]{:S(2)}, u32[]{:S(2)}) %collective-permute-start.14) | collective-permute-done | bytes 262176 | tf_op jit(solution)/shard_map/ppermute | solution.py:299
  72.9 3.2 %collective-permute-start.17 = (bf16[4,8,4096]{2,1,0:T(8,128)(2,1)S(1)}, bf16[4,8,4096]{2,1,0:T(8,128)(2,1)S(1)}, u32[]{:S(2)}, u32[]{:S(2)}) collective-permute-start(bf16[4,8,4096]{2,1,0:T(8,128)(2,1)S(1)} %collective-permute-done.15.refs_5_), channel_id=1, source_target_pairs={{0,224},{32,0},{64,32},{96,64},{128,96},{160,128},{192,160},{224,1... | collective-permute-start | bytes 786440 | tf_op jit(solution)/shard_map/ppermute | solution.py:299
  76.1 1.4 %collective-permute-start.24 = (bf16[64,4096]{1,0:T(8,128)(2,1)S(1)}, bf16[64,4096]{1,0:T(8,128)(2,1)S(1)}, u32[]{:S(2)}, u32[]{:S(2)}) collective-permute-start(bf16[64,4096]{1,0:T(8,128)(2,1)S(1)} %collective-permute-done.18.rows_ref), channel_id=1, source_target_pairs={{0,8},{8,0},{16,24},{24,16},{1,9},{9,1},{17,25},{25,17},{2,10},{10... | collective-permute-start | bytes 1572872 | tf_op jit(solution)/shard_map/ppermute | solution.py:307
  78.8 2.6 %collective-permute-done.16.refs_6_ = bf16[4,8,4096]{2,1,0:T(8,128)(2,1)S(1)} collective-permute-done((bf16[4,8,4096]{2,1,0:T(8,128)(2,1)S(1)}, bf16[4,8,4096]{2,1,0:T(8,128)(2,1)S(1)}, u32[]{:S(2)}, u32[]{:S(2)}) %collective-permute-start.16) | collective-permute-done | bytes 262176 | tf_op jit(solution)/shard_map/ppermute | solution.py:299
  81.6 3.3 %collective-permute-start.20 = (bf16[2,8,4096]{2,1,0:T(8,128)(2,1)S(1)}, bf16[2,8,4096]{2,1,0:T(8,128)(2,1)S(1)}, u32[]{:S(2)}, u32[]{:S(2)}) collective-permute-start(bf16[2,8,4096]{2,1,0:T(8,128)(2,1)S(1)} %slice.7), channel_id=1, source_target_pairs={{0,224},{32,0},{64,32},{96,64},{128,96},{160,128},{192,160},{224,1... | collective-permute-start | bytes 393224 | tf_op jit(solution)/shard_map/ppermute | solution.py:299
  84.9 1.3 %lags.6 = (bf16[9,64,4096]{2,1,0:T(8,128)(2,1)S(1)}, f32[64,128]{1,0:T(8,128)S(1)}) custom-call(bf16[64,4096]{1,0:T(8,128)(2,1)S(1)} %collective-permute-done.22.rows_ref), custom_call_target="tpu_custom_call" | custom-call | flops 10485760 | bytes 6291456 | tf_op jit(solution)/shard_map/lags/pallas_call | solution.py:166
  86.2 1.6 %collective-permute-done.19.refs_8_ = bf16[2,8,4096]{2,1,0:T(8,128)(2,1)S(1)} collective-permute-done((bf16[2,8,4096]{2,1,0:T(8,128)(2,1)S(1)}, bf16[2,8,4096]{2,1,0:T(8,128)(2,1)S(1)}, u32[]{:S(2)}, u32[]{:S(2)}) %collective-permute-start.19) | collective-permute-done | bytes 131104 | tf_op jit(solution)/shard_map/ppermute | solution.py:299
  87.8 1.4 %columns.1 = (bf16[32,8,4096]{2,1,0:T(8,128)(2,1)S(1)}, f32[8,256]{1,0:T(8,128)S(1)}) custom-call(s32[5]{0:T(128)S(1)} %stack.23.place.refs_0_, bf16[4,8,4096]{2,1,0:T(8,128)(2,1)S(1)} %pad_maximum_fusion.refs_1_, bf16[4,8,4096]{2,1,0:T(8,128)(2,1)S(1)} %collective-permute-done.12.refs_2_, bf16[4,8,4096]{2,1,0:T(8,128)(2,1)S(1)} %collective-permute-done.13.refs_3_, ...), custom_call_target="tpu_custom_call" | custom-call | flops 8388608 | bytes 4194304 | tf_op jit(solution)/shard_map/columns/pallas_call | solution.py:214
  89.1 1.4 %weigh.5 = f32[9,64,256]{2,1,0:T(8,128)S(1)} custom-call(bf16[9,64,4096]{2,1,0:T(8,128)(2,1)S(1)} %get-tuple-element.47.refs_0_, f32[64,128]{1,0:T(8,128)S(1)} %get-tuple-element.48.refs_1_, bf16[32,8,4096]{2,1,0:T(8,128)(2,1)S(1)} %get-tuple-element.51.refs_2_, f32[8,256]{1,0:T(8,128)S(1)} %get-tuple-element.52.refs_3_), custom_call_target="tpu_custom_call" | custom-call | flops 1207959552 | bytes 589824 | tf_op jit(solution)/shard_map/weigh/pallas_call | solution.py:249
  91.0 1.4 %weigh.6 = f32[9,64,256]{2,1,0:T(8,128)S(1)} custom-call(bf16[9,64,4096]{2,1,0:T(8,128)(2,1)S(1)} %get-tuple-element.54.refs_0_, f32[64,128]{1,0:T(8,128)S(1)} %get-tuple-element.55.refs_1_, bf16[32,8,4096]{2,1,0:T(8,128)(2,1)S(1)} %get-tuple-element.51.refs_2_, f32[8,256]{1,0:T(8,128)S(1)} %get-tuple-element.52.refs_3_), custom_call_target="tpu_custom_call" | custom-call | flops 1207959552 | bytes 589824 | tf_op jit(solution)/shard_map/weigh/pallas_call | solution.py:249
  92.5 1.5 %collective-permute-start.23 = (f16[9,64,256]{2,1,0:T(8,128)(2,1)S(1)}, f16[9,64,256]{2,1,0:T(8,128)(2,1)S(1)}, u32[]{:S(2)}, u32[]{:S(2)}) collective-permute-start(f16[9,64,256]{2,1,0:T(8,128)(2,1)S(1)} %convert_element_type.20), channel_id=1, source_target_pairs={{0,8},{8,0},{16,24},{24,16},{1,9},{9,1},{17,25},{25,17},{2,10},{10... | collective-permute-start | bytes 884744 | tf_op jit(solution)/shard_map/ppermute | solution.py:307
  95.3 1.4 %weigh.7 = f32[9,64,256]{2,1,0:T(8,128)S(1)} custom-call(bf16[9,64,4096]{2,1,0:T(8,128)(2,1)S(1)} %get-tuple-element.57.refs_0_, f32[64,128]{1,0:T(8,128)S(1)} %get-tuple-element.58.refs_1_, bf16[32,8,4096]{2,1,0:T(8,128)(2,1)S(1)} %get-tuple-element.51.refs_2_, f32[8,256]{1,0:T(8,128)S(1)} %get-tuple-element.52.refs_3_), custom_call_target="tpu_custom_call" | custom-call | flops 1207959552 | bytes 589824 | tf_op jit(solution)/shard_map/weigh/pallas_call | solution.py:249
  96.8 3.3 %collective-permute-start.25 = (f16[9,64,256]{2,1,0:T(8,128)(2,1)S(1)}, f16[9,64,256]{2,1,0:T(8,128)(2,1)S(1)}, u32[]{:S(2)}, u32[]{:S(2)}) collective-permute-start(f16[9,64,256]{2,1,0:T(8,128)(2,1)S(1)} %convert_element_type.22), channel_id=1, source_target_pairs={{0,12},{4,8},{8,4},{12,0},{16,28},{20,24},{24,20},{28,16},{1,13},{... | collective-permute-start | bytes 884744 | tf_op jit(solution)/shard_map/ppermute | solution.py:311
  100.1 1.4 %weigh.4.own = f32[9,64,256]{2,1,0:T(8,128)S(1)} custom-call(bf16[9,64,4096]{2,1,0:T(8,128)(2,1)S(1)} %get-tuple-element.42.refs_0_, f32[64,128]{1,0:T(8,128)S(1)} %get-tuple-element.43.refs_1_, bf16[32,8,4096]{2,1,0:T(8,128)(2,1)S(1)} %get-tuple-element.51.refs_2_, f32[8,256]{1,0:T(8,128)S(1)} %get-tuple-element.52.refs_3_), custom_call_target="tpu_custom_call" | custom-call | flops 1207959552 | bytes 589824 | tf_op jit(solution)/shard_map/weigh/pallas_call | solution.py:249
  101.7 6.3 %collective-permute-done.25 = f16[9,64,256]{2,1,0:T(8,128)(2,1)S(1)} collective-permute-done((f16[9,64,256]{2,1,0:T(8,128)(2,1)S(1)}, f16[9,64,256]{2,1,0:T(8,128)(2,1)S(1)}, u32[]{:S(2)}, u32[]{:S(2)}) %collective-permute-start.25) | collective-permute-done | bytes 294944 | tf_op jit(solution)/shard_map/ppermute | solution.py:311
  108.1 2.9 %join.1 = f32[9,64,1024]{2,1,0:T(8,128)} custom-call(s32[5]{0:T(128)S(1)} %stack.23.place.refs_0_, f32[9,64,256]{2,1,0:T(8,128)S(1)} %weigh.4.own, f32[9,64,256]{2,1,0:T(8,128)S(1)} %convert_element_type.19.got_y, f32[9,64,256]{2,1,0:T(8,128)S(1)} %convert_element_type.21.got_x, f32[9,64,256]{2,1,0:T(8,128)S(1)} %convert_element_type.23.got_xy), custom_call_target="tpu_custom_call" | custom-call | tf_op jit(solution)/shard_map/join/pallas_call | solution.py:286
  (51 shorter events, 12.3 us)
Async XLA Ops:
  0.7 0.9 copy-start
  2.2 22.1 %collective-permute-start = (bf16[8,1024]{1,0:T(8,128)(2,1)S(1)}, bf16[8,1024]{1,0:T(8,128)(2,1)S(1)}, u32[]{:S(2)}, u32[]{:S(2)}) collective-permute-start(bf16[8,1024]{1,0:T(8,128)(2,1)S(1)} %get-tuple-element.31), channel_id=1, source_target_pairs={{0,0},{1,32},{2,64},{3,96},{32,128},{33,160},{34,192},{35,224},{64... | collective-permute-start | bytes 49160 | tf_op jit(solution)/shard_map/ppermute | solution.py:323
  2.9 28.2 %collective-permute-start.1 = (bf16[8,1024]{1,0:T(8,128)(2,1)S(1)}, bf16[8,1024]{1,0:T(8,128)(2,1)S(1)}, u32[]{:S(2)}, u32[]{:S(2)}) collective-permute-start(bf16[8,1024]{1,0:T(8,128)(2,1)S(1)} %get-tuple-element.32), channel_id=1, source_target_pairs={{0,32},{1,64},{2,96},{3,128},{32,160},{33,192},{34,224},{35,0},{64... | collective-permute-start | bytes 49160 | tf_op jit(solution)/shard_map/ppermute | solution.py:323
  13.8 19.3 %collective-permute-start.2 = (bf16[8,1024]{1,0:T(8,128)(2,1)S(1)}, bf16[8,1024]{1,0:T(8,128)(2,1)S(1)}, u32[]{:S(2)}, u32[]{:S(2)}) collective-permute-start(bf16[8,1024]{1,0:T(8,128)(2,1)S(1)} %get-tuple-element.33), channel_id=1, source_target_pairs={{0,64},{1,96},{2,128},{3,160},{32,192},{33,224},{34,0},{35,32},{64... | collective-permute-start | bytes 49160 | tf_op jit(solution)/shard_map/ppermute | solution.py:323
  17.3 17.7 %collective-permute-start.3 = (bf16[8,1024]{1,0:T(8,128)(2,1)S(1)}, bf16[8,1024]{1,0:T(8,128)(2,1)S(1)}, u32[]{:S(2)}, u32[]{:S(2)}) collective-permute-start(bf16[8,1024]{1,0:T(8,128)(2,1)S(1)} %get-tuple-element.34), channel_id=1, source_target_pairs={{0,96},{1,128},{2,160},{3,192},{32,224},{33,0},{34,32},{35,64},{64... | collective-permute-start | bytes 49160 | tf_op jit(solution)/shard_map/ppermute | solution.py:323
  20.8 14.3 %collective-permute-start.4 = (bf16[8,1024]{1,0:T(8,128)(2,1)S(1)}, bf16[8,1024]{1,0:T(8,128)(2,1)S(1)}, u32[]{:S(2)}, u32[]{:S(2)}) collective-permute-start(bf16[8,1024]{1,0:T(8,128)(2,1)S(1)} %get-tuple-element.35), channel_id=1, source_target_pairs={{0,128},{1,160},{2,192},{3,224},{32,0},{33,32},{34,64},{35,96},{64... | collective-permute-start | bytes 49160 | tf_op jit(solution)/shard_map/ppermute | solution.py:323
  24.3 10.8 %collective-permute-start.5 = (bf16[8,1024]{1,0:T(8,128)(2,1)S(1)}, bf16[8,1024]{1,0:T(8,128)(2,1)S(1)}, u32[]{:S(2)}, u32[]{:S(2)}) collective-permute-start(bf16[8,1024]{1,0:T(8,128)(2,1)S(1)} %get-tuple-element.36), channel_id=1, source_target_pairs={{0,160},{1,192},{2,224},{3,0},{32,32},{33,64},{34,96},{35,128},{64... | collective-permute-start | bytes 49160 | tf_op jit(solution)/shard_map/ppermute | solution.py:323
  31.1 5.6 %collective-permute-start.6 = (bf16[8,1024]{1,0:T(8,128)(2,1)S(1)}, bf16[8,1024]{1,0:T(8,128)(2,1)S(1)}, u32[]{:S(2)}, u32[]{:S(2)}) collective-permute-start(bf16[8,1024]{1,0:T(8,128)(2,1)S(1)} %get-tuple-element.37), channel_id=1, source_target_pairs={{0,192},{1,224},{2,0},{3,32},{32,64},{33,96},{34,128},{35,160},{64... | collective-permute-start | bytes 49160 | tf_op jit(solution)/shard_map/ppermute | solution.py:323
  33.0 3.7 %collective-permute-start.7 = (bf16[8,1024]{1,0:T(8,128)(2,1)S(1)}, bf16[8,1024]{1,0:T(8,128)(2,1)S(1)}, u32[]{:S(2)}, u32[]{:S(2)}) collective-permute-start(bf16[8,1024]{1,0:T(8,128)(2,1)S(1)} %get-tuple-element.38), channel_id=1, source_target_pairs={{0,224},{1,0},{2,32},{3,64},{32,96},{33,128},{34,160},{35,192},{64... | collective-permute-start | bytes 49160 | tf_op jit(solution)/shard_map/ppermute | solution.py:323
  36.7 0.7 copy-start.2
  38.5 10.5 %collective-permute-start.11 = (bf16[2,8,4096]{2,1,0:T(8,128)(2,1)S(1)}, bf16[2,8,4096]{2,1,0:T(8,128)(2,1)S(1)}, u32[]{:S(2)}, u32[]{:S(2)}) collective-permute-start(bf16[2,8,4096]{2,1,0:T(8,128)(2,1)S(1)} %pieces.1), channel_id=1, source_target_pairs={{0,16},{8,24},{16,0},{24,8},{1,17},{9,25},{17,1},{25,9},{2,18},{10... | collective-permute-start | bytes 393224 | tf_op jit(solution)/shard_map/ppermute | solution.py:299
  40.8 11.7 %collective-permute-start.8 = (bf16[64,1024]{1,0:T(8,128)(2,1)}, bf16[64,1024]{1,0:T(8,128)(2,1)S(1)}, u32[]{:S(2)}, u32[]{:S(2)}) collective-permute-start(bf16[64,1024]{1,0:T(8,128)(2,1)} %own), channel_id=1, source_target_pairs={{0,1},{1,0},{2,3},{3,2},{4,5},{5,4},{6,7},{7,6},{8,9},{9,8},{10,11... | collective-permute-start | bytes 393224 | tf_op jit(solution)/shard_map/ppermute | solution.py:327
  41.0 12.5 %collective-permute-start.9 = (bf16[64,1024]{1,0:T(8,128)(2,1)}, bf16[64,1024]{1,0:T(8,128)(2,1)S(1)}, u32[]{:S(2)}, u32[]{:S(2)}) collective-permute-start(bf16[64,1024]{1,0:T(8,128)(2,1)} %own), channel_id=1, source_target_pairs={{0,2},{1,3},{2,0},{3,1},{4,6},{5,7},{6,4},{7,5},{8,10},{9,11},{10,... | collective-permute-start | bytes 393224 | tf_op jit(solution)/shard_map/ppermute | solution.py:327
  48.9 7.0 %collective-permute-start.10 = (bf16[64,1024]{1,0:T(8,128)(2,1)}, bf16[64,1024]{1,0:T(8,128)(2,1)S(1)}, u32[]{:S(2)}, u32[]{:S(2)}) collective-permute-start(bf16[64,1024]{1,0:T(8,128)(2,1)} %own), channel_id=1, source_target_pairs={{0,3},{1,2},{2,1},{3,0},{4,7},{5,6},{6,5},{7,4},{8,11},{9,10},{10,... | collective-permute-start | bytes 393224 | tf_op jit(solution)/shard_map/ppermute | solution.py:327
  49.1 14.3 %collective-permute-start.12 = (bf16[4,8,4096]{2,1,0:T(8,128)(2,1)S(1)}, bf16[4,8,4096]{2,1,0:T(8,128)(2,1)S(1)}, u32[]{:S(2)}, u32[]{:S(2)}) collective-permute-start(bf16[4,8,4096]{2,1,0:T(8,128)(2,1)S(1)} %pad_maximum_fusion.refs_1_), channel_id=1, source_target_pairs={{0,32},{32,64},{64,96},{96,128},{128,160},{160,192},{192,224},{224... | collective-permute-start | bytes 786440 | tf_op jit(solution)/shard_map/ppermute | solution.py:299
  49.6 13.8 %collective-permute-start.13 = (bf16[4,8,4096]{2,1,0:T(8,128)(2,1)S(1)}, bf16[4,8,4096]{2,1,0:T(8,128)(2,1)S(1)}, u32[]{:S(2)}, u32[]{:S(2)}) collective-permute-start(bf16[4,8,4096]{2,1,0:T(8,128)(2,1)S(1)} %pad_maximum_fusion.refs_1_), channel_id=1, source_target_pairs={{0,224},{32,0},{64,32},{96,64},{128,96},{160,128},{192,160},{224,1... | collective-permute-start | bytes 786440 | tf_op jit(solution)/shard_map/ppermute | solution.py:299
  55.9 0.9 copy-start.1
  56.8 0.7 copy-start.3
  60.2 15.9 %collective-permute-start.18 = (bf16[64,4096]{1,0:T(8,128)(2,1)S(1)}, bf16[64,4096]{1,0:T(8,128)(2,1)S(1)}, u32[]{:S(2)}, u32[]{:S(2)}) collective-permute-start(bf16[64,4096]{1,0:T(8,128)(2,1)S(1)} %get-tuple-element.41.rows_ref), channel_id=1, source_target_pairs={{0,4},{4,0},{1,5},{5,1},{2,6},{6,2},{3,7},{7,3},{8,12},{12,8},{9,1... | collective-permute-start | bytes 1572872 | tf_op jit(solution)/shard_map/ppermute | solution.py:303
  63.4 9.4 %collective-permute-start.14 = (bf16[4,8,4096]{2,1,0:T(8,128)(2,1)S(1)}, bf16[4,8,4096]{2,1,0:T(8,128)(2,1)S(1)}, u32[]{:S(2)}, u32[]{:S(2)}) collective-permute-start(bf16[4,8,4096]{2,1,0:T(8,128)(2,1)S(1)} %collective-permute-done.12.refs_2_), channel_id=1, source_target_pairs={{0,32},{32,64},{64,96},{96,128},{128,160},{160,192},{192,224},{224... | collective-permute-start | bytes 786440 | tf_op jit(solution)/shard_map/ppermute | solution.py:299
  63.4 9.4 %collective-permute-start.15 = (bf16[4,8,4096]{2,1,0:T(8,128)(2,1)S(1)}, bf16[4,8,4096]{2,1,0:T(8,128)(2,1)S(1)}, u32[]{:S(2)}, u32[]{:S(2)}) collective-permute-start(bf16[4,8,4096]{2,1,0:T(8,128)(2,1)S(1)} %collective-permute-done.13.refs_3_), channel_id=1, source_target_pairs={{0,224},{32,0},{64,32},{96,64},{128,96},{160,128},{192,160},{224,1... | collective-permute-start | bytes 786440 | tf_op jit(solution)/shard_map/ppermute | solution.py:299
  66.7 18.2 %collective-permute-start.22 = (bf16[64,4096]{1,0:T(8,128)(2,1)S(1)}, bf16[64,4096]{1,0:T(8,128)(2,1)S(1)}, u32[]{:S(2)}, u32[]{:S(2)}) collective-permute-start(bf16[64,4096]{1,0:T(8,128)(2,1)S(1)} %get-tuple-element.41.rows_ref), channel_id=1, source_target_pairs={{0,8},{8,0},{16,24},{24,16},{1,9},{9,1},{17,25},{25,17},{2,10},{10... | collective-permute-start | bytes 1572872 | tf_op jit(solution)/shard_map/ppermute | solution.py:307
  72.9 8.6 %collective-permute-start.16 = (bf16[4,8,4096]{2,1,0:T(8,128)(2,1)S(1)}, bf16[4,8,4096]{2,1,0:T(8,128)(2,1)S(1)}, u32[]{:S(2)}, u32[]{:S(2)}) collective-permute-start(bf16[4,8,4096]{2,1,0:T(8,128)(2,1)S(1)} %collective-permute-done.14.refs_4_), channel_id=1, source_target_pairs={{0,32},{32,64},{64,96},{96,128},{128,160},{160,192},{192,224},{224... | collective-permute-start | bytes 786440 | tf_op jit(solution)/shard_map/ppermute | solution.py:299
  72.9 8.6 %collective-permute-start.17 = (bf16[4,8,4096]{2,1,0:T(8,128)(2,1)S(1)}, bf16[4,8,4096]{2,1,0:T(8,128)(2,1)S(1)}, u32[]{:S(2)}, u32[]{:S(2)}) collective-permute-start(bf16[4,8,4096]{2,1,0:T(8,128)(2,1)S(1)} %collective-permute-done.15.refs_5_), channel_id=1, source_target_pairs={{0,224},{32,0},{64,32},{96,64},{128,96},{160,128},{192,160},{224,1... | collective-permute-start | bytes 786440 | tf_op jit(solution)/shard_map/ppermute | solution.py:299
  76.1 17.9 %collective-permute-start.24 = (bf16[64,4096]{1,0:T(8,128)(2,1)S(1)}, bf16[64,4096]{1,0:T(8,128)(2,1)S(1)}, u32[]{:S(2)}, u32[]{:S(2)}) collective-permute-start(bf16[64,4096]{1,0:T(8,128)(2,1)S(1)} %collective-permute-done.18.rows_ref), channel_id=1, source_target_pairs={{0,8},{8,0},{16,24},{24,16},{1,9},{9,1},{17,25},{25,17},{2,10},{10... | collective-permute-start | bytes 1572872 | tf_op jit(solution)/shard_map/ppermute | solution.py:307
  81.5 6.3 %collective-permute-start.19 = (bf16[2,8,4096]{2,1,0:T(8,128)(2,1)S(1)}, bf16[2,8,4096]{2,1,0:T(8,128)(2,1)S(1)}, u32[]{:S(2)}, u32[]{:S(2)}) collective-permute-start(bf16[2,8,4096]{2,1,0:T(8,128)(2,1)S(1)} %slice.6), channel_id=1, source_target_pairs={{0,32},{32,64},{64,96},{96,128},{128,160},{160,192},{192,224},{224... | collective-permute-start | bytes 393224 | tf_op jit(solution)/shard_map/ppermute | solution.py:299
  81.6 6.1 %collective-permute-start.20 = (bf16[2,8,4096]{2,1,0:T(8,128)(2,1)S(1)}, bf16[2,8,4096]{2,1,0:T(8,128)(2,1)S(1)}, u32[]{:S(2)}, u32[]{:S(2)}) collective-permute-start(bf16[2,8,4096]{2,1,0:T(8,128)(2,1)S(1)} %slice.7), channel_id=1, source_target_pairs={{0,224},{32,0},{64,32},{96,64},{128,96},{160,128},{192,160},{224,1... | collective-permute-start | bytes 393224 | tf_op jit(solution)/shard_map/ppermute | solution.py:299
  90.6 11.0 %collective-permute-start.21 = (f16[9,64,256]{2,1,0:T(8,128)(2,1)S(1)}, f16[9,64,256]{2,1,0:T(8,128)(2,1)S(1)}, u32[]{:S(2)}, u32[]{:S(2)}) collective-permute-start(f16[9,64,256]{2,1,0:T(8,128)(2,1)S(1)} %convert_element_type.18), channel_id=1, source_target_pairs={{0,4},{4,0},{1,5},{5,1},{2,6},{6,2},{3,7},{7,3},{8,12},{12,8},{9,1... | collective-permute-start | bytes 884744 | tf_op jit(solution)/shard_map/ppermute | solution.py:303
  92.5 9.1 %collective-permute-start.23 = (f16[9,64,256]{2,1,0:T(8,128)(2,1)S(1)}, f16[9,64,256]{2,1,0:T(8,128)(2,1)S(1)}, u32[]{:S(2)}, u32[]{:S(2)}) collective-permute-start(f16[9,64,256]{2,1,0:T(8,128)(2,1)S(1)} %convert_element_type.20), channel_id=1, source_target_pairs={{0,8},{8,0},{16,24},{24,16},{1,9},{9,1},{17,25},{25,17},{2,10},{10... | collective-permute-start | bytes 884744 | tf_op jit(solution)/shard_map/ppermute | solution.py:307
  96.8 11.2 %collective-permute-start.25 = (f16[9,64,256]{2,1,0:T(8,128)(2,1)S(1)}, f16[9,64,256]{2,1,0:T(8,128)(2,1)S(1)}, u32[]{:S(2)}, u32[]{:S(2)}) collective-permute-start(f16[9,64,256]{2,1,0:T(8,128)(2,1)S(1)} %convert_element_type.22), channel_id=1, source_target_pairs={{0,12},{4,8},{8,4},{12,0},{16,28},{20,24},{24,20},{28,16},{1,13},{... | collective-permute-start | bytes 884744 | tf_op jit(solution)/shard_map/ppermute | solution.py:311

commit v4 on v3

--- a/solution.py
+++ b/solution.py
@@ -13,26 +13,6 @@
 MB = 1 << 20
 SENT = jnp.float16
 SCALE = 65536.0
-
-
-def cut_kernel(place, raw, *outs):
-    for k, out in enumerate(outs):
-        at = pl.multiple_of(((place[0] + k) & 7) * 8, 8)
-        out[...] = raw[pl.ds(at, 8), :]
-
-
-def run_cut(place, raw):
-    rows, bins = raw.shape
-    vmem = pl.BlockSpec(memory_space=pltpu.VMEM)
-    piece = jax.ShapeDtypeStruct((8, bins), raw.dtype)
-    return pl.pallas_call(
-        cut_kernel,
-        in_specs=[pl.BlockSpec(memory_space=pltpu.SMEM), vmem],
-        out_specs=[vmem] * (rows // 8),
-        out_shape=[piece] * (rows // 8),
-        compiler_params=pltpu.CompilerParams(vmem_limit_bytes=4 * MB),
-        name="cut",
-    )(place, raw)
 
 
 def band(taps, line, weights):
@@ -62,53 +42,51 @@
     return value.astype(jnp.bfloat16)
 
 
-def piece_filter_kernel(place, taps, *refs):
-    pieces = refs[:8]
-    out, blocks, weights, line = refs[8:]
-    per = pieces[0].shape[1] // 128
-    count = 4 * per
-    for e in range(2):
-        blocks[e, 0] = jnp.zeros((8, 128), jnp.bfloat16)
-        blocks[e, count + 1] = jnp.zeros((8, 128), jnp.bfloat16)
-    for k, piece in enumerate(pieces):
-        u = (place[1] - k) & 7
-        for b in range(per):
-            blocks[u >> 2, 1 + (u & 3) * per + b] = piece[:, b * 128 : (b + 1) * 128]
+def piece_filter_kernel(place, taps, parts, out, blocks, weights, line):
+    count, bins = parts.shape[0], parts.shape[2]
+    per = bins // 128
+    count = count * per
+    at = pl.multiple_of(place[2] * 16, 16)
+    blocks[0] = jnp.zeros((16, 128), jnp.bfloat16)
+    blocks[count + 1] = jnp.zeros((16, 128), jnp.bfloat16)
+    for n in range(count):
+        b = n % per
+        blocks[1 + n] = parts[n // per, pl.ds(at, 16), b * 128 : (b + 1) * 128]
     band(taps, line, weights)
-    for e in range(2):
-        value = filtered_blocks(lambda k: blocks[e, k : k + count], weights)
-        for n in range(count):
-            out[e, :, n * 128 : (n + 1) * 128] = value[n * 8 : (n + 1) * 8]
-
-
-def run_piece_filter(place, taps, pieces):
-    bins = pieces[0].shape[1]
+    value = filtered_blocks(lambda k: blocks[k : k + count], weights)
+    for n in range(count):
+        for h in range(2):
+            lo = n * 16 + h * 8
+            out[h, :, n * 128 : (n + 1) * 128] = value[lo : lo + 8]
+
+
+def run_piece_filter(place, taps, parts):
+    count, _, bins = parts.shape
     vmem = pl.BlockSpec(memory_space=pltpu.VMEM)
     return pl.pallas_call(
         piece_filter_kernel,
-        in_specs=[pl.BlockSpec(memory_space=pltpu.SMEM)] + [vmem] * 9,
+        in_specs=[pl.BlockSpec(memory_space=pltpu.SMEM), vmem, vmem],
         out_specs=vmem,
-        out_shape=jax.ShapeDtypeStruct((2, 8, 4 * bins), jnp.bfloat16),
+        out_shape=jax.ShapeDtypeStruct((2, 8, count * bins), jnp.bfloat16),
         scratch_shapes=[
-            pltpu.VMEM((2, 4 * bins // 128 + 2, 8, 128), jnp.bfloat16),
+            pltpu.VMEM((count * bins // 128 + 2, 16, 128), jnp.bfloat16),
             pltpu.VMEM((384, 384), jnp.bfloat16),
             pltpu.VMEM((8, 384), jnp.float32),
         ],
         compiler_params=pltpu.CompilerParams(vmem_limit_bytes=8 * MB),
         name="pieces",
-    )(place, taps, *pieces)
-
-
-def row_filter_kernel(place, taps, own, core, line_y, both, out, mine, blocks, weights, line):
-    rows, bins = own.shape
+    )(place, taps, parts)
+
+
+def row_filter_kernel(place, taps, parts, out, mine, blocks, weights, line):
+    rows, bins = parts.shape[1:]
     per = bins // 128
-    count = 4 * per
-    q = place[2]
+    count = parts.shape[0] * per
     blocks[0] = jnp.zeros((rows, 128), jnp.bfloat16)
     blocks[count + 1] = jnp.zeros((rows, 128), jnp.bfloat16)
-    for flip, part in enumerate((own, core, line_y, both)):
-        for b in range(per):
-            blocks[1 + (q ^ flip) * per + b] = part[:, b * 128 : (b + 1) * 128]
+    for n in range(count):
+        b = n % per
+        blocks[1 + n] = parts[n // per, :, b * 128 : (b + 1) * 128]
     band(taps, line, weights)
     group = 8
     for g in range(0, count, group):
@@ -116,29 +94,29 @@
         for b in range(group):
             n = g + b
             out[:, n * 128 : (n + 1) * 128] = value[b * rows : (b + 1) * rows]
-    mine[...] = out[:, pl.ds(pl.multiple_of(q * bins, 128), bins)]
+    mine[...] = out[:, pl.ds(pl.multiple_of(place[2] * bins, 128), bins)]
 
 
 def run_row_filter(place, taps, parts):
-    rows, bins = parts[0].shape
+    count, rows, bins = parts.shape
     vmem = pl.BlockSpec(memory_space=pltpu.VMEM)
     return pl.pallas_call(
         row_filter_kernel,
-        in_specs=[pl.BlockSpec(memory_space=pltpu.SMEM)] + [vmem] * 5,
+        in_specs=[pl.BlockSpec(memory_space=pltpu.SMEM), vmem, vmem],
         out_specs=[vmem, vmem],
         out_shape=[
-            jax.ShapeDtypeStruct((rows, 4 * bins), jnp.bfloat16),
+            jax.ShapeDtypeStruct((rows, count * bins), jnp.bfloat16),
             jax.ShapeDtypeStruct((rows, bins), jnp.bfloat16),
         ],
         scratch_shapes=[
-            pltpu.VMEM((4 * bins // 128 + 2, rows, 128), jnp.bfloat16),
+            pltpu.VMEM((count * bins // 128 + 2, rows, 128), jnp.bfloat16),
             pltpu.VMEM((384, 384), jnp.bfloat16),
             pltpu.VMEM((8, 384), jnp.float32),
         ],
         compiler_params=pltpu.CompilerParams(vmem_limit_bytes=8 * MB),
         cost_estimate=pl.CostEstimate(flops=1 << 30, bytes_accessed=4 * MB, transcendentals=0),
         name="rows",
-    )(place, taps, *parts)
+    )(place, taps, parts)
 
 
 def lag_kernel(rows_ref, out, energy):
@@ -193,7 +171,8 @@
     z = place[1]
     for ref, moves in zip(units, steps):
         for k, (part, z_step) in enumerate(moves):
-            columns[part * 8 + ((z + z_step) & 7)] = ref[k]
+            far = (z + z_step) & 7
+            columns[(far & 1) * 16 + (part >> 1) * 8 + (far >> 1) * 2 + (part & 1)] = ref[k]
     width = columns.shape[0] * columns.shape[1]
     for g in range(width // 128):
         block = columns[g * 16 : (g + 1) * 16].astype(jnp.float32).reshape(128, -1)
@@ -261,33 +240,33 @@
     )(lagged, energy, columns, scale)
 
 
-def join_kernel(place, own, got_y, got_x, got_xy, out):
+def join_kernel(place, own, got_xy, got_x, got_y, out):
     low = place[4] == 0
     rows = out.shape[1]
+    lag = pl.program_id(0)
     lane = lax.broadcasted_iota(jnp.int32, (rows, 128), 1) < 64
     for half in range(2):
         span = slice(half * 128, (half + 1) * 128)
         for flip, (same, cross) in enumerate(((own, got_y), (got_x, got_xy))):
             here_x = place[3] ^ flip
-            for lag in range(out.shape[0]):
-                here = same[lag, :, span] * (1.0 / SCALE) if flip else same[lag, :, span]
-                there = cross[lag, :, span] * (1.0 / SCALE)
-                one = jnp.where(low, here, there)
-                two = jnp.where(low, there, here)
-                at = pl.multiple_of((half * 4 + here_x) * 128, 128)
-                out[lag, :, pl.ds(at, 128)] = jnp.where(lane, one, pltpu.roll(two, 64, axis=1))
-                at = pl.multiple_of((half * 4 + (here_x ^ 2)) * 128, 128)
-                out[lag, :, pl.ds(at, 128)] = jnp.where(lane, pltpu.roll(one, 64, axis=1), two)
+            here = same[lag, :, span] * (1.0 / SCALE) if flip else same[lag, :, span]
+            there = cross[lag, :, span] * (1.0 / SCALE)
+            one = jnp.where(low, here, there)
+            two = jnp.where(low, there, here)
+            at = pl.multiple_of((half * 4 + here_x) * 128, 128)
+            out[0, :, pl.ds(at, 128)] = jnp.where(lane, one, pltpu.roll(two, 64, axis=1))
+            at = pl.multiple_of((half * 4 + (here_x ^ 2)) * 128, 128)
+            out[0, :, pl.ds(at, 128)] = jnp.where(lane, pltpu.roll(one, 64, axis=1), two)
 
 
 def run_join(place, *quarters):
     lags, rows, width = quarters[0].shape
-    spec = pl.BlockSpec((3, rows, width), lambda i: (i, 0, 0))
+    vmem = pl.BlockSpec(memory_space=pltpu.VMEM)
     return pl.pallas_call(
         join_kernel,
-        grid=(lags // 3,),
-        in_specs=[pl.BlockSpec(memory_space=pltpu.SMEM)] + [spec] * 4,
-        out_specs=pl.BlockSpec((3, rows, 4 * width), lambda i: (i, 0, 0)),
+        grid=(lags,),
+        in_specs=[pl.BlockSpec(memory_space=pltpu.SMEM)] + [vmem] * 4,
+        out_specs=pl.BlockSpec((1, rows, 4 * width), lambda i: (i, 0, 0)),
         out_shape=jax.ShapeDtypeStruct((lags, rows, 4 * width), jnp.float32),
         compiler_params=pltpu.CompilerParams(vmem_limit_bytes=8 * MB),
         name="join",
@@ -311,20 +290,12 @@
     return lax.ppermute(value, ("x", "yh"), [(i, i ^ 3) for i in range(8)])
 
 
-def sent(move, value):
-    return move(value.astype(SENT)).astype(jnp.float32)
-
-
-def spread(value, k):
+def spread(value):
     pairs = []
     for z in range(8):
         for q in range(4):
-            pairs.append((z * 4 + q, ((4 * (z & 1) + q + k) & 7) * 4 + (z >> 1)))
+            pairs.append((z * 4 + q, (2 * q + (z & 1)) * 4 + (z >> 1)))
     return lax.ppermute(value, ("z", "yl", "core"), pairs)
-
-
-def flipped(value, flip):
-    return lax.ppermute(value, ("yl", "core"), [(i, i ^ flip) for i in range(4)])
 
 
 def after(value, *others):
@@ -336,17 +307,17 @@
     x = lax.axis_index("x")
     yh = lax.axis_index("yh")
     q = lax.axis_index(("yl", "core"))
-    place = jnp.stack([4 * (z % 2) + q, z, q, x, yh]).astype(jnp.int32)
+    place = jnp.stack([yh, z, q, x, yh]).astype(jnp.int32)
     taps = taps.reshape(1, -1)
-    pieces = [spread(piece, k) for k, piece in enumerate(run_cut(place, raw))]
-    parts = [raw] + [flipped(raw, flip) for flip in (1, 2, 3)]
-    unit = run_piece_filter(place, taps, pieces)
+    parts = lax.all_gather(raw, ("yl", "core"), axis=0, tiled=False)
+    given = run_piece_filter(place, taps, parts)
+    unit = spread(given)
     base = jnp.concatenate([unit, around(unit, "x", 2)], axis=0)
-    units, steps = [base], [[(0, 0), (2, 0), (1, 0), (3, 0)]]
-    order = [part for part, _ in steps[0]]
+    order = (0, 1, 2, 3)
+    units, steps = [base], [[(part, 0) for part in order]]
     first = (around(base, "z", 1), around(base, "z", -1))
     second = (around(first[0], "z", 1), around(first[1], "z", -1))
-    full, mine = run_row_filter(place, taps, [after(raw, unit)] + parts[1:])
+    full, mine = run_row_filter(place, taps, after(parts, given))
     row_y = cross_y(full)
     row_x = cross_x(full)
     row_xy = cross_x(after(row_y, *first))
@@ -362,10 +333,12 @@
     far_x = run_lags(after(row_x, *third))
     far_xy = run_lags(row_xy)
     columns, scale = run_columns(place, units, steps)
-    got_xy = sent(cross_xy, run_weigh(far_xy, columns, scale, SCALE))
-    got_x = sent(cross_x, run_weigh(far_x, columns, scale, SCALE))
-    got_y = sent(cross_y, run_weigh(far_y, columns, scale, SCALE))
-    information = run_join(place, run_weigh(own, columns, scale, 1), got_y, got_x, got_xy)
+    got = []
+    for rows, move in ((far_xy, cross_xy), (far_x, cross_x), (far_y, cross_y)):
+        send = run_weigh(rows, columns, scale, SCALE).astype(SENT)
+        got.append(move(send).astype(jnp.float32))
+    kept = run_weigh(own, columns, scale, 1)
+    information = run_join(place, kept, *got)
     return (information, mine)
 
 

time: 112 us -> 94.6 us (0.84)
  starting transfers between devices: 67.8 us -> 33.1 us
  waiting for transfers between devices: 19.2 us -> 31.1 us
  blocking collectives: 0 us -> 7.47 us
  local copies, waits for them, and re-layouts: 3.22 us -> 0.78 us
  Pallas kernels: 19.5 us -> 20.7 us
    ppermute x8 -> x1, starting transfers between devices: 32.8 us -> 0.67 us  [spread(): return lax.ppermute(value, ('z', 'yl', 'core'), pairs)]
    ppermute x3, waiting for transfers between devices: 0.01 us -> 10.3 us  [cross_x(): return lax.ppermute(value, 'x', [(0, 1), (1, 0), (2, 3), (3, 2)])]
    ppermute x9, waiting for transfers between devices: 7.73 us -> 17.6 us  [around(): lax.ppermute(value, axis, [(i, (i + step) % size) for i in range(size)])]
    ppermute x3 -> x0, starting transfers between devices: 8.33 us -> none  [flipped(): lax.ppermute(value, ('yl', 'core'), [(i, i ^ flip) for i in range(4)])]
    all_gather x0 -> x1, blocking collectives: none -> 7.47 us  [shards(): parts = lax.all_gather(raw, ('yl', 'core'), axis=0, tiled=False)]
    ppermute x9, starting transfers between devices: 15.4 us -> 22.2 us  [around(): lax.ppermute(value, axis, [(i, (i + step) % size) for i in range(size)])]
    ppermute x3 -> x0, waiting for transfers between devices: 3.5 us -> none  [flipped(): lax.ppermute(value, ('yl', 'core'), [(i, i ^ flip) for i in range(4)])]
    ppermute x1, waiting for transfers between devices: 6.32 us -> 3.2 us  [cross_xy(): return lax.ppermute(value, ('x', 'yh'), [(i, i ^ 3) for i in range(8)])]
  transfers between devices with their start and end apart: 26 -> 16, of which waited for: 7 -> 7; matrix products, arithmetic and copies ran while one was open for 0% -> 0% of each run, Pallas kernels for 13% -> 13%
where the time goes in v4:
time: 94.6 us; the launch traced here: 94.3 us
  starting transfers between devices  33.1 us (35%)
  waiting for transfers between devices  31.1 us (33%)
  Pallas kernels  20.7 us (22%)
  blocking collectives  7.47 us (8%)
    ppermute x9, starting transfers between devices, around(): lax.ppermute(value, axis, [(i, (i + step) % size) for i in range(size)])  22.2 us
    ppermute x9, waiting for transfers between devices, around(): lax.ppermute(value, axis, [(i, (i + step) % size) for i in range(size)])  17.6 us
    ppermute x3, waiting for transfers between devices, cross_x(): return lax.ppermute(value, 'x', [(0, 1), (1, 0), (2, 3), (3, 2)])  10.3 us
    all_gather x1, blocking collectives, shards(): parts = lax.all_gather(raw, ('yl', 'core'), axis=0, tiled=False)  7.47 us
    ppermute x2, starting transfers between devices, cross_y(): return lax.ppermute(value, 'yh', [(0, 1), (1, 0)])  5.9 us
    pallas_call x4, Pallas kernels, run_weigh(): pl.pallas_call(body, in_specs=[vmem] * 4, out_specs=vmem, out_shape=jax.S...  5.73 us
    pallas_call x4, Pallas kernels, run_lags(): pl.pallas_call(lag_kernel, in_specs=[vmem], out_specs=[vmem, vmem], out_s...  5.05 us
    pallas_call x1, Pallas kernels, run_join(): pl.pallas_call(join_kernel, grid=(lags,), in_specs=[pl.BlockSpec(memory_s...  4.81 us
  transfers between devices with their start and end apart: 16, of which 7 were waited for; matrix products, arithmetic and copies ran while one was open for 0% of the time, Pallas kernels for 13%

profile of v4, /device:TPU:2, one launch (start us, length us, event | category | flops | bytes accessed | tf_op | source)
XLA Modules:
  0.0 94.3 jit_solution(11240628916037760293)
XLA Ops:
  0.6 7.5 %all-gather = bf16[256,1024]{1,0:T(8,128)(2,1)S(1)} all-gather(bf16[64,1024]{1,0:T(8,128)(2,1)} %param.2), channel_id=2, replica_groups=mesh['z'=8,'x'=4,'yh'=2,'yl'=2,'core'=2] {'yl','core'}, dimensions={0}, use_global_device_ids=true | all-gather | bytes 655360 | tf_op jit(solution)/shard_map/all_gather | solution.py:312
  8.2 0.7 copy-done
  8.8 1.1 %pieces.1 = bf16[2,8,4096]{2,1,0:T(8,128)(2,1)S(1)} custom-call(s32[5]{0:T(128)S(1)} %stack.20.place.refs_0_, f32[1,65]{1,0:T(1,128)S(1)} %bitcast.8, bf16[4,64,1024]{2,1,0:T(8,128)(2,1)S(1)} %bitcast.6), custom_call_target="tpu_custom_call" | custom-call | tf_op jit(solution)/shard_map/pieces/pallas_call | solution.py:66
  10.0 0.7 collective-permute-start
  10.7 2.7 %rows.1 = (bf16[64,4096]{1,0:T(8,128)(2,1)S(1)}, bf16[64,1024]{1,0:T(8,128)(2,1)}) custom-call(s32[5]{0:T(128)S(1)} %stack.20.place.refs_0_, f32[1,65]{1,0:T(1,128)S(1)} %bitcast.9, bf16[4,64,1024]{2,1,0:T(8,128)(2,1)S(1)} %bitcast.7), custom_call_target="tpu_custom_call" | custom-call | flops 1073741824 | bytes 4194304 | tf_op jit(solution)/shard_map/rows/pallas_call | solution.py:103
  13.4 2.9 %collective-permute-start.8 = (bf16[64,4096]{1,0:T(8,128)(2,1)S(1)}, bf16[64,4096]{1,0:T(8,128)(2,1)S(1)}, u32[]{:S(2)}, u32[]{:S(2)}) collective-permute-start(bf16[64,4096]{1,0:T(8,128)(2,1)S(1)} %get-tuple-element.25.rows_ref), channel_id=1, source_target_pairs={{0,4},{4,0},{1,5},{5,1},{2,6},{6,2},{3,7},{7,3},{8,12},{12,8},{9,1... | collective-permute-start | bytes 1572872 | tf_op jit(solution)/shard_map/ppermute | solution.py:282
  16.3 2.1 %collective-permute-start.1 = (bf16[2,8,4096]{2,1,0:T(8,128)(2,1)S(1)}, bf16[2,8,4096]{2,1,0:T(8,128)(2,1)S(1)}, u32[]{:S(2)}, u32[]{:S(2)}) collective-permute-start(bf16[2,8,4096]{2,1,0:T(8,128)(2,1)S(1)} %collective-permute-done), channel_id=1, source_target_pairs={{0,16},{8,24},{16,0},{24,8},{1,17},{9,25},{17,1},{25,9},{2,18},{10... | collective-permute-start | bytes 393224 | tf_op jit(solution)/shard_map/ppermute | solution.py:278
  18.4 4.3 %collective-permute-done.1 = bf16[2,8,4096]{2,1,0:T(8,128)(2,1)S(1)} collective-permute-done((bf16[2,8,4096]{2,1,0:T(8,128)(2,1)S(1)}, bf16[2,8,4096]{2,1,0:T(8,128)(2,1)S(1)}, u32[]{:S(2)}, u32[]{:S(2)}) %collective-permute-start.1) | collective-permute-done | bytes 131104 | tf_op jit(solution)/shard_map/ppermute | solution.py:278
  22.8 2.0 %collective-permute-start.2 = (bf16[4,8,4096]{2,1,0:T(8,128)(2,1)S(1)}, bf16[4,8,4096]{2,1,0:T(8,128)(2,1)S(1)}, u32[]{:S(2)}, u32[]{:S(2)}) collective-permute-start(bf16[4,8,4096]{2,1,0:T(8,128)(2,1)S(1)} %constant_dynamic-update-slice_fusion.refs_1_), channel_id=1, source_target_pairs={{0,32},{32,64},{64,96},{96,128},{128,160},{160,192},{192,224},{224... | collective-permute-start | bytes 786440 | tf_op jit(solution)/shard_map/ppermute | solution.py:278
  24.8 7.9 %collective-permute-start.3 = (bf16[4,8,4096]{2,1,0:T(8,128)(2,1)S(1)}, bf16[4,8,4096]{2,1,0:T(8,128)(2,1)S(1)}, u32[]{:S(2)}, u32[]{:S(2)}) collective-permute-start(bf16[4,8,4096]{2,1,0:T(8,128)(2,1)S(1)} %constant_dynamic-update-slice_fusion.refs_1_), channel_id=1, source_target_pairs={{0,224},{32,0},{64,32},{96,64},{128,96},{160,128},{192,160},{224,1... | collective-permute-start | bytes 786440 | tf_op jit(solution)/shard_map/ppermute | solution.py:278
  32.7 7.0 %collective-permute-done.2.refs_2_ = bf16[4,8,4096]{2,1,0:T(8,128)(2,1)S(1)} collective-permute-done((bf16[4,8,4096]{2,1,0:T(8,128)(2,1)S(1)}, bf16[4,8,4096]{2,1,0:T(8,128)(2,1)S(1)}, u32[]{:S(2)}, u32[]{:S(2)}) %collective-permute-start.2) | collective-permute-done | bytes 262176 | tf_op jit(solution)/shard_map/ppermute | solution.py:278
  39.7 3.7 %collective-permute-start.5 = (bf16[4,8,4096]{2,1,0:T(8,128)(2,1)S(1)}, bf16[4,8,4096]{2,1,0:T(8,128)(2,1)S(1)}, u32[]{:S(2)}, u32[]{:S(2)}) collective-permute-start(bf16[4,8,4096]{2,1,0:T(8,128)(2,1)S(1)} %collective-permute-done.3.refs_3_), channel_id=1, source_target_pairs={{0,224},{32,0},{64,32},{96,64},{128,96},{160,128},{192,160},{224,1... | collective-permute-start | bytes 786440 | tf_op jit(solution)/shard_map/ppermute | solution.py:278
  44.0 1.5 %collective-permute-start.11 = (bf16[64,4096]{1,0:T(8,128)(2,1)S(1)}, bf16[64,4096]{1,0:T(8,128)(2,1)S(1)}, u32[]{:S(2)}, u32[]{:S(2)}) collective-permute-start(bf16[64,4096]{1,0:T(8,128)(2,1)S(1)} %collective-permute-done.8.rows_ref), channel_id=1, source_target_pairs={{0,8},{8,0},{16,24},{24,16},{1,9},{9,1},{17,25},{25,17},{2,10},{10... | collective-permute-start | bytes 1572872 | tf_op jit(solution)/shard_map/ppermute | solution.py:286
  45.5 1.3 %lags.4 = (bf16[9,64,4096]{2,1,0:T(8,128)(2,1)S(1)}, f32[64,128]{1,0:T(8,128)S(1)}) custom-call(bf16[64,4096]{1,0:T(8,128)(2,1)S(1)} %get-tuple-element.25.rows_ref), custom_call_target="tpu_custom_call" | custom-call | flops 10485760 | bytes 6291456 | tf_op jit(solution)/shard_map/lags/pallas_call | solution.py:144
  46.7 2.5 %collective-permute-done.4.refs_4_ = bf16[4,8,4096]{2,1,0:T(8,128)(2,1)S(1)} collective-permute-done((bf16[4,8,4096]{2,1,0:T(8,128)(2,1)S(1)}, bf16[4,8,4096]{2,1,0:T(8,128)(2,1)S(1)}, u32[]{:S(2)}, u32[]{:S(2)}) %collective-permute-start.4) | collective-permute-done | bytes 262176 | tf_op jit(solution)/shard_map/ppermute | solution.py:278
  49.3 3.2 %collective-permute-start.7 = (bf16[4,8,4096]{2,1,0:T(8,128)(2,1)S(1)}, bf16[4,8,4096]{2,1,0:T(8,128)(2,1)S(1)}, u32[]{:S(2)}, u32[]{:S(2)}) collective-permute-start(bf16[4,8,4096]{2,1,0:T(8,128)(2,1)S(1)} %collective-permute-done.5.refs_5_), channel_id=1, source_target_pairs={{0,224},{32,0},{64,32},{96,64},{128,96},{160,128},{192,160},{224,1... | collective-permute-start | bytes 786440 | tf_op jit(solution)/shard_map/ppermute | solution.py:278
  52.5 1.3 %lags.5 = (bf16[9,64,4096]{2,1,0:T(8,128)(2,1)S(1)}, f32[64,128]{1,0:T(8,128)S(1)}) custom-call(bf16[64,4096]{1,0:T(8,128)(2,1)S(1)} %collective-permute-done.8.rows_ref), custom_call_target="tpu_custom_call" | custom-call | flops 10485760 | bytes 6291456 | tf_op jit(solution)/shard_map/lags/pallas_call | solution.py:144
  53.8 3.7 %collective-permute-done.6.refs_6_ = bf16[4,8,4096]{2,1,0:T(8,128)(2,1)S(1)} collective-permute-done((bf16[4,8,4096]{2,1,0:T(8,128)(2,1)S(1)}, bf16[4,8,4096]{2,1,0:T(8,128)(2,1)S(1)}, u32[]{:S(2)}, u32[]{:S(2)}) %collective-permute-start.6) | collective-permute-done | bytes 262176 | tf_op jit(solution)/shard_map/ppermute | solution.py:278
  57.5 3.2 %collective-permute-start.10 = (bf16[2,8,4096]{2,1,0:T(8,128)(2,1)S(1)}, bf16[2,8,4096]{2,1,0:T(8,128)(2,1)S(1)}, u32[]{:S(2)}, u32[]{:S(2)}) collective-permute-start(bf16[2,8,4096]{2,1,0:T(8,128)(2,1)S(1)} %slice.7), channel_id=1, source_target_pairs={{0,224},{32,0},{64,32},{96,64},{128,96},{160,128},{192,160},{224,1... | collective-permute-start | bytes 393224 | tf_op jit(solution)/shard_map/ppermute | solution.py:278
  60.8 1.3 %lags.7 = (bf16[9,64,4096]{2,1,0:T(8,128)(2,1)S(1)}, f32[64,128]{1,0:T(8,128)S(1)}) custom-call(bf16[64,4096]{1,0:T(8,128)(2,1)S(1)} %collective-permute-done.13.rows_ref), custom_call_target="tpu_custom_call" | custom-call | flops 10485760 | bytes 6291456 | tf_op jit(solution)/shard_map/lags/pallas_call | solution.py:144
  62.1 5.5 %collective-permute-done.11.rows_ref = bf16[64,4096]{1,0:T(8,128)(2,1)S(1)} collective-permute-done((bf16[64,4096]{1,0:T(8,128)(2,1)S(1)}, bf16[64,4096]{1,0:T(8,128)(2,1)S(1)}, u32[]{:S(2)}, u32[]{:S(2)}) %collective-permute-start.11) | collective-permute-done | bytes 524320 | tf_op jit(solution)/shard_map/ppermute | solution.py:286
  67.6 1.3 %lags.6 = (bf16[9,64,4096]{2,1,0:T(8,128)(2,1)S(1)}, f32[64,128]{1,0:T(8,128)S(1)}) custom-call(bf16[64,4096]{1,0:T(8,128)(2,1)S(1)} %collective-permute-done.11.rows_ref), custom_call_target="tpu_custom_call" | custom-call | flops 10485760 | bytes 6291456 | tf_op jit(solution)/shard_map/lags/pallas_call | solution.py:144
  68.9 1.3 %columns.1 = (bf16[32,8,4096]{2,1,0:T(8,128)(2,1)S(1)}, f32[8,256]{1,0:T(8,128)S(1)}) custom-call(s32[5]{0:T(128)S(1)} %stack.20.place.refs_0_, bf16[4,8,4096]{2,1,0:T(8,128)(2,1)S(1)} %constant_dynamic-update-slice_fusion.refs_1_, bf16[4,8,4096]{2,1,0:T(8,128)(2,1)S(1)} %collective-permute-done.2.refs_2_, ...), custom_call_target="tpu_custom_call" | custom-call | flops 8388608 | bytes 4194304 | tf_op jit(solution)/shard_map/columns/pallas_call | solution.py:193
  70.1 1.4 %weigh.7 = f32[9,64,256]{2,1,0:T(8,128)S(1)} custom-call(bf16[9,64,4096]{2,1,0:T(8,128)(2,1)S(1)} %get-tuple-element.31.refs_0_, f32[64,128]{1,0:T(8,128)S(1)} %get-tuple-element.32.refs_1_, bf16[32,8,4096]{2,1,0:T(8,128)(2,1)S(1)} %get-tuple-element.35.refs_2_, f32[8,256]{1,0:T(8,128)S(1)} %get-tuple-element.36.refs_3_), custom_call_target="tpu_custom_call" | custom-call | flops 1207959552 | bytes 589824 | tf_op jit(solution)/shard_map/weigh/pallas_call | solution.py:228
  71.7 3.0 %collective-permute-start.15 = (f16[9,64,256]{2,1,0:T(8,128)(2,1)S(1)}, f16[9,64,256]{2,1,0:T(8,128)(2,1)S(1)}, u32[]{:S(2)}, u32[]{:S(2)}) collective-permute-start(f16[9,64,256]{2,1,0:T(8,128)(2,1)S(1)} %convert_element_type.22), channel_id=1, source_target_pairs={{0,4},{4,0},{1,5},{5,1},{2,6},{6,2},{3,7},{7,3},{8,12},{12,8},{9,1... | collective-permute-start | bytes 884744 | tf_op jit(solution)/shard_map/ppermute | solution.py:282
  74.6 1.4 %weigh.6 = f32[9,64,256]{2,1,0:T(8,128)S(1)} custom-call(bf16[9,64,4096]{2,1,0:T(8,128)(2,1)S(1)} %get-tuple-element.41.refs_0_, f32[64,128]{1,0:T(8,128)S(1)} %get-tuple-element.42.refs_1_, bf16[32,8,4096]{2,1,0:T(8,128)(2,1)S(1)} %get-tuple-element.35.refs_2_, f32[8,256]{1,0:T(8,128)S(1)} %get-tuple-element.36.refs_3_), custom_call_target="tpu_custom_call" | custom-call | flops 1207959552 | bytes 589824 | tf_op jit(solution)/shard_map/weigh/pallas_call | solution.py:228
  76.5 1.4 %weigh.5 = f32[9,64,256]{2,1,0:T(8,128)S(1)} custom-call(bf16[9,64,4096]{2,1,0:T(8,128)(2,1)S(1)} %get-tuple-element.38.refs_0_, f32[64,128]{1,0:T(8,128)S(1)} %get-tuple-element.39.refs_1_, bf16[32,8,4096]{2,1,0:T(8,128)(2,1)S(1)} %get-tuple-element.35.refs_2_, f32[8,256]{1,0:T(8,128)S(1)} %get-tuple-element.36.refs_3_), custom_call_target="tpu_custom_call" | custom-call | flops 1207959552 | bytes 589824 | tf_op jit(solution)/shard_map/weigh/pallas_call | solution.py:228
  78.0 1.9 %collective-permute-start.12 = (f16[9,64,256]{2,1,0:T(8,128)(2,1)S(1)}, f16[9,64,256]{2,1,0:T(8,128)(2,1)S(1)}, u32[]{:S(2)}, u32[]{:S(2)}) collective-permute-start(f16[9,64,256]{2,1,0:T(8,128)(2,1)S(1)} %convert_element_type.18), channel_id=1, source_target_pairs={{0,12},{4,8},{8,4},{12,0},{16,28},{20,24},{24,20},{28,16},{1,13},{... | collective-permute-start | bytes 884744 | tf_op jit(solution)/shard_map/ppermute | solution.py:290
  79.9 1.4 %weigh.4.own = f32[9,64,256]{2,1,0:T(8,128)S(1)} custom-call(bf16[9,64,4096]{2,1,0:T(8,128)(2,1)S(1)} %get-tuple-element.26.refs_0_, f32[64,128]{1,0:T(8,128)S(1)} %get-tuple-element.27.refs_1_, bf16[32,8,4096]{2,1,0:T(8,128)(2,1)S(1)} %get-tuple-element.35.refs_2_, f32[8,256]{1,0:T(8,128)S(1)} %get-tuple-element.36.refs_3_), custom_call_target="tpu_custom_call" | custom-call | flops 1207959552 | bytes 589824 | tf_op jit(solution)/shard_map/weigh/pallas_call | solution.py:228
  81.4 4.8 %collective-permute-done.14 = f16[9,64,256]{2,1,0:T(8,128)(2,1)S(1)} collective-permute-done((f16[9,64,256]{2,1,0:T(8,128)(2,1)S(1)}, f16[9,64,256]{2,1,0:T(8,128)(2,1)S(1)}, u32[]{:S(2)}, u32[]{:S(2)}) %collective-permute-start.14) | collective-permute-done | bytes 294944 | tf_op jit(solution)/shard_map/ppermute | solution.py:286
  86.2 3.2 %collective-permute-done.12 = f16[9,64,256]{2,1,0:T(8,128)(2,1)S(1)} collective-permute-done((f16[9,64,256]{2,1,0:T(8,128)(2,1)S(1)}, f16[9,64,256]{2,1,0:T(8,128)(2,1)S(1)}, u32[]{:S(2)}, u32[]{:S(2)}) %collective-permute-start.12) | collective-permute-done | bytes 294944 | tf_op jit(solution)/shard_map/ppermute | solution.py:290
  89.5 4.8 %join.1 = f32[9,64,1024]{2,1,0:T(8,128)} custom-call(s32[5]{0:T(128)S(1)} %stack.20.place.refs_0_, f32[9,64,256]{2,1,0:T(8,128)S(1)} %weigh.4.own, f32[9,64,256]{2,1,0:T(8,128)S(1)} %convert_element_type.19.got_xy, f32[9,64,256]{2,1,0:T(8,128)S(1)} %convert_element_type.21.got_x, f32[9,64,256]{2,1,0:T(8,128)S(1)} %convert_element_type.23.got_y), custom_call_target="tpu_custom_call" | custom-call | tf_op jit(solution)/shard_map/join/pallas_call | solution.py:265
  (26 shorter events, 1.4 us)
Async XLA Ops:
  8.2 0.7 copy-start
  10.0 6.3 %collective-permute-start = (bf16[2,8,4096]{2,1,0:T(8,128)(2,1)S(1)}, bf16[2,8,4096]{2,1,0:T(8,128)(2,1)S(1)}, u32[]{:S(2)}, u32[]{:S(2)}) collective-permute-start(bf16[2,8,4096]{2,1,0:T(8,128)(2,1)S(1)} %pieces.1), channel_id=1, source_target_pairs={{0,0},{1,64},{2,128},{3,192},{32,32},{33,96},{34,160},{35,224},{64... | collective-permute-start | bytes 393224 | tf_op jit(solution)/shard_map/ppermute | solution.py:298
  13.4 30.6 %collective-permute-start.8 = (bf16[64,4096]{1,0:T(8,128)(2,1)S(1)}, bf16[64,4096]{1,0:T(8,128)(2,1)S(1)}, u32[]{:S(2)}, u32[]{:S(2)}) collective-permute-start(bf16[64,4096]{1,0:T(8,128)(2,1)S(1)} %get-tuple-element.25.rows_ref), channel_id=1, source_target_pairs={{0,4},{4,0},{1,5},{5,1},{2,6},{6,2},{3,7},{7,3},{8,12},{12,8},{9,1... | collective-permute-start | bytes 1572872 | tf_op jit(solution)/shard_map/ppermute | solution.py:282
  16.3 6.5 %collective-permute-start.1 = (bf16[2,8,4096]{2,1,0:T(8,128)(2,1)S(1)}, bf16[2,8,4096]{2,1,0:T(8,128)(2,1)S(1)}, u32[]{:S(2)}, u32[]{:S(2)}) collective-permute-start(bf16[2,8,4096]{2,1,0:T(8,128)(2,1)S(1)} %collective-permute-done), channel_id=1, source_target_pairs={{0,16},{8,24},{16,0},{24,8},{1,17},{9,25},{17,1},{25,9},{2,18},{10... | collective-permute-start | bytes 393224 | tf_op jit(solution)/shard_map/ppermute | solution.py:278
  22.8 17.0 %collective-permute-start.2 = (bf16[4,8,4096]{2,1,0:T(8,128)(2,1)S(1)}, bf16[4,8,4096]{2,1,0:T(8,128)(2,1)S(1)}, u32[]{:S(2)}, u32[]{:S(2)}) collective-permute-start(bf16[4,8,4096]{2,1,0:T(8,128)(2,1)S(1)} %constant_dynamic-update-slice_fusion.refs_1_), channel_id=1, source_target_pairs={{0,32},{32,64},{64,96},{96,128},{128,160},{160,192},{192,224},{224... | collective-permute-start | bytes 786440 | tf_op jit(solution)/shard_map/ppermute | solution.py:278
  24.8 15.0 %collective-permute-start.3 = (bf16[4,8,4096]{2,1,0:T(8,128)(2,1)S(1)}, bf16[4,8,4096]{2,1,0:T(8,128)(2,1)S(1)}, u32[]{:S(2)}, u32[]{:S(2)}) collective-permute-start(bf16[4,8,4096]{2,1,0:T(8,128)(2,1)S(1)} %constant_dynamic-update-slice_fusion.refs_1_), channel_id=1, source_target_pairs={{0,224},{32,0},{64,32},{96,64},{128,96},{160,128},{192,160},{224,1... | collective-permute-start | bytes 786440 | tf_op jit(solution)/shard_map/ppermute | solution.py:278
  39.7 9.5 %collective-permute-start.4 = (bf16[4,8,4096]{2,1,0:T(8,128)(2,1)S(1)}, bf16[4,8,4096]{2,1,0:T(8,128)(2,1)S(1)}, u32[]{:S(2)}, u32[]{:S(2)}) collective-permute-start(bf16[4,8,4096]{2,1,0:T(8,128)(2,1)S(1)} %collective-permute-done.2.refs_2_), channel_id=1, source_target_pairs={{0,32},{32,64},{64,96},{96,128},{128,160},{160,192},{192,224},{224... | collective-permute-start | bytes 786440 | tf_op jit(solution)/shard_map/ppermute | solution.py:278
  39.7 9.5 %collective-permute-start.5 = (bf16[4,8,4096]{2,1,0:T(8,128)(2,1)S(1)}, bf16[4,8,4096]{2,1,0:T(8,128)(2,1)S(1)}, u32[]{:S(2)}, u32[]{:S(2)}) collective-permute-start(bf16[4,8,4096]{2,1,0:T(8,128)(2,1)S(1)} %collective-permute-done.3.refs_3_), channel_id=1, source_target_pairs={{0,224},{32,0},{64,32},{96,64},{128,96},{160,128},{192,160},{224,1... | collective-permute-start | bytes 786440 | tf_op jit(solution)/shard_map/ppermute | solution.py:278
  43.4 17.4 %collective-permute-start.13 = (bf16[64,4096]{1,0:T(8,128)(2,1)S(1)}, bf16[64,4096]{1,0:T(8,128)(2,1)S(1)}, u32[]{:S(2)}, u32[]{:S(2)}) collective-permute-start(bf16[64,4096]{1,0:T(8,128)(2,1)S(1)} %get-tuple-element.25.rows_ref), channel_id=1, source_target_pairs={{0,8},{8,0},{16,24},{24,16},{1,9},{9,1},{17,25},{25,17},{2,10},{10... | collective-permute-start | bytes 1572872 | tf_op jit(solution)/shard_map/ppermute | solution.py:286
  44.0 23.6 %collective-permute-start.11 = (bf16[64,4096]{1,0:T(8,128)(2,1)S(1)}, bf16[64,4096]{1,0:T(8,128)(2,1)S(1)}, u32[]{:S(2)}, u32[]{:S(2)}) collective-permute-start(bf16[64,4096]{1,0:T(8,128)(2,1)S(1)} %collective-permute-done.8.rows_ref), channel_id=1, source_target_pairs={{0,8},{8,0},{16,24},{24,16},{1,9},{9,1},{17,25},{25,17},{2,10},{10... | collective-permute-start | bytes 1572872 | tf_op jit(solution)/shard_map/ppermute | solution.py:286
  49.3 8.2 %collective-permute-start.6 = (bf16[4,8,4096]{2,1,0:T(8,128)(2,1)S(1)}, bf16[4,8,4096]{2,1,0:T(8,128)(2,1)S(1)}, u32[]{:S(2)}, u32[]{:S(2)}) collective-permute-start(bf16[4,8,4096]{2,1,0:T(8,128)(2,1)S(1)} %collective-permute-done.4.refs_4_), channel_id=1, source_target_pairs={{0,32},{32,64},{64,96},{96,128},{128,160},{160,192},{192,224},{224... | collective-permute-start | bytes 786440 | tf_op jit(solution)/shard_map/ppermute | solution.py:278
  49.3 8.2 %collective-permute-start.7 = (bf16[4,8,4096]{2,1,0:T(8,128)(2,1)S(1)}, bf16[4,8,4096]{2,1,0:T(8,128)(2,1)S(1)}, u32[]{:S(2)}, u32[]{:S(2)}) collective-permute-start(bf16[4,8,4096]{2,1,0:T(8,128)(2,1)S(1)} %collective-permute-done.5.refs_5_), channel_id=1, source_target_pairs={{0,224},{32,0},{64,32},{96,64},{128,96},{160,128},{192,160},{224,1... | collective-permute-start | bytes 786440 | tf_op jit(solution)/shard_map/ppermute | solution.py:278
  57.5 11.4 %collective-permute-start.10 = (bf16[2,8,4096]{2,1,0:T(8,128)(2,1)S(1)}, bf16[2,8,4096]{2,1,0:T(8,128)(2,1)S(1)}, u32[]{:S(2)}, u32[]{:S(2)}) collective-permute-start(bf16[2,8,4096]{2,1,0:T(8,128)(2,1)S(1)} %slice.7), channel_id=1, source_target_pairs={{0,224},{32,0},{64,32},{96,64},{128,96},{160,128},{192,160},{224,1... | collective-permute-start | bytes 393224 | tf_op jit(solution)/shard_map/ppermute | solution.py:278
  60.7 8.2 %collective-permute-start.9 = (bf16[2,8,4096]{2,1,0:T(8,128)(2,1)S(1)}, bf16[2,8,4096]{2,1,0:T(8,128)(2,1)S(1)}, u32[]{:S(2)}, u32[]{:S(2)}) collective-permute-start(bf16[2,8,4096]{2,1,0:T(8,128)(2,1)S(1)} %slice.6), channel_id=1, source_target_pairs={{0,32},{32,64},{64,96},{96,128},{128,160},{160,192},{192,224},{224... | collective-permute-start | bytes 393224 | tf_op jit(solution)/shard_map/ppermute | solution.py:278
  71.7 9.7 %collective-permute-start.15 = (f16[9,64,256]{2,1,0:T(8,128)(2,1)S(1)}, f16[9,64,256]{2,1,0:T(8,128)(2,1)S(1)}, u32[]{:S(2)}, u32[]{:S(2)}) collective-permute-start(f16[9,64,256]{2,1,0:T(8,128)(2,1)S(1)} %convert_element_type.22), channel_id=1, source_target_pairs={{0,4},{4,0},{1,5},{5,1},{2,6},{6,2},{3,7},{7,3},{8,12},{12,8},{9,1... | collective-permute-start | bytes 884744 | tf_op jit(solution)/shard_map/ppermute | solution.py:282
  76.1 10.0 %collective-permute-start.14 = (f16[9,64,256]{2,1,0:T(8,128)(2,1)S(1)}, f16[9,64,256]{2,1,0:T(8,128)(2,1)S(1)}, u32[]{:S(2)}, u32[]{:S(2)}) collective-permute-start(f16[9,64,256]{2,1,0:T(8,128)(2,1)S(1)} %convert_element_type.20), channel_id=1, source_target_pairs={{0,8},{8,0},{16,24},{24,16},{1,9},{9,1},{17,25},{25,17},{2,10},{10... | collective-permute-start | bytes 884744 | tf_op jit(solution)/shard_map/ppermute | solution.py:286
  78.0 11.4 %collective-permute-start.12 = (f16[9,64,256]{2,1,0:T(8,128)(2,1)S(1)}, f16[9,64,256]{2,1,0:T(8,128)(2,1)S(1)}, u32[]{:S(2)}, u32[]{:S(2)}) collective-permute-start(f16[9,64,256]{2,1,0:T(8,128)(2,1)S(1)} %convert_element_type.18), channel_id=1, source_target_pairs={{0,12},{4,8},{8,4},{12,0},{16,28},{20,24},{24,20},{28,16},{1,13},{... | collective-permute-start | bytes 884744 | tf_op jit(solution)/shard_map/ppermute | solution.py:290

commit v5 on v4

--- a/solution.py
+++ b/solution.py
@@ -240,23 +240,28 @@
     )(lagged, energy, columns, scale)
 
 
-def join_kernel(place, own, got_xy, got_x, got_y, out):
+def join_kernel(place, own, got_xy, got_x, got_y, out, buffer, sems):
     low = place[4] == 0
-    rows = out.shape[1]
-    lag = pl.program_id(0)
+    lags, rows = buffer.shape[:2]
     lane = lax.broadcasted_iota(jnp.int32, (rows, 128), 1) < 64
-    for half in range(2):
-        span = slice(half * 128, (half + 1) * 128)
-        for flip, (same, cross) in enumerate(((own, got_y), (got_x, got_xy))):
-            here_x = place[3] ^ flip
-            here = same[lag, :, span] * (1.0 / SCALE) if flip else same[lag, :, span]
-            there = cross[lag, :, span] * (1.0 / SCALE)
-            one = jnp.where(low, here, there)
-            two = jnp.where(low, there, here)
-            at = pl.multiple_of((half * 4 + here_x) * 128, 128)
-            out[0, :, pl.ds(at, 128)] = jnp.where(lane, one, pltpu.roll(two, 64, axis=1))
-            at = pl.multiple_of((half * 4 + (here_x ^ 2)) * 128, 128)
-            out[0, :, pl.ds(at, 128)] = jnp.where(lane, pltpu.roll(one, 64, axis=1), two)
+    copies = []
+    for lag in range(lags):
+        for half in range(2):
+            span = slice(half * 128, (half + 1) * 128)
+            for flip, (same, cross) in enumerate(((own, got_y), (got_x, got_xy))):
+                here_x = place[3] ^ flip
+                here = same[lag, :, span] * (1.0 / SCALE) if flip else same[lag, :, span]
+                there = cross[lag, :, span] * (1.0 / SCALE)
+                one = jnp.where(low, here, there)
+                two = jnp.where(low, there, here)
+                at = pl.multiple_of((half * 4 + here_x) * 128, 128)
+                buffer[lag, :, pl.ds(at, 128)] = jnp.where(lane, one, pltpu.roll(two, 64, axis=1))
+                at = pl.multiple_of((half * 4 + (here_x ^ 2)) * 128, 128)
+                buffer[lag, :, pl.ds(at, 128)] = jnp.where(lane, pltpu.roll(one, 64, axis=1), two)
+        copies.append(pltpu.make_async_copy(buffer.at[lag], out.at[lag], sems.at[lag]))
+        copies[-1].start()
+    for copy in copies:
+        copy.wait()
 
 
 def run_join(place, *quarters):
@@ -264,10 +269,13 @@
     vmem = pl.BlockSpec(memory_space=pltpu.VMEM)
     return pl.pallas_call(
         join_kernel,
-        grid=(lags,),
         in_specs=[pl.BlockSpec(memory_space=pltpu.SMEM)] + [vmem] * 4,
-        out_specs=pl.BlockSpec((1, rows, 4 * width), lambda i: (i, 0, 0)),
+        out_specs=pl.BlockSpec(memory_space=pltpu.HBM),
         out_shape=jax.ShapeDtypeStruct((lags, rows, 4 * width), jnp.float32),
+        scratch_shapes=[
+            pltpu.VMEM((lags, rows, 4 * width), jnp.float32),
+            pltpu.SemaphoreType.DMA((lags,)),
+        ],
         compiler_params=pltpu.CompilerParams(vmem_limit_bytes=8 * MB),
         name="join",
     )(place, *quarters)
@@ -321,22 +329,21 @@
     row_y = cross_y(full)
     row_x = cross_x(full)
     row_xy = cross_x(after(row_y, *first))
-    own = run_lags(after(full, *first))
-    ready = after(second, own)
-    third = (around(ready[0], "z", 1), around(ready[1], "z", -1))
-    far_y = run_lags(after(row_y, *second))
-    ready = after(third, far_y)
+    far_y = run_lags(after(row_y, *first))
+    third = (around(after(second[0], far_y), "z", 1), around(after(second[1], far_y), "z", -1))
+    far_x = run_lags(after(row_x, *second))
+    ready = after(third[0], far_x), after(third[1], far_x)
     units += [*first, *second, *third, around(ready[0][0:2], "z", 1), around(ready[1][2:4], "z", -1)]
     for step in (1, 2, 3):
         steps += [[(part, -step) for part in order], [(part, step) for part in order]]
     steps += [[(part, 4) for part in order[0:2]], [(part, 4) for part in order[2:4]]]
-    far_x = run_lags(after(row_x, *third))
-    far_xy = run_lags(row_xy)
+    far_xy = run_lags(after(row_xy, *third))
     columns, scale = run_columns(place, units, steps)
     got = []
     for rows, move in ((far_xy, cross_xy), (far_x, cross_x), (far_y, cross_y)):
-        send = run_weigh(rows, columns, scale, SCALE).astype(SENT)
-        got.append(move(send).astype(jnp.float32))
+        came = move(run_weigh(rows, columns, scale, SCALE).astype(SENT))
+        got.append(after(came, *got[-1:]).astype(jnp.float32))
+    own = run_lags(after(full, scale))
     kept = run_weigh(own, columns, scale, 1)
     information = run_join(place, kept, *got)
     return (information, mine)

time: 94.6 us -> 87.6 us (0.926)
  waiting for transfers between devices: 31.1 us -> 27.5 us
  Pallas kernels: 20.7 us -> 18.1 us
    ppermute x3, waiting for transfers between devices: 10.3 us -> 0.01 us  [cross_x(): return lax.ppermute(value, 'x', [(0, 1), (1, 0), (2, 3), (3, 2)])]
    ppermute x2, waiting for transfers between devices: 0.01 us -> 3.84 us  [cross_y(): return lax.ppermute(value, 'yh', [(0, 1), (1, 0)])]
    pallas_call x1, Pallas kernels: 4.81 us -> 2.15 us  [run_join(): pl.pallas_call(join_kernel, in_specs=[pl.BlockSpec(memory_space=pltpu.SME...]
    ppermute x9, waiting for transfers between devices: 17.6 us -> 20.2 us  [around(): lax.ppermute(value, axis, [(i, (i + step) % size) for i in range(size)])]
    ppermute x2, starting transfers between devices: 5.9 us -> 3.62 us  [cross_y(): return lax.ppermute(value, 'yh', [(0, 1), (1, 0)])]
    ppermute x1, starting transfers between devices: 1.88 us -> 3.91 us  [cross_xy(): return lax.ppermute(value, ('x', 'yh'), [(i, i ^ 3) for i in range(8)])]
  transfers between devices with their start and end apart: 16 -> 16, of which waited for: 7 -> 7; matrix products, arithmetic and copies ran while one was open for 0% -> 0% of each run, Pallas kernels for 13% -> 14%
where the time goes in v5:
time: 87.6 us; the launch traced here: 87.5 us
  starting transfers between devices  32.4 us (37%)
  waiting for transfers between devices  27.5 us (31%)
  Pallas kernels  18.1 us (21%)
  blocking collectives  7.47 us (9%)
  between operations  0.97 us (1%)
    ppermute x9, starting transfers between devices, around(): lax.ppermute(value, axis, [(i, (i + step) % size) for i in range(size)])  22.5 us
    ppermute x9, waiting for transfers between devices, around(): lax.ppermute(value, axis, [(i, (i + step) % size) for i in range(size)])  20.2 us
    all_gather x1, blocking collectives, shards(): parts = lax.all_gather(raw, ('yl', 'core'), axis=0, tiled=False)  7.47 us
    pallas_call x4, Pallas kernels, run_weigh(): pl.pallas_call(body, in_specs=[vmem] * 4, out_specs=vmem, out_shape=jax.S...  5.74 us
    pallas_call x4, Pallas kernels, run_lags(): pl.pallas_call(lag_kernel, in_specs=[vmem], out_specs=[vmem, vmem], out_s...  5.05 us
    ppermute x1, starting transfers between devices, cross_xy(): return lax.ppermute(value, ('x', 'yh'), [(i, i ^ 3) for i in range(8)])  3.91 us
    ppermute x2, waiting for transfers between devices, cross_y(): return lax.ppermute(value, 'yh', [(0, 1), (1, 0)])  3.84 us
    ppermute x2, starting transfers between devices, cross_y(): return lax.ppermute(value, 'yh', [(0, 1), (1, 0)])  3.62 us
  transfers between devices with their start and end apart: 16, of which 7 were waited for; matrix products, arithmetic and copies ran while one was open for 0% of the time, Pallas kernels for 14%

profile of v5, /device:TPU:2, one launch (start us, length us, event | category | flops | bytes accessed | tf_op | source)
XLA Modules:
  0.0 87.5 jit_solution(14590267484847354778)
XLA Ops:
  0.6 7.5 %all-gather = bf16[256,1024]{1,0:T(8,128)(2,1)S(1)} all-gather(bf16[64,1024]{1,0:T(8,128)(2,1)} %param.2), channel_id=2, replica_groups=mesh['z'=8,'x'=4,'yh'=2,'yl'=2,'core'=2] {'yl','core'}, dimensions={0}, use_global_device_ids=true | all-gather | bytes 655360 | tf_op jit(solution)/shard_map/all_gather | solution.py:320
  8.2 0.7 copy-done
  8.8 1.1 %pieces.1 = bf16[2,8,4096]{2,1,0:T(8,128)(2,1)S(1)} custom-call(s32[5]{0:T(128)S(1)} %stack.20.place.refs_0_, f32[1,65]{1,0:T(1,128)S(1)} %bitcast.8, bf16[4,64,1024]{2,1,0:T(8,128)(2,1)S(1)} %bitcast.6), custom_call_target="tpu_custom_call" | custom-call | tf_op jit(solution)/shard_map/pieces/pallas_call | solution.py:66
  10.0 0.7 collective-permute-start
  10.7 2.7 %rows.1 = (bf16[64,4096]{1,0:T(8,128)(2,1)S(1)}, bf16[64,1024]{1,0:T(8,128)(2,1)}) custom-call(s32[5]{0:T(128)S(1)} %stack.20.place.refs_0_, f32[1,65]{1,0:T(1,128)S(1)} %bitcast.9, bf16[4,64,1024]{2,1,0:T(8,128)(2,1)S(1)} %bitcast.7), custom_call_target="tpu_custom_call" | custom-call | flops 1073741824 | bytes 4194304 | tf_op jit(solution)/shard_map/rows/pallas_call | solution.py:103
  13.4 2.9 %collective-permute-start.6 = (bf16[64,4096]{1,0:T(8,128)(2,1)S(1)}, bf16[64,4096]{1,0:T(8,128)(2,1)S(1)}, u32[]{:S(2)}, u32[]{:S(2)}) collective-permute-start(bf16[64,4096]{1,0:T(8,128)(2,1)S(1)} %get-tuple-element.38.rows_ref), channel_id=1, source_target_pairs={{0,4},{4,0},{1,5},{5,1},{2,6},{6,2},{3,7},{7,3},{8,12},{12,8},{9,1... | collective-permute-start | bytes 1572872 | tf_op jit(solution)/shard_map/ppermute | solution.py:290
  16.3 2.1 %collective-permute-start.1 = (bf16[2,8,4096]{2,1,0:T(8,128)(2,1)S(1)}, bf16[2,8,4096]{2,1,0:T(8,128)(2,1)S(1)}, u32[]{:S(2)}, u32[]{:S(2)}) collective-permute-start(bf16[2,8,4096]{2,1,0:T(8,128)(2,1)S(1)} %collective-permute-done), channel_id=1, source_target_pairs={{0,16},{8,24},{16,0},{24,8},{1,17},{9,25},{17,1},{25,9},{2,18},{10... | collective-permute-start | bytes 393224 | tf_op jit(solution)/shard_map/ppermute | solution.py:286
  18.4 4.3 %collective-permute-done.1 = bf16[2,8,4096]{2,1,0:T(8,128)(2,1)S(1)} collective-permute-done((bf16[2,8,4096]{2,1,0:T(8,128)(2,1)S(1)}, bf16[2,8,4096]{2,1,0:T(8,128)(2,1)S(1)}, u32[]{:S(2)}, u32[]{:S(2)}) %collective-permute-start.1) | collective-permute-done | bytes 131104 | tf_op jit(solution)/shard_map/ppermute | solution.py:286
  22.8 2.0 %collective-permute-start.2 = (bf16[4,8,4096]{2,1,0:T(8,128)(2,1)S(1)}, bf16[4,8,4096]{2,1,0:T(8,128)(2,1)S(1)}, u32[]{:S(2)}, u32[]{:S(2)}) collective-permute-start(bf16[4,8,4096]{2,1,0:T(8,128)(2,1)S(1)} %constant_dynamic-update-slice_fusion.refs_1_), channel_id=1, source_target_pairs={{0,32},{32,64},{64,96},{96,128},{128,160},{160,192},{192,224},{224... | collective-permute-start | bytes 786440 | tf_op jit(solution)/shard_map/ppermute | solution.py:286
  24.8 7.9 %collective-permute-start.3 = (bf16[4,8,4096]{2,1,0:T(8,128)(2,1)S(1)}, bf16[4,8,4096]{2,1,0:T(8,128)(2,1)S(1)}, u32[]{:S(2)}, u32[]{:S(2)}) collective-permute-start(bf16[4,8,4096]{2,1,0:T(8,128)(2,1)S(1)} %constant_dynamic-update-slice_fusion.refs_1_), channel_id=1, source_target_pairs={{0,224},{32,0},{64,32},{96,64},{128,96},{160,128},{192,160},{224,1... | collective-permute-start | bytes 786440 | tf_op jit(solution)/shard_map/ppermute | solution.py:286
  33.2 6.5 %collective-permute-done.2.refs_2_ = bf16[4,8,4096]{2,1,0:T(8,128)(2,1)S(1)} collective-permute-done((bf16[4,8,4096]{2,1,0:T(8,128)(2,1)S(1)}, bf16[4,8,4096]{2,1,0:T(8,128)(2,1)S(1)}, u32[]{:S(2)}, u32[]{:S(2)}) %collective-permute-start.2) | collective-permute-done | bytes 262176 | tf_op jit(solution)/shard_map/ppermute | solution.py:286
  39.7 3.7 %collective-permute-start.5 = (bf16[4,8,4096]{2,1,0:T(8,128)(2,1)S(1)}, bf16[4,8,4096]{2,1,0:T(8,128)(2,1)S(1)}, u32[]{:S(2)}, u32[]{:S(2)}) collective-permute-start(bf16[4,8,4096]{2,1,0:T(8,128)(2,1)S(1)} %collective-permute-done.3.refs_3_), channel_id=1, source_target_pairs={{0,224},{32,0},{64,32},{96,64},{128,96},{160,128},{192,160},{224,1... | collective-permute-start | bytes 786440 | tf_op jit(solution)/shard_map/ppermute | solution.py:286
  44.0 1.3 %lags.4 = (bf16[9,64,4096]{2,1,0:T(8,128)(2,1)S(1)}, f32[64,128]{1,0:T(8,128)S(1)}) custom-call(bf16[64,4096]{1,0:T(8,128)(2,1)S(1)} %collective-permute-done.6.rows_ref), custom_call_target="tpu_custom_call" | custom-call | flops 10485760 | bytes 6291456 | tf_op jit(solution)/shard_map/lags/pallas_call | solution.py:144
  45.2 4.0 %collective-permute-done.4.refs_4_ = bf16[4,8,4096]{2,1,0:T(8,128)(2,1)S(1)} collective-permute-done((bf16[4,8,4096]{2,1,0:T(8,128)(2,1)S(1)}, bf16[4,8,4096]{2,1,0:T(8,128)(2,1)S(1)}, u32[]{:S(2)}, u32[]{:S(2)}) %collective-permute-start.4) | collective-permute-done | bytes 262176 | tf_op jit(solution)/shard_map/ppermute | solution.py:286
  49.3 3.2 %collective-permute-start.8 = (bf16[4,8,4096]{2,1,0:T(8,128)(2,1)S(1)}, bf16[4,8,4096]{2,1,0:T(8,128)(2,1)S(1)}, u32[]{:S(2)}, u32[]{:S(2)}) collective-permute-start(bf16[4,8,4096]{2,1,0:T(8,128)(2,1)S(1)} %collective-permute-done.5.refs_5_), channel_id=1, source_target_pairs={{0,224},{32,0},{64,32},{96,64},{128,96},{160,128},{192,160},{224,1... | collective-permute-start | bytes 786440 | tf_op jit(solution)/shard_map/ppermute | solution.py:286
  52.5 1.3 %lags.5 = (bf16[9,64,4096]{2,1,0:T(8,128)(2,1)S(1)}, f32[64,128]{1,0:T(8,128)S(1)}) custom-call(bf16[64,4096]{1,0:T(8,128)(2,1)S(1)} %collective-permute-done.9.rows_ref), custom_call_target="tpu_custom_call" | custom-call | flops 10485760 | bytes 6291456 | tf_op jit(solution)/shard_map/lags/pallas_call | solution.py:144
  53.8 3.7 %collective-permute-done.7.refs_6_ = bf16[4,8,4096]{2,1,0:T(8,128)(2,1)S(1)} collective-permute-done((bf16[4,8,4096]{2,1,0:T(8,128)(2,1)S(1)}, bf16[4,8,4096]{2,1,0:T(8,128)(2,1)S(1)}, u32[]{:S(2)}, u32[]{:S(2)}) %collective-permute-start.7) | collective-permute-done | bytes 262176 | tf_op jit(solution)/shard_map/ppermute | solution.py:286
  57.8 3.3 %collective-permute-start.11 = (bf16[2,8,4096]{2,1,0:T(8,128)(2,1)S(1)}, bf16[2,8,4096]{2,1,0:T(8,128)(2,1)S(1)}, u32[]{:S(2)}, u32[]{:S(2)}) collective-permute-start(bf16[2,8,4096]{2,1,0:T(8,128)(2,1)S(1)} %slice.7), channel_id=1, source_target_pairs={{0,224},{32,0},{64,32},{96,64},{128,96},{160,128},{192,160},{224,1... | collective-permute-start | bytes 393224 | tf_op jit(solution)/shard_map/ppermute | solution.py:286
  61.1 1.3 %lags.7 = (bf16[9,64,4096]{2,1,0:T(8,128)(2,1)S(1)}, f32[64,128]{1,0:T(8,128)S(1)}) custom-call(bf16[64,4096]{1,0:T(8,128)(2,1)S(1)} %collective-permute-done.12.rows_ref), custom_call_target="tpu_custom_call" | custom-call | flops 10485760 | bytes 6291456 | tf_op jit(solution)/shard_map/lags/pallas_call | solution.py:144
  62.4 1.6 %collective-permute-done.10.refs_8_ = bf16[2,8,4096]{2,1,0:T(8,128)(2,1)S(1)} collective-permute-done((bf16[2,8,4096]{2,1,0:T(8,128)(2,1)S(1)}, bf16[2,8,4096]{2,1,0:T(8,128)(2,1)S(1)}, u32[]{:S(2)}, u32[]{:S(2)}) %collective-permute-start.10) | collective-permute-done | bytes 131104 | tf_op jit(solution)/shard_map/ppermute | solution.py:286
  63.9 1.3 %columns.1 = (bf16[32,8,4096]{2,1,0:T(8,128)(2,1)S(1)}, f32[8,256]{1,0:T(8,128)S(1)}) custom-call(s32[5]{0:T(128)S(1)} %stack.20.place.refs_0_, bf16[4,8,4096]{2,1,0:T(8,128)(2,1)S(1)} %constant_dynamic-update-slice_fusion.refs_1_, bf16[4,8,4096]{2,1,0:T(8,128)(2,1)S(1)} %collective-permute-done.2.refs_2_, ...), custom_call_target="tpu_custom_call" | custom-call | flops 8388608 | bytes 4194304 | tf_op jit(solution)/shard_map/columns/pallas_call | solution.py:193
  65.2 1.4 %weigh.6 = f32[9,64,256]{2,1,0:T(8,128)S(1)} custom-call(bf16[9,64,4096]{2,1,0:T(8,128)(2,1)S(1)} %get-tuple-element.33.refs_0_, f32[64,128]{1,0:T(8,128)S(1)} %get-tuple-element.34.refs_1_, bf16[32,8,4096]{2,1,0:T(8,128)(2,1)S(1)} %get-tuple-element.41.refs_2_, f32[8,256]{1,0:T(8,128)S(1)} %get-tuple-element.37.refs_3_), custom_call_target="tpu_custom_call" | custom-call | flops 1207959552 | bytes 589824 | tf_op jit(solution)/shard_map/weigh/pallas_call | solution.py:228
  66.7 0.6 collective-permute-start.14
  67.3 1.4 %weigh.5 = f32[9,64,256]{2,1,0:T(8,128)S(1)} custom-call(bf16[9,64,4096]{2,1,0:T(8,128)(2,1)S(1)} %get-tuple-element.43.refs_0_, f32[64,128]{1,0:T(8,128)S(1)} %get-tuple-element.44.refs_1_, bf16[32,8,4096]{2,1,0:T(8,128)(2,1)S(1)} %get-tuple-element.41.refs_2_, f32[8,256]{1,0:T(8,128)S(1)} %get-tuple-element.37.refs_3_), custom_call_target="tpu_custom_call" | custom-call | flops 1207959552 | bytes 589824 | tf_op jit(solution)/shard_map/weigh/pallas_call | solution.py:228
  68.8 3.9 %collective-permute-start.13 = (f16[9,64,256]{2,1,0:T(8,128)(2,1)S(1)}, f16[9,64,256]{2,1,0:T(8,128)(2,1)S(1)}, u32[]{:S(2)}, u32[]{:S(2)}) collective-permute-start(f16[9,64,256]{2,1,0:T(8,128)(2,1)S(1)} %convert_element_type.18), channel_id=1, source_target_pairs={{0,12},{4,8},{8,4},{12,0},{16,28},{20,24},{24,20},{28,16},{1,13},{... | collective-permute-start | bytes 884744 | tf_op jit(solution)/shard_map/ppermute | solution.py:298
  72.7 1.4 %weigh.7 = f32[9,64,256]{2,1,0:T(8,128)S(1)} custom-call(bf16[9,64,4096]{2,1,0:T(8,128)(2,1)S(1)} %get-tuple-element.28.refs_0_, f32[64,128]{1,0:T(8,128)S(1)} %get-tuple-element.29.refs_1_, bf16[32,8,4096]{2,1,0:T(8,128)(2,1)S(1)} %get-tuple-element.41.refs_2_, f32[8,256]{1,0:T(8,128)S(1)} %get-tuple-element.37.refs_3_), custom_call_target="tpu_custom_call" | custom-call | flops 1207959552 | bytes 589824 | tf_op jit(solution)/shard_map/weigh/pallas_call | solution.py:228
  74.2 0.7 collective-permute-start.15
  74.9 1.3 %lags.6 = (bf16[9,64,4096]{2,1,0:T(8,128)(2,1)S(1)}, f32[64,128]{1,0:T(8,128)S(1)}) custom-call(bf16[64,4096]{1,0:T(8,128)(2,1)S(1)} %get-tuple-element.38.rows_ref), custom_call_target="tpu_custom_call" | custom-call | flops 10485760 | bytes 6291456 | tf_op jit(solution)/shard_map/lags/pallas_call | solution.py:144
  76.2 1.4 %weigh.4.own = f32[9,64,256]{2,1,0:T(8,128)S(1)} custom-call(bf16[9,64,4096]{2,1,0:T(8,128)(2,1)S(1)} %get-tuple-element.39.refs_0_, f32[64,128]{1,0:T(8,128)S(1)} %get-tuple-element.40.refs_1_, bf16[32,8,4096]{2,1,0:T(8,128)(2,1)S(1)} %get-tuple-element.41.refs_2_, f32[8,256]{1,0:T(8,128)S(1)} %get-tuple-element.37.refs_3_), custom_call_target="tpu_custom_call" | custom-call | flops 1207959552 | bytes 589824 | tf_op jit(solution)/shard_map/weigh/pallas_call | solution.py:228
  77.6 3.5 %collective-permute-done.13 = f16[9,64,256]{2,1,0:T(8,128)(2,1)S(1)} collective-permute-done((f16[9,64,256]{2,1,0:T(8,128)(2,1)S(1)}, f16[9,64,256]{2,1,0:T(8,128)(2,1)S(1)}, u32[]{:S(2)}, u32[]{:S(2)}) %collective-permute-start.13) | collective-permute-done | bytes 294944 | tf_op jit(solution)/shard_map/ppermute | solution.py:298
  81.3 3.8 %collective-permute-done.15 = f16[9,64,256]{2,1,0:T(8,128)(2,1)S(1)} collective-permute-done((f16[9,64,256]{2,1,0:T(8,128)(2,1)S(1)}, f16[9,64,256]{2,1,0:T(8,128)(2,1)S(1)}, u32[]{:S(2)}, u32[]{:S(2)}) %collective-permute-start.15) | collective-permute-done | bytes 294944 | tf_op jit(solution)/shard_map/ppermute | solution.py:290
  85.2 2.2 %join.1 = f32[9,64,1024]{2,1,0:T(8,128)} custom-call(s32[5]{0:T(128)S(1)} %stack.20.place.refs_0_, f32[9,64,256]{2,1,0:T(8,128)S(1)} %weigh.4.own, f32[9,64,256]{2,1,0:T(8,128)S(1)} %convert_element_type.19.got_xy, f32[9,64,256]{2,1,0:T(8,128)S(1)} %convert_element_type.21.got_x, f32[9,64,256]{2,1,0:T(8,128)S(1)} %convert_element_type.23.got_y), custom_call_target="tpu_custom_call" | custom-call | tf_op jit(solution)/shard_map/join/pallas_call | solution.py:270
  (26 shorter events, 1.8 us)
Async XLA Ops:
  8.2 0.7 copy-start
  10.0 6.3 %collective-permute-start = (bf16[2,8,4096]{2,1,0:T(8,128)(2,1)S(1)}, bf16[2,8,4096]{2,1,0:T(8,128)(2,1)S(1)}, u32[]{:S(2)}, u32[]{:S(2)}) collective-permute-start(bf16[2,8,4096]{2,1,0:T(8,128)(2,1)S(1)} %pieces.1), channel_id=1, source_target_pairs={{0,0},{1,64},{2,128},{3,192},{32,32},{33,96},{34,160},{35,224},{64... | collective-permute-start | bytes 393224 | tf_op jit(solution)/shard_map/ppermute | solution.py:306
  13.4 30.0 %collective-permute-start.6 = (bf16[64,4096]{1,0:T(8,128)(2,1)S(1)}, bf16[64,4096]{1,0:T(8,128)(2,1)S(1)}, u32[]{:S(2)}, u32[]{:S(2)}) collective-permute-start(bf16[64,4096]{1,0:T(8,128)(2,1)S(1)} %get-tuple-element.38.rows_ref), channel_id=1, source_target_pairs={{0,4},{4,0},{1,5},{5,1},{2,6},{6,2},{3,7},{7,3},{8,12},{12,8},{9,1... | collective-permute-start | bytes 1572872 | tf_op jit(solution)/shard_map/ppermute | solution.py:290
  16.3 6.5 %collective-permute-start.1 = (bf16[2,8,4096]{2,1,0:T(8,128)(2,1)S(1)}, bf16[2,8,4096]{2,1,0:T(8,128)(2,1)S(1)}, u32[]{:S(2)}, u32[]{:S(2)}) collective-permute-start(bf16[2,8,4096]{2,1,0:T(8,128)(2,1)S(1)} %collective-permute-done), channel_id=1, source_target_pairs={{0,16},{8,24},{16,0},{24,8},{1,17},{9,25},{17,1},{25,9},{2,18},{10... | collective-permute-start | bytes 393224 | tf_op jit(solution)/shard_map/ppermute | solution.py:286
  22.8 17.0 %collective-permute-start.2 = (bf16[4,8,4096]{2,1,0:T(8,128)(2,1)S(1)}, bf16[4,8,4096]{2,1,0:T(8,128)(2,1)S(1)}, u32[]{:S(2)}, u32[]{:S(2)}) collective-permute-start(bf16[4,8,4096]{2,1,0:T(8,128)(2,1)S(1)} %constant_dynamic-update-slice_fusion.refs_1_), channel_id=1, source_target_pairs={{0,32},{32,64},{64,96},{96,128},{128,160},{160,192},{192,224},{224... | collective-permute-start | bytes 786440 | tf_op jit(solution)/shard_map/ppermute | solution.py:286
  24.8 15.0 %collective-permute-start.3 = (bf16[4,8,4096]{2,1,0:T(8,128)(2,1)S(1)}, bf16[4,8,4096]{2,1,0:T(8,128)(2,1)S(1)}, u32[]{:S(2)}, u32[]{:S(2)}) collective-permute-start(bf16[4,8,4096]{2,1,0:T(8,128)(2,1)S(1)} %constant_dynamic-update-slice_fusion.refs_1_), channel_id=1, source_target_pairs={{0,224},{32,0},{64,32},{96,64},{128,96},{160,128},{192,160},{224,1... | collective-permute-start | bytes 786440 | tf_op jit(solution)/shard_map/ppermute | solution.py:286
  32.7 19.8 %collective-permute-start.9 = (bf16[64,4096]{1,0:T(8,128)(2,1)S(1)}, bf16[64,4096]{1,0:T(8,128)(2,1)S(1)}, u32[]{:S(2)}, u32[]{:S(2)}) collective-permute-start(bf16[64,4096]{1,0:T(8,128)(2,1)S(1)} %get-tuple-element.38.rows_ref), channel_id=1, source_target_pairs={{0,8},{8,0},{16,24},{24,16},{1,9},{9,1},{17,25},{25,17},{2,10},{10... | collective-permute-start | bytes 1572872 | tf_op jit(solution)/shard_map/ppermute | solution.py:294
  39.7 9.5 %collective-permute-start.4 = (bf16[4,8,4096]{2,1,0:T(8,128)(2,1)S(1)}, bf16[4,8,4096]{2,1,0:T(8,128)(2,1)S(1)}, u32[]{:S(2)}, u32[]{:S(2)}) collective-permute-start(bf16[4,8,4096]{2,1,0:T(8,128)(2,1)S(1)} %collective-permute-done.2.refs_2_), channel_id=1, source_target_pairs={{0,32},{32,64},{64,96},{96,128},{128,160},{160,192},{192,224},{224... | collective-permute-start | bytes 786440 | tf_op jit(solution)/shard_map/ppermute | solution.py:286
  39.7 9.5 %collective-permute-start.5 = (bf16[4,8,4096]{2,1,0:T(8,128)(2,1)S(1)}, bf16[4,8,4096]{2,1,0:T(8,128)(2,1)S(1)}, u32[]{:S(2)}, u32[]{:S(2)}) collective-permute-start(bf16[4,8,4096]{2,1,0:T(8,128)(2,1)S(1)} %collective-permute-done.3.refs_3_), channel_id=1, source_target_pairs={{0,224},{32,0},{64,32},{96,64},{128,96},{160,128},{192,160},{224,1... | collective-permute-start | bytes 786440 | tf_op jit(solution)/shard_map/ppermute | solution.py:286
  43.4 17.7 %collective-permute-start.12 = (bf16[64,4096]{1,0:T(8,128)(2,1)S(1)}, bf16[64,4096]{1,0:T(8,128)(2,1)S(1)}, u32[]{:S(2)}, u32[]{:S(2)}) collective-permute-start(bf16[64,4096]{1,0:T(8,128)(2,1)S(1)} %collective-permute-done.6.rows_ref), channel_id=1, source_target_pairs={{0,8},{8,0},{16,24},{24,16},{1,9},{9,1},{17,25},{25,17},{2,10},{10... | collective-permute-start | bytes 1572872 | tf_op jit(solution)/shard_map/ppermute | solution.py:294
  49.3 8.2 %collective-permute-start.7 = (bf16[4,8,4096]{2,1,0:T(8,128)(2,1)S(1)}, bf16[4,8,4096]{2,1,0:T(8,128)(2,1)S(1)}, u32[]{:S(2)}, u32[]{:S(2)}) collective-permute-start(bf16[4,8,4096]{2,1,0:T(8,128)(2,1)S(1)} %collective-permute-done.4.refs_4_), channel_id=1, source_target_pairs={{0,32},{32,64},{64,96},{96,128},{128,160},{160,192},{192,224},{224... | collective-permute-start | bytes 786440 | tf_op jit(solution)/shard_map/ppermute | solution.py:286
  49.3 8.5 %collective-permute-start.8 = (bf16[4,8,4096]{2,1,0:T(8,128)(2,1)S(1)}, bf16[4,8,4096]{2,1,0:T(8,128)(2,1)S(1)}, u32[]{:S(2)}, u32[]{:S(2)}) collective-permute-start(bf16[4,8,4096]{2,1,0:T(8,128)(2,1)S(1)} %collective-permute-done.5.refs_5_), channel_id=1, source_target_pairs={{0,224},{32,0},{64,32},{96,64},{128,96},{160,128},{192,160},{224,1... | collective-permute-start | bytes 786440 | tf_op jit(solution)/shard_map/ppermute | solution.py:286
  57.5 6.4 %collective-permute-start.10 = (bf16[2,8,4096]{2,1,0:T(8,128)(2,1)S(1)}, bf16[2,8,4096]{2,1,0:T(8,128)(2,1)S(1)}, u32[]{:S(2)}, u32[]{:S(2)}) collective-permute-start(bf16[2,8,4096]{2,1,0:T(8,128)(2,1)S(1)} %slice.6), channel_id=1, source_target_pairs={{0,32},{32,64},{64,96},{96,128},{128,160},{160,192},{192,224},{224... | collective-permute-start | bytes 393224 | tf_op jit(solution)/shard_map/ppermute | solution.py:286
  57.8 6.1 %collective-permute-start.11 = (bf16[2,8,4096]{2,1,0:T(8,128)(2,1)S(1)}, bf16[2,8,4096]{2,1,0:T(8,128)(2,1)S(1)}, u32[]{:S(2)}, u32[]{:S(2)}) collective-permute-start(bf16[2,8,4096]{2,1,0:T(8,128)(2,1)S(1)} %slice.7), channel_id=1, source_target_pairs={{0,224},{32,0},{64,32},{96,64},{128,96},{160,128},{192,160},{224,1... | collective-permute-start | bytes 393224 | tf_op jit(solution)/shard_map/ppermute | solution.py:286
  66.7 14.5 %collective-permute-start.14 = (f16[9,64,256]{2,1,0:T(8,128)(2,1)S(1)}, f16[9,64,256]{2,1,0:T(8,128)(2,1)S(1)}, u32[]{:S(2)}, u32[]{:S(2)}) collective-permute-start(f16[9,64,256]{2,1,0:T(8,128)(2,1)S(1)} %convert_element_type.20), channel_id=1, source_target_pairs={{0,8},{8,0},{16,24},{24,16},{1,9},{9,1},{17,25},{25,17},{2,10},{10... | collective-permute-start | bytes 884744 | tf_op jit(solution)/shard_map/ppermute | solution.py:294
  68.8 12.3 %collective-permute-start.13 = (f16[9,64,256]{2,1,0:T(8,128)(2,1)S(1)}, f16[9,64,256]{2,1,0:T(8,128)(2,1)S(1)}, u32[]{:S(2)}, u32[]{:S(2)}) collective-permute-start(f16[9,64,256]{2,1,0:T(8,128)(2,1)S(1)} %convert_element_type.18), channel_id=1, source_target_pairs={{0,12},{4,8},{8,4},{12,0},{16,28},{20,24},{24,20},{28,16},{1,13},{... | collective-permute-start | bytes 884744 | tf_op jit(solution)/shard_map/ppermute | solution.py:298
  74.2 10.9 %collective-permute-start.15 = (f16[9,64,256]{2,1,0:T(8,128)(2,1)S(1)}, f16[9,64,256]{2,1,0:T(8,128)(2,1)S(1)}, u32[]{:S(2)}, u32[]{:S(2)}) collective-permute-start(f16[9,64,256]{2,1,0:T(8,128)(2,1)S(1)} %convert_element_type.22), channel_id=1, source_target_pairs={{0,4},{4,0},{1,5},{5,1},{2,6},{6,2},{3,7},{7,3},{8,12},{12,8},{9,1... | collective-permute-start | bytes 884744 | tf_op jit(solution)/shard_map/ppermute | solution.py:290

commit v6 on v5

--- a/solution.py
+++ b/solution.py
@@ -240,7 +240,7 @@
     )(lagged, energy, columns, scale)
 
 
-def join_kernel(place, own, got_xy, got_x, got_y, out, buffer, sems):
+def join_kernel(place, own, got_x, got_xy, got_y, out, buffer, sems):
     low = place[4] == 0
     lags, rows = buffer.shape[:2]
     lane = lax.broadcasted_iota(jnp.int32, (rows, 128), 1) < 64
@@ -298,12 +298,14 @@
     return lax.ppermute(value, ("x", "yh"), [(i, i ^ 3) for i in range(8)])
 
 
-def spread(value):
+def spread(value, across):
     pairs = []
     for z in range(8):
-        for q in range(4):
-            pairs.append((z * 4 + q, (2 * q + (z & 1)) * 4 + (z >> 1)))
-    return lax.ppermute(value, ("z", "yl", "core"), pairs)
+        for x in range(4):
+            for q in range(4):
+                source = (z * 4 + x) * 4 + q
+                pairs.append((source, ((2 * q + (z & 1)) * 4 + (x ^ across)) * 4 + (z >> 1)))
+    return lax.ppermute(value, ("z", "x", "yl", "core"), pairs)
 
 
 def after(value, *others):
@@ -319,8 +321,7 @@
     taps = taps.reshape(1, -1)
     parts = lax.all_gather(raw, ("yl", "core"), axis=0, tiled=False)
     given = run_piece_filter(place, taps, parts)
-    unit = spread(given)
-    base = jnp.concatenate([unit, around(unit, "x", 2)], axis=0)
+    base = jnp.concatenate([spread(given, 0), spread(given, 2)], axis=0)
     order = (0, 1, 2, 3)
     units, steps = [base], [[(part, 0) for part in order]]
     first = (around(base, "z", 1), around(base, "z", -1))
@@ -338,14 +339,19 @@
         steps += [[(part, -step) for part in order], [(part, step) for part in order]]
     steps += [[(part, 4) for part in order[0:2]], [(part, 4) for part in order[2:4]]]
     far_xy = run_lags(after(row_xy, *third))
-    columns, scale = run_columns(place, units, steps)
-    got = []
-    for rows, move in ((far_xy, cross_xy), (far_x, cross_x), (far_y, cross_y)):
-        came = move(run_weigh(rows, columns, scale, SCALE).astype(SENT))
-        got.append(after(came, *got[-1:]).astype(jnp.float32))
+    columns, scale = run_columns(after(place, far_xy), units, steps)
+    send_xy = run_weigh(far_xy, columns, scale, SCALE).astype(SENT)
+    send_x = run_weigh(far_x, columns, after(scale, send_xy), SCALE).astype(SENT)
+    send_y = run_weigh(far_y, columns, scale, SCALE).astype(SENT)
+    came_xy = cross_xy(send_xy)
+    came_x = cross_x(send_x)
+    came_y = cross_y(send_y)
+    got_xy = came_xy.astype(jnp.float32)
+    got_x = after(came_x, got_xy).astype(jnp.float32)
+    got_y = after(came_y, got_x).astype(jnp.float32)
     own = run_lags(after(full, scale))
     kept = run_weigh(own, columns, scale, 1)
-    information = run_join(place, kept, *got)
+    information = run_join(place, kept, got_x, got_xy, got_y)
     return (information, mine)
 
 

time: 87.6 us -> 88.3 us (level)
  the two profiles are of different devices: /device:TPU:2 before, /device:TPU:96 now
where the time goes in v6:
time: 88.3 us; the launch traced here: 88.2 us
  starting transfers between devices  35.5 us (40%)
  waiting for transfers between devices  25.2 us (29%)
  Pallas kernels  18.1 us (20%)
  blocking collectives  7.47 us (8%)
  between operations  0.96 us (1%)
    ppermute x8, waiting for transfers between devices, around(): lax.ppermute(value, axis, [(i, (i + step) % size) for i in range(size)])  17.8 us
    ppermute x8, starting transfers between devices, around(): lax.ppermute(value, axis, [(i, (i + step) % size) for i in range(size)])  17.3 us
    all_gather x1, blocking collectives, shards(): parts = lax.all_gather(raw, ('yl', 'core'), axis=0, tiled=False)  7.47 us
    ppermute x2, starting transfers between devices, spread(): return lax.ppermute(value, ('z', 'x', 'yl', 'core'), pairs)  7.1 us
    pallas_call x4, Pallas kernels, run_weigh(): pl.pallas_call(body, in_specs=[vmem] * 4, out_specs=vmem, out_shape=jax.S...  5.74 us
    pallas_call x4, Pallas kernels, run_lags(): pl.pallas_call(lag_kernel, in_specs=[vmem], out_specs=[vmem, vmem], out_s...  5.06 us
    ppermute x3, starting transfers between devices, cross_x(): return lax.ppermute(value, 'x', [(0, 1), (1, 0), (2, 3), (3, 2)])  3.75 us
    ppermute x1, starting transfers between devices, cross_xy(): return lax.ppermute(value, ('x', 'yh'), [(i, i ^ 3) for i in range(8)])  3.71 us
  transfers between devices with their start and end apart: 16, of which 12 were waited for; matrix products, arithmetic and copies ran while one was open for 0% of the time, Pallas kernels for 14%

profile of v6, /device:TPU:96, one launch (start us, length us, event | category | flops | bytes accessed | tf_op | source)
XLA Modules:
  0.0 88.2 jit_solution(8047770765846145850)
XLA Ops:
  0.6 7.5 %all-gather = bf16[256,1024]{1,0:T(8,128)(2,1)S(1)} all-gather(bf16[64,1024]{1,0:T(8,128)(2,1)} %param.2), channel_id=2, replica_groups=mesh['z'=8,'x'=4,'yh'=2,'yl'=2,'core'=2] {'yl','core'}, dimensions={0}, use_global_device_ids=true | all-gather | bytes 655360 | tf_op jit(solution)/shard_map/all_gather | solution.py:322
  8.8 1.1 %pieces.1 = bf16[2,8,4096]{2,1,0:T(8,128)(2,1)S(1)} custom-call(s32[5]{0:T(128)S(1)} %stack.20.place.refs_0_, f32[1,65]{1,0:T(1,128)S(1)} %bitcast.8, bf16[4,64,1024]{2,1,0:T(8,128)(2,1)S(1)} %bitcast.6), custom_call_target="tpu_custom_call" | custom-call | tf_op jit(solution)/shard_map/pieces/pallas_call | solution.py:66
  10.0 1.9 %collective-permute-start.1 = (bf16[2,8,4096]{2,1,0:T(8,128)(2,1)S(1)}, bf16[2,8,4096]{2,1,0:T(8,128)(2,1)S(1)}, u32[]{:S(2)}, u32[]{:S(2)}) collective-permute-start(bf16[2,8,4096]{2,1,0:T(8,128)(2,1)S(1)} %pieces.1), channel_id=1, source_target_pairs={{0,0},{1,64},{2,128},{3,192},{8,8},{9,72},{10,136},{11,200},{16,16... | collective-permute-start | bytes 393224 | tf_op jit(solution)/shard_map/ppermute | solution.py:308
  11.9 5.2 %collective-permute-start.2 = (bf16[2,8,4096]{2,1,0:T(8,128)(2,1)S(1)}, bf16[2,8,4096]{2,1,0:T(8,128)(2,1)S(1)}, u32[]{:S(2)}, u32[]{:S(2)}) collective-permute-start(bf16[2,8,4096]{2,1,0:T(8,128)(2,1)S(1)} %pieces.1), channel_id=1, source_target_pairs={{0,16},{1,80},{2,144},{3,208},{8,24},{9,88},{10,152},{11,216},{16,... | collective-permute-start | bytes 393224 | tf_op jit(solution)/shard_map/ppermute | solution.py:308
  17.1 2.7 %rows.1 = (bf16[64,4096]{1,0:T(8,128)(2,1)S(1)}, bf16[64,1024]{1,0:T(8,128)(2,1)}) custom-call(s32[5]{0:T(128)S(1)} %stack.20.place.refs_0_, f32[1,65]{1,0:T(1,128)S(1)} %bitcast.9, bf16[4,64,1024]{2,1,0:T(8,128)(2,1)S(1)} %bitcast.7), custom_call_target="tpu_custom_call" | custom-call | flops 1073741824 | bytes 4194304 | tf_op jit(solution)/shard_map/rows/pallas_call | solution.py:103
  19.8 2.9 %collective-permute-start = (bf16[64,4096]{1,0:T(8,128)(2,1)S(1)}, bf16[64,4096]{1,0:T(8,128)(2,1)S(1)}, u32[]{:S(2)}, u32[]{:S(2)}) collective-permute-start(bf16[64,4096]{1,0:T(8,128)(2,1)S(1)} %get-tuple-element.44.rows_ref), channel_id=1, source_target_pairs={{0,4},{4,0},{1,5},{5,1},{2,6},{6,2},{3,7},{7,3},{8,12},{12,8},{9,1... | collective-permute-start | bytes 1572872 | tf_op jit(solution)/shard_map/ppermute | solution.py:290
  22.7 1.5 %collective-permute-done.2 = bf16[2,8,4096]{2,1,0:T(8,128)(2,1)S(1)} collective-permute-done((bf16[2,8,4096]{2,1,0:T(8,128)(2,1)S(1)}, bf16[2,8,4096]{2,1,0:T(8,128)(2,1)S(1)}, u32[]{:S(2)}, u32[]{:S(2)}) %collective-permute-start.2) | collective-permute-done | bytes 131104 | tf_op jit(solution)/shard_map/ppermute | solution.py:308
  24.3 5.9 %collective-permute-start.3 = (bf16[4,8,4096]{2,1,0:T(8,128)(2,1)S(1)}, bf16[4,8,4096]{2,1,0:T(8,128)(2,1)S(1)}, u32[]{:S(2)}, u32[]{:S(2)}) collective-permute-start(bf16[4,8,4096]{2,1,0:T(8,128)(2,1)S(1)} %constant_dynamic-update-slice_fusion.refs_1_), channel_id=1, source_target_pairs={{0,32},{32,64},{64,96},{96,128},{128,160},{160,192},{192,224},{224... | collective-permute-start | bytes 786440 | tf_op jit(solution)/shard_map/ppermute | solution.py:286
  30.8 5.2 %collective-permute-done.3.refs_2_ = bf16[4,8,4096]{2,1,0:T(8,128)(2,1)S(1)} collective-permute-done((bf16[4,8,4096]{2,1,0:T(8,128)(2,1)S(1)}, bf16[4,8,4096]{2,1,0:T(8,128)(2,1)S(1)}, u32[]{:S(2)}, u32[]{:S(2)}) %collective-permute-start.3) | collective-permute-done | bytes 262176 | tf_op jit(solution)/shard_map/ppermute | solution.py:286
  35.9 3.7 %collective-permute-start.6 = (bf16[4,8,4096]{2,1,0:T(8,128)(2,1)S(1)}, bf16[4,8,4096]{2,1,0:T(8,128)(2,1)S(1)}, u32[]{:S(2)}, u32[]{:S(2)}) collective-permute-start(bf16[4,8,4096]{2,1,0:T(8,128)(2,1)S(1)} %collective-permute-done.3.refs_2_), channel_id=1, source_target_pairs={{0,32},{32,64},{64,96},{96,128},{128,160},{160,192},{192,224},{224... | collective-permute-start | bytes 786440 | tf_op jit(solution)/shard_map/ppermute | solution.py:286
  40.1 2.3 %collective-permute-start.5 = (bf16[64,4096]{1,0:T(8,128)(2,1)S(1)}, bf16[64,4096]{1,0:T(8,128)(2,1)S(1)}, u32[]{:S(2)}, u32[]{:S(2)}) collective-permute-start(bf16[64,4096]{1,0:T(8,128)(2,1)S(1)} %collective-permute-done.rows_ref), channel_id=1, source_target_pairs={{0,8},{8,0},{16,24},{24,16},{1,9},{9,1},{17,25},{25,17},{2,10},{10... | collective-permute-start | bytes 1572872 | tf_op jit(solution)/shard_map/ppermute | solution.py:294
  42.4 1.3 %lags.4 = (bf16[9,64,4096]{2,1,0:T(8,128)(2,1)S(1)}, f32[64,128]{1,0:T(8,128)S(1)}) custom-call(bf16[64,4096]{1,0:T(8,128)(2,1)S(1)} %collective-permute-done.rows_ref), custom_call_target="tpu_custom_call" | custom-call | flops 10485760 | bytes 6291456 | tf_op jit(solution)/shard_map/lags/pallas_call | solution.py:144
  43.7 2.3 %collective-permute-done.6.refs_4_ = bf16[4,8,4096]{2,1,0:T(8,128)(2,1)S(1)} collective-permute-done((bf16[4,8,4096]{2,1,0:T(8,128)(2,1)S(1)}, bf16[4,8,4096]{2,1,0:T(8,128)(2,1)S(1)}, u32[]{:S(2)}, u32[]{:S(2)}) %collective-permute-start.6) | collective-permute-done | bytes 262176 | tf_op jit(solution)/shard_map/ppermute | solution.py:286
  46.0 3.7 %collective-permute-start.7 = (bf16[4,8,4096]{2,1,0:T(8,128)(2,1)S(1)}, bf16[4,8,4096]{2,1,0:T(8,128)(2,1)S(1)}, u32[]{:S(2)}, u32[]{:S(2)}) collective-permute-start(bf16[4,8,4096]{2,1,0:T(8,128)(2,1)S(1)} %collective-permute-done.6.refs_4_), channel_id=1, source_target_pairs={{0,32},{32,64},{64,96},{96,128},{128,160},{160,192},{192,224},{224... | collective-permute-start | bytes 786440 | tf_op jit(solution)/shard_map/ppermute | solution.py:286
  49.7 1.1 %collective-permute-done.8.refs_5_ = bf16[4,8,4096]{2,1,0:T(8,128)(2,1)S(1)} collective-permute-done((bf16[4,8,4096]{2,1,0:T(8,128)(2,1)S(1)}, bf16[4,8,4096]{2,1,0:T(8,128)(2,1)S(1)}, u32[]{:S(2)}, u32[]{:S(2)}) %collective-permute-start.8) | collective-permute-done | bytes 262176 | tf_op jit(solution)/shard_map/ppermute | solution.py:286
  50.8 1.3 %lags.6 = (bf16[9,64,4096]{2,1,0:T(8,128)(2,1)S(1)}, f32[64,128]{1,0:T(8,128)S(1)}) custom-call(bf16[64,4096]{1,0:T(8,128)(2,1)S(1)} %collective-permute-done.10.rows_ref), custom_call_target="tpu_custom_call" | custom-call | flops 10485760 | bytes 6291456 | tf_op jit(solution)/shard_map/lags/pallas_call | solution.py:144
  52.1 3.5 %collective-permute-done.7.refs_6_ = bf16[4,8,4096]{2,1,0:T(8,128)(2,1)S(1)} collective-permute-done((bf16[4,8,4096]{2,1,0:T(8,128)(2,1)S(1)}, bf16[4,8,4096]{2,1,0:T(8,128)(2,1)S(1)}, u32[]{:S(2)}, u32[]{:S(2)}) %collective-permute-start.7) | collective-permute-done | bytes 262176 | tf_op jit(solution)/shard_map/ppermute | solution.py:286
  55.6 4.0 %collective-permute-start.11 = (bf16[2,8,4096]{2,1,0:T(8,128)(2,1)S(1)}, bf16[2,8,4096]{2,1,0:T(8,128)(2,1)S(1)}, u32[]{:S(2)}, u32[]{:S(2)}) collective-permute-start(bf16[2,8,4096]{2,1,0:T(8,128)(2,1)S(1)} %slice.6), channel_id=1, source_target_pairs={{0,32},{32,64},{64,96},{96,128},{128,160},{160,192},{192,224},{224... | collective-permute-start | bytes 393224 | tf_op jit(solution)/shard_map/ppermute | solution.py:286
  60.0 1.3 %lags.5 = (bf16[9,64,4096]{2,1,0:T(8,128)(2,1)S(1)}, f32[64,128]{1,0:T(8,128)S(1)}) custom-call(bf16[64,4096]{1,0:T(8,128)(2,1)S(1)} %collective-permute-done.5.rows_ref), custom_call_target="tpu_custom_call" | custom-call | flops 10485760 | bytes 6291456 | tf_op jit(solution)/shard_map/lags/pallas_call | solution.py:144
  62.0 4.1 %collective-permute-done.12.refs_9_ = bf16[2,8,4096]{2,1,0:T(8,128)(2,1)S(1)} collective-permute-done((bf16[2,8,4096]{2,1,0:T(8,128)(2,1)S(1)}, bf16[2,8,4096]{2,1,0:T(8,128)(2,1)S(1)}, u32[]{:S(2)}, u32[]{:S(2)}) %collective-permute-start.12) | collective-permute-done | bytes 131104 | tf_op jit(solution)/shard_map/ppermute | solution.py:286
  66.1 1.3 %columns.1 = (bf16[32,8,4096]{2,1,0:T(8,128)(2,1)S(1)}, f32[8,256]{1,0:T(8,128)S(1)}) custom-call(s32[5]{0:T(128)S(1)} %stack.20.place.refs_0_, bf16[4,8,4096]{2,1,0:T(8,128)(2,1)S(1)} %constant_dynamic-update-slice_fusion.refs_1_, bf16[4,8,4096]{2,1,0:T(8,128)(2,1)S(1)} %collective-permute-done.3.refs_2_, ...), custom_call_target="tpu_custom_call" | custom-call | flops 8388608 | bytes 4194304 | tf_op jit(solution)/shard_map/columns/pallas_call | solution.py:193
  67.4 1.4 %weigh.5 = f32[9,64,256]{2,1,0:T(8,128)S(1)} custom-call(bf16[9,64,4096]{2,1,0:T(8,128)(2,1)S(1)} %get-tuple-element.35.refs_0_, f32[64,128]{1,0:T(8,128)S(1)} %get-tuple-element.36.refs_1_, bf16[32,8,4096]{2,1,0:T(8,128)(2,1)S(1)} %get-tuple-element.47.refs_2_, f32[8,256]{1,0:T(8,128)S(1)} %get-tuple-element.48.refs_3_), custom_call_target="tpu_custom_call" | custom-call | flops 1207959552 | bytes 589824 | tf_op jit(solution)/shard_map/weigh/pallas_call | solution.py:228
  68.9 3.7 %collective-permute-start.14 = (f16[9,64,256]{2,1,0:T(8,128)(2,1)S(1)}, f16[9,64,256]{2,1,0:T(8,128)(2,1)S(1)}, u32[]{:S(2)}, u32[]{:S(2)}) collective-permute-start(f16[9,64,256]{2,1,0:T(8,128)(2,1)S(1)} %convert_element_type.18), channel_id=1, source_target_pairs={{0,12},{4,8},{8,4},{12,0},{16,28},{20,24},{24,20},{28,16},{1,13},{... | collective-permute-start | bytes 884744 | tf_op jit(solution)/shard_map/ppermute | solution.py:298
  72.6 1.4 %weigh.6 = f32[9,64,256]{2,1,0:T(8,128)S(1)} custom-call(bf16[9,64,4096]{2,1,0:T(8,128)(2,1)S(1)} %get-tuple-element.39.refs_0_, f32[64,128]{1,0:T(8,128)S(1)} %get-tuple-element.40.refs_1_, bf16[32,8,4096]{2,1,0:T(8,128)(2,1)S(1)} %get-tuple-element.47.refs_2_, f32[8,256]{1,0:T(8,128)S(1)} %get-tuple-element.48.refs_3_), custom_call_target="tpu_custom_call" | custom-call | flops 1207959552 | bytes 589824 | tf_op jit(solution)/shard_map/weigh/pallas_call | solution.py:228
  74.1 0.8 collective-permute-start.13
  74.9 1.4 %weigh.7 = f32[9,64,256]{2,1,0:T(8,128)S(1)} custom-call(bf16[9,64,4096]{2,1,0:T(8,128)(2,1)S(1)} %get-tuple-element.30.refs_0_, f32[64,128]{1,0:T(8,128)S(1)} %get-tuple-element.31.refs_1_, bf16[32,8,4096]{2,1,0:T(8,128)(2,1)S(1)} %get-tuple-element.47.refs_2_, f32[8,256]{1,0:T(8,128)S(1)} %get-tuple-element.48.refs_3_), custom_call_target="tpu_custom_call" | custom-call | flops 1207959552 | bytes 589824 | tf_op jit(solution)/shard_map/weigh/pallas_call | solution.py:228
  77.1 1.3 %lags.7 = (bf16[9,64,4096]{2,1,0:T(8,128)(2,1)S(1)}, f32[64,128]{1,0:T(8,128)S(1)}) custom-call(bf16[64,4096]{1,0:T(8,128)(2,1)S(1)} %get-tuple-element.44.rows_ref), custom_call_target="tpu_custom_call" | custom-call | flops 10485760 | bytes 6291456 | tf_op jit(solution)/shard_map/lags/pallas_call | solution.py:144
  78.4 1.4 %weigh.4.own = f32[9,64,256]{2,1,0:T(8,128)S(1)} custom-call(bf16[9,64,4096]{2,1,0:T(8,128)(2,1)S(1)} %get-tuple-element.45.refs_0_, f32[64,128]{1,0:T(8,128)S(1)} %get-tuple-element.46.refs_1_, bf16[32,8,4096]{2,1,0:T(8,128)(2,1)S(1)} %get-tuple-element.47.refs_2_, f32[8,256]{1,0:T(8,128)S(1)} %get-tuple-element.48.refs_3_), custom_call_target="tpu_custom_call" | custom-call | flops 1207959552 | bytes 589824 | tf_op jit(solution)/shard_map/weigh/pallas_call | solution.py:228
  79.8 1.3 %collective-permute-done.14 = f16[9,64,256]{2,1,0:T(8,128)(2,1)S(1)} collective-permute-done((f16[9,64,256]{2,1,0:T(8,128)(2,1)S(1)}, f16[9,64,256]{2,1,0:T(8,128)(2,1)S(1)}, u32[]{:S(2)}, u32[]{:S(2)}) %collective-permute-start.14) | collective-permute-done | bytes 294944 | tf_op jit(solution)/shard_map/ppermute | solution.py:298
  81.2 3.0 %collective-permute-done.13 = f16[9,64,256]{2,1,0:T(8,128)(2,1)S(1)} collective-permute-done((f16[9,64,256]{2,1,0:T(8,128)(2,1)S(1)}, f16[9,64,256]{2,1,0:T(8,128)(2,1)S(1)}, u32[]{:S(2)}, u32[]{:S(2)}) %collective-permute-start.13) | collective-permute-done | bytes 294944 | tf_op jit(solution)/shard_map/ppermute | solution.py:294
  84.3 1.6 %collective-permute-done.15 = f16[9,64,256]{2,1,0:T(8,128)(2,1)S(1)} collective-permute-done((f16[9,64,256]{2,1,0:T(8,128)(2,1)S(1)}, f16[9,64,256]{2,1,0:T(8,128)(2,1)S(1)}, u32[]{:S(2)}, u32[]{:S(2)}) %collective-permute-start.15) | collective-permute-done | bytes 294944 | tf_op jit(solution)/shard_map/ppermute | solution.py:290
  85.9 2.2 %join.1 = f32[9,64,1024]{2,1,0:T(8,128)} custom-call(s32[5]{0:T(128)S(1)} %stack.20.place.refs_0_, f32[9,64,256]{2,1,0:T(8,128)S(1)} %weigh.4.own, f32[9,64,256]{2,1,0:T(8,128)S(1)} %convert_element_type.21.got_x, f32[9,64,256]{2,1,0:T(8,128)S(1)} %convert_element_type.20.got_xy, f32[9,64,256]{2,1,0:T(8,128)S(1)} %convert_element_type.23.got_y), custom_call_target="tpu_custom_call" | custom-call | tf_op jit(solution)/shard_map/join/pallas_call | solution.py:270
  (26 shorter events, 4.1 us)
Async XLA Ops:
  8.2 0.7 copy-start
  10.0 12.7 %collective-permute-start.1 = (bf16[2,8,4096]{2,1,0:T(8,128)(2,1)S(1)}, bf16[2,8,4096]{2,1,0:T(8,128)(2,1)S(1)}, u32[]{:S(2)}, u32[]{:S(2)}) collective-permute-start(bf16[2,8,4096]{2,1,0:T(8,128)(2,1)S(1)} %pieces.1), channel_id=1, source_target_pairs={{0,0},{1,64},{2,128},{3,192},{8,8},{9,72},{10,136},{11,200},{16,16... | collective-permute-start | bytes 393224 | tf_op jit(solution)/shard_map/ppermute | solution.py:308
  11.9 12.4 %collective-permute-start.2 = (bf16[2,8,4096]{2,1,0:T(8,128)(2,1)S(1)}, bf16[2,8,4096]{2,1,0:T(8,128)(2,1)S(1)}, u32[]{:S(2)}, u32[]{:S(2)}) collective-permute-start(bf16[2,8,4096]{2,1,0:T(8,128)(2,1)S(1)} %pieces.1), channel_id=1, source_target_pairs={{0,16},{1,80},{2,144},{3,208},{8,24},{9,88},{10,152},{11,216},{16,... | collective-permute-start | bytes 393224 | tf_op jit(solution)/shard_map/ppermute | solution.py:308
  19.8 20.3 %collective-permute-start = (bf16[64,4096]{1,0:T(8,128)(2,1)S(1)}, bf16[64,4096]{1,0:T(8,128)(2,1)S(1)}, u32[]{:S(2)}, u32[]{:S(2)}) collective-permute-start(bf16[64,4096]{1,0:T(8,128)(2,1)S(1)} %get-tuple-element.44.rows_ref), channel_id=1, source_target_pairs={{0,4},{4,0},{1,5},{5,1},{2,6},{6,2},{3,7},{7,3},{8,12},{12,8},{9,1... | collective-permute-start | bytes 1572872 | tf_op jit(solution)/shard_map/ppermute | solution.py:290
  24.3 11.6 %collective-permute-start.3 = (bf16[4,8,4096]{2,1,0:T(8,128)(2,1)S(1)}, bf16[4,8,4096]{2,1,0:T(8,128)(2,1)S(1)}, u32[]{:S(2)}, u32[]{:S(2)}) collective-permute-start(bf16[4,8,4096]{2,1,0:T(8,128)(2,1)S(1)} %constant_dynamic-update-slice_fusion.refs_1_), channel_id=1, source_target_pairs={{0,32},{32,64},{64,96},{96,128},{128,160},{160,192},{192,224},{224... | collective-permute-start | bytes 786440 | tf_op jit(solution)/shard_map/ppermute | solution.py:286
  30.2 9.9 %collective-permute-start.4 = (bf16[4,8,4096]{2,1,0:T(8,128)(2,1)S(1)}, bf16[4,8,4096]{2,1,0:T(8,128)(2,1)S(1)}, u32[]{:S(2)}, u32[]{:S(2)}) collective-permute-start(bf16[4,8,4096]{2,1,0:T(8,128)(2,1)S(1)} %constant_dynamic-update-slice_fusion.refs_1_), channel_id=1, source_target_pairs={{0,224},{32,0},{64,32},{96,64},{128,96},{160,128},{192,160},{224,1... | collective-permute-start | bytes 786440 | tf_op jit(solution)/shard_map/ppermute | solution.py:286
  30.2 20.7 %collective-permute-start.10 = (bf16[64,4096]{1,0:T(8,128)(2,1)S(1)}, bf16[64,4096]{1,0:T(8,128)(2,1)S(1)}, u32[]{:S(2)}, u32[]{:S(2)}) collective-permute-start(bf16[64,4096]{1,0:T(8,128)(2,1)S(1)} %get-tuple-element.44.rows_ref), channel_id=1, source_target_pairs={{0,8},{8,0},{16,24},{24,16},{1,9},{9,1},{17,25},{25,17},{2,10},{10... | collective-permute-start | bytes 1572872 | tf_op jit(solution)/shard_map/ppermute | solution.py:294
  35.9 10.1 %collective-permute-start.6 = (bf16[4,8,4096]{2,1,0:T(8,128)(2,1)S(1)}, bf16[4,8,4096]{2,1,0:T(8,128)(2,1)S(1)}, u32[]{:S(2)}, u32[]{:S(2)}) collective-permute-start(bf16[4,8,4096]{2,1,0:T(8,128)(2,1)S(1)} %collective-permute-done.3.refs_2_), channel_id=1, source_target_pairs={{0,32},{32,64},{64,96},{96,128},{128,160},{160,192},{192,224},{224... | collective-permute-start | bytes 786440 | tf_op jit(solution)/shard_map/ppermute | solution.py:286
  40.1 10.7 %collective-permute-start.8 = (bf16[4,8,4096]{2,1,0:T(8,128)(2,1)S(1)}, bf16[4,8,4096]{2,1,0:T(8,128)(2,1)S(1)}, u32[]{:S(2)}, u32[]{:S(2)}) collective-permute-start(bf16[4,8,4096]{2,1,0:T(8,128)(2,1)S(1)} %collective-permute-done.4.refs_3_), channel_id=1, source_target_pairs={{0,224},{32,0},{64,32},{96,64},{128,96},{160,128},{192,160},{224,1... | collective-permute-start | bytes 786440 | tf_op jit(solution)/shard_map/ppermute | solution.py:286
  40.1 19.9 %collective-permute-start.5 = (bf16[64,4096]{1,0:T(8,128)(2,1)S(1)}, bf16[64,4096]{1,0:T(8,128)(2,1)S(1)}, u32[]{:S(2)}, u32[]{:S(2)}) collective-permute-start(bf16[64,4096]{1,0:T(8,128)(2,1)S(1)} %collective-permute-done.rows_ref), channel_id=1, source_target_pairs={{0,8},{8,0},{16,24},{24,16},{1,9},{9,1},{17,25},{25,17},{2,10},{10... | collective-permute-start | bytes 1572872 | tf_op jit(solution)/shard_map/ppermute | solution.py:294
  46.0 9.5 %collective-permute-start.7 = (bf16[4,8,4096]{2,1,0:T(8,128)(2,1)S(1)}, bf16[4,8,4096]{2,1,0:T(8,128)(2,1)S(1)}, u32[]{:S(2)}, u32[]{:S(2)}) collective-permute-start(bf16[4,8,4096]{2,1,0:T(8,128)(2,1)S(1)} %collective-permute-done.6.refs_4_), channel_id=1, source_target_pairs={{0,32},{32,64},{64,96},{96,128},{128,160},{160,192},{192,224},{224... | collective-permute-start | bytes 786440 | tf_op jit(solution)/shard_map/ppermute | solution.py:286
  50.8 9.1 %collective-permute-start.9 = (bf16[4,8,4096]{2,1,0:T(8,128)(2,1)S(1)}, bf16[4,8,4096]{2,1,0:T(8,128)(2,1)S(1)}, u32[]{:S(2)}, u32[]{:S(2)}) collective-permute-start(bf16[4,8,4096]{2,1,0:T(8,128)(2,1)S(1)} %collective-permute-done.8.refs_5_), channel_id=1, source_target_pairs={{0,224},{32,0},{64,32},{96,64},{128,96},{160,128},{192,160},{224,1... | collective-permute-start | bytes 786440 | tf_op jit(solution)/shard_map/ppermute | solution.py:286
  55.6 6.5 %collective-permute-start.11 = (bf16[2,8,4096]{2,1,0:T(8,128)(2,1)S(1)}, bf16[2,8,4096]{2,1,0:T(8,128)(2,1)S(1)}, u32[]{:S(2)}, u32[]{:S(2)}) collective-permute-start(bf16[2,8,4096]{2,1,0:T(8,128)(2,1)S(1)} %slice.6), channel_id=1, source_target_pairs={{0,32},{32,64},{64,96},{96,128},{128,160},{160,192},{192,224},{224... | collective-permute-start | bytes 393224 | tf_op jit(solution)/shard_map/ppermute | solution.py:286
  59.9 6.3 %collective-permute-start.12 = (bf16[2,8,4096]{2,1,0:T(8,128)(2,1)S(1)}, bf16[2,8,4096]{2,1,0:T(8,128)(2,1)S(1)}, u32[]{:S(2)}, u32[]{:S(2)}) collective-permute-start(bf16[2,8,4096]{2,1,0:T(8,128)(2,1)S(1)} %slice.7), channel_id=1, source_target_pairs={{0,224},{32,0},{64,32},{96,64},{128,96},{160,128},{192,160},{224,1... | collective-permute-start | bytes 393224 | tf_op jit(solution)/shard_map/ppermute | solution.py:286
  68.9 12.3 %collective-permute-start.14 = (f16[9,64,256]{2,1,0:T(8,128)(2,1)S(1)}, f16[9,64,256]{2,1,0:T(8,128)(2,1)S(1)}, u32[]{:S(2)}, u32[]{:S(2)}) collective-permute-start(f16[9,64,256]{2,1,0:T(8,128)(2,1)S(1)} %convert_element_type.18), channel_id=1, source_target_pairs={{0,12},{4,8},{8,4},{12,0},{16,28},{20,24},{24,20},{28,16},{1,13},{... | collective-permute-start | bytes 884744 | tf_op jit(solution)/shard_map/ppermute | solution.py:298
  74.1 10.1 %collective-permute-start.13 = (f16[9,64,256]{2,1,0:T(8,128)(2,1)S(1)}, f16[9,64,256]{2,1,0:T(8,128)(2,1)S(1)}, u32[]{:S(2)}, u32[]{:S(2)}) collective-permute-start(f16[9,64,256]{2,1,0:T(8,128)(2,1)S(1)} %convert_element_type.19), channel_id=1, source_target_pairs={{0,8},{8,0},{16,24},{24,16},{1,9},{9,1},{17,25},{25,17},{2,10},{10... | collective-permute-start | bytes 884744 | tf_op jit(solution)/shard_map/ppermute | solution.py:294
  76.4 9.4 %collective-permute-start.15 = (f16[9,64,256]{2,1,0:T(8,128)(2,1)S(1)}, f16[9,64,256]{2,1,0:T(8,128)(2,1)S(1)}, u32[]{:S(2)}, u32[]{:S(2)}) collective-permute-start(f16[9,64,256]{2,1,0:T(8,128)(2,1)S(1)} %convert_element_type.22), channel_id=1, source_target_pairs={{0,4},{4,0},{1,5},{5,1},{2,6},{6,2},{3,7},{7,3},{8,12},{12,8},{9,1... | collective-permute-start | bytes 884744 | tf_op jit(solution)/shard_map/ppermute | solution.py:290

commit v7 on v6

--- a/solution.py
+++ b/solution.py
@@ -169,10 +169,13 @@
     units = refs[: len(steps)]
     columns, scale = refs[len(steps) :]
     z = place[1]
+    slab = place[2]
     for ref, moves in zip(units, steps):
         for k, (part, z_step) in enumerate(moves):
-            far = (z + z_step) & 7
-            columns[(far & 1) * 16 + (part >> 1) * 8 + (far >> 1) * 2 + (part & 1)] = ref[k]
+            up = (z + z_step - 2 * slab - 1) & 7
+            e = (up < 4).astype(jnp.int32)
+            giver = (3 - jnp.where(up < 4, up, 7 - up)) ^ slab
+            columns[e * 16 + (part >> 1) * 8 + giver * 2 + (part & 1)] = ref[k]
     width = columns.shape[0] * columns.shape[1]
     for g in range(width // 128):
         block = columns[g * 16 : (g + 1) * 16].astype(jnp.float32).reshape(128, -1)
@@ -301,10 +304,12 @@
 def spread(value, across):
     pairs = []
     for z in range(8):
+        a, e = z >> 1, z & 1
         for x in range(4):
             for q in range(4):
-                source = (z * 4 + x) * 4 + q
-                pairs.append((source, ((2 * q + (z & 1)) * 4 + (x ^ across)) * 4 + (z >> 1)))
+                far = 3 - (q ^ a)
+                to = (z + far if e else z - far) % 8
+                pairs.append(((z * 4 + x) * 4 + q, (to * 4 + (x ^ across)) * 4 + a))
     return lax.ppermute(value, ("z", "x", "yl", "core"), pairs)
 
 

time: 88.3 us -> 83 us (0.940)
  the two profiles are of different devices: /device:TPU:96 before, /device:TPU:2 now
where the time goes in v7:
time: 83 us; the launch traced here: 82.9 us
  starting transfers between devices  34.3 us (41%)
  waiting for transfers between devices  21.1 us (25%)
  Pallas kernels  18 us (22%)
  blocking collectives  7.47 us (9%)
  between operations  0.99 us (1%)
    ppermute x8, waiting for transfers between devices, around(): lax.ppermute(value, axis, [(i, (i + step) % size) for i in range(size)])  15.1 us
    ppermute x8, starting transfers between devices, around(): lax.ppermute(value, axis, [(i, (i + step) % size) for i in range(size)])  13.2 us
    ppermute x2, starting transfers between devices, spread(): return lax.ppermute(value, ('z', 'x', 'yl', 'core'), pairs)  9.94 us
    all_gather x1, blocking collectives, shards(): parts = lax.all_gather(raw, ('yl', 'core'), axis=0, tiled=False)  7.47 us
    pallas_call x4, Pallas kernels, run_weigh(): pl.pallas_call(body, in_specs=[vmem] * 4, out_specs=vmem, out_shape=jax.S...  5.74 us
    pallas_call x4, Pallas kernels, run_lags(): pl.pallas_call(lag_kernel, in_specs=[vmem], out_specs=[vmem, vmem], out_s...  5.05 us
    ppermute x2, starting transfers between devices, cross_y(): return lax.ppermute(value, 'yh', [(0, 1), (1, 0)])  3.86 us
    ppermute x1, starting transfers between devices, cross_xy(): return lax.ppermute(value, ('x', 'yh'), [(i, i ^ 3) for i in range(8)])  3.68 us
  transfers between devices with their start and end apart: 16, of which 7 were waited for; matrix products, arithmetic and copies ran while one was open for 0% of the time, Pallas kernels for 15%

profile of v7, /device:TPU:2, one launch (start us, length us, event | category | flops | bytes accessed | tf_op | source)
XLA Modules:
  0.0 82.9 jit_solution(8378400454990019066)
XLA Ops:
  0.6 7.5 %all-gather = bf16[256,1024]{1,0:T(8,128)(2,1)S(1)} all-gather(bf16[64,1024]{1,0:T(8,128)(2,1)} %param.2), channel_id=2, replica_groups=mesh['z'=8,'x'=4,'yh'=2,'yl'=2,'core'=2] {'yl','core'}, dimensions={0}, use_global_device_ids=true | all-gather | bytes 655360 | tf_op jit(solution)/shard_map/all_gather | solution.py:327
  8.8 1.1 %pieces.1 = bf16[2,8,4096]{2,1,0:T(8,128)(2,1)S(1)} custom-call(s32[5]{0:T(128)S(1)} %stack.20.place.refs_0_, f32[1,65]{1,0:T(1,128)S(1)} %bitcast.8, bf16[4,64,1024]{2,1,0:T(8,128)(2,1)S(1)} %bitcast.6), custom_call_target="tpu_custom_call" | custom-call | tf_op jit(solution)/shard_map/pieces/pallas_call | solution.py:66
  10.0 6.8 %collective-permute-start.1 = (bf16[2,8,4096]{2,1,0:T(8,128)(2,1)S(1)}, bf16[2,8,4096]{2,1,0:T(8,128)(2,1)S(1)}, u32[]{:S(2)}, u32[]{:S(2)}) collective-permute-start(bf16[2,8,4096]{2,1,0:T(8,128)(2,1)S(1)} %pieces.1), channel_id=1, source_target_pairs={{0,160},{1,192},{2,224},{3,0},{8,168},{9,200},{10,232},{11,8},{16,... | collective-permute-start | bytes 393224 | tf_op jit(solution)/shard_map/ppermute | solution.py:313
  16.8 3.1 %collective-permute-start.2 = (bf16[2,8,4096]{2,1,0:T(8,128)(2,1)S(1)}, bf16[2,8,4096]{2,1,0:T(8,128)(2,1)S(1)}, u32[]{:S(2)}, u32[]{:S(2)}) collective-permute-start(bf16[2,8,4096]{2,1,0:T(8,128)(2,1)S(1)} %pieces.1), channel_id=1, source_target_pairs={{0,176},{1,208},{2,240},{3,16},{8,184},{9,216},{10,248},{11,24},{1... | collective-permute-start | bytes 393224 | tf_op jit(solution)/shard_map/ppermute | solution.py:313
  19.9 2.7 %rows.1 = (bf16[64,4096]{1,0:T(8,128)(2,1)S(1)}, bf16[64,1024]{1,0:T(8,128)(2,1)}) custom-call(s32[5]{0:T(128)S(1)} %stack.20.place.refs_0_, f32[1,65]{1,0:T(1,128)S(1)} %bitcast.9, bf16[4,64,1024]{2,1,0:T(8,128)(2,1)S(1)} %bitcast.7), custom_call_target="tpu_custom_call" | custom-call | flops 1073741824 | bytes 4194304 | tf_op jit(solution)/shard_map/rows/pallas_call | solution.py:103
  22.6 2.9 %collective-permute-start = (bf16[64,4096]{1,0:T(8,128)(2,1)S(1)}, bf16[64,4096]{1,0:T(8,128)(2,1)S(1)}, u32[]{:S(2)}, u32[]{:S(2)}) collective-permute-start(bf16[64,4096]{1,0:T(8,128)(2,1)S(1)} %get-tuple-element.44.rows_ref), channel_id=1, source_target_pairs={{0,4},{4,0},{1,5},{5,1},{2,6},{6,2},{3,7},{7,3},{8,12},{12,8},{9,1... | collective-permute-start | bytes 1572872 | tf_op jit(solution)/shard_map/ppermute | solution.py:293
  25.8 3.1 %collective-permute-start.4 = (bf16[4,8,4096]{2,1,0:T(8,128)(2,1)S(1)}, bf16[4,8,4096]{2,1,0:T(8,128)(2,1)S(1)}, u32[]{:S(2)}, u32[]{:S(2)}) collective-permute-start(bf16[4,8,4096]{2,1,0:T(8,128)(2,1)S(1)} %constant_dynamic-update-slice_fusion.refs_1_), channel_id=1, source_target_pairs={{0,224},{32,0},{64,32},{96,64},{128,96},{160,128},{192,160},{224,1... | collective-permute-start | bytes 786440 | tf_op jit(solution)/shard_map/ppermute | solution.py:289
  28.9 1.4 %collective-permute-start.10 = (bf16[64,4096]{1,0:T(8,128)(2,1)S(1)}, bf16[64,4096]{1,0:T(8,128)(2,1)S(1)}, u32[]{:S(2)}, u32[]{:S(2)}) collective-permute-start(bf16[64,4096]{1,0:T(8,128)(2,1)S(1)} %get-tuple-element.44.rows_ref), channel_id=1, source_target_pairs={{0,8},{8,0},{16,24},{24,16},{1,9},{9,1},{17,25},{25,17},{2,10},{10... | collective-permute-start | bytes 1572872 | tf_op jit(solution)/shard_map/ppermute | solution.py:297
  30.4 4.0 %collective-permute-done.3.refs_2_ = bf16[4,8,4096]{2,1,0:T(8,128)(2,1)S(1)} collective-permute-done((bf16[4,8,4096]{2,1,0:T(8,128)(2,1)S(1)}, bf16[4,8,4096]{2,1,0:T(8,128)(2,1)S(1)}, u32[]{:S(2)}, u32[]{:S(2)}) %collective-permute-start.3) | collective-permute-done | bytes 262176 | tf_op jit(solution)/shard_map/ppermute | solution.py:289
  34.4 3.2 %collective-permute-start.8 = (bf16[4,8,4096]{2,1,0:T(8,128)(2,1)S(1)}, bf16[4,8,4096]{2,1,0:T(8,128)(2,1)S(1)}, u32[]{:S(2)}, u32[]{:S(2)}) collective-permute-start(bf16[4,8,4096]{2,1,0:T(8,128)(2,1)S(1)} %collective-permute-done.4.refs_3_), channel_id=1, source_target_pairs={{0,224},{32,0},{64,32},{96,64},{128,96},{160,128},{192,160},{224,1... | collective-permute-start | bytes 786440 | tf_op jit(solution)/shard_map/ppermute | solution.py:289
  37.6 1.4 %collective-permute-start.5 = (bf16[64,4096]{1,0:T(8,128)(2,1)S(1)}, bf16[64,4096]{1,0:T(8,128)(2,1)S(1)}, u32[]{:S(2)}, u32[]{:S(2)}) collective-permute-start(bf16[64,4096]{1,0:T(8,128)(2,1)S(1)} %collective-permute-done.rows_ref), channel_id=1, source_target_pairs={{0,8},{8,0},{16,24},{24,16},{1,9},{9,1},{17,25},{25,17},{2,10},{10... | collective-permute-start | bytes 1572872 | tf_op jit(solution)/shard_map/ppermute | solution.py:297
  39.0 1.3 %lags.4 = (bf16[9,64,4096]{2,1,0:T(8,128)(2,1)S(1)}, f32[64,128]{1,0:T(8,128)S(1)}) custom-call(bf16[64,4096]{1,0:T(8,128)(2,1)S(1)} %collective-permute-done.rows_ref), custom_call_target="tpu_custom_call" | custom-call | flops 10485760 | bytes 6291456 | tf_op jit(solution)/shard_map/lags/pallas_call | solution.py:144
  40.2 4.4 %collective-permute-done.6.refs_4_ = bf16[4,8,4096]{2,1,0:T(8,128)(2,1)S(1)} collective-permute-done((bf16[4,8,4096]{2,1,0:T(8,128)(2,1)S(1)}, bf16[4,8,4096]{2,1,0:T(8,128)(2,1)S(1)}, u32[]{:S(2)}, u32[]{:S(2)}) %collective-permute-start.6) | collective-permute-done | bytes 262176 | tf_op jit(solution)/shard_map/ppermute | solution.py:289
  44.7 3.2 %collective-permute-start.9 = (bf16[4,8,4096]{2,1,0:T(8,128)(2,1)S(1)}, bf16[4,8,4096]{2,1,0:T(8,128)(2,1)S(1)}, u32[]{:S(2)}, u32[]{:S(2)}) collective-permute-start(bf16[4,8,4096]{2,1,0:T(8,128)(2,1)S(1)} %collective-permute-done.8.refs_5_), channel_id=1, source_target_pairs={{0,224},{32,0},{64,32},{96,64},{128,96},{160,128},{192,160},{224,1... | collective-permute-start | bytes 786440 | tf_op jit(solution)/shard_map/ppermute | solution.py:289
  47.9 1.3 %lags.6 = (bf16[9,64,4096]{2,1,0:T(8,128)(2,1)S(1)}, f32[64,128]{1,0:T(8,128)S(1)}) custom-call(bf16[64,4096]{1,0:T(8,128)(2,1)S(1)} %collective-permute-done.10.rows_ref), custom_call_target="tpu_custom_call" | custom-call | flops 10485760 | bytes 6291456 | tf_op jit(solution)/shard_map/lags/pallas_call | solution.py:144
  49.2 5.0 %collective-permute-done.7.refs_6_ = bf16[4,8,4096]{2,1,0:T(8,128)(2,1)S(1)} collective-permute-done((bf16[4,8,4096]{2,1,0:T(8,128)(2,1)S(1)}, bf16[4,8,4096]{2,1,0:T(8,128)(2,1)S(1)}, u32[]{:S(2)}, u32[]{:S(2)}) %collective-permute-start.7) | collective-permute-done | bytes 262176 | tf_op jit(solution)/shard_map/ppermute | solution.py:289
  54.3 3.3 %collective-permute-start.12 = (bf16[2,8,4096]{2,1,0:T(8,128)(2,1)S(1)}, bf16[2,8,4096]{2,1,0:T(8,128)(2,1)S(1)}, u32[]{:S(2)}, u32[]{:S(2)}) collective-permute-start(bf16[2,8,4096]{2,1,0:T(8,128)(2,1)S(1)} %slice.7), channel_id=1, source_target_pairs={{0,224},{32,0},{64,32},{96,64},{128,96},{160,128},{192,160},{224,1... | collective-permute-start | bytes 393224 | tf_op jit(solution)/shard_map/ppermute | solution.py:289
  57.6 1.3 %lags.5 = (bf16[9,64,4096]{2,1,0:T(8,128)(2,1)S(1)}, f32[64,128]{1,0:T(8,128)S(1)}) custom-call(bf16[64,4096]{1,0:T(8,128)(2,1)S(1)} %collective-permute-done.5.rows_ref), custom_call_target="tpu_custom_call" | custom-call | flops 10485760 | bytes 6291456 | tf_op jit(solution)/shard_map/lags/pallas_call | solution.py:144
  58.9 1.6 %collective-permute-done.11.refs_8_ = bf16[2,8,4096]{2,1,0:T(8,128)(2,1)S(1)} collective-permute-done((bf16[2,8,4096]{2,1,0:T(8,128)(2,1)S(1)}, bf16[2,8,4096]{2,1,0:T(8,128)(2,1)S(1)}, u32[]{:S(2)}, u32[]{:S(2)}) %collective-permute-start.11) | collective-permute-done | bytes 131104 | tf_op jit(solution)/shard_map/ppermute | solution.py:289
  60.5 1.2 %columns.1 = (bf16[32,8,4096]{2,1,0:T(8,128)(2,1)S(1)}, f32[8,256]{1,0:T(8,128)S(1)}) custom-call(s32[5]{0:T(128)S(1)} %stack.20.place.refs_0_, bf16[4,8,4096]{2,1,0:T(8,128)(2,1)S(1)} %constant_dynamic-update-slice_fusion.refs_1_, bf16[4,8,4096]{2,1,0:T(8,128)(2,1)S(1)} %collective-permute-done.3.refs_2_, ...), custom_call_target="tpu_custom_call" | custom-call | flops 8388608 | bytes 4194304 | tf_op jit(solution)/shard_map/columns/pallas_call | solution.py:196
  61.7 1.4 %weigh.5 = f32[9,64,256]{2,1,0:T(8,128)S(1)} custom-call(bf16[9,64,4096]{2,1,0:T(8,128)(2,1)S(1)} %get-tuple-element.35.refs_0_, f32[64,128]{1,0:T(8,128)S(1)} %get-tuple-element.36.refs_1_, bf16[32,8,4096]{2,1,0:T(8,128)(2,1)S(1)} %get-tuple-element.47.refs_2_, f32[8,256]{1,0:T(8,128)S(1)} %get-tuple-element.48.refs_3_), custom_call_target="tpu_custom_call" | custom-call | flops 1207959552 | bytes 589824 | tf_op jit(solution)/shard_map/weigh/pallas_call | solution.py:231
  63.2 3.7 %collective-permute-start.14 = (f16[9,64,256]{2,1,0:T(8,128)(2,1)S(1)}, f16[9,64,256]{2,1,0:T(8,128)(2,1)S(1)}, u32[]{:S(2)}, u32[]{:S(2)}) collective-permute-start(f16[9,64,256]{2,1,0:T(8,128)(2,1)S(1)} %convert_element_type.18), channel_id=1, source_target_pairs={{0,12},{4,8},{8,4},{12,0},{16,28},{20,24},{24,20},{28,16},{1,13},{... | collective-permute-start | bytes 884744 | tf_op jit(solution)/shard_map/ppermute | solution.py:301
  66.9 1.4 %weigh.6 = f32[9,64,256]{2,1,0:T(8,128)S(1)} custom-call(bf16[9,64,4096]{2,1,0:T(8,128)(2,1)S(1)} %get-tuple-element.39.refs_0_, f32[64,128]{1,0:T(8,128)S(1)} %get-tuple-element.40.refs_1_, bf16[32,8,4096]{2,1,0:T(8,128)(2,1)S(1)} %get-tuple-element.47.refs_2_, f32[8,256]{1,0:T(8,128)S(1)} %get-tuple-element.48.refs_3_), custom_call_target="tpu_custom_call" | custom-call | flops 1207959552 | bytes 589824 | tf_op jit(solution)/shard_map/weigh/pallas_call | solution.py:231
  68.4 0.8 %collective-permute-start.13 = (f16[9,64,256]{2,1,0:T(8,128)(2,1)S(1)}, f16[9,64,256]{2,1,0:T(8,128)(2,1)S(1)}, u32[]{:S(2)}, u32[]{:S(2)}) collective-permute-start(f16[9,64,256]{2,1,0:T(8,128)(2,1)S(1)} %convert_element_type.19), channel_id=1, source_target_pairs={{0,8},{8,0},{16,24},{24,16},{1,9},{9,1},{17,25},{25,17},{2,10},{10... | collective-permute-start | bytes 884744 | tf_op jit(solution)/shard_map/ppermute | solution.py:297
  69.2 1.4 %weigh.7 = f32[9,64,256]{2,1,0:T(8,128)S(1)} custom-call(bf16[9,64,4096]{2,1,0:T(8,128)(2,1)S(1)} %get-tuple-element.30.refs_0_, f32[64,128]{1,0:T(8,128)S(1)} %get-tuple-element.31.refs_1_, bf16[32,8,4096]{2,1,0:T(8,128)(2,1)S(1)} %get-tuple-element.47.refs_2_, f32[8,256]{1,0:T(8,128)S(1)} %get-tuple-element.48.refs_3_), custom_call_target="tpu_custom_call" | custom-call | flops 1207959552 | bytes 589824 | tf_op jit(solution)/shard_map/weigh/pallas_call | solution.py:231
  70.7 1.0 %collective-permute-start.15 = (f16[9,64,256]{2,1,0:T(8,128)(2,1)S(1)}, f16[9,64,256]{2,1,0:T(8,128)(2,1)S(1)}, u32[]{:S(2)}, u32[]{:S(2)}) collective-permute-start(f16[9,64,256]{2,1,0:T(8,128)(2,1)S(1)} %convert_element_type.22), channel_id=1, source_target_pairs={{0,4},{4,0},{1,5},{5,1},{2,6},{6,2},{3,7},{7,3},{8,12},{12,8},{9,1... | collective-permute-start | bytes 884744 | tf_op jit(solution)/shard_map/ppermute | solution.py:293
  71.7 1.3 %lags.7 = (bf16[9,64,4096]{2,1,0:T(8,128)(2,1)S(1)}, f32[64,128]{1,0:T(8,128)S(1)}) custom-call(bf16[64,4096]{1,0:T(8,128)(2,1)S(1)} %get-tuple-element.44.rows_ref), custom_call_target="tpu_custom_call" | custom-call | flops 10485760 | bytes 6291456 | tf_op jit(solution)/shard_map/lags/pallas_call | solution.py:144
  72.9 1.4 %weigh.4.own = f32[9,64,256]{2,1,0:T(8,128)S(1)} custom-call(bf16[9,64,4096]{2,1,0:T(8,128)(2,1)S(1)} %get-tuple-element.45.refs_0_, f32[64,128]{1,0:T(8,128)S(1)} %get-tuple-element.46.refs_1_, bf16[32,8,4096]{2,1,0:T(8,128)(2,1)S(1)} %get-tuple-element.47.refs_2_, f32[8,256]{1,0:T(8,128)S(1)} %get-tuple-element.48.refs_3_), custom_call_target="tpu_custom_call" | custom-call | flops 1207959552 | bytes 589824 | tf_op jit(solution)/shard_map/weigh/pallas_call | solution.py:231
  74.4 1.3 %collective-permute-done.14 = f16[9,64,256]{2,1,0:T(8,128)(2,1)S(1)} collective-permute-done((f16[9,64,256]{2,1,0:T(8,128)(2,1)S(1)}, f16[9,64,256]{2,1,0:T(8,128)(2,1)S(1)}, u32[]{:S(2)}, u32[]{:S(2)}) %collective-permute-start.14) | collective-permute-done | bytes 294944 | tf_op jit(solution)/shard_map/ppermute | solution.py:301
  75.7 3.3 %collective-permute-done.13 = f16[9,64,256]{2,1,0:T(8,128)(2,1)S(1)} collective-permute-done((f16[9,64,256]{2,1,0:T(8,128)(2,1)S(1)}, f16[9,64,256]{2,1,0:T(8,128)(2,1)S(1)}, u32[]{:S(2)}, u32[]{:S(2)}) %collective-permute-start.13) | collective-permute-done | bytes 294944 | tf_op jit(solution)/shard_map/ppermute | solution.py:297
  79.0 1.5 %collective-permute-done.15 = f16[9,64,256]{2,1,0:T(8,128)(2,1)S(1)} collective-permute-done((f16[9,64,256]{2,1,0:T(8,128)(2,1)S(1)}, f16[9,64,256]{2,1,0:T(8,128)(2,1)S(1)}, u32[]{:S(2)}, u32[]{:S(2)}) %collective-permute-start.15) | collective-permute-done | bytes 294944 | tf_op jit(solution)/shard_map/ppermute | solution.py:293
  80.5 2.2 %join.1 = f32[9,64,1024]{2,1,0:T(8,128)} custom-call(s32[5]{0:T(128)S(1)} %stack.20.place.refs_0_, f32[9,64,256]{2,1,0:T(8,128)S(1)} %weigh.4.own, f32[9,64,256]{2,1,0:T(8,128)S(1)} %convert_element_type.21.got_x, f32[9,64,256]{2,1,0:T(8,128)S(1)} %convert_element_type.20.got_xy, f32[9,64,256]{2,1,0:T(8,128)S(1)} %convert_element_type.23.got_y), custom_call_target="tpu_custom_call" | custom-call | tf_op jit(solution)/shard_map/join/pallas_call | solution.py:273
  (26 shorter events, 1.4 us)
Async XLA Ops:
  8.2 0.7 copy-start
  10.0 15.6 %collective-permute-start.1 = (bf16[2,8,4096]{2,1,0:T(8,128)(2,1)S(1)}, bf16[2,8,4096]{2,1,0:T(8,128)(2,1)S(1)}, u32[]{:S(2)}, u32[]{:S(2)}) collective-permute-start(bf16[2,8,4096]{2,1,0:T(8,128)(2,1)S(1)} %pieces.1), channel_id=1, source_target_pairs={{0,160},{1,192},{2,224},{3,0},{8,168},{9,200},{10,232},{11,8},{16,... | collective-permute-start | bytes 393224 | tf_op jit(solution)/shard_map/ppermute | solution.py:313
  16.8 8.8 %collective-permute-start.2 = (bf16[2,8,4096]{2,1,0:T(8,128)(2,1)S(1)}, bf16[2,8,4096]{2,1,0:T(8,128)(2,1)S(1)}, u32[]{:S(2)}, u32[]{:S(2)}) collective-permute-start(bf16[2,8,4096]{2,1,0:T(8,128)(2,1)S(1)} %pieces.1), channel_id=1, source_target_pairs={{0,176},{1,208},{2,240},{3,16},{8,184},{9,216},{10,248},{11,24},{1... | collective-permute-start | bytes 393224 | tf_op jit(solution)/shard_map/ppermute | solution.py:313
  22.6 15.0 %collective-permute-start = (bf16[64,4096]{1,0:T(8,128)(2,1)S(1)}, bf16[64,4096]{1,0:T(8,128)(2,1)S(1)}, u32[]{:S(2)}, u32[]{:S(2)}) collective-permute-start(bf16[64,4096]{1,0:T(8,128)(2,1)S(1)} %get-tuple-element.44.rows_ref), channel_id=1, source_target_pairs={{0,4},{4,0},{1,5},{5,1},{2,6},{6,2},{3,7},{7,3},{8,12},{12,8},{9,1... | collective-permute-start | bytes 1572872 | tf_op jit(solution)/shard_map/ppermute | solution.py:293
  25.6 8.8 %collective-permute-start.3 = (bf16[4,8,4096]{2,1,0:T(8,128)(2,1)S(1)}, bf16[4,8,4096]{2,1,0:T(8,128)(2,1)S(1)}, u32[]{:S(2)}, u32[]{:S(2)}) collective-permute-start(bf16[4,8,4096]{2,1,0:T(8,128)(2,1)S(1)} %constant_dynamic-update-slice_fusion.refs_1_), channel_id=1, source_target_pairs={{0,32},{32,64},{64,96},{96,128},{128,160},{160,192},{192,224},{224... | collective-permute-start | bytes 786440 | tf_op jit(solution)/shard_map/ppermute | solution.py:289
  25.8 8.6 %collective-permute-start.4 = (bf16[4,8,4096]{2,1,0:T(8,128)(2,1)S(1)}, bf16[4,8,4096]{2,1,0:T(8,128)(2,1)S(1)}, u32[]{:S(2)}, u32[]{:S(2)}) collective-permute-start(bf16[4,8,4096]{2,1,0:T(8,128)(2,1)S(1)} %constant_dynamic-update-slice_fusion.refs_1_), channel_id=1, source_target_pairs={{0,224},{32,0},{64,32},{96,64},{128,96},{160,128},{192,160},{224,1... | collective-permute-start | bytes 786440 | tf_op jit(solution)/shard_map/ppermute | solution.py:289
  28.9 19.0 %collective-permute-start.10 = (bf16[64,4096]{1,0:T(8,128)(2,1)S(1)}, bf16[64,4096]{1,0:T(8,128)(2,1)S(1)}, u32[]{:S(2)}, u32[]{:S(2)}) collective-permute-start(bf16[64,4096]{1,0:T(8,128)(2,1)S(1)} %get-tuple-element.44.rows_ref), channel_id=1, source_target_pairs={{0,8},{8,0},{16,24},{24,16},{1,9},{9,1},{17,25},{25,17},{2,10},{10... | collective-permute-start | bytes 1572872 | tf_op jit(solution)/shard_map/ppermute | solution.py:297
  34.4 10.3 %collective-permute-start.6 = (bf16[4,8,4096]{2,1,0:T(8,128)(2,1)S(1)}, bf16[4,8,4096]{2,1,0:T(8,128)(2,1)S(1)}, u32[]{:S(2)}, u32[]{:S(2)}) collective-permute-start(bf16[4,8,4096]{2,1,0:T(8,128)(2,1)S(1)} %collective-permute-done.3.refs_2_), channel_id=1, source_target_pairs={{0,32},{32,64},{64,96},{96,128},{128,160},{160,192},{192,224},{224... | collective-permute-start | bytes 786440 | tf_op jit(solution)/shard_map/ppermute | solution.py:289
  34.4 10.3 %collective-permute-start.8 = (bf16[4,8,4096]{2,1,0:T(8,128)(2,1)S(1)}, bf16[4,8,4096]{2,1,0:T(8,128)(2,1)S(1)}, u32[]{:S(2)}, u32[]{:S(2)}) collective-permute-start(bf16[4,8,4096]{2,1,0:T(8,128)(2,1)S(1)} %collective-permute-done.4.refs_3_), channel_id=1, source_target_pairs={{0,224},{32,0},{64,32},{96,64},{128,96},{160,128},{192,160},{224,1... | collective-permute-start | bytes 786440 | tf_op jit(solution)/shard_map/ppermute | solution.py:289
  37.6 20.0 %collective-permute-start.5 = (bf16[64,4096]{1,0:T(8,128)(2,1)S(1)}, bf16[64,4096]{1,0:T(8,128)(2,1)S(1)}, u32[]{:S(2)}, u32[]{:S(2)}) collective-permute-start(bf16[64,4096]{1,0:T(8,128)(2,1)S(1)} %collective-permute-done.rows_ref), channel_id=1, source_target_pairs={{0,8},{8,0},{16,24},{24,16},{1,9},{9,1},{17,25},{25,17},{2,10},{10... | collective-permute-start | bytes 1572872 | tf_op jit(solution)/shard_map/ppermute | solution.py:297
  44.7 9.5 %collective-permute-start.7 = (bf16[4,8,4096]{2,1,0:T(8,128)(2,1)S(1)}, bf16[4,8,4096]{2,1,0:T(8,128)(2,1)S(1)}, u32[]{:S(2)}, u32[]{:S(2)}) collective-permute-start(bf16[4,8,4096]{2,1,0:T(8,128)(2,1)S(1)} %collective-permute-done.6.refs_4_), channel_id=1, source_target_pairs={{0,32},{32,64},{64,96},{96,128},{128,160},{160,192},{192,224},{224... | collective-permute-start | bytes 786440 | tf_op jit(solution)/shard_map/ppermute | solution.py:289
  44.7 9.6 %collective-permute-start.9 = (bf16[4,8,4096]{2,1,0:T(8,128)(2,1)S(1)}, bf16[4,8,4096]{2,1,0:T(8,128)(2,1)S(1)}, u32[]{:S(2)}, u32[]{:S(2)}) collective-permute-start(bf16[4,8,4096]{2,1,0:T(8,128)(2,1)S(1)} %collective-permute-done.8.refs_5_), channel_id=1, source_target_pairs={{0,224},{32,0},{64,32},{96,64},{128,96},{160,128},{192,160},{224,1... | collective-permute-start | bytes 786440 | tf_op jit(solution)/shard_map/ppermute | solution.py:289
  54.2 6.3 %collective-permute-start.11 = (bf16[2,8,4096]{2,1,0:T(8,128)(2,1)S(1)}, bf16[2,8,4096]{2,1,0:T(8,128)(2,1)S(1)}, u32[]{:S(2)}, u32[]{:S(2)}) collective-permute-start(bf16[2,8,4096]{2,1,0:T(8,128)(2,1)S(1)} %slice.6), channel_id=1, source_target_pairs={{0,32},{32,64},{64,96},{96,128},{128,160},{160,192},{192,224},{224... | collective-permute-start | bytes 393224 | tf_op jit(solution)/shard_map/ppermute | solution.py:289
  54.3 6.1 %collective-permute-start.12 = (bf16[2,8,4096]{2,1,0:T(8,128)(2,1)S(1)}, bf16[2,8,4096]{2,1,0:T(8,128)(2,1)S(1)}, u32[]{:S(2)}, u32[]{:S(2)}) collective-permute-start(bf16[2,8,4096]{2,1,0:T(8,128)(2,1)S(1)} %slice.7), channel_id=1, source_target_pairs={{0,224},{32,0},{64,32},{96,64},{128,96},{160,128},{192,160},{224,1... | collective-permute-start | bytes 393224 | tf_op jit(solution)/shard_map/ppermute | solution.py:289
  63.2 12.4 %collective-permute-start.14 = (f16[9,64,256]{2,1,0:T(8,128)(2,1)S(1)}, f16[9,64,256]{2,1,0:T(8,128)(2,1)S(1)}, u32[]{:S(2)}, u32[]{:S(2)}) collective-permute-start(f16[9,64,256]{2,1,0:T(8,128)(2,1)S(1)} %convert_element_type.18), channel_id=1, source_target_pairs={{0,12},{4,8},{8,4},{12,0},{16,28},{20,24},{24,20},{28,16},{1,13},{... | collective-permute-start | bytes 884744 | tf_op jit(solution)/shard_map/ppermute | solution.py:301
  68.4 10.6 %collective-permute-start.13 = (f16[9,64,256]{2,1,0:T(8,128)(2,1)S(1)}, f16[9,64,256]{2,1,0:T(8,128)(2,1)S(1)}, u32[]{:S(2)}, u32[]{:S(2)}) collective-permute-start(f16[9,64,256]{2,1,0:T(8,128)(2,1)S(1)} %convert_element_type.19), channel_id=1, source_target_pairs={{0,8},{8,0},{16,24},{24,16},{1,9},{9,1},{17,25},{25,17},{2,10},{10... | collective-permute-start | bytes 884744 | tf_op jit(solution)/shard_map/ppermute | solution.py:297
  70.7 9.8 %collective-permute-start.15 = (f16[9,64,256]{2,1,0:T(8,128)(2,1)S(1)}, f16[9,64,256]{2,1,0:T(8,128)(2,1)S(1)}, u32[]{:S(2)}, u32[]{:S(2)}) collective-permute-start(f16[9,64,256]{2,1,0:T(8,128)(2,1)S(1)} %convert_element_type.22), channel_id=1, source_target_pairs={{0,4},{4,0},{1,5},{5,1},{2,6},{6,2},{3,7},{7,3},{8,12},{12,8},{9,1... | collective-permute-start | bytes 884744 | tf_op jit(solution)/shard_map/ppermute | solution.py:293

commit v8 on v7

--- a/solution.py
+++ b/solution.py
@@ -42,81 +42,84 @@
     return value.astype(jnp.bfloat16)
 
 
-def piece_filter_kernel(place, taps, parts, out, blocks, weights, line):
-    count, bins = parts.shape[0], parts.shape[2]
-    per = bins // 128
-    count = count * per
-    at = pl.multiple_of(place[2] * 16, 16)
-    blocks[0] = jnp.zeros((16, 128), jnp.bfloat16)
-    blocks[count + 1] = jnp.zeros((16, 128), jnp.bfloat16)
+def edges_kernel(raw, low, high, held):
+    low[...] = raw[:, :128]
+    high[...] = raw[:, raw.shape[1] - 128 :]
+    held[...] = raw[...]
+
+
+def run_edges(raw):
+    rows, bins = raw.shape
+    vmem = pl.BlockSpec(memory_space=pltpu.VMEM)
+    edge = jax.ShapeDtypeStruct((rows, 128), jnp.bfloat16)
+    return pl.pallas_call(
+        edges_kernel,
+        in_specs=[vmem],
+        out_specs=[vmem] * 3,
+        out_shape=[edge, edge, jax.ShapeDtypeStruct((rows, bins), jnp.bfloat16)],
+        compiler_params=pltpu.CompilerParams(vmem_limit_bytes=8 * MB),
+        name="edges",
+    )(raw)
+
+
+def run_band(taps):
+    vmem = pl.BlockSpec(memory_space=pltpu.VMEM)
+    return pl.pallas_call(
+        lambda taps, weights, line: band(taps, line, weights),
+        in_specs=[vmem],
+        out_specs=vmem,
+        out_shape=jax.ShapeDtypeStruct((384, 384), jnp.bfloat16),
+        scratch_shapes=[pltpu.VMEM((8, 384), jnp.float32)],
+        compiler_params=pltpu.CompilerParams(vmem_limit_bytes=8 * MB),
+        name="band",
+    )(taps)
+
+
+def filter_kernel(weights, left, raw, right, out, kept, blocks):
+    rows, bins = raw.shape
+    count = bins // 128
+    blocks[0] = left[...]
+    blocks[count + 1] = right[...]
     for n in range(count):
-        b = n % per
-        blocks[1 + n] = parts[n // per, pl.ds(at, 16), b * 128 : (b + 1) * 128]
-    band(taps, line, weights)
+        blocks[1 + n] = raw[:, n * 128 : (n + 1) * 128]
     value = filtered_blocks(lambda k: blocks[k : k + count], weights)
     for n in range(count):
-        for h in range(2):
-            lo = n * 16 + h * 8
-            out[h, :, n * 128 : (n + 1) * 128] = value[lo : lo + 8]
-
-
-def run_piece_filter(place, taps, parts):
-    count, _, bins = parts.shape
-    vmem = pl.BlockSpec(memory_space=pltpu.VMEM)
-    return pl.pallas_call(
-        piece_filter_kernel,
-        in_specs=[pl.BlockSpec(memory_space=pltpu.SMEM), vmem, vmem],
+        out[:, n * 128 : (n + 1) * 128] = value[n * rows : (n + 1) * rows]
+    kept[...] = out[...]
+
+
+def run_filter(weights, left, raw, right):
+    rows, bins = raw.shape
+    vmem = pl.BlockSpec(memory_space=pltpu.VMEM)
+    return pl.pallas_call(
+        filter_kernel,
+        in_specs=[vmem] * 4,
+        out_specs=[vmem, vmem],
+        out_shape=[jax.ShapeDtypeStruct((rows, bins), jnp.bfloat16)] * 2,
+        scratch_shapes=[pltpu.VMEM((bins // 128 + 2, rows, 128), jnp.bfloat16)],
+        compiler_params=pltpu.CompilerParams(vmem_limit_bytes=8 * MB),
+        name="fir",
+    )(weights, left, raw, right)
+
+
+def slab_kernel(place, *refs):
+    parts, out = refs[:-1], refs[-1]
+    bins = parts[0].shape[1]
+    for flip, part in enumerate(parts):
+        out[:, pl.ds(pl.multiple_of((place[2] ^ flip) * bins, 128), bins)] = part[...]
+
+
+def run_slab(place, parts):
+    rows, bins = parts[0].shape
+    vmem = pl.BlockSpec(memory_space=pltpu.VMEM)
+    return pl.pallas_call(
+        slab_kernel,
+        in_specs=[pl.BlockSpec(memory_space=pltpu.SMEM)] + [vmem] * len(parts),
         out_specs=vmem,
-        out_shape=jax.ShapeDtypeStruct((2, 8, count * bins), jnp.bfloat16),
-        scratch_shapes=[
-            pltpu.VMEM((count * bins // 128 + 2, 16, 128), jnp.bfloat16),
-            pltpu.VMEM((384, 384), jnp.bfloat16),
-            pltpu.VMEM((8, 384), jnp.float32),
-        ],
-        compiler_params=pltpu.CompilerParams(vmem_limit_bytes=8 * MB),
-        name="pieces",
-    )(place, taps, parts)
-
-
-def row_filter_kernel(place, taps, parts, out, mine, blocks, weights, line):
-    rows, bins = parts.shape[1:]
-    per = bins // 128
-    count = parts.shape[0] * per
-    blocks[0] = jnp.zeros((rows, 128), jnp.bfloat16)
-    blocks[count + 1] = jnp.zeros((rows, 128), jnp.bfloat16)
-    for n in range(count):
-        b = n % per
-        blocks[1 + n] = parts[n // per, :, b * 128 : (b + 1) * 128]
-    band(taps, line, weights)
-    group = 8
-    for g in range(0, count, group):
-        value = filtered_blocks(lambda k: blocks[g + k : g + k + group], weights)
-        for b in range(group):
-            n = g + b
-            out[:, n * 128 : (n + 1) * 128] = value[b * rows : (b + 1) * rows]
-    mine[...] = out[:, pl.ds(pl.multiple_of(place[2] * bins, 128), bins)]
-
-
-def run_row_filter(place, taps, parts):
-    count, rows, bins = parts.shape
-    vmem = pl.BlockSpec(memory_space=pltpu.VMEM)
-    return pl.pallas_call(
-        row_filter_kernel,
-        in_specs=[pl.BlockSpec(memory_space=pltpu.SMEM), vmem, vmem],
-        out_specs=[vmem, vmem],
-        out_shape=[
-            jax.ShapeDtypeStruct((rows, count * bins), jnp.bfloat16),
-            jax.ShapeDtypeStruct((rows, bins), jnp.bfloat16),
-        ],
-        scratch_shapes=[
-            pltpu.VMEM((count * bins // 128 + 2, rows, 128), jnp.bfloat16),
-            pltpu.VMEM((384, 384), jnp.bfloat16),
-            pltpu.VMEM((8, 384), jnp.float32),
-        ],
-        compiler_params=pltpu.CompilerParams(vmem_limit_bytes=8 * MB),
-        cost_estimate=pl.CostEstimate(flops=1 << 30, bytes_accessed=4 * MB, transcendentals=0),
-        name="rows",
-    )(place, taps, parts)
+        out_shape=jax.ShapeDtypeStruct((rows, len(parts) * bins), jnp.bfloat16),
+        compiler_params=pltpu.CompilerParams(vmem_limit_bytes=8 * MB),
+        name="slab",
+    )(place, *parts)
 
 
 def lag_kernel(rows_ref, out, energy):
@@ -170,24 +173,23 @@
     columns, scale = refs[len(steps) :]
     z = place[1]
     slab = place[2]
+    bins = units[0].shape[2]
     for ref, moves in zip(units, steps):
-        for k, (part, z_step) in enumerate(moves):
+        for k, (pair, z_step) in enumerate(moves):
             up = (z + z_step - 2 * slab - 1) & 7
             e = (up < 4).astype(jnp.int32)
             giver = (3 - jnp.where(up < 4, up, 7 - up)) ^ slab
-            columns[e * 16 + (part >> 1) * 8 + giver * 2 + (part & 1)] = ref[k]
-    width = columns.shape[0] * columns.shape[1]
-    for g in range(width // 128):
-        block = columns[g * 16 : (g + 1) * 16].astype(jnp.float32).reshape(128, -1)
+            columns[e * 2 + pair, :, pl.ds(pl.multiple_of(giver * bins, 128), bins)] = ref[k]
+    for e in range(2):
+        block = columns[2 * e : 2 * e + 2].astype(jnp.float32).reshape(128, -1)
         total = jnp.sum(block * block, axis=1, keepdims=True)
         root = 0.8 / jnp.sqrt(total + 1e-05)
         root = jnp.transpose(jnp.broadcast_to(root, (128, 128)))
-        scale[:, g * 128 : (g + 1) * 128] = root[0:8]
+        scale[:, e * 128 : (e + 1) * 128] = root[0:8]
 
 
 def run_columns(place, units, steps):
-    slots = sum(len(moves) for moves in steps)
-    bins = units[0].shape[2]
+    rows, bins = units[0].shape[1:]
 
     def body(*refs):
         columns_kernel(steps, *refs)
@@ -198,8 +200,8 @@
         in_specs=[pl.BlockSpec(memory_space=pltpu.SMEM)] + [vmem] * len(units),
         out_specs=[vmem, vmem],
         out_shape=[
-            jax.ShapeDtypeStruct((slots, 8, bins), jnp.bfloat16),
-            jax.ShapeDtypeStruct((8, slots * 8), jnp.float32),
+            jax.ShapeDtypeStruct((4, rows, 4 * bins), jnp.bfloat16),
+            jax.ShapeDtypeStruct((8, 4 * rows), jnp.float32),
         ],
         compiler_params=pltpu.CompilerParams(vmem_limit_bytes=8 * MB),
         cost_estimate=pl.CostEstimate(flops=8 * MB, bytes_accessed=4 * MB, transcendentals=0),
@@ -313,6 +315,10 @@
     return lax.ppermute(value, ("z", "x", "yl", "core"), pairs)
 
 
+def flipped(value, flip):
+    return lax.ppermute(value, ("yl", "core"), [(i, i ^ flip) for i in range(4)])
+
+
 def after(value, *others):
     return lax.optimization_barrier((value, *others))[0]
 
@@ -324,14 +330,15 @@
     q = lax.axis_index(("yl", "core"))
     place = jnp.stack([yh, z, q, x, yh]).astype(jnp.int32)
     taps = taps.reshape(1, -1)
-    parts = lax.all_gather(raw, ("yl", "core"), axis=0, tiled=False)
-    given = run_piece_filter(place, taps, parts)
-    base = jnp.concatenate([spread(given, 0), spread(given, 2)], axis=0)
-    order = (0, 1, 2, 3)
-    units, steps = [base], [[(part, 0) for part in order]]
+    low, high, held = run_edges(raw)
+    left = lax.ppermute(high, ("yl", "core"), [(i, i + 1) for i in range(3)])
+    right = lax.ppermute(low, ("yl", "core"), [(i + 1, i) for i in range(3)])
+    mine, kept_mine = run_filter(run_band(after(taps, low)), left, held, right)
+    base = jnp.stack([spread(mine, 0), spread(mine, 2)], axis=0)
+    units, steps = [base], [[(0, 0), (1, 0)]]
     first = (around(base, "z", 1), around(base, "z", -1))
     second = (around(first[0], "z", 1), around(first[1], "z", -1))
-    full, mine = run_row_filter(place, taps, after(parts, given))
+    full = run_slab(after(place, base), [mine] + [flipped(mine, flip) for flip in (1, 2, 3)])
     row_y = cross_y(full)
     row_x = cross_x(full)
     row_xy = cross_x(after(row_y, *first))
@@ -339,10 +346,10 @@
     third = (around(after(second[0], far_y), "z", 1), around(after(second[1], far_y), "z", -1))
     far_x = run_lags(after(row_x, *second))
     ready = after(third[0], far_x), after(third[1], far_x)
-    units += [*first, *second, *third, around(ready[0][0:2], "z", 1), around(ready[1][2:4], "z", -1)]
-    for step in (1, 2, 3):
-        steps += [[(part, -step) for part in order], [(part, step) for part in order]]
-    steps += [[(part, 4) for part in order[0:2]], [(part, 4) for part in order[2:4]]]
+    units += [*first, *second, *third, around(ready[0][0:1], "z", 1), around(ready[1][1:2], "z", -1)]
+    for step in (-1, 1, -2, 2, -3, 3):
+        steps.append([(0, step), (1, step)])
+    steps += [[(0, 4)], [(1, 4)]]
     far_xy = run_lags(after(row_xy, *third))
     columns, scale = run_columns(after(place, far_xy), units, steps)
     send_xy = run_weigh(far_xy, columns, scale, SCALE).astype(SENT)
@@ -357,7 +364,7 @@
     own = run_lags(after(full, scale))
     kept = run_weigh(own, columns, scale, 1)
     information = run_join(place, kept, got_x, got_xy, got_y)
-    return (information, mine)
+    return (information, kept_mine)
 
 
 def solution(mesh):

time: 83 us -> 85.2 us (1.027); the launches traced: 82.9 us -> 83.5 us
  blocking collectives: 7.47 us -> 0 us
  starting transfers between devices: 34.3 us -> 40.6 us
  waiting for transfers between devices: 21.1 us -> 23.9 us
  Pallas kernels: 18 us -> 16 us
  local copies, waits for them, and re-layouts: 0.78 us -> 1.65 us
    all_gather x1 -> x0, blocking collectives: 7.47 us -> none  [shards(): parts = lax.all_gather(raw, ('yl', 'core'), axis=0, tiled=False)]
    ppermute x0 -> x5, starting transfers between devices: none -> 4.89 us  [the longest x3 1.86 us: flipped(): lax.ppermute(value, ('yl', 'core'), [(i, i ^ flip) for i in range(4)])]
    ppermute x2, waiting for transfers between devices: 0.01 us -> 3.7 us  [spread(): return lax.ppermute(value, ('z', 'x', 'yl', 'core'), pairs)]
    ppermute x0 -> x5, waiting for transfers between devices: none -> 3.48 us  [the longest x1 2.33 us: shards(): right = lax.ppermute(low, ('yl', 'core'), [(i + 1, i) for i in range(3)])]
    ppermute x8, waiting for transfers between devices: 15.1 us -> 12.3 us  [around(): lax.ppermute(value, axis, [(i, (i + step) % size) for i in range(size)])]
    pallas_call x2 -> x4, Pallas kernels: 3.86 us -> 1.88 us  [the longest x1 1.16 us: run_filter(): pl.pallas_call(filter_kernel, in_specs=[vmem] * 4, out_specs=[vmem, vmem]...]
    ppermute x2, starting transfers between devices: 3.86 us -> 5.56 us  [cross_y(): return lax.ppermute(value, 'yh', [(0, 1), (1, 0)])]
    ppermute x3, waiting for transfers between devices: 3.29 us -> 1.85 us  [cross_x(): return lax.ppermute(value, 'x', [(0, 1), (1, 0), (2, 3), (3, 2)])]
  transfers between devices with their start and end apart: 16 -> 21, of which waited for: 7 -> 10; matrix products, arithmetic and copies ran while one was open for 0% -> 0% of each run, Pallas kernels for 15% -> 11%
where the time goes in v8:
time: 85.2 us; the launch traced here: 83.5 us
  starting transfers between devices  40.6 us (48%)
  waiting for transfers between devices  23.9 us (28%)
  Pallas kernels  16 us (19%)
  local copies, waits for them, and re-layouts  1.65 us (2%)
  between operations  1.03 us (1%)
    ppermute x8, starting transfers between devices, around(): lax.ppermute(value, axis, [(i, (i + step) % size) for i in range(size)])  13.1 us
    ppermute x8, waiting for transfers between devices, around(): lax.ppermute(value, axis, [(i, (i + step) % size) for i in range(size)])  12.3 us
    ppermute x2, starting transfers between devices, spread(): return lax.ppermute(value, ('z', 'x', 'yl', 'core'), pairs)  11.1 us
    pallas_call x4, Pallas kernels, run_weigh(): pl.pallas_call(body, in_specs=[vmem] * 4, out_specs=vmem, out_shape=jax.S...  5.74 us
    ppermute x2, starting transfers between devices, cross_y(): return lax.ppermute(value, 'yh', [(0, 1), (1, 0)])  5.56 us
    pallas_call x4, Pallas kernels, run_lags(): pl.pallas_call(lag_kernel, in_specs=[vmem], out_specs=[vmem, vmem], out_s...  5.05 us
    ppermute x2, waiting for transfers between devices, spread(): return lax.ppermute(value, ('z', 'x', 'yl', 'core'), pairs)  3.7 us
    ppermute x3, starting transfers between devices, cross_x(): return lax.ppermute(value, 'x', [(0, 1), (1, 0), (2, 3), (3, 2)])  3.13 us
  transfers between devices with their start and end apart: 21, of which 10 were waited for; matrix products, arithmetic and copies ran while one was open for 0% of the time, Pallas kernels for 11%

profile of v8, /device:TPU:2, one launch (start us, length us, event | category | flops | bytes accessed | tf_op | source)
XLA Modules:
  0.0 83.5 jit_solution(14367573986342226714)
XLA Ops:
  1.6 1.7 %collective-permute-start = (bf16[64,128]{1,0:T(8,128)(2,1)S(1)}, bf16[64,128]{1,0:T(8,128)(2,1)S(1)}, u32[]{:S(2)}, u32[]{:S(2)}) collective-permute-start(bf16[64,128]{1,0:T(8,128)(2,1)S(1)} %get-tuple-element.33), channel_id=1, source_target_pairs={{0,1},{1,2},{2,3},{4,5},{5,6},{6,7},{8,9},{9,10},{10,11},{12,13},{... | collective-permute-start | bytes 49160 | tf_op jit(solution)/shard_map/ppermute | solution.py:334
  3.3 1.3 %collective-permute-start.1 = (bf16[64,128]{1,0:T(8,128)(2,1)S(1)}, bf16[64,128]{1,0:T(8,128)(2,1)S(1)}, u32[]{:S(2)}, u32[]{:S(2)}) collective-permute-start(bf16[64,128]{1,0:T(8,128)(2,1)S(1)} %get-tuple-element.31), channel_id=1, source_target_pairs={{1,0},{2,1},{3,2},{5,4},{6,5},{7,6},{9,8},{10,9},{11,10},{13,12},{... | collective-permute-start | bytes 49160 | tf_op jit(solution)/shard_map/ppermute | solution.py:335
  5.4 2.3 %collective-permute-done.1.right = bf16[64,128]{1,0:T(8,128)(2,1)S(1)} collective-permute-done((bf16[64,128]{1,0:T(8,128)(2,1)S(1)}, bf16[64,128]{1,0:T(8,128)(2,1)S(1)}, u32[]{:S(2)}, u32[]{:S(2)}) %collective-permute-start.1) | collective-permute-done | bytes 16416 | tf_op jit(solution)/shard_map/ppermute | solution.py:335
  7.7 1.2 %fir.1 = (bf16[64,1024]{1,0:T(8,128)(2,1)S(1)}, bf16[64,1024]{1,0:T(8,128)(2,1)}) custom-call(bf16[384,384]{1,0:T(8,128)(2,1)S(1)} %band.1.weights, bf16[64,128]{1,0:T(8,128)(2,1)S(1)} %collective-permute-done.left, bf16[64,1024]{1,0:T(8,128)(2,1)S(1)} %get-tuple-element.34.raw, bf16[64,128]{1,0:T(8,128)(2,1)S(1)} %collective-permute-done.1.right), custom_call_target="tpu_custom_call" | custom-call | tf_op jit(solution)/shard_map/fir/pallas_call | solution.py:94
  8.9 8.3 %collective-permute-start.3 = (bf16[64,1024]{1,0:T(8,128)(2,1)S(1)}, bf16[64,1024]{1,0:T(8,128)(2,1)S(1)}, u32[]{:S(2)}, u32[]{:S(2)}) collective-permute-start(bf16[64,1024]{1,0:T(8,128)(2,1)S(1)} %get-tuple-element.35.refs_0_), channel_id=1, source_target_pairs={{0,176},{1,208},{2,240},{3,16},{8,184},{9,216},{10,248},{11,24},{1... | collective-permute-start | bytes 393224 | tf_op jit(solution)/shard_map/ppermute | solution.py:315
  17.2 2.8 %collective-permute-start.2 = (bf16[64,1024]{1,0:T(8,128)(2,1)S(1)}, bf16[64,1024]{1,0:T(8,128)(2,1)S(1)}, u32[]{:S(2)}, u32[]{:S(2)}) collective-permute-start(bf16[64,1024]{1,0:T(8,128)(2,1)S(1)} %get-tuple-element.35.refs_0_), channel_id=1, source_target_pairs={{0,160},{1,192},{2,224},{3,0},{8,168},{9,200},{10,232},{11,8},{16,... | collective-permute-start | bytes 393224 | tf_op jit(solution)/shard_map/ppermute | solution.py:315
  20.1 1.9 %collective-permute-start.4 = (bf16[64,1024]{1,0:T(8,128)(2,1)S(1)}, bf16[64,1024]{1,0:T(8,128)(2,1)S(1)}, u32[]{:S(2)}, u32[]{:S(2)}) collective-permute-start(bf16[64,1024]{1,0:T(8,128)(2,1)S(1)} %get-tuple-element.35.refs_0_), channel_id=1, source_target_pairs={{0,1},{1,0},{2,3},{3,2},{4,5},{5,4},{6,7},{7,6},{8,9},{9,8},{10,11... | collective-permute-start | bytes 393224 | tf_op jit(solution)/shard_map/ppermute | solution.py:319
  22.0 3.7 %collective-permute-done.2 = bf16[64,1024]{1,0:T(8,128)(2,1)S(1)} collective-permute-done((bf16[64,1024]{1,0:T(8,128)(2,1)S(1)}, bf16[64,1024]{1,0:T(8,128)(2,1)S(1)}, u32[]{:S(2)}, u32[]{:S(2)}) %collective-permute-start.2) | collective-permute-done | bytes 131104 | tf_op jit(solution)/shard_map/ppermute | solution.py:315
  27.5 3.0 %collective-permute-start.7 = (bf16[64,4096]{1,0:T(8,128)(2,1)S(1)}, bf16[64,4096]{1,0:T(8,128)(2,1)S(1)}, u32[]{:S(2)}, u32[]{:S(2)}) collective-permute-start(bf16[64,4096]{1,0:T(8,128)(2,1)S(1)} %slab.1.rows_ref), channel_id=1, source_target_pairs={{0,4},{4,0},{1,5},{5,1},{2,6},{6,2},{3,7},{7,3},{8,12},{12,8},{9,1... | collective-permute-start | bytes 1572872 | tf_op jit(solution)/shard_map/ppermute | solution.py:295
  30.5 2.1 %collective-permute-start.8 = (bf16[2,64,1024]{2,1,0:T(8,128)(2,1)S(1)}, bf16[2,64,1024]{2,1,0:T(8,128)(2,1)S(1)}, u32[]{:S(2)}, u32[]{:S(2)}) collective-permute-start(bf16[2,64,1024]{2,1,0:T(8,128)(2,1)S(1)} %pad_maximum_fusion.refs_1_), channel_id=1, source_target_pairs={{0,32},{32,64},{64,96},{96,128},{128,160},{160,192},{192,224},{224... | collective-permute-start | bytes 786440 | tf_op jit(solution)/shard_map/ppermute | solution.py:291
  34.6 5.1 %collective-permute-done.8.refs_2_ = bf16[2,64,1024]{2,1,0:T(8,128)(2,1)S(1)} collective-permute-done((bf16[2,64,1024]{2,1,0:T(8,128)(2,1)S(1)}, bf16[2,64,1024]{2,1,0:T(8,128)(2,1)S(1)}, u32[]{:S(2)}, u32[]{:S(2)}) %collective-permute-start.8) | collective-permute-done | bytes 262176 | tf_op jit(solution)/shard_map/ppermute | solution.py:291
  39.8 3.2 %collective-permute-start.13 = (bf16[2,64,1024]{2,1,0:T(8,128)(2,1)S(1)}, bf16[2,64,1024]{2,1,0:T(8,128)(2,1)S(1)}, u32[]{:S(2)}, u32[]{:S(2)}) collective-permute-start(bf16[2,64,1024]{2,1,0:T(8,128)(2,1)S(1)} %collective-permute-done.9.refs_3_), channel_id=1, source_target_pairs={{0,224},{32,0},{64,32},{96,64},{128,96},{160,128},{192,160},{224,1... | collective-permute-start | bytes 786440 | tf_op jit(solution)/shard_map/ppermute | solution.py:291
  43.1 1.4 %collective-permute-start.10 = (bf16[64,4096]{1,0:T(8,128)(2,1)S(1)}, bf16[64,4096]{1,0:T(8,128)(2,1)S(1)}, u32[]{:S(2)}, u32[]{:S(2)}) collective-permute-start(bf16[64,4096]{1,0:T(8,128)(2,1)S(1)} %collective-permute-done.7.rows_ref), channel_id=1, source_target_pairs={{0,8},{8,0},{16,24},{24,16},{1,9},{9,1},{17,25},{25,17},{2,10},{10... | collective-permute-start | bytes 1572872 | tf_op jit(solution)/shard_map/ppermute | solution.py:299
  44.5 1.3 %lags.4 = (bf16[9,64,4096]{2,1,0:T(8,128)(2,1)S(1)}, f32[64,128]{1,0:T(8,128)S(1)}) custom-call(bf16[64,4096]{1,0:T(8,128)(2,1)S(1)} %collective-permute-done.7.rows_ref), custom_call_target="tpu_custom_call" | custom-call | flops 10485760 | bytes 6291456 | tf_op jit(solution)/shard_map/lags/pallas_call | solution.py:147
  45.8 2.5 %collective-permute-done.11.refs_4_ = bf16[2,64,1024]{2,1,0:T(8,128)(2,1)S(1)} collective-permute-done((bf16[2,64,1024]{2,1,0:T(8,128)(2,1)S(1)}, bf16[2,64,1024]{2,1,0:T(8,128)(2,1)S(1)}, u32[]{:S(2)}, u32[]{:S(2)}) %collective-permute-start.11) | collective-permute-done | bytes 262176 | tf_op jit(solution)/shard_map/ppermute | solution.py:291
  48.3 3.2 %collective-permute-start.14 = (bf16[2,64,1024]{2,1,0:T(8,128)(2,1)S(1)}, bf16[2,64,1024]{2,1,0:T(8,128)(2,1)S(1)}, u32[]{:S(2)}, u32[]{:S(2)}) collective-permute-start(bf16[2,64,1024]{2,1,0:T(8,128)(2,1)S(1)} %collective-permute-done.13.refs_5_), channel_id=1, source_target_pairs={{0,224},{32,0},{64,32},{96,64},{128,96},{160,128},{192,160},{224,1... | collective-permute-start | bytes 786440 | tf_op jit(solution)/shard_map/ppermute | solution.py:291
  51.5 1.3 %lags.6 = (bf16[9,64,4096]{2,1,0:T(8,128)(2,1)S(1)}, f32[64,128]{1,0:T(8,128)S(1)}) custom-call(bf16[64,4096]{1,0:T(8,128)(2,1)S(1)} %collective-permute-done.15.rows_ref), custom_call_target="tpu_custom_call" | custom-call | flops 10485760 | bytes 6291456 | tf_op jit(solution)/shard_map/lags/pallas_call | solution.py:147
  52.8 3.1 %collective-permute-done.12.refs_6_ = bf16[2,64,1024]{2,1,0:T(8,128)(2,1)S(1)} collective-permute-done((bf16[2,64,1024]{2,1,0:T(8,128)(2,1)S(1)}, bf16[2,64,1024]{2,1,0:T(8,128)(2,1)S(1)}, u32[]{:S(2)}, u32[]{:S(2)}) %collective-permute-start.12) | collective-permute-done | bytes 262176 | tf_op jit(solution)/shard_map/ppermute | solution.py:291
  56.0 3.3 %collective-permute-start.17 = (bf16[1,64,1024]{2,1,0:T(8,128)(2,1)S(1)}, bf16[1,64,1024]{2,1,0:T(8,128)(2,1)S(1)}, u32[]{:S(2)}, u32[]{:S(2)}) collective-permute-start(bf16[1,64,1024]{2,1,0:T(8,128)(2,1)S(1)} %slice.7), channel_id=1, source_target_pairs={{0,224},{32,0},{64,32},{96,64},{128,96},{160,128},{192,160},{224,1... | collective-permute-start | bytes 393224 | tf_op jit(solution)/shard_map/ppermute | solution.py:291
  59.3 1.3 %lags.5 = (bf16[9,64,4096]{2,1,0:T(8,128)(2,1)S(1)}, f32[64,128]{1,0:T(8,128)S(1)}) custom-call(bf16[64,4096]{1,0:T(8,128)(2,1)S(1)} %collective-permute-done.10.rows_ref), custom_call_target="tpu_custom_call" | custom-call | flops 10485760 | bytes 6291456 | tf_op jit(solution)/shard_map/lags/pallas_call | solution.py:147
  60.5 1.6 %collective-permute-done.16.refs_8_ = bf16[1,64,1024]{2,1,0:T(8,128)(2,1)S(1)} collective-permute-done((bf16[1,64,1024]{2,1,0:T(8,128)(2,1)S(1)}, bf16[1,64,1024]{2,1,0:T(8,128)(2,1)S(1)}, u32[]{:S(2)}, u32[]{:S(2)}) %collective-permute-start.16) | collective-permute-done | bytes 131104 | tf_op jit(solution)/shard_map/ppermute | solution.py:291
  62.1 1.2 %columns.1 = (bf16[4,64,4096]{2,1,0:T(8,128)(2,1)S(1)}, f32[8,256]{1,0:T(8,128)S(1)}) custom-call(s32[5]{0:T(128)S(1)} %stack.29.place.refs_0_, bf16[2,64,1024]{2,1,0:T(8,128)(2,1)S(1)} %pad_maximum_fusion.refs_1_, bf16[2,64,1024]{2,1,0:T(8,128)(2,1)S(1)} %collective-permute-done.8.refs_2_, bf16[2,64,1024]{2,1,0:T(8,128)(2,1)S(1)} %collective-permute-done.9.refs_3_, ...), custom_call_target="tpu_custom_call" | custom-call | flops 8388608 | bytes 4194304 | tf_op jit(solution)/shard_map/columns/pallas_call | solution.py:198
  63.3 1.4 %weigh.5 = f32[9,64,256]{2,1,0:T(8,128)S(1)} custom-call(bf16[9,64,4096]{2,1,0:T(8,128)(2,1)S(1)} %get-tuple-element.43.refs_0_, f32[64,128]{1,0:T(8,128)S(1)} %get-tuple-element.44.refs_1_, bf16[4,64,4096]{2,1,0:T(8,128)(2,1)S(1)} %get-tuple-element.55.refs_2_, f32[8,256]{1,0:T(8,128)S(1)} %get-tuple-element.56.refs_3_), custom_call_target="tpu_custom_call" | custom-call | flops 1207959552 | bytes 589824 | tf_op jit(solution)/shard_map/weigh/pallas_call | solution.py:233
  64.8 2.8 %collective-permute-start.19 = (f16[9,64,256]{2,1,0:T(8,128)(2,1)S(1)}, f16[9,64,256]{2,1,0:T(8,128)(2,1)S(1)}, u32[]{:S(2)}, u32[]{:S(2)}) collective-permute-start(f16[9,64,256]{2,1,0:T(8,128)(2,1)S(1)} %convert_element_type.18), channel_id=1, source_target_pairs={{0,12},{4,8},{8,4},{12,0},{16,28},{20,24},{24,20},{28,16},{1,13},{... | collective-permute-start | bytes 884744 | tf_op jit(solution)/shard_map/ppermute | solution.py:303
  67.6 1.4 %weigh.6 = f32[9,64,256]{2,1,0:T(8,128)S(1)} custom-call(bf16[9,64,4096]{2,1,0:T(8,128)(2,1)S(1)} %get-tuple-element.47.refs_0_, f32[64,128]{1,0:T(8,128)S(1)} %get-tuple-element.48.refs_1_, bf16[4,64,4096]{2,1,0:T(8,128)(2,1)S(1)} %get-tuple-element.55.refs_2_, f32[8,256]{1,0:T(8,128)S(1)} %get-tuple-element.56.refs_3_), custom_call_target="tpu_custom_call" | custom-call | flops 1207959552 | bytes 589824 | tf_op jit(solution)/shard_map/weigh/pallas_call | solution.py:233
  69.9 1.4 %weigh.7 = f32[9,64,256]{2,1,0:T(8,128)S(1)} custom-call(bf16[9,64,4096]{2,1,0:T(8,128)(2,1)S(1)} %get-tuple-element.38.refs_0_, f32[64,128]{1,0:T(8,128)S(1)} %get-tuple-element.39.refs_1_, bf16[4,64,4096]{2,1,0:T(8,128)(2,1)S(1)} %get-tuple-element.55.refs_2_, f32[8,256]{1,0:T(8,128)S(1)} %get-tuple-element.56.refs_3_), custom_call_target="tpu_custom_call" | custom-call | flops 1207959552 | bytes 589824 | tf_op jit(solution)/shard_map/weigh/pallas_call | solution.py:233
  71.4 2.6 %collective-permute-start.20 = (f16[9,64,256]{2,1,0:T(8,128)(2,1)S(1)}, f16[9,64,256]{2,1,0:T(8,128)(2,1)S(1)}, u32[]{:S(2)}, u32[]{:S(2)}) collective-permute-start(f16[9,64,256]{2,1,0:T(8,128)(2,1)S(1)} %convert_element_type.22), channel_id=1, source_target_pairs={{0,4},{4,0},{1,5},{5,1},{2,6},{6,2},{3,7},{7,3},{8,12},{12,8},{9,1... | collective-permute-start | bytes 884744 | tf_op jit(solution)/shard_map/ppermute | solution.py:295
  73.9 1.3 %lags.7 = (bf16[9,64,4096]{2,1,0:T(8,128)(2,1)S(1)}, f32[64,128]{1,0:T(8,128)S(1)}) custom-call(bf16[64,4096]{1,0:T(8,128)(2,1)S(1)} %slab.1.rows_ref), custom_call_target="tpu_custom_call" | custom-call | flops 10485760 | bytes 6291456 | tf_op jit(solution)/shard_map/lags/pallas_call | solution.py:147
  75.2 1.4 %weigh.4.own = f32[9,64,256]{2,1,0:T(8,128)S(1)} custom-call(bf16[9,64,4096]{2,1,0:T(8,128)(2,1)S(1)} %get-tuple-element.53.refs_0_, f32[64,128]{1,0:T(8,128)S(1)} %get-tuple-element.54.refs_1_, bf16[4,64,4096]{2,1,0:T(8,128)(2,1)S(1)} %get-tuple-element.55.refs_2_, f32[8,256]{1,0:T(8,128)S(1)} %get-tuple-element.56.refs_3_), custom_call_target="tpu_custom_call" | custom-call | flops 1207959552 | bytes 589824 | tf_op jit(solution)/shard_map/weigh/pallas_call | solution.py:233
  77.0 1.8 %collective-permute-done.18 = f16[9,64,256]{2,1,0:T(8,128)(2,1)S(1)} collective-permute-done((f16[9,64,256]{2,1,0:T(8,128)(2,1)S(1)}, f16[9,64,256]{2,1,0:T(8,128)(2,1)S(1)}, u32[]{:S(2)}, u32[]{:S(2)}) %collective-permute-start.18) | collective-permute-done | bytes 294944 | tf_op jit(solution)/shard_map/ppermute | solution.py:299
  78.9 2.3 %collective-permute-done.20 = f16[9,64,256]{2,1,0:T(8,128)(2,1)S(1)} collective-permute-done((f16[9,64,256]{2,1,0:T(8,128)(2,1)S(1)}, f16[9,64,256]{2,1,0:T(8,128)(2,1)S(1)}, u32[]{:S(2)}, u32[]{:S(2)}) %collective-permute-start.20) | collective-permute-done | bytes 294944 | tf_op jit(solution)/shard_map/ppermute | solution.py:295
  81.2 2.2 %join.1 = f32[9,64,1024]{2,1,0:T(8,128)} custom-call(s32[5]{0:T(128)S(1)} %stack.29.place.refs_0_, f32[9,64,256]{2,1,0:T(8,128)S(1)} %weigh.4.own, f32[9,64,256]{2,1,0:T(8,128)S(1)} %convert_element_type.21.got_x, f32[9,64,256]{2,1,0:T(8,128)S(1)} %convert_element_type.20.got_xy, f32[9,64,256]{2,1,0:T(8,128)S(1)} %convert_element_type.23.got_y), custom_call_target="tpu_custom_call" | custom-call | tf_op jit(solution)/shard_map/join/pallas_call | solution.py:275
  (38 shorter events, 7.1 us)
Async XLA Ops:
  0.6 0.9 %copy-start = (bf16[64,1024]{1,0:T(8,128)(2,1)S(1)}, bf16[64,1024]{1,0:T(8,128)(2,1)}, u32[]{:S(2)}) copy-start(bf16[64,1024]{1,0:T(8,128)(2,1)} %raw.1) | copy-start | bytes 393220
  1.6 3.8 %collective-permute-start = (bf16[64,128]{1,0:T(8,128)(2,1)S(1)}, bf16[64,128]{1,0:T(8,128)(2,1)S(1)}, u32[]{:S(2)}, u32[]{:S(2)}) collective-permute-start(bf16[64,128]{1,0:T(8,128)(2,1)S(1)} %get-tuple-element.33), channel_id=1, source_target_pairs={{0,1},{1,2},{2,3},{4,5},{5,6},{6,7},{8,9},{9,10},{10,11},{12,13},{... | collective-permute-start | bytes 49160 | tf_op jit(solution)/shard_map/ppermute | solution.py:334
  3.3 4.4 %collective-permute-start.1 = (bf16[64,128]{1,0:T(8,128)(2,1)S(1)}, bf16[64,128]{1,0:T(8,128)(2,1)S(1)}, u32[]{:S(2)}, u32[]{:S(2)}) collective-permute-start(bf16[64,128]{1,0:T(8,128)(2,1)S(1)} %get-tuple-element.31), channel_id=1, source_target_pairs={{1,0},{2,1},{3,2},{5,4},{6,5},{7,6},{9,8},{10,9},{11,10},{13,12},{... | collective-permute-start | bytes 49160 | tf_op jit(solution)/shard_map/ppermute | solution.py:335
  4.6 0.7 copy-start.1
  8.9 13.1 %collective-permute-start.3 = (bf16[64,1024]{1,0:T(8,128)(2,1)S(1)}, bf16[64,1024]{1,0:T(8,128)(2,1)S(1)}, u32[]{:S(2)}, u32[]{:S(2)}) collective-permute-start(bf16[64,1024]{1,0:T(8,128)(2,1)S(1)} %get-tuple-element.35.refs_0_), channel_id=1, source_target_pairs={{0,176},{1,208},{2,240},{3,16},{8,184},{9,216},{10,248},{11,24},{1... | collective-permute-start | bytes 393224 | tf_op jit(solution)/shard_map/ppermute | solution.py:315
  17.2 8.5 %collective-permute-start.2 = (bf16[64,1024]{1,0:T(8,128)(2,1)S(1)}, bf16[64,1024]{1,0:T(8,128)(2,1)S(1)}, u32[]{:S(2)}, u32[]{:S(2)}) collective-permute-start(bf16[64,1024]{1,0:T(8,128)(2,1)S(1)} %get-tuple-element.35.refs_0_), channel_id=1, source_target_pairs={{0,160},{1,192},{2,224},{3,0},{8,168},{9,200},{10,232},{11,8},{16,... | collective-permute-start | bytes 393224 | tf_op jit(solution)/shard_map/ppermute | solution.py:315
  20.0 5.7 %collective-permute-start.6 = (bf16[64,1024]{1,0:T(8,128)(2,1)S(1)}, bf16[64,1024]{1,0:T(8,128)(2,1)S(1)}, u32[]{:S(2)}, u32[]{:S(2)}) collective-permute-start(bf16[64,1024]{1,0:T(8,128)(2,1)S(1)} %get-tuple-element.35.refs_0_), channel_id=1, source_target_pairs={{0,3},{1,2},{2,1},{3,0},{4,7},{5,6},{6,5},{7,4},{8,11},{9,10},{10,... | collective-permute-start | bytes 393224 | tf_op jit(solution)/shard_map/ppermute | solution.py:319
  20.0 6.8 %collective-permute-start.5 = (bf16[64,1024]{1,0:T(8,128)(2,1)S(1)}, bf16[64,1024]{1,0:T(8,128)(2,1)S(1)}, u32[]{:S(2)}, u32[]{:S(2)}) collective-permute-start(bf16[64,1024]{1,0:T(8,128)(2,1)S(1)} %get-tuple-element.35.refs_0_), channel_id=1, source_target_pairs={{0,2},{1,3},{2,0},{3,1},{4,6},{5,7},{6,4},{7,5},{8,10},{9,11},{10,... | collective-permute-start | bytes 393224 | tf_op jit(solution)/shard_map/ppermute | solution.py:319
  20.1 6.8 %collective-permute-start.4 = (bf16[64,1024]{1,0:T(8,128)(2,1)S(1)}, bf16[64,1024]{1,0:T(8,128)(2,1)S(1)}, u32[]{:S(2)}, u32[]{:S(2)}) collective-permute-start(bf16[64,1024]{1,0:T(8,128)(2,1)S(1)} %get-tuple-element.35.refs_0_), channel_id=1, source_target_pairs={{0,1},{1,0},{2,3},{3,2},{4,5},{5,4},{6,7},{7,6},{8,9},{9,8},{10,11... | collective-permute-start | bytes 393224 | tf_op jit(solution)/shard_map/ppermute | solution.py:319
  27.5 15.6 %collective-permute-start.7 = (bf16[64,4096]{1,0:T(8,128)(2,1)S(1)}, bf16[64,4096]{1,0:T(8,128)(2,1)S(1)}, u32[]{:S(2)}, u32[]{:S(2)}) collective-permute-start(bf16[64,4096]{1,0:T(8,128)(2,1)S(1)} %slab.1.rows_ref), channel_id=1, source_target_pairs={{0,4},{4,0},{1,5},{5,1},{2,6},{6,2},{3,7},{7,3},{8,12},{12,8},{9,1... | collective-permute-start | bytes 1572872 | tf_op jit(solution)/shard_map/ppermute | solution.py:295
  30.5 9.3 %collective-permute-start.8 = (bf16[2,64,1024]{2,1,0:T(8,128)(2,1)S(1)}, bf16[2,64,1024]{2,1,0:T(8,128)(2,1)S(1)}, u32[]{:S(2)}, u32[]{:S(2)}) collective-permute-start(bf16[2,64,1024]{2,1,0:T(8,128)(2,1)S(1)} %pad_maximum_fusion.refs_1_), channel_id=1, source_target_pairs={{0,32},{32,64},{64,96},{96,128},{128,160},{160,192},{192,224},{224... | collective-permute-start | bytes 786440 | tf_op jit(solution)/shard_map/ppermute | solution.py:291
  32.6 7.2 %collective-permute-start.9 = (bf16[2,64,1024]{2,1,0:T(8,128)(2,1)S(1)}, bf16[2,64,1024]{2,1,0:T(8,128)(2,1)S(1)}, u32[]{:S(2)}, u32[]{:S(2)}) collective-permute-start(bf16[2,64,1024]{2,1,0:T(8,128)(2,1)S(1)} %pad_maximum_fusion.refs_1_), channel_id=1, source_target_pairs={{0,224},{32,0},{64,32},{96,64},{128,96},{160,128},{192,160},{224,1... | collective-permute-start | bytes 786440 | tf_op jit(solution)/shard_map/ppermute | solution.py:291
  33.7 17.8 %collective-permute-start.15 = (bf16[64,4096]{1,0:T(8,128)(2,1)S(1)}, bf16[64,4096]{1,0:T(8,128)(2,1)S(1)}, u32[]{:S(2)}, u32[]{:S(2)}) collective-permute-start(bf16[64,4096]{1,0:T(8,128)(2,1)S(1)} %slab.1.rows_ref), channel_id=1, source_target_pairs={{0,8},{8,0},{16,24},{24,16},{1,9},{9,1},{17,25},{25,17},{2,10},{10... | collective-permute-start | bytes 1572872 | tf_op jit(solution)/shard_map/ppermute | solution.py:299
  39.8 8.5 %collective-permute-start.11 = (bf16[2,64,1024]{2,1,0:T(8,128)(2,1)S(1)}, bf16[2,64,1024]{2,1,0:T(8,128)(2,1)S(1)}, u32[]{:S(2)}, u32[]{:S(2)}) collective-permute-start(bf16[2,64,1024]{2,1,0:T(8,128)(2,1)S(1)} %collective-permute-done.8.refs_2_), channel_id=1, source_target_pairs={{0,32},{32,64},{64,96},{96,128},{128,160},{160,192},{192,224},{224... | collective-permute-start | bytes 786440 | tf_op jit(solution)/shard_map/ppermute | solution.py:291
  39.8 8.5 %collective-permute-start.13 = (bf16[2,64,1024]{2,1,0:T(8,128)(2,1)S(1)}, bf16[2,64,1024]{2,1,0:T(8,128)(2,1)S(1)}, u32[]{:S(2)}, u32[]{:S(2)}) collective-permute-start(bf16[2,64,1024]{2,1,0:T(8,128)(2,1)S(1)} %collective-permute-done.9.refs_3_), channel_id=1, source_target_pairs={{0,224},{32,0},{64,32},{96,64},{128,96},{160,128},{192,160},{224,1... | collective-permute-start | bytes 786440 | tf_op jit(solution)/shard_map/ppermute | solution.py:291
  43.1 16.2 %collective-permute-start.10 = (bf16[64,4096]{1,0:T(8,128)(2,1)S(1)}, bf16[64,4096]{1,0:T(8,128)(2,1)S(1)}, u32[]{:S(2)}, u32[]{:S(2)}) collective-permute-start(bf16[64,4096]{1,0:T(8,128)(2,1)S(1)} %collective-permute-done.7.rows_ref), channel_id=1, source_target_pairs={{0,8},{8,0},{16,24},{24,16},{1,9},{9,1},{17,25},{25,17},{2,10},{10... | collective-permute-start | bytes 1572872 | tf_op jit(solution)/shard_map/ppermute | solution.py:299
  48.3 7.6 %collective-permute-start.12 = (bf16[2,64,1024]{2,1,0:T(8,128)(2,1)S(1)}, bf16[2,64,1024]{2,1,0:T(8,128)(2,1)S(1)}, u32[]{:S(2)}, u32[]{:S(2)}) collective-permute-start(bf16[2,64,1024]{2,1,0:T(8,128)(2,1)S(1)} %collective-permute-done.11.refs_4_), channel_id=1, source_target_pairs={{0,32},{32,64},{64,96},{96,128},{128,160},{160,192},{192,224},{224... | collective-permute-start | bytes 786440 | tf_op jit(solution)/shard_map/ppermute | solution.py:291
  48.3 7.7 %collective-permute-start.14 = (bf16[2,64,1024]{2,1,0:T(8,128)(2,1)S(1)}, bf16[2,64,1024]{2,1,0:T(8,128)(2,1)S(1)}, u32[]{:S(2)}, u32[]{:S(2)}) collective-permute-start(bf16[2,64,1024]{2,1,0:T(8,128)(2,1)S(1)} %collective-permute-done.13.refs_5_), channel_id=1, source_target_pairs={{0,224},{32,0},{64,32},{96,64},{128,96},{160,128},{192,160},{224,1... | collective-permute-start | bytes 786440 | tf_op jit(solution)/shard_map/ppermute | solution.py:291
  55.9 6.3 %collective-permute-start.16 = (bf16[1,64,1024]{2,1,0:T(8,128)(2,1)S(1)}, bf16[1,64,1024]{2,1,0:T(8,128)(2,1)S(1)}, u32[]{:S(2)}, u32[]{:S(2)}) collective-permute-start(bf16[1,64,1024]{2,1,0:T(8,128)(2,1)S(1)} %slice.6), channel_id=1, source_target_pairs={{0,32},{32,64},{64,96},{96,128},{128,160},{160,192},{192,224},{224... | collective-permute-start | bytes 393224 | tf_op jit(solution)/shard_map/ppermute | solution.py:291
  56.0 6.1 %collective-permute-start.17 = (bf16[1,64,1024]{2,1,0:T(8,128)(2,1)S(1)}, bf16[1,64,1024]{2,1,0:T(8,128)(2,1)S(1)}, u32[]{:S(2)}, u32[]{:S(2)}) collective-permute-start(bf16[1,64,1024]{2,1,0:T(8,128)(2,1)S(1)} %slice.7), channel_id=1, source_target_pairs={{0,224},{32,0},{64,32},{96,64},{128,96},{160,128},{192,160},{224,1... | collective-permute-start | bytes 393224 | tf_op jit(solution)/shard_map/ppermute | solution.py:291
  64.8 12.1 %collective-permute-start.19 = (f16[9,64,256]{2,1,0:T(8,128)(2,1)S(1)}, f16[9,64,256]{2,1,0:T(8,128)(2,1)S(1)}, u32[]{:S(2)}, u32[]{:S(2)}) collective-permute-start(f16[9,64,256]{2,1,0:T(8,128)(2,1)S(1)} %convert_element_type.18), channel_id=1, source_target_pairs={{0,12},{4,8},{8,4},{12,0},{16,28},{20,24},{24,20},{28,16},{1,13},{... | collective-permute-start | bytes 884744 | tf_op jit(solution)/shard_map/ppermute | solution.py:303
  69.1 9.7 %collective-permute-start.18 = (f16[9,64,256]{2,1,0:T(8,128)(2,1)S(1)}, f16[9,64,256]{2,1,0:T(8,128)(2,1)S(1)}, u32[]{:S(2)}, u32[]{:S(2)}) collective-permute-start(f16[9,64,256]{2,1,0:T(8,128)(2,1)S(1)} %convert_element_type.19), channel_id=1, source_target_pairs={{0,8},{8,0},{16,24},{24,16},{1,9},{9,1},{17,25},{25,17},{2,10},{10... | collective-permute-start | bytes 884744 | tf_op jit(solution)/shard_map/ppermute | solution.py:299
  71.4 9.8 %collective-permute-start.20 = (f16[9,64,256]{2,1,0:T(8,128)(2,1)S(1)}, f16[9,64,256]{2,1,0:T(8,128)(2,1)S(1)}, u32[]{:S(2)}, u32[]{:S(2)}) collective-permute-start(f16[9,64,256]{2,1,0:T(8,128)(2,1)S(1)} %convert_element_type.22), channel_id=1, source_target_pairs={{0,4},{4,0},{1,5},{5,1},{2,6},{6,2},{3,7},{7,3},{8,12},{12,8},{9,1... | collective-permute-start | bytes 884744 | tf_op jit(solution)/shard_map/ppermute | solution.py:295

commit v9 on v7

--- a/solution.py
+++ b/solution.py
@@ -243,45 +243,54 @@
     )(lagged, energy, columns, scale)
 
 
-def join_kernel(place, own, got_x, got_xy, got_y, out, buffer, sems):
+def join_kernel(flip, place, same, cross, *refs):
+    out, tiles, sems = refs[-3:]
     low = place[4] == 0
-    lags, rows = buffer.shape[:2]
+    here_x = place[3] ^ flip
+    lags, rows, width = same.shape
     lane = lax.broadcasted_iota(jnp.int32, (rows, 128), 1) < 64
     copies = []
-    for lag in range(lags):
-        for half in range(2):
-            span = slice(half * 128, (half + 1) * 128)
-            for flip, (same, cross) in enumerate(((own, got_y), (got_x, got_xy))):
-                here_x = place[3] ^ flip
-                here = same[lag, :, span] * (1.0 / SCALE) if flip else same[lag, :, span]
-                there = cross[lag, :, span] * (1.0 / SCALE)
-                one = jnp.where(low, here, there)
-                two = jnp.where(low, there, here)
-                at = pl.multiple_of((half * 4 + here_x) * 128, 128)
-                buffer[lag, :, pl.ds(at, 128)] = jnp.where(lane, one, pltpu.roll(two, 64, axis=1))
-                at = pl.multiple_of((half * 4 + (here_x ^ 2)) * 128, 128)
-                buffer[lag, :, pl.ds(at, 128)] = jnp.where(lane, pltpu.roll(one, 64, axis=1), two)
-        copies.append(pltpu.make_async_copy(buffer.at[lag], out.at[lag], sems.at[lag]))
-        copies[-1].start()
+    for half in range(width // 128):
+        span = slice(half * 128, (half + 1) * 128)
+        for lag in range(lags):
+            here = same[lag, :, span] * (1.0 / SCALE) if flip else same[lag, :, span]
+            there = cross[lag, :, span] * (1.0 / SCALE)
+            one = jnp.where(low, here, there)
+            two = jnp.where(low, there, here)
+            tiles[half * 2, lag] = jnp.where(lane, one, pltpu.roll(two, 64, axis=1))
+            tiles[half * 2 + 1, lag] = jnp.where(lane, pltpu.roll(one, 64, axis=1), two)
+        for k, to_x in enumerate((here_x, here_x ^ 2)):
+            at = pl.multiple_of((half * 4 + to_x) * 128, 128)
+            tile = half * 2 + k
+            copies.append(
+                pltpu.make_async_copy(tiles.at[tile], out.at[:, :, pl.ds(at, 128)], sems.at[tile])
+            )
+            copies[-1].start()
     for copy in copies:
         copy.wait()
 
 
-def run_join(place, *quarters):
-    lags, rows, width = quarters[0].shape
-    vmem = pl.BlockSpec(memory_space=pltpu.VMEM)
-    return pl.pallas_call(
-        join_kernel,
-        in_specs=[pl.BlockSpec(memory_space=pltpu.SMEM)] + [vmem] * 4,
-        out_specs=pl.BlockSpec(memory_space=pltpu.HBM),
+def run_join(place, flip, same, cross, *base):
+    lags, rows, width = same.shape
+    vmem = pl.BlockSpec(memory_space=pltpu.VMEM)
+    hbm = pl.BlockSpec(memory_space=pltpu.HBM)
+
+    def body(*refs):
+        join_kernel(flip, *refs)
+
+    return pl.pallas_call(
+        body,
+        in_specs=[pl.BlockSpec(memory_space=pltpu.SMEM), vmem, vmem] + [hbm] * len(base),
+        out_specs=hbm,
         out_shape=jax.ShapeDtypeStruct((lags, rows, 4 * width), jnp.float32),
+        input_output_aliases={3: 0} if base else {},
         scratch_shapes=[
-            pltpu.VMEM((lags, rows, 4 * width), jnp.float32),
-            pltpu.SemaphoreType.DMA((lags,)),
+            pltpu.VMEM((width // 64, lags, rows, 128), jnp.float32),
+            pltpu.SemaphoreType.DMA((width // 64,)),
         ],
         compiler_params=pltpu.CompilerParams(vmem_limit_bytes=8 * MB),
         name="join",
-    )(place, *quarters)
+    )(place, same, cross, *base)
 
 
 def around(value, axis, step):
@@ -353,10 +362,11 @@
     came_y = cross_y(send_y)
     got_xy = came_xy.astype(jnp.float32)
     got_x = after(came_x, got_xy).astype(jnp.float32)
-    got_y = after(came_y, got_x).astype(jnp.float32)
+    base = run_join(place, 1, got_x, got_xy)
+    got_y = after(came_y, base).astype(jnp.float32)
     own = run_lags(after(full, scale))
     kept = run_weigh(own, columns, scale, 1)
-    information = run_join(place, kept, got_x, got_xy, got_y)
+    information = run_join(place, 0, kept, got_y, base)
     return (information, mine)
 
 

time: 83 us -> 83 us (level)
  Pallas kernels: 18 us -> 19.5 us
  waiting for transfers between devices: 21.1 us -> 19.6 us
    pallas_call x1 -> x2, Pallas kernels: 2.15 us -> 3.62 us  [run_join(): pl.pallas_call(body, in_specs=[pl.BlockSpec(memory_space=pltpu.SMEM), vme...]
    ppermute x2, waiting for transfers between devices: 1.46 us -> 0.01 us  [cross_y(): return lax.ppermute(value, 'yh', [(0, 1), (1, 0)])]
  transfers between devices with their start and end apart: 16 -> 16, of which waited for: 7 -> 6; matrix products, arithmetic and copies ran while one was open for 0% -> 0% of each run, Pallas kernels for 15% -> 17%
where the time goes in v9:
time: 83 us; the launch traced here: 82.9 us
  starting transfers between devices  34.3 us (41%)
  waiting for transfers between devices  19.6 us (24%)
  Pallas kernels  19.5 us (23%)
  blocking collectives  7.47 us (9%)
  between operations  1 us (1%)
    ppermute x8, waiting for transfers between devices, around(): lax.ppermute(value, axis, [(i, (i + step) % size) for i in range(size)])  15.1 us
    ppermute x8, starting transfers between devices, around(): lax.ppermute(value, axis, [(i, (i + step) % size) for i in range(size)])  13.2 us
    ppermute x2, starting transfers between devices, spread(): return lax.ppermute(value, ('z', 'x', 'yl', 'core'), pairs)  9.94 us
    all_gather x1, blocking collectives, shards(): parts = lax.all_gather(raw, ('yl', 'core'), axis=0, tiled=False)  7.47 us
    pallas_call x4, Pallas kernels, run_weigh(): pl.pallas_call(body, in_specs=[vmem] * 4, out_specs=vmem, out_shape=jax.S...  5.74 us
    pallas_call x4, Pallas kernels, run_lags(): pl.pallas_call(lag_kernel, in_specs=[vmem], out_specs=[vmem, vmem], out_s...  5.05 us
    ppermute x2, starting transfers between devices, cross_y(): return lax.ppermute(value, 'yh', [(0, 1), (1, 0)])  3.86 us
    ppermute x1, starting transfers between devices, cross_xy(): return lax.ppermute(value, ('x', 'yh'), [(i, i ^ 3) for i in range(8)])  3.68 us
  transfers between devices with their start and end apart: 16, of which 6 were waited for; matrix products, arithmetic and copies ran while one was open for 0% of the time, Pallas kernels for 17%

profile of v9, /device:TPU:2, one launch (start us, length us, event | category | flops | bytes accessed | tf_op | source)
XLA Modules:
  0.0 82.9 jit_solution(12900316721432113020)
XLA Ops:
  0.6 7.5 %all-gather = bf16[256,1024]{1,0:T(8,128)(2,1)S(1)} all-gather(bf16[64,1024]{1,0:T(8,128)(2,1)} %param.2), channel_id=2, replica_groups=mesh['z'=8,'x'=4,'yh'=2,'yl'=2,'core'=2] {'yl','core'}, dimensions={0}, use_global_device_ids=true | all-gather | bytes 655360 | tf_op jit(solution)/shard_map/all_gather | solution.py:336
  8.8 1.1 %pieces.1 = bf16[2,8,4096]{2,1,0:T(8,128)(2,1)S(1)} custom-call(s32[5]{0:T(128)S(1)} %stack.20.place.refs_0_, f32[1,65]{1,0:T(1,128)S(1)} %bitcast.8, bf16[4,64,1024]{2,1,0:T(8,128)(2,1)S(1)} %bitcast.6), custom_call_target="tpu_custom_call" | custom-call | tf_op jit(solution)/shard_map/pieces/pallas_call | solution.py:66
  10.0 6.8 %collective-permute-start.1 = (bf16[2,8,4096]{2,1,0:T(8,128)(2,1)S(1)}, bf16[2,8,4096]{2,1,0:T(8,128)(2,1)S(1)}, u32[]{:S(2)}, u32[]{:S(2)}) collective-permute-start(bf16[2,8,4096]{2,1,0:T(8,128)(2,1)S(1)} %pieces.1), channel_id=1, source_target_pairs={{0,160},{1,192},{2,224},{3,0},{8,168},{9,200},{10,232},{11,8},{16,... | collective-permute-start | bytes 393224 | tf_op jit(solution)/shard_map/ppermute | solution.py:322
  16.8 3.1 %collective-permute-start.2 = (bf16[2,8,4096]{2,1,0:T(8,128)(2,1)S(1)}, bf16[2,8,4096]{2,1,0:T(8,128)(2,1)S(1)}, u32[]{:S(2)}, u32[]{:S(2)}) collective-permute-start(bf16[2,8,4096]{2,1,0:T(8,128)(2,1)S(1)} %pieces.1), channel_id=1, source_target_pairs={{0,176},{1,208},{2,240},{3,16},{8,184},{9,216},{10,248},{11,24},{1... | collective-permute-start | bytes 393224 | tf_op jit(solution)/shard_map/ppermute | solution.py:322
  19.9 2.7 %rows.1 = (bf16[64,4096]{1,0:T(8,128)(2,1)S(1)}, bf16[64,1024]{1,0:T(8,128)(2,1)}) custom-call(s32[5]{0:T(128)S(1)} %stack.20.place.refs_0_, f32[1,65]{1,0:T(1,128)S(1)} %bitcast.9, bf16[4,64,1024]{2,1,0:T(8,128)(2,1)S(1)} %bitcast.7), custom_call_target="tpu_custom_call" | custom-call | flops 1073741824 | bytes 4194304 | tf_op jit(solution)/shard_map/rows/pallas_call | solution.py:103
  22.6 2.9 %collective-permute-start = (bf16[64,4096]{1,0:T(8,128)(2,1)S(1)}, bf16[64,4096]{1,0:T(8,128)(2,1)S(1)}, u32[]{:S(2)}, u32[]{:S(2)}) collective-permute-start(bf16[64,4096]{1,0:T(8,128)(2,1)S(1)} %get-tuple-element.44.rows_ref), channel_id=1, source_target_pairs={{0,4},{4,0},{1,5},{5,1},{2,6},{6,2},{3,7},{7,3},{8,12},{12,8},{9,1... | collective-permute-start | bytes 1572872 | tf_op jit(solution)/shard_map/ppermute | solution.py:302
  25.8 3.1 %collective-permute-start.4 = (bf16[4,8,4096]{2,1,0:T(8,128)(2,1)S(1)}, bf16[4,8,4096]{2,1,0:T(8,128)(2,1)S(1)}, u32[]{:S(2)}, u32[]{:S(2)}) collective-permute-start(bf16[4,8,4096]{2,1,0:T(8,128)(2,1)S(1)} %constant_dynamic-update-slice_fusion.refs_1_), channel_id=1, source_target_pairs={{0,224},{32,0},{64,32},{96,64},{128,96},{160,128},{192,160},{224,1... | collective-permute-start | bytes 786440 | tf_op jit(solution)/shard_map/ppermute | solution.py:298
  28.9 1.4 %collective-permute-start.10 = (bf16[64,4096]{1,0:T(8,128)(2,1)S(1)}, bf16[64,4096]{1,0:T(8,128)(2,1)S(1)}, u32[]{:S(2)}, u32[]{:S(2)}) collective-permute-start(bf16[64,4096]{1,0:T(8,128)(2,1)S(1)} %get-tuple-element.44.rows_ref), channel_id=1, source_target_pairs={{0,8},{8,0},{16,24},{24,16},{1,9},{9,1},{17,25},{25,17},{2,10},{10... | collective-permute-start | bytes 1572872 | tf_op jit(solution)/shard_map/ppermute | solution.py:306
  30.4 4.0 %collective-permute-done.3.refs_2_ = bf16[4,8,4096]{2,1,0:T(8,128)(2,1)S(1)} collective-permute-done((bf16[4,8,4096]{2,1,0:T(8,128)(2,1)S(1)}, bf16[4,8,4096]{2,1,0:T(8,128)(2,1)S(1)}, u32[]{:S(2)}, u32[]{:S(2)}) %collective-permute-start.3) | collective-permute-done | bytes 262176 | tf_op jit(solution)/shard_map/ppermute | solution.py:298
  34.4 3.2 %collective-permute-start.8 = (bf16[4,8,4096]{2,1,0:T(8,128)(2,1)S(1)}, bf16[4,8,4096]{2,1,0:T(8,128)(2,1)S(1)}, u32[]{:S(2)}, u32[]{:S(2)}) collective-permute-start(bf16[4,8,4096]{2,1,0:T(8,128)(2,1)S(1)} %collective-permute-done.4.refs_3_), channel_id=1, source_target_pairs={{0,224},{32,0},{64,32},{96,64},{128,96},{160,128},{192,160},{224,1... | collective-permute-start | bytes 786440 | tf_op jit(solution)/shard_map/ppermute | solution.py:298
  37.6 1.4 %collective-permute-start.5 = (bf16[64,4096]{1,0:T(8,128)(2,1)S(1)}, bf16[64,4096]{1,0:T(8,128)(2,1)S(1)}, u32[]{:S(2)}, u32[]{:S(2)}) collective-permute-start(bf16[64,4096]{1,0:T(8,128)(2,1)S(1)} %collective-permute-done.rows_ref), channel_id=1, source_target_pairs={{0,8},{8,0},{16,24},{24,16},{1,9},{9,1},{17,25},{25,17},{2,10},{10... | collective-permute-start | bytes 1572872 | tf_op jit(solution)/shard_map/ppermute | solution.py:306
  39.0 1.3 %lags.4 = (bf16[9,64,4096]{2,1,0:T(8,128)(2,1)S(1)}, f32[64,128]{1,0:T(8,128)S(1)}) custom-call(bf16[64,4096]{1,0:T(8,128)(2,1)S(1)} %collective-permute-done.rows_ref), custom_call_target="tpu_custom_call" | custom-call | flops 10485760 | bytes 6291456 | tf_op jit(solution)/shard_map/lags/pallas_call | solution.py:144
  40.2 4.4 %collective-permute-done.6.refs_4_ = bf16[4,8,4096]{2,1,0:T(8,128)(2,1)S(1)} collective-permute-done((bf16[4,8,4096]{2,1,0:T(8,128)(2,1)S(1)}, bf16[4,8,4096]{2,1,0:T(8,128)(2,1)S(1)}, u32[]{:S(2)}, u32[]{:S(2)}) %collective-permute-start.6) | collective-permute-done | bytes 262176 | tf_op jit(solution)/shard_map/ppermute | solution.py:298
  44.7 3.2 %collective-permute-start.9 = (bf16[4,8,4096]{2,1,0:T(8,128)(2,1)S(1)}, bf16[4,8,4096]{2,1,0:T(8,128)(2,1)S(1)}, u32[]{:S(2)}, u32[]{:S(2)}) collective-permute-start(bf16[4,8,4096]{2,1,0:T(8,128)(2,1)S(1)} %collective-permute-done.8.refs_5_), channel_id=1, source_target_pairs={{0,224},{32,0},{64,32},{96,64},{128,96},{160,128},{192,160},{224,1... | collective-permute-start | bytes 786440 | tf_op jit(solution)/shard_map/ppermute | solution.py:298
  47.9 1.3 %lags.6 = (bf16[9,64,4096]{2,1,0:T(8,128)(2,1)S(1)}, f32[64,128]{1,0:T(8,128)S(1)}) custom-call(bf16[64,4096]{1,0:T(8,128)(2,1)S(1)} %collective-permute-done.10.rows_ref), custom_call_target="tpu_custom_call" | custom-call | flops 10485760 | bytes 6291456 | tf_op jit(solution)/shard_map/lags/pallas_call | solution.py:144
  49.2 5.0 %collective-permute-done.7.refs_6_ = bf16[4,8,4096]{2,1,0:T(8,128)(2,1)S(1)} collective-permute-done((bf16[4,8,4096]{2,1,0:T(8,128)(2,1)S(1)}, bf16[4,8,4096]{2,1,0:T(8,128)(2,1)S(1)}, u32[]{:S(2)}, u32[]{:S(2)}) %collective-permute-start.7) | collective-permute-done | bytes 262176 | tf_op jit(solution)/shard_map/ppermute | solution.py:298
  54.3 3.3 %collective-permute-start.12 = (bf16[2,8,4096]{2,1,0:T(8,128)(2,1)S(1)}, bf16[2,8,4096]{2,1,0:T(8,128)(2,1)S(1)}, u32[]{:S(2)}, u32[]{:S(2)}) collective-permute-start(bf16[2,8,4096]{2,1,0:T(8,128)(2,1)S(1)} %slice.7), channel_id=1, source_target_pairs={{0,224},{32,0},{64,32},{96,64},{128,96},{160,128},{192,160},{224,1... | collective-permute-start | bytes 393224 | tf_op jit(solution)/shard_map/ppermute | solution.py:298
  57.6 1.3 %lags.5 = (bf16[9,64,4096]{2,1,0:T(8,128)(2,1)S(1)}, f32[64,128]{1,0:T(8,128)S(1)}) custom-call(bf16[64,4096]{1,0:T(8,128)(2,1)S(1)} %collective-permute-done.5.rows_ref), custom_call_target="tpu_custom_call" | custom-call | flops 10485760 | bytes 6291456 | tf_op jit(solution)/shard_map/lags/pallas_call | solution.py:144
  58.9 1.6 %collective-permute-done.11.refs_8_ = bf16[2,8,4096]{2,1,0:T(8,128)(2,1)S(1)} collective-permute-done((bf16[2,8,4096]{2,1,0:T(8,128)(2,1)S(1)}, bf16[2,8,4096]{2,1,0:T(8,128)(2,1)S(1)}, u32[]{:S(2)}, u32[]{:S(2)}) %collective-permute-start.11) | collective-permute-done | bytes 131104 | tf_op jit(solution)/shard_map/ppermute | solution.py:298
  60.5 1.2 %columns.1 = (bf16[32,8,4096]{2,1,0:T(8,128)(2,1)S(1)}, f32[8,256]{1,0:T(8,128)S(1)}) custom-call(s32[5]{0:T(128)S(1)} %stack.20.place.refs_0_, bf16[4,8,4096]{2,1,0:T(8,128)(2,1)S(1)} %constant_dynamic-update-slice_fusion.refs_1_, bf16[4,8,4096]{2,1,0:T(8,128)(2,1)S(1)} %collective-permute-done.3.refs_2_, ...), custom_call_target="tpu_custom_call" | custom-call | flops 8388608 | bytes 4194304 | tf_op jit(solution)/shard_map/columns/pallas_call | solution.py:196
  61.7 1.4 %weigh.6 = f32[9,64,256]{2,1,0:T(8,128)S(1)} custom-call(bf16[9,64,4096]{2,1,0:T(8,128)(2,1)S(1)} %get-tuple-element.35.refs_0_, f32[64,128]{1,0:T(8,128)S(1)} %get-tuple-element.36.refs_1_, bf16[32,8,4096]{2,1,0:T(8,128)(2,1)S(1)} %get-tuple-element.47.refs_2_, f32[8,256]{1,0:T(8,128)S(1)} %get-tuple-element.48.refs_3_), custom_call_target="tpu_custom_call" | custom-call | flops 1207959552 | bytes 589824 | tf_op jit(solution)/shard_map/weigh/pallas_call | solution.py:231
  63.2 3.7 %collective-permute-start.15 = (f16[9,64,256]{2,1,0:T(8,128)(2,1)S(1)}, f16[9,64,256]{2,1,0:T(8,128)(2,1)S(1)}, u32[]{:S(2)}, u32[]{:S(2)}) collective-permute-start(f16[9,64,256]{2,1,0:T(8,128)(2,1)S(1)} %convert_element_type.19), channel_id=1, source_target_pairs={{0,12},{4,8},{8,4},{12,0},{16,28},{20,24},{24,20},{28,16},{1,13},{... | collective-permute-start | bytes 884744 | tf_op jit(solution)/shard_map/ppermute | solution.py:310
  66.9 1.4 %weigh.7 = f32[9,64,256]{2,1,0:T(8,128)S(1)} custom-call(bf16[9,64,4096]{2,1,0:T(8,128)(2,1)S(1)} %get-tuple-element.39.refs_0_, f32[64,128]{1,0:T(8,128)S(1)} %get-tuple-element.40.refs_1_, bf16[32,8,4096]{2,1,0:T(8,128)(2,1)S(1)} %get-tuple-element.47.refs_2_, f32[8,256]{1,0:T(8,128)S(1)} %get-tuple-element.48.refs_3_), custom_call_target="tpu_custom_call" | custom-call | flops 1207959552 | bytes 589824 | tf_op jit(solution)/shard_map/weigh/pallas_call | solution.py:231
  68.4 0.8 %collective-permute-start.14 = (f16[9,64,256]{2,1,0:T(8,128)(2,1)S(1)}, f16[9,64,256]{2,1,0:T(8,128)(2,1)S(1)}, u32[]{:S(2)}, u32[]{:S(2)}) collective-permute-start(f16[9,64,256]{2,1,0:T(8,128)(2,1)S(1)} %convert_element_type.20), channel_id=1, source_target_pairs={{0,8},{8,0},{16,24},{24,16},{1,9},{9,1},{17,25},{25,17},{2,10},{10... | collective-permute-start | bytes 884744 | tf_op jit(solution)/shard_map/ppermute | solution.py:306
  69.2 1.4 %weigh.5 = f32[9,64,256]{2,1,0:T(8,128)S(1)} custom-call(bf16[9,64,4096]{2,1,0:T(8,128)(2,1)S(1)} %get-tuple-element.30.refs_0_, f32[64,128]{1,0:T(8,128)S(1)} %get-tuple-element.31.refs_1_, bf16[32,8,4096]{2,1,0:T(8,128)(2,1)S(1)} %get-tuple-element.47.refs_2_, f32[8,256]{1,0:T(8,128)S(1)} %get-tuple-element.48.refs_3_), custom_call_target="tpu_custom_call" | custom-call | flops 1207959552 | bytes 589824 | tf_op jit(solution)/shard_map/weigh/pallas_call | solution.py:231
  70.7 1.0 %collective-permute-start.13 = (f16[9,64,256]{2,1,0:T(8,128)(2,1)S(1)}, f16[9,64,256]{2,1,0:T(8,128)(2,1)S(1)}, u32[]{:S(2)}, u32[]{:S(2)}) collective-permute-start(f16[9,64,256]{2,1,0:T(8,128)(2,1)S(1)} %convert_element_type.18), channel_id=1, source_target_pairs={{0,4},{4,0},{1,5},{5,1},{2,6},{6,2},{3,7},{7,3},{8,12},{12,8},{9,1... | collective-permute-start | bytes 884744 | tf_op jit(solution)/shard_map/ppermute | solution.py:302
  71.7 1.3 %lags.7 = (bf16[9,64,4096]{2,1,0:T(8,128)(2,1)S(1)}, f32[64,128]{1,0:T(8,128)S(1)}) custom-call(bf16[64,4096]{1,0:T(8,128)(2,1)S(1)} %get-tuple-element.44.rows_ref), custom_call_target="tpu_custom_call" | custom-call | flops 10485760 | bytes 6291456 | tf_op jit(solution)/shard_map/lags/pallas_call | solution.py:144
  72.9 1.4 %weigh.4.refs_1_ = f32[9,64,256]{2,1,0:T(8,128)S(1)} custom-call(bf16[9,64,4096]{2,1,0:T(8,128)(2,1)S(1)} %get-tuple-element.45.refs_0_, f32[64,128]{1,0:T(8,128)S(1)} %get-tuple-element.46.refs_1_, bf16[32,8,4096]{2,1,0:T(8,128)(2,1)S(1)} %get-tuple-element.47.refs_2_, f32[8,256]{1,0:T(8,128)S(1)} %get-tuple-element.48.refs_3_), custom_call_target="tpu_custom_call" | custom-call | flops 1207959552 | bytes 589824 | tf_op jit(solution)/shard_map/weigh/pallas_call | solution.py:231
  74.4 1.3 %collective-permute-done.15 = f16[9,64,256]{2,1,0:T(8,128)(2,1)S(1)} collective-permute-done((f16[9,64,256]{2,1,0:T(8,128)(2,1)S(1)}, f16[9,64,256]{2,1,0:T(8,128)(2,1)S(1)}, u32[]{:S(2)}, u32[]{:S(2)}) %collective-permute-start.15) | collective-permute-done | bytes 294944 | tf_op jit(solution)/shard_map/ppermute | solution.py:310
  75.7 3.3 %collective-permute-done.14 = f16[9,64,256]{2,1,0:T(8,128)(2,1)S(1)} collective-permute-done((f16[9,64,256]{2,1,0:T(8,128)(2,1)S(1)}, f16[9,64,256]{2,1,0:T(8,128)(2,1)S(1)}, u32[]{:S(2)}, u32[]{:S(2)}) %collective-permute-start.14) | collective-permute-done | bytes 294944 | tf_op jit(solution)/shard_map/ppermute | solution.py:306
  79.0 1.8 %join.2.refs_3_ = f32[9,64,1024]{2,1,0:T(8,128)} custom-call(s32[5]{0:T(128)S(1)} %stack.20.place.refs_0_, f32[9,64,256]{2,1,0:T(8,128)S(1)} %convert_element_type.22.refs_1_, f32[9,64,256]{2,1,0:T(8,128)S(1)} %convert_element_type.21.refs_2_), custom_call_target="tpu_custom_call" | custom-call | tf_op jit(solution)/shard_map/join/pallas_call | solution.py:281
  80.9 1.8 %join.3 = f32[9,64,1024]{2,1,0:T(8,128)} custom-call(s32[5]{0:T(128)S(1)} %stack.20.place.refs_0_, f32[9,64,256]{2,1,0:T(8,128)S(1)} %weigh.4.refs_1_, f32[9,64,256]{2,1,0:T(8,128)S(1)} %convert_element_type.23.refs_2_, f32[9,64,1024]{2,1,0:T(8,128)} %join.2.refs_3_), custom_call_target="tpu_custom_call", output_to_operand_aliasing={{}: (3, {})} | custom-call | tf_op jit(solution)/shard_map/join/pallas_call | solution.py:281
  (27 shorter events, 1.4 us)
Async XLA Ops:
  8.2 0.7 copy-start
  10.0 15.6 %collective-permute-start.1 = (bf16[2,8,4096]{2,1,0:T(8,128)(2,1)S(1)}, bf16[2,8,4096]{2,1,0:T(8,128)(2,1)S(1)}, u32[]{:S(2)}, u32[]{:S(2)}) collective-permute-start(bf16[2,8,4096]{2,1,0:T(8,128)(2,1)S(1)} %pieces.1), channel_id=1, source_target_pairs={{0,160},{1,192},{2,224},{3,0},{8,168},{9,200},{10,232},{11,8},{16,... | collective-permute-start | bytes 393224 | tf_op jit(solution)/shard_map/ppermute | solution.py:322
  16.8 8.8 %collective-permute-start.2 = (bf16[2,8,4096]{2,1,0:T(8,128)(2,1)S(1)}, bf16[2,8,4096]{2,1,0:T(8,128)(2,1)S(1)}, u32[]{:S(2)}, u32[]{:S(2)}) collective-permute-start(bf16[2,8,4096]{2,1,0:T(8,128)(2,1)S(1)} %pieces.1), channel_id=1, source_target_pairs={{0,176},{1,208},{2,240},{3,16},{8,184},{9,216},{10,248},{11,24},{1... | collective-permute-start | bytes 393224 | tf_op jit(solution)/shard_map/ppermute | solution.py:322
  22.6 15.0 %collective-permute-start = (bf16[64,4096]{1,0:T(8,128)(2,1)S(1)}, bf16[64,4096]{1,0:T(8,128)(2,1)S(1)}, u32[]{:S(2)}, u32[]{:S(2)}) collective-permute-start(bf16[64,4096]{1,0:T(8,128)(2,1)S(1)} %get-tuple-element.44.rows_ref), channel_id=1, source_target_pairs={{0,4},{4,0},{1,5},{5,1},{2,6},{6,2},{3,7},{7,3},{8,12},{12,8},{9,1... | collective-permute-start | bytes 1572872 | tf_op jit(solution)/shard_map/ppermute | solution.py:302
  25.6 8.8 %collective-permute-start.3 = (bf16[4,8,4096]{2,1,0:T(8,128)(2,1)S(1)}, bf16[4,8,4096]{2,1,0:T(8,128)(2,1)S(1)}, u32[]{:S(2)}, u32[]{:S(2)}) collective-permute-start(bf16[4,8,4096]{2,1,0:T(8,128)(2,1)S(1)} %constant_dynamic-update-slice_fusion.refs_1_), channel_id=1, source_target_pairs={{0,32},{32,64},{64,96},{96,128},{128,160},{160,192},{192,224},{224... | collective-permute-start | bytes 786440 | tf_op jit(solution)/shard_map/ppermute | solution.py:298
  25.8 8.6 %collective-permute-start.4 = (bf16[4,8,4096]{2,1,0:T(8,128)(2,1)S(1)}, bf16[4,8,4096]{2,1,0:T(8,128)(2,1)S(1)}, u32[]{:S(2)}, u32[]{:S(2)}) collective-permute-start(bf16[4,8,4096]{2,1,0:T(8,128)(2,1)S(1)} %constant_dynamic-update-slice_fusion.refs_1_), channel_id=1, source_target_pairs={{0,224},{32,0},{64,32},{96,64},{128,96},{160,128},{192,160},{224,1... | collective-permute-start | bytes 786440 | tf_op jit(solution)/shard_map/ppermute | solution.py:298
  28.9 19.0 %collective-permute-start.10 = (bf16[64,4096]{1,0:T(8,128)(2,1)S(1)}, bf16[64,4096]{1,0:T(8,128)(2,1)S(1)}, u32[]{:S(2)}, u32[]{:S(2)}) collective-permute-start(bf16[64,4096]{1,0:T(8,128)(2,1)S(1)} %get-tuple-element.44.rows_ref), channel_id=1, source_target_pairs={{0,8},{8,0},{16,24},{24,16},{1,9},{9,1},{17,25},{25,17},{2,10},{10... | collective-permute-start | bytes 1572872 | tf_op jit(solution)/shard_map/ppermute | solution.py:306
  34.4 10.3 %collective-permute-start.6 = (bf16[4,8,4096]{2,1,0:T(8,128)(2,1)S(1)}, bf16[4,8,4096]{2,1,0:T(8,128)(2,1)S(1)}, u32[]{:S(2)}, u32[]{:S(2)}) collective-permute-start(bf16[4,8,4096]{2,1,0:T(8,128)(2,1)S(1)} %collective-permute-done.3.refs_2_), channel_id=1, source_target_pairs={{0,32},{32,64},{64,96},{96,128},{128,160},{160,192},{192,224},{224... | collective-permute-start | bytes 786440 | tf_op jit(solution)/shard_map/ppermute | solution.py:298
  34.4 10.3 %collective-permute-start.8 = (bf16[4,8,4096]{2,1,0:T(8,128)(2,1)S(1)}, bf16[4,8,4096]{2,1,0:T(8,128)(2,1)S(1)}, u32[]{:S(2)}, u32[]{:S(2)}) collective-permute-start(bf16[4,8,4096]{2,1,0:T(8,128)(2,1)S(1)} %collective-permute-done.4.refs_3_), channel_id=1, source_target_pairs={{0,224},{32,0},{64,32},{96,64},{128,96},{160,128},{192,160},{224,1... | collective-permute-start | bytes 786440 | tf_op jit(solution)/shard_map/ppermute | solution.py:298
  37.6 20.0 %collective-permute-start.5 = (bf16[64,4096]{1,0:T(8,128)(2,1)S(1)}, bf16[64,4096]{1,0:T(8,128)(2,1)S(1)}, u32[]{:S(2)}, u32[]{:S(2)}) collective-permute-start(bf16[64,4096]{1,0:T(8,128)(2,1)S(1)} %collective-permute-done.rows_ref), channel_id=1, source_target_pairs={{0,8},{8,0},{16,24},{24,16},{1,9},{9,1},{17,25},{25,17},{2,10},{10... | collective-permute-start | bytes 1572872 | tf_op jit(solution)/shard_map/ppermute | solution.py:306
  44.7 9.5 %collective-permute-start.7 = (bf16[4,8,4096]{2,1,0:T(8,128)(2,1)S(1)}, bf16[4,8,4096]{2,1,0:T(8,128)(2,1)S(1)}, u32[]{:S(2)}, u32[]{:S(2)}) collective-permute-start(bf16[4,8,4096]{2,1,0:T(8,128)(2,1)S(1)} %collective-permute-done.6.refs_4_), channel_id=1, source_target_pairs={{0,32},{32,64},{64,96},{96,128},{128,160},{160,192},{192,224},{224... | collective-permute-start | bytes 786440 | tf_op jit(solution)/shard_map/ppermute | solution.py:298
  44.7 9.6 %collective-permute-start.9 = (bf16[4,8,4096]{2,1,0:T(8,128)(2,1)S(1)}, bf16[4,8,4096]{2,1,0:T(8,128)(2,1)S(1)}, u32[]{:S(2)}, u32[]{:S(2)}) collective-permute-start(bf16[4,8,4096]{2,1,0:T(8,128)(2,1)S(1)} %collective-permute-done.8.refs_5_), channel_id=1, source_target_pairs={{0,224},{32,0},{64,32},{96,64},{128,96},{160,128},{192,160},{224,1... | collective-permute-start | bytes 786440 | tf_op jit(solution)/shard_map/ppermute | solution.py:298
  54.2 6.3 %collective-permute-start.11 = (bf16[2,8,4096]{2,1,0:T(8,128)(2,1)S(1)}, bf16[2,8,4096]{2,1,0:T(8,128)(2,1)S(1)}, u32[]{:S(2)}, u32[]{:S(2)}) collective-permute-start(bf16[2,8,4096]{2,1,0:T(8,128)(2,1)S(1)} %slice.6), channel_id=1, source_target_pairs={{0,32},{32,64},{64,96},{96,128},{128,160},{160,192},{192,224},{224... | collective-permute-start | bytes 393224 | tf_op jit(solution)/shard_map/ppermute | solution.py:298
  54.3 6.1 %collective-permute-start.12 = (bf16[2,8,4096]{2,1,0:T(8,128)(2,1)S(1)}, bf16[2,8,4096]{2,1,0:T(8,128)(2,1)S(1)}, u32[]{:S(2)}, u32[]{:S(2)}) collective-permute-start(bf16[2,8,4096]{2,1,0:T(8,128)(2,1)S(1)} %slice.7), channel_id=1, source_target_pairs={{0,224},{32,0},{64,32},{96,64},{128,96},{160,128},{192,160},{224,1... | collective-permute-start | bytes 393224 | tf_op jit(solution)/shard_map/ppermute | solution.py:298
  63.2 12.4 %collective-permute-start.15 = (f16[9,64,256]{2,1,0:T(8,128)(2,1)S(1)}, f16[9,64,256]{2,1,0:T(8,128)(2,1)S(1)}, u32[]{:S(2)}, u32[]{:S(2)}) collective-permute-start(f16[9,64,256]{2,1,0:T(8,128)(2,1)S(1)} %convert_element_type.19), channel_id=1, source_target_pairs={{0,12},{4,8},{8,4},{12,0},{16,28},{20,24},{24,20},{28,16},{1,13},{... | collective-permute-start | bytes 884744 | tf_op jit(solution)/shard_map/ppermute | solution.py:310
  68.4 10.6 %collective-permute-start.14 = (f16[9,64,256]{2,1,0:T(8,128)(2,1)S(1)}, f16[9,64,256]{2,1,0:T(8,128)(2,1)S(1)}, u32[]{:S(2)}, u32[]{:S(2)}) collective-permute-start(f16[9,64,256]{2,1,0:T(8,128)(2,1)S(1)} %convert_element_type.20), channel_id=1, source_target_pairs={{0,8},{8,0},{16,24},{24,16},{1,9},{9,1},{17,25},{25,17},{2,10},{10... | collective-permute-start | bytes 884744 | tf_op jit(solution)/shard_map/ppermute | solution.py:306
  70.7 10.1 %collective-permute-start.13 = (f16[9,64,256]{2,1,0:T(8,128)(2,1)S(1)}, f16[9,64,256]{2,1,0:T(8,128)(2,1)S(1)}, u32[]{:S(2)}, u32[]{:S(2)}) collective-permute-start(f16[9,64,256]{2,1,0:T(8,128)(2,1)S(1)} %convert_element_type.18), channel_id=1, source_target_pairs={{0,4},{4,0},{1,5},{5,1},{2,6},{6,2},{3,7},{7,3},{8,12},{12,8},{9,1... | collective-permute-start | bytes 884744 | tf_op jit(solution)/shard_map/ppermute | solution.py:302

commit v10 on v9

--- a/solution.py
+++ b/solution.py
@@ -165,9 +165,9 @@
         emit(lag, -0.5 * jnp.log(1.0 - ratio * ratio))
 
 
-def columns_kernel(steps, place, *refs):
+def columns_kernel(steps, last, place, *refs):
     units = refs[: len(steps)]
-    columns, scale = refs[len(steps) :]
+    columns = refs[-2] if last else refs[-1]
     z = place[1]
     slab = place[2]
     for ref, moves in zip(units, steps):
@@ -176,35 +176,36 @@
             e = (up < 4).astype(jnp.int32)
             giver = (3 - jnp.where(up < 4, up, 7 - up)) ^ slab
             columns[e * 16 + (part >> 1) * 8 + giver * 2 + (part & 1)] = ref[k]
-    width = columns.shape[0] * columns.shape[1]
-    for g in range(width // 128):
-        block = columns[g * 16 : (g + 1) * 16].astype(jnp.float32).reshape(128, -1)
-        total = jnp.sum(block * block, axis=1, keepdims=True)
-        root = 0.8 / jnp.sqrt(total + 1e-05)
-        root = jnp.transpose(jnp.broadcast_to(root, (128, 128)))
-        scale[:, g * 128 : (g + 1) * 128] = root[0:8]
-
-
-def run_columns(place, units, steps):
-    slots = sum(len(moves) for moves in steps)
+    if last:
+        scale = refs[-1]
+        for g in range(columns.shape[0] * columns.shape[1] // 128):
+            block = columns[g * 16 : (g + 1) * 16].astype(jnp.float32).reshape(128, -1)
+            total = jnp.sum(block * block, axis=1, keepdims=True)
+            root = 0.8 / jnp.sqrt(total + 1e-05)
+            root = jnp.transpose(jnp.broadcast_to(root, (128, 128)))
+            scale[:, g * 128 : (g + 1) * 128] = root[0:8]
+
+
+def run_columns(place, slots, units, steps, *begun):
     bins = units[0].shape[2]
+    last = bool(begun)
 
     def body(*refs):
-        columns_kernel(steps, *refs)
-
-    vmem = pl.BlockSpec(memory_space=pltpu.VMEM)
+        columns_kernel(steps, last, *refs)
+
+    vmem = pl.BlockSpec(memory_space=pltpu.VMEM)
+    columns = jax.ShapeDtypeStruct((slots, 8, bins), jnp.bfloat16)
+    scale = jax.ShapeDtypeStruct((8, slots * 8), jnp.float32)
     return pl.pallas_call(
         body,
-        in_specs=[pl.BlockSpec(memory_space=pltpu.SMEM)] + [vmem] * len(units),
-        out_specs=[vmem, vmem],
-        out_shape=[
-            jax.ShapeDtypeStruct((slots, 8, bins), jnp.bfloat16),
-            jax.ShapeDtypeStruct((8, slots * 8), jnp.float32),
-        ],
+        in_specs=[pl.BlockSpec(memory_space=pltpu.SMEM)] + [vmem] * (len(units) + len(begun)),
+        out_specs=[vmem, vmem] if last else vmem,
+        out_shape=[columns, scale] if last else columns,
+        input_output_aliases={1 + len(units): 0} if last else {},
         compiler_params=pltpu.CompilerParams(vmem_limit_bytes=8 * MB),
         cost_estimate=pl.CostEstimate(flops=8 * MB, bytes_accessed=4 * MB, transcendentals=0),
         name="columns",
-    )(place, *units)
+    )(place, *units, *begun)
 
 
 def weigh_kernel(factor, lagged, energy, columns, scale, out):
@@ -353,20 +354,24 @@
         steps += [[(part, -step) for part in order], [(part, step) for part in order]]
     steps += [[(part, 4) for part in order[0:2]], [(part, 4) for part in order[2:4]]]
     far_xy = run_lags(after(row_xy, *third))
-    columns, scale = run_columns(after(place, far_xy), units, steps)
+    slots = sum(len(moves) for moves in steps)
+    begun = run_columns(place, slots, units[:-2], steps[:-2])
+    ends = after(place, far_xy)
+    columns, scale = run_columns(ends, slots, units[-2:], steps[-2:], begun)
     send_xy = run_weigh(far_xy, columns, scale, SCALE).astype(SENT)
-    send_x = run_weigh(far_x, columns, after(scale, send_xy), SCALE).astype(SENT)
-    send_y = run_weigh(far_y, columns, scale, SCALE).astype(SENT)
+    later = after(scale, send_xy)
+    send_y = run_weigh(far_y, columns, later, SCALE).astype(SENT)
+    send_x = run_weigh(far_x, columns, later, SCALE).astype(SENT)
     came_xy = cross_xy(send_xy)
+    came_y = cross_y(send_y)
     came_x = cross_x(send_x)
-    came_y = cross_y(send_y)
     got_xy = came_xy.astype(jnp.float32)
-    got_x = after(came_x, got_xy).astype(jnp.float32)
-    base = run_join(place, 1, got_x, got_xy)
-    got_y = after(came_y, base).astype(jnp.float32)
+    got_y = after(came_y, got_xy).astype(jnp.float32)
     own = run_lags(after(full, scale))
     kept = run_weigh(own, columns, scale, 1)
-    information = run_join(place, 0, kept, got_y, base)
+    base = run_join(place, 0, kept, got_y)
+    got_x = after(came_x, base).astype(jnp.float32)
+    information = run_join(place, 1, got_x, got_xy, base)
     return (information, mine)
 
 

time: 83 us -> 84.5 us (1.018); the launches traced: 82.9 us -> 82.9 us
    ppermute x2, waiting for transfers between devices: 0.01 us -> 4.62 us  [cross_y(): return lax.ppermute(value, 'yh', [(0, 1), (1, 0)])]
    ppermute x3, waiting for transfers between devices: 3.29 us -> 0.01 us  [cross_x(): return lax.ppermute(value, 'x', [(0, 1), (1, 0), (2, 3), (3, 2)])]
    ppermute x1, waiting for transfers between devices: 1.28 us -> 0.01 us  [cross_xy(): return lax.ppermute(value, ('x', 'yh'), [(i, i ^ 3) for i in range(8)])]
    pallas_call x1 -> x2, Pallas kernels: 1.21 us -> 1.76 us  [run_columns(): pl.pallas_call(body, in_specs=[pl.BlockSpec(memory_space=pltpu.SMEM)] + [...]
  transfers between devices with their start and end apart: 16 -> 16, of which waited for: 6 -> 5; matrix products, arithmetic and copies ran while one was open for 0% -> 0% of each run, Pallas kernels for 17% -> 18%
where the time goes in v10:
time: 84.5 us; the launch traced here: 82.9 us
  starting transfers between devices  34.3 us (41%)
  Pallas kernels  20 us (24%)
  waiting for transfers between devices  19 us (22%)
  blocking collectives  7.47 us (9%)
  between operations  1.02 us (1%)
    ppermute x8, waiting for transfers between devices, around(): lax.ppermute(value, axis, [(i, (i + step) % size) for i in range(size)])  14.4 us
    ppermute x8, starting transfers between devices, around(): lax.ppermute(value, axis, [(i, (i + step) % size) for i in range(size)])  13.2 us
    ppermute x2, starting transfers between devices, spread(): return lax.ppermute(value, ('z', 'x', 'yl', 'core'), pairs)  9.94 us
    all_gather x1, blocking collectives, shards(): parts = lax.all_gather(raw, ('yl', 'core'), axis=0, tiled=False)  7.47 us
    pallas_call x4, Pallas kernels, run_weigh(): pl.pallas_call(body, in_specs=[vmem] * 4, out_specs=vmem, out_shape=jax.S...  5.74 us
    pallas_call x4, Pallas kernels, run_lags(): pl.pallas_call(lag_kernel, in_specs=[vmem], out_specs=[vmem, vmem], out_s...  5.06 us
    ppermute x2, waiting for transfers between devices, cross_y(): return lax.ppermute(value, 'yh', [(0, 1), (1, 0)])  4.62 us
    ppermute x3, starting transfers between devices, cross_x(): return lax.ppermute(value, 'x', [(0, 1), (1, 0), (2, 3), (3, 2)])  3.86 us
  transfers between devices with their start and end apart: 16, of which 5 were waited for; matrix products, arithmetic and copies ran while one was open for 0% of the time, Pallas kernels for 18%

profile of v10, /device:TPU:2, one launch (start us, length us, event | category | flops | bytes accessed | tf_op | source)
XLA Modules:
  0.0 82.9 jit_solution(5493476797650210964)
XLA Ops:
  0.6 7.5 %all-gather = bf16[256,1024]{1,0:T(8,128)(2,1)S(1)} all-gather(bf16[64,1024]{1,0:T(8,128)(2,1)} %param.2), channel_id=2, replica_groups=mesh['z'=8,'x'=4,'yh'=2,'yl'=2,'core'=2] {'yl','core'}, dimensions={0}, use_global_device_ids=true | all-gather | bytes 655360 | tf_op jit(solution)/shard_map/all_gather | solution.py:337
  8.8 1.1 %pieces.1 = bf16[2,8,4096]{2,1,0:T(8,128)(2,1)S(1)} custom-call(s32[5]{0:T(128)S(1)} %stack.20.place.refs_0_, f32[1,65]{1,0:T(1,128)S(1)} %bitcast.8, bf16[4,64,1024]{2,1,0:T(8,128)(2,1)S(1)} %bitcast.6), custom_call_target="tpu_custom_call" | custom-call | tf_op jit(solution)/shard_map/pieces/pallas_call | solution.py:66
  10.0 6.8 %collective-permute-start.1 = (bf16[2,8,4096]{2,1,0:T(8,128)(2,1)S(1)}, bf16[2,8,4096]{2,1,0:T(8,128)(2,1)S(1)}, u32[]{:S(2)}, u32[]{:S(2)}) collective-permute-start(bf16[2,8,4096]{2,1,0:T(8,128)(2,1)S(1)} %pieces.1), channel_id=1, source_target_pairs={{0,160},{1,192},{2,224},{3,0},{8,168},{9,200},{10,232},{11,8},{16,... | collective-permute-start | bytes 393224 | tf_op jit(solution)/shard_map/ppermute | solution.py:323
  16.8 3.1 %collective-permute-start.2 = (bf16[2,8,4096]{2,1,0:T(8,128)(2,1)S(1)}, bf16[2,8,4096]{2,1,0:T(8,128)(2,1)S(1)}, u32[]{:S(2)}, u32[]{:S(2)}) collective-permute-start(bf16[2,8,4096]{2,1,0:T(8,128)(2,1)S(1)} %pieces.1), channel_id=1, source_target_pairs={{0,176},{1,208},{2,240},{3,16},{8,184},{9,216},{10,248},{11,24},{1... | collective-permute-start | bytes 393224 | tf_op jit(solution)/shard_map/ppermute | solution.py:323
  19.9 2.7 %rows.1 = (bf16[64,4096]{1,0:T(8,128)(2,1)S(1)}, bf16[64,1024]{1,0:T(8,128)(2,1)}) custom-call(s32[5]{0:T(128)S(1)} %stack.20.place.refs_0_, f32[1,65]{1,0:T(1,128)S(1)} %bitcast.9, bf16[4,64,1024]{2,1,0:T(8,128)(2,1)S(1)} %bitcast.7), custom_call_target="tpu_custom_call" | custom-call | flops 1073741824 | bytes 4194304 | tf_op jit(solution)/shard_map/rows/pallas_call | solution.py:103
  22.6 2.9 %collective-permute-start.7 = (bf16[64,4096]{1,0:T(8,128)(2,1)S(1)}, bf16[64,4096]{1,0:T(8,128)(2,1)S(1)}, u32[]{:S(2)}, u32[]{:S(2)}) collective-permute-start(bf16[64,4096]{1,0:T(8,128)(2,1)S(1)} %get-tuple-element.46.rows_ref), channel_id=1, source_target_pairs={{0,4},{4,0},{1,5},{5,1},{2,6},{6,2},{3,7},{7,3},{8,12},{12,8},{9,1... | collective-permute-start | bytes 1572872 | tf_op jit(solution)/shard_map/ppermute | solution.py:303
  25.8 3.1 %collective-permute-start.5 = (bf16[4,8,4096]{2,1,0:T(8,128)(2,1)S(1)}, bf16[4,8,4096]{2,1,0:T(8,128)(2,1)S(1)}, u32[]{:S(2)}, u32[]{:S(2)}) collective-permute-start(bf16[4,8,4096]{2,1,0:T(8,128)(2,1)S(1)} %constant_dynamic-update-slice_fusion.refs_1_), channel_id=1, source_target_pairs={{0,224},{32,0},{64,32},{96,64},{128,96},{160,128},{192,160},{224,1... | collective-permute-start | bytes 786440 | tf_op jit(solution)/shard_map/ppermute | solution.py:299
  28.9 1.4 %collective-permute-start = (bf16[64,4096]{1,0:T(8,128)(2,1)S(1)}, bf16[64,4096]{1,0:T(8,128)(2,1)S(1)}, u32[]{:S(2)}, u32[]{:S(2)}) collective-permute-start(bf16[64,4096]{1,0:T(8,128)(2,1)S(1)} %get-tuple-element.46.rows_ref), channel_id=1, source_target_pairs={{0,8},{8,0},{16,24},{24,16},{1,9},{9,1},{17,25},{25,17},{2,10},{10... | collective-permute-start | bytes 1572872 | tf_op jit(solution)/shard_map/ppermute | solution.py:307
  30.4 4.0 %collective-permute-done.3.refs_2_ = bf16[4,8,4096]{2,1,0:T(8,128)(2,1)S(1)} collective-permute-done((bf16[4,8,4096]{2,1,0:T(8,128)(2,1)S(1)}, bf16[4,8,4096]{2,1,0:T(8,128)(2,1)S(1)}, u32[]{:S(2)}, u32[]{:S(2)}) %collective-permute-start.3) | collective-permute-done | bytes 262176 | tf_op jit(solution)/shard_map/ppermute | solution.py:299
  34.4 3.2 %collective-permute-start.6 = (bf16[4,8,4096]{2,1,0:T(8,128)(2,1)S(1)}, bf16[4,8,4096]{2,1,0:T(8,128)(2,1)S(1)}, u32[]{:S(2)}, u32[]{:S(2)}) collective-permute-start(bf16[4,8,4096]{2,1,0:T(8,128)(2,1)S(1)} %collective-permute-done.5.refs_3_), channel_id=1, source_target_pairs={{0,224},{32,0},{64,32},{96,64},{128,96},{160,128},{192,160},{224,1... | collective-permute-start | bytes 786440 | tf_op jit(solution)/shard_map/ppermute | solution.py:299
  37.6 1.4 %collective-permute-start.8 = (bf16[64,4096]{1,0:T(8,128)(2,1)S(1)}, bf16[64,4096]{1,0:T(8,128)(2,1)S(1)}, u32[]{:S(2)}, u32[]{:S(2)}) collective-permute-start(bf16[64,4096]{1,0:T(8,128)(2,1)S(1)} %collective-permute-done.7.rows_ref), channel_id=1, source_target_pairs={{0,8},{8,0},{16,24},{24,16},{1,9},{9,1},{17,25},{25,17},{2,10},{10... | collective-permute-start | bytes 1572872 | tf_op jit(solution)/shard_map/ppermute | solution.py:307
  39.0 1.3 %lags.5 = (bf16[9,64,4096]{2,1,0:T(8,128)(2,1)S(1)}, f32[64,128]{1,0:T(8,128)S(1)}) custom-call(bf16[64,4096]{1,0:T(8,128)(2,1)S(1)} %collective-permute-done.7.rows_ref), custom_call_target="tpu_custom_call" | custom-call | flops 10485760 | bytes 6291456 | tf_op jit(solution)/shard_map/lags/pallas_call | solution.py:144
  40.2 4.4 %collective-permute-done.4.refs_4_ = bf16[4,8,4096]{2,1,0:T(8,128)(2,1)S(1)} collective-permute-done((bf16[4,8,4096]{2,1,0:T(8,128)(2,1)S(1)}, bf16[4,8,4096]{2,1,0:T(8,128)(2,1)S(1)}, u32[]{:S(2)}, u32[]{:S(2)}) %collective-permute-start.4) | collective-permute-done | bytes 262176 | tf_op jit(solution)/shard_map/ppermute | solution.py:299
  44.7 3.2 %collective-permute-start.10 = (bf16[4,8,4096]{2,1,0:T(8,128)(2,1)S(1)}, bf16[4,8,4096]{2,1,0:T(8,128)(2,1)S(1)}, u32[]{:S(2)}, u32[]{:S(2)}) collective-permute-start(bf16[4,8,4096]{2,1,0:T(8,128)(2,1)S(1)} %collective-permute-done.6.refs_5_), channel_id=1, source_target_pairs={{0,224},{32,0},{64,32},{96,64},{128,96},{160,128},{192,160},{224,1... | collective-permute-start | bytes 786440 | tf_op jit(solution)/shard_map/ppermute | solution.py:299
  47.9 1.3 %lags.4 = (bf16[9,64,4096]{2,1,0:T(8,128)(2,1)S(1)}, f32[64,128]{1,0:T(8,128)S(1)}) custom-call(bf16[64,4096]{1,0:T(8,128)(2,1)S(1)} %collective-permute-done.rows_ref), custom_call_target="tpu_custom_call" | custom-call | flops 10485760 | bytes 6291456 | tf_op jit(solution)/shard_map/lags/pallas_call | solution.py:144
  49.2 5.0 %collective-permute-done.9.refs_6_ = bf16[4,8,4096]{2,1,0:T(8,128)(2,1)S(1)} collective-permute-done((bf16[4,8,4096]{2,1,0:T(8,128)(2,1)S(1)}, bf16[4,8,4096]{2,1,0:T(8,128)(2,1)S(1)}, u32[]{:S(2)}, u32[]{:S(2)}) %collective-permute-start.9) | collective-permute-done | bytes 262176 | tf_op jit(solution)/shard_map/ppermute | solution.py:299
  54.3 3.3 %collective-permute-start.12 = (bf16[2,8,4096]{2,1,0:T(8,128)(2,1)S(1)}, bf16[2,8,4096]{2,1,0:T(8,128)(2,1)S(1)}, u32[]{:S(2)}, u32[]{:S(2)}) collective-permute-start(bf16[2,8,4096]{2,1,0:T(8,128)(2,1)S(1)} %slice.7), channel_id=1, source_target_pairs={{0,224},{32,0},{64,32},{96,64},{128,96},{160,128},{192,160},{224,1... | collective-permute-start | bytes 393224 | tf_op jit(solution)/shard_map/ppermute | solution.py:299
  57.6 0.7 columns.2.refs_3_
  58.3 1.3 %lags.6 = (bf16[9,64,4096]{2,1,0:T(8,128)(2,1)S(1)}, f32[64,128]{1,0:T(8,128)S(1)}) custom-call(bf16[64,4096]{1,0:T(8,128)(2,1)S(1)} %collective-permute-done.8.rows_ref), custom_call_target="tpu_custom_call" | custom-call | flops 10485760 | bytes 6291456 | tf_op jit(solution)/shard_map/lags/pallas_call | solution.py:144
  59.6 0.9 %collective-permute-done.11.refs_1_ = bf16[2,8,4096]{2,1,0:T(8,128)(2,1)S(1)} collective-permute-done((bf16[2,8,4096]{2,1,0:T(8,128)(2,1)S(1)}, bf16[2,8,4096]{2,1,0:T(8,128)(2,1)S(1)}, u32[]{:S(2)}, u32[]{:S(2)}) %collective-permute-start.11) | collective-permute-done | bytes 131104 | tf_op jit(solution)/shard_map/ppermute | solution.py:299
  60.5 1.1 %columns.3 = (bf16[32,8,4096]{2,1,0:T(8,128)(2,1)S(1)}, f32[8,256]{1,0:T(8,128)S(1)}) custom-call(s32[5]{0:T(128)S(1)} %stack.20.place.refs_0_, bf16[2,8,4096]{2,1,0:T(8,128)(2,1)S(1)} %collective-permute-done.11.refs_1_, bf16[2,8,4096]{2,1,0:T(8,128)(2,1)S(1)} %collective-permute-done.12.refs_2_, ...), custom_call_target="tpu_custom_call", output_to_operand_aliasing={{0}: (3, {})} | custom-call | flops 8388608 | bytes 4194304 | tf_op jit(solution)/shard_map/columns/pallas_call | solution.py:199
  61.6 1.4 %weigh.4 = f32[9,64,256]{2,1,0:T(8,128)S(1)} custom-call(bf16[9,64,4096]{2,1,0:T(8,128)(2,1)S(1)} %get-tuple-element.38.refs_0_, f32[64,128]{1,0:T(8,128)S(1)} %get-tuple-element.39.refs_1_, bf16[32,8,4096]{2,1,0:T(8,128)(2,1)S(1)} %get-tuple-element.43.refs_2_, f32[8,256]{1,0:T(8,128)S(1)} %get-tuple-element.45.refs_3_), custom_call_target="tpu_custom_call" | custom-call | flops 1207959552 | bytes 589824 | tf_op jit(solution)/shard_map/weigh/pallas_call | solution.py:232
  63.1 3.7 %collective-permute-start.15 = (f16[9,64,256]{2,1,0:T(8,128)(2,1)S(1)}, f16[9,64,256]{2,1,0:T(8,128)(2,1)S(1)}, u32[]{:S(2)}, u32[]{:S(2)}) collective-permute-start(f16[9,64,256]{2,1,0:T(8,128)(2,1)S(1)} %convert_element_type.18), channel_id=1, source_target_pairs={{0,12},{4,8},{8,4},{12,0},{16,28},{20,24},{24,20},{28,16},{1,13},{... | collective-permute-start | bytes 884744 | tf_op jit(solution)/shard_map/ppermute | solution.py:311
  66.8 1.4 %weigh.7 = f32[9,64,256]{2,1,0:T(8,128)S(1)} custom-call(bf16[9,64,4096]{2,1,0:T(8,128)(2,1)S(1)} %get-tuple-element.33.refs_0_, f32[64,128]{1,0:T(8,128)S(1)} %get-tuple-element.34.refs_1_, bf16[32,8,4096]{2,1,0:T(8,128)(2,1)S(1)} %get-tuple-element.43.refs_2_, f32[8,256]{1,0:T(8,128)S(1)} %get-tuple-element.45.refs_3_), custom_call_target="tpu_custom_call" | custom-call | flops 1207959552 | bytes 589824 | tf_op jit(solution)/shard_map/weigh/pallas_call | solution.py:232
  68.3 0.7 collective-permute-start.14
  69.0 1.4 %weigh.5 = f32[9,64,256]{2,1,0:T(8,128)S(1)} custom-call(bf16[9,64,4096]{2,1,0:T(8,128)(2,1)S(1)} %get-tuple-element.30.refs_0_, f32[64,128]{1,0:T(8,128)S(1)} %get-tuple-element.31.refs_1_, bf16[32,8,4096]{2,1,0:T(8,128)(2,1)S(1)} %get-tuple-element.43.refs_2_, f32[8,256]{1,0:T(8,128)S(1)} %get-tuple-element.45.refs_3_), custom_call_target="tpu_custom_call" | custom-call | flops 1207959552 | bytes 589824 | tf_op jit(solution)/shard_map/weigh/pallas_call | solution.py:232
  70.5 1.1 %collective-permute-start.13 = (f16[9,64,256]{2,1,0:T(8,128)(2,1)S(1)}, f16[9,64,256]{2,1,0:T(8,128)(2,1)S(1)}, u32[]{:S(2)}, u32[]{:S(2)}) collective-permute-start(f16[9,64,256]{2,1,0:T(8,128)(2,1)S(1)} %convert_element_type.19), channel_id=1, source_target_pairs={{0,8},{8,0},{16,24},{24,16},{1,9},{9,1},{17,25},{25,17},{2,10},{10... | collective-permute-start | bytes 884744 | tf_op jit(solution)/shard_map/ppermute | solution.py:307
  71.5 1.3 %lags.7 = (bf16[9,64,4096]{2,1,0:T(8,128)(2,1)S(1)}, f32[64,128]{1,0:T(8,128)S(1)}) custom-call(bf16[64,4096]{1,0:T(8,128)(2,1)S(1)} %get-tuple-element.46.rows_ref), custom_call_target="tpu_custom_call" | custom-call | flops 10485760 | bytes 6291456 | tf_op jit(solution)/shard_map/lags/pallas_call | solution.py:144
  72.8 1.4 %weigh.6.refs_1_ = f32[9,64,256]{2,1,0:T(8,128)S(1)} custom-call(bf16[9,64,4096]{2,1,0:T(8,128)(2,1)S(1)} %get-tuple-element.47.refs_0_, f32[64,128]{1,0:T(8,128)S(1)} %get-tuple-element.48.refs_1_, bf16[32,8,4096]{2,1,0:T(8,128)(2,1)S(1)} %get-tuple-element.43.refs_2_, f32[8,256]{1,0:T(8,128)S(1)} %get-tuple-element.45.refs_3_), custom_call_target="tpu_custom_call" | custom-call | flops 1207959552 | bytes 589824 | tf_op jit(solution)/shard_map/weigh/pallas_call | solution.py:232
  74.3 4.6 %collective-permute-done.14 = f16[9,64,256]{2,1,0:T(8,128)(2,1)S(1)} collective-permute-done((f16[9,64,256]{2,1,0:T(8,128)(2,1)S(1)}, f16[9,64,256]{2,1,0:T(8,128)(2,1)S(1)}, u32[]{:S(2)}, u32[]{:S(2)}) %collective-permute-start.14) | collective-permute-done | bytes 294944 | tf_op jit(solution)/shard_map/ppermute | solution.py:303
  79.0 1.8 %join.2.refs_3_ = f32[9,64,1024]{2,1,0:T(8,128)} custom-call(s32[5]{0:T(128)S(1)} %stack.20.place.refs_0_, f32[9,64,256]{2,1,0:T(8,128)S(1)} %weigh.6.refs_1_, f32[9,64,256]{2,1,0:T(8,128)S(1)} %convert_element_type.22.refs_2_), custom_call_target="tpu_custom_call" | custom-call | tf_op jit(solution)/shard_map/join/pallas_call | solution.py:282
  80.9 1.8 %join.3 = f32[9,64,1024]{2,1,0:T(8,128)} custom-call(s32[5]{0:T(128)S(1)} %stack.20.place.refs_0_, f32[9,64,256]{2,1,0:T(8,128)S(1)} %convert_element_type.23.refs_1_, f32[9,64,256]{2,1,0:T(8,128)S(1)} %convert_element_type.21.refs_2_, f32[9,64,1024]{2,1,0:T(8,128)} %join.2.refs_3_), custom_call_target="tpu_custom_call", output_to_operand_aliasing={{}: (3, {})} | custom-call | tf_op jit(solution)/shard_map/join/pallas_call | solution.py:282
  (28 shorter events, 1.4 us)
Async XLA Ops:
  8.2 0.7 copy-start
  10.0 15.6 %collective-permute-start.1 = (bf16[2,8,4096]{2,1,0:T(8,128)(2,1)S(1)}, bf16[2,8,4096]{2,1,0:T(8,128)(2,1)S(1)}, u32[]{:S(2)}, u32[]{:S(2)}) collective-permute-start(bf16[2,8,4096]{2,1,0:T(8,128)(2,1)S(1)} %pieces.1), channel_id=1, source_target_pairs={{0,160},{1,192},{2,224},{3,0},{8,168},{9,200},{10,232},{11,8},{16,... | collective-permute-start | bytes 393224 | tf_op jit(solution)/shard_map/ppermute | solution.py:323
  16.8 8.8 %collective-permute-start.2 = (bf16[2,8,4096]{2,1,0:T(8,128)(2,1)S(1)}, bf16[2,8,4096]{2,1,0:T(8,128)(2,1)S(1)}, u32[]{:S(2)}, u32[]{:S(2)}) collective-permute-start(bf16[2,8,4096]{2,1,0:T(8,128)(2,1)S(1)} %pieces.1), channel_id=1, source_target_pairs={{0,176},{1,208},{2,240},{3,16},{8,184},{9,216},{10,248},{11,24},{1... | collective-permute-start | bytes 393224 | tf_op jit(solution)/shard_map/ppermute | solution.py:323
  22.6 15.0 %collective-permute-start.7 = (bf16[64,4096]{1,0:T(8,128)(2,1)S(1)}, bf16[64,4096]{1,0:T(8,128)(2,1)S(1)}, u32[]{:S(2)}, u32[]{:S(2)}) collective-permute-start(bf16[64,4096]{1,0:T(8,128)(2,1)S(1)} %get-tuple-element.46.rows_ref), channel_id=1, source_target_pairs={{0,4},{4,0},{1,5},{5,1},{2,6},{6,2},{3,7},{7,3},{8,12},{12,8},{9,1... | collective-permute-start | bytes 1572872 | tf_op jit(solution)/shard_map/ppermute | solution.py:303
  25.6 8.8 %collective-permute-start.3 = (bf16[4,8,4096]{2,1,0:T(8,128)(2,1)S(1)}, bf16[4,8,4096]{2,1,0:T(8,128)(2,1)S(1)}, u32[]{:S(2)}, u32[]{:S(2)}) collective-permute-start(bf16[4,8,4096]{2,1,0:T(8,128)(2,1)S(1)} %constant_dynamic-update-slice_fusion.refs_1_), channel_id=1, source_target_pairs={{0,32},{32,64},{64,96},{96,128},{128,160},{160,192},{192,224},{224... | collective-permute-start | bytes 786440 | tf_op jit(solution)/shard_map/ppermute | solution.py:299
  25.8 8.6 %collective-permute-start.5 = (bf16[4,8,4096]{2,1,0:T(8,128)(2,1)S(1)}, bf16[4,8,4096]{2,1,0:T(8,128)(2,1)S(1)}, u32[]{:S(2)}, u32[]{:S(2)}) collective-permute-start(bf16[4,8,4096]{2,1,0:T(8,128)(2,1)S(1)} %constant_dynamic-update-slice_fusion.refs_1_), channel_id=1, source_target_pairs={{0,224},{32,0},{64,32},{96,64},{128,96},{160,128},{192,160},{224,1... | collective-permute-start | bytes 786440 | tf_op jit(solution)/shard_map/ppermute | solution.py:299
  28.9 19.0 %collective-permute-start = (bf16[64,4096]{1,0:T(8,128)(2,1)S(1)}, bf16[64,4096]{1,0:T(8,128)(2,1)S(1)}, u32[]{:S(2)}, u32[]{:S(2)}) collective-permute-start(bf16[64,4096]{1,0:T(8,128)(2,1)S(1)} %get-tuple-element.46.rows_ref), channel_id=1, source_target_pairs={{0,8},{8,0},{16,24},{24,16},{1,9},{9,1},{17,25},{25,17},{2,10},{10... | collective-permute-start | bytes 1572872 | tf_op jit(solution)/shard_map/ppermute | solution.py:307
  34.4 10.3 %collective-permute-start.4 = (bf16[4,8,4096]{2,1,0:T(8,128)(2,1)S(1)}, bf16[4,8,4096]{2,1,0:T(8,128)(2,1)S(1)}, u32[]{:S(2)}, u32[]{:S(2)}) collective-permute-start(bf16[4,8,4096]{2,1,0:T(8,128)(2,1)S(1)} %collective-permute-done.3.refs_2_), channel_id=1, source_target_pairs={{0,32},{32,64},{64,96},{96,128},{128,160},{160,192},{192,224},{224... | collective-permute-start | bytes 786440 | tf_op jit(solution)/shard_map/ppermute | solution.py:299
  34.4 10.3 %collective-permute-start.6 = (bf16[4,8,4096]{2,1,0:T(8,128)(2,1)S(1)}, bf16[4,8,4096]{2,1,0:T(8,128)(2,1)S(1)}, u32[]{:S(2)}, u32[]{:S(2)}) collective-permute-start(bf16[4,8,4096]{2,1,0:T(8,128)(2,1)S(1)} %collective-permute-done.5.refs_3_), channel_id=1, source_target_pairs={{0,224},{32,0},{64,32},{96,64},{128,96},{160,128},{192,160},{224,1... | collective-permute-start | bytes 786440 | tf_op jit(solution)/shard_map/ppermute | solution.py:299
  37.6 20.7 %collective-permute-start.8 = (bf16[64,4096]{1,0:T(8,128)(2,1)S(1)}, bf16[64,4096]{1,0:T(8,128)(2,1)S(1)}, u32[]{:S(2)}, u32[]{:S(2)}) collective-permute-start(bf16[64,4096]{1,0:T(8,128)(2,1)S(1)} %collective-permute-done.7.rows_ref), channel_id=1, source_target_pairs={{0,8},{8,0},{16,24},{24,16},{1,9},{9,1},{17,25},{25,17},{2,10},{10... | collective-permute-start | bytes 1572872 | tf_op jit(solution)/shard_map/ppermute | solution.py:307
  44.7 9.5 %collective-permute-start.9 = (bf16[4,8,4096]{2,1,0:T(8,128)(2,1)S(1)}, bf16[4,8,4096]{2,1,0:T(8,128)(2,1)S(1)}, u32[]{:S(2)}, u32[]{:S(2)}) collective-permute-start(bf16[4,8,4096]{2,1,0:T(8,128)(2,1)S(1)} %collective-permute-done.4.refs_4_), channel_id=1, source_target_pairs={{0,32},{32,64},{64,96},{96,128},{128,160},{160,192},{192,224},{224... | collective-permute-start | bytes 786440 | tf_op jit(solution)/shard_map/ppermute | solution.py:299
  44.7 9.6 %collective-permute-start.10 = (bf16[4,8,4096]{2,1,0:T(8,128)(2,1)S(1)}, bf16[4,8,4096]{2,1,0:T(8,128)(2,1)S(1)}, u32[]{:S(2)}, u32[]{:S(2)}) collective-permute-start(bf16[4,8,4096]{2,1,0:T(8,128)(2,1)S(1)} %collective-permute-done.6.refs_5_), channel_id=1, source_target_pairs={{0,224},{32,0},{64,32},{96,64},{128,96},{160,128},{192,160},{224,1... | collective-permute-start | bytes 786440 | tf_op jit(solution)/shard_map/ppermute | solution.py:299
  54.2 6.3 %collective-permute-start.11 = (bf16[2,8,4096]{2,1,0:T(8,128)(2,1)S(1)}, bf16[2,8,4096]{2,1,0:T(8,128)(2,1)S(1)}, u32[]{:S(2)}, u32[]{:S(2)}) collective-permute-start(bf16[2,8,4096]{2,1,0:T(8,128)(2,1)S(1)} %slice.6), channel_id=1, source_target_pairs={{0,32},{32,64},{64,96},{96,128},{128,160},{160,192},{192,224},{224... | collective-permute-start | bytes 393224 | tf_op jit(solution)/shard_map/ppermute | solution.py:299
  54.3 6.1 %collective-permute-start.12 = (bf16[2,8,4096]{2,1,0:T(8,128)(2,1)S(1)}, bf16[2,8,4096]{2,1,0:T(8,128)(2,1)S(1)}, u32[]{:S(2)}, u32[]{:S(2)}) collective-permute-start(bf16[2,8,4096]{2,1,0:T(8,128)(2,1)S(1)} %slice.7), channel_id=1, source_target_pairs={{0,224},{32,0},{64,32},{96,64},{128,96},{160,128},{192,160},{224,1... | collective-permute-start | bytes 393224 | tf_op jit(solution)/shard_map/ppermute | solution.py:299
  63.1 11.2 %collective-permute-start.15 = (f16[9,64,256]{2,1,0:T(8,128)(2,1)S(1)}, f16[9,64,256]{2,1,0:T(8,128)(2,1)S(1)}, u32[]{:S(2)}, u32[]{:S(2)}) collective-permute-start(f16[9,64,256]{2,1,0:T(8,128)(2,1)S(1)} %convert_element_type.18), channel_id=1, source_target_pairs={{0,12},{4,8},{8,4},{12,0},{16,28},{20,24},{24,20},{28,16},{1,13},{... | collective-permute-start | bytes 884744 | tf_op jit(solution)/shard_map/ppermute | solution.py:311
  68.3 10.7 %collective-permute-start.14 = (f16[9,64,256]{2,1,0:T(8,128)(2,1)S(1)}, f16[9,64,256]{2,1,0:T(8,128)(2,1)S(1)}, u32[]{:S(2)}, u32[]{:S(2)}) collective-permute-start(f16[9,64,256]{2,1,0:T(8,128)(2,1)S(1)} %convert_element_type.20), channel_id=1, source_target_pairs={{0,4},{4,0},{1,5},{5,1},{2,6},{6,2},{3,7},{7,3},{8,12},{12,8},{9,1... | collective-permute-start | bytes 884744 | tf_op jit(solution)/shard_map/ppermute | solution.py:303
  70.5 10.3 %collective-permute-start.13 = (f16[9,64,256]{2,1,0:T(8,128)(2,1)S(1)}, f16[9,64,256]{2,1,0:T(8,128)(2,1)S(1)}, u32[]{:S(2)}, u32[]{:S(2)}) collective-permute-start(f16[9,64,256]{2,1,0:T(8,128)(2,1)S(1)} %convert_element_type.19), channel_id=1, source_target_pairs={{0,8},{8,0},{16,24},{24,16},{1,9},{9,1},{17,25},{25,17},{2,10},{10... | collective-permute-start | bytes 884744 | tf_op jit(solution)/shard_map/ppermute | solution.py:307

commit v11 on v9

--- a/solution.py
+++ b/solution.py
@@ -250,22 +250,22 @@
     lags, rows, width = same.shape
     lane = lax.broadcasted_iota(jnp.int32, (rows, 128), 1) < 64
     copies = []
-    for half in range(width // 128):
-        span = slice(half * 128, (half + 1) * 128)
-        for lag in range(lags):
-            here = same[lag, :, span] * (1.0 / SCALE) if flip else same[lag, :, span]
-            there = cross[lag, :, span] * (1.0 / SCALE)
-            one = jnp.where(low, here, there)
-            two = jnp.where(low, there, here)
-            tiles[half * 2, lag] = jnp.where(lane, one, pltpu.roll(two, 64, axis=1))
-            tiles[half * 2 + 1, lag] = jnp.where(lane, pltpu.roll(one, 64, axis=1), two)
-        for k, to_x in enumerate((here_x, here_x ^ 2)):
-            at = pl.multiple_of((half * 4 + to_x) * 128, 128)
-            tile = half * 2 + k
-            copies.append(
-                pltpu.make_async_copy(tiles.at[tile], out.at[:, :, pl.ds(at, 128)], sems.at[tile])
-            )
-            copies[-1].start()
+    for group in range(0, lags, 3):
+        for half in range(width // 128):
+            span = slice(half * 128, (half + 1) * 128)
+            for lag in range(group, group + 3):
+                here = same[lag, :, span] * (1.0 / SCALE) if flip else same[lag, :, span]
+                there = cross[lag, :, span] * (1.0 / SCALE)
+                one = jnp.where(low, here, there)
+                two = jnp.where(low, there, here)
+                tiles[half * 2, lag] = jnp.where(lane, one, pltpu.roll(two, 64, axis=1))
+                tiles[half * 2 + 1, lag] = jnp.where(lane, pltpu.roll(one, 64, axis=1), two)
+            for k, to_x in enumerate((here_x, here_x ^ 2)):
+                at = pl.multiple_of((half * 4 + to_x) * 128, 128)
+                source = tiles.at[half * 2 + k, pl.ds(group, 3)]
+                target = out.at[pl.ds(group, 3), :, pl.ds(at, 128)]
+                copies.append(pltpu.make_async_copy(source, target, sems.at[len(copies)]))
+                copies[-1].start()
     for copy in copies:
         copy.wait()
 
@@ -286,7 +286,7 @@
         input_output_aliases={3: 0} if base else {},
         scratch_shapes=[
             pltpu.VMEM((width // 64, lags, rows, 128), jnp.float32),
-            pltpu.SemaphoreType.DMA((width // 64,)),
+            pltpu.SemaphoreType.DMA((width // 64 * (lags // 3),)),
         ],
         compiler_params=pltpu.CompilerParams(vmem_limit_bytes=8 * MB),
         name="join",
@@ -335,8 +335,8 @@
     taps = taps.reshape(1, -1)
     parts = lax.all_gather(raw, ("yl", "core"), axis=0, tiled=False)
     given = run_piece_filter(place, taps, parts)
-    base = jnp.concatenate([spread(given, 0), spread(given, 2)], axis=0)
-    order = (0, 1, 2, 3)
+    base = jnp.concatenate([spread(given, 2), spread(given, 0)], axis=0)
+    order = (2, 3, 0, 1)
     units, steps = [base], [[(part, 0) for part in order]]
     first = (around(base, "z", 1), around(base, "z", -1))
     second = (around(first[0], "z", 1), around(first[1], "z", -1))

time: 83 us -> 81.5 us (0.982)
  waiting for transfers between devices: 19.6 us -> 18.1 us
    ppermute x8, waiting for transfers between devices: 15.1 us -> 13 us  [around(): lax.ppermute(value, axis, [(i, (i + step) % size) for i in range(size)])]
    ppermute x2, waiting for transfers between devices: 0.01 us -> 1.29 us  [spread(): return lax.ppermute(value, ('z', 'x', 'yl', 'core'), pairs)]
  transfers between devices with their start and end apart: 16 -> 16, of which waited for: 6 -> 8; matrix products, arithmetic and copies ran while one was open for 0% -> 0% of each run, Pallas kernels for 17% -> 17%
where the time goes in v11:
time: 81.5 us; the launch traced here: 81.4 us
  starting transfers between devices  34.3 us (42%)
  Pallas kernels  19.4 us (24%)
  waiting for transfers between devices  18.1 us (22%)
  blocking collectives  7.47 us (9%)
  between operations  0.99 us (1%)
    ppermute x8, starting transfers between devices, around(): lax.ppermute(value, axis, [(i, (i + step) % size) for i in range(size)])  13.2 us
    ppermute x8, waiting for transfers between devices, around(): lax.ppermute(value, axis, [(i, (i + step) % size) for i in range(size)])  13 us
    ppermute x2, starting transfers between devices, spread(): return lax.ppermute(value, ('z', 'x', 'yl', 'core'), pairs)  9.94 us
    all_gather x1, blocking collectives, shards(): parts = lax.all_gather(raw, ('yl', 'core'), axis=0, tiled=False)  7.47 us
    pallas_call x4, Pallas kernels, run_weigh(): pl.pallas_call(body, in_specs=[vmem] * 4, out_specs=vmem, out_shape=jax.S...  5.74 us
    pallas_call x4, Pallas kernels, run_lags(): pl.pallas_call(lag_kernel, in_specs=[vmem], out_specs=[vmem, vmem], out_s...  5.05 us
    ppermute x1, starting transfers between devices, cross_xy(): return lax.ppermute(value, ('x', 'yh'), [(i, i ^ 3) for i in range(8)])  3.85 us
    ppermute x2, starting transfers between devices, cross_y(): return lax.ppermute(value, 'yh', [(0, 1), (1, 0)])  3.84 us
  transfers between devices with their start and end apart: 16, of which 8 were waited for; matrix products, arithmetic and copies ran while one was open for 0% of the time, Pallas kernels for 17%

profile of v11, /device:TPU:2, one launch (start us, length us, event | category | flops | bytes accessed | tf_op | source)
XLA Modules:
  0.0 81.4 jit_solution(10619725623467089464)
XLA Ops:
  0.6 7.5 %all-gather = bf16[256,1024]{1,0:T(8,128)(2,1)S(1)} all-gather(bf16[64,1024]{1,0:T(8,128)(2,1)} %param.2), channel_id=2, replica_groups=mesh['z'=8,'x'=4,'yh'=2,'yl'=2,'core'=2] {'yl','core'}, dimensions={0}, use_global_device_ids=true | all-gather | bytes 655360 | tf_op jit(solution)/shard_map/all_gather | solution.py:336
  8.8 1.1 %pieces.1 = bf16[2,8,4096]{2,1,0:T(8,128)(2,1)S(1)} custom-call(s32[5]{0:T(128)S(1)} %stack.20.place.refs_0_, f32[1,65]{1,0:T(1,128)S(1)} %bitcast.8, bf16[4,64,1024]{2,1,0:T(8,128)(2,1)S(1)} %bitcast.6), custom_call_target="tpu_custom_call" | custom-call | tf_op jit(solution)/shard_map/pieces/pallas_call | solution.py:66
  10.0 8.4 %collective-permute-start.1 = (bf16[2,8,4096]{2,1,0:T(8,128)(2,1)S(1)}, bf16[2,8,4096]{2,1,0:T(8,128)(2,1)S(1)}, u32[]{:S(2)}, u32[]{:S(2)}) collective-permute-start(bf16[2,8,4096]{2,1,0:T(8,128)(2,1)S(1)} %pieces.1), channel_id=1, source_target_pairs={{0,176},{1,208},{2,240},{3,16},{8,184},{9,216},{10,248},{11,24},{1... | collective-permute-start | bytes 393224 | tf_op jit(solution)/shard_map/ppermute | solution.py:322
  18.4 1.5 %collective-permute-start.2 = (bf16[2,8,4096]{2,1,0:T(8,128)(2,1)S(1)}, bf16[2,8,4096]{2,1,0:T(8,128)(2,1)S(1)}, u32[]{:S(2)}, u32[]{:S(2)}) collective-permute-start(bf16[2,8,4096]{2,1,0:T(8,128)(2,1)S(1)} %pieces.1), channel_id=1, source_target_pairs={{0,160},{1,192},{2,224},{3,0},{8,168},{9,200},{10,232},{11,8},{16,... | collective-permute-start | bytes 393224 | tf_op jit(solution)/shard_map/ppermute | solution.py:322
  19.9 2.7 %rows.1 = (bf16[64,4096]{1,0:T(8,128)(2,1)S(1)}, bf16[64,1024]{1,0:T(8,128)(2,1)}) custom-call(s32[5]{0:T(128)S(1)} %stack.20.place.refs_0_, f32[1,65]{1,0:T(1,128)S(1)} %bitcast.9, bf16[4,64,1024]{2,1,0:T(8,128)(2,1)S(1)} %bitcast.7), custom_call_target="tpu_custom_call" | custom-call | flops 1073741824 | bytes 4194304 | tf_op jit(solution)/shard_map/rows/pallas_call | solution.py:103
  22.6 2.9 %collective-permute-start = (bf16[64,4096]{1,0:T(8,128)(2,1)S(1)}, bf16[64,4096]{1,0:T(8,128)(2,1)S(1)}, u32[]{:S(2)}, u32[]{:S(2)}) collective-permute-start(bf16[64,4096]{1,0:T(8,128)(2,1)S(1)} %get-tuple-element.44.rows_ref), channel_id=1, source_target_pairs={{0,4},{4,0},{1,5},{5,1},{2,6},{6,2},{3,7},{7,3},{8,12},{12,8},{9,1... | collective-permute-start | bytes 1572872 | tf_op jit(solution)/shard_map/ppermute | solution.py:302
  25.6 1.3 %collective-permute-done.2 = bf16[2,8,4096]{2,1,0:T(8,128)(2,1)S(1)} collective-permute-done((bf16[2,8,4096]{2,1,0:T(8,128)(2,1)S(1)}, bf16[2,8,4096]{2,1,0:T(8,128)(2,1)S(1)}, u32[]{:S(2)}, u32[]{:S(2)}) %collective-permute-start.2) | collective-permute-done | bytes 131104 | tf_op jit(solution)/shard_map/ppermute | solution.py:322
  27.0 3.2 %collective-permute-start.4 = (bf16[4,8,4096]{2,1,0:T(8,128)(2,1)S(1)}, bf16[4,8,4096]{2,1,0:T(8,128)(2,1)S(1)}, u32[]{:S(2)}, u32[]{:S(2)}) collective-permute-start(bf16[4,8,4096]{2,1,0:T(8,128)(2,1)S(1)} %constant_dynamic-update-slice_fusion.refs_1_), channel_id=1, source_target_pairs={{0,224},{32,0},{64,32},{96,64},{128,96},{160,128},{192,160},{224,1... | collective-permute-start | bytes 786440 | tf_op jit(solution)/shard_map/ppermute | solution.py:298
  30.2 1.4 %collective-permute-start.10 = (bf16[64,4096]{1,0:T(8,128)(2,1)S(1)}, bf16[64,4096]{1,0:T(8,128)(2,1)S(1)}, u32[]{:S(2)}, u32[]{:S(2)}) collective-permute-start(bf16[64,4096]{1,0:T(8,128)(2,1)S(1)} %get-tuple-element.44.rows_ref), channel_id=1, source_target_pairs={{0,8},{8,0},{16,24},{24,16},{1,9},{9,1},{17,25},{25,17},{2,10},{10... | collective-permute-start | bytes 1572872 | tf_op jit(solution)/shard_map/ppermute | solution.py:306
  31.6 3.8 %collective-permute-done.3.refs_2_ = bf16[4,8,4096]{2,1,0:T(8,128)(2,1)S(1)} collective-permute-done((bf16[4,8,4096]{2,1,0:T(8,128)(2,1)S(1)}, bf16[4,8,4096]{2,1,0:T(8,128)(2,1)S(1)}, u32[]{:S(2)}, u32[]{:S(2)}) %collective-permute-start.3) | collective-permute-done | bytes 262176 | tf_op jit(solution)/shard_map/ppermute | solution.py:298
  35.5 3.2 %collective-permute-start.8 = (bf16[4,8,4096]{2,1,0:T(8,128)(2,1)S(1)}, bf16[4,8,4096]{2,1,0:T(8,128)(2,1)S(1)}, u32[]{:S(2)}, u32[]{:S(2)}) collective-permute-start(bf16[4,8,4096]{2,1,0:T(8,128)(2,1)S(1)} %collective-permute-done.4.refs_3_), channel_id=1, source_target_pairs={{0,224},{32,0},{64,32},{96,64},{128,96},{160,128},{192,160},{224,1... | collective-permute-start | bytes 786440 | tf_op jit(solution)/shard_map/ppermute | solution.py:298
  38.7 1.4 %collective-permute-start.5 = (bf16[64,4096]{1,0:T(8,128)(2,1)S(1)}, bf16[64,4096]{1,0:T(8,128)(2,1)S(1)}, u32[]{:S(2)}, u32[]{:S(2)}) collective-permute-start(bf16[64,4096]{1,0:T(8,128)(2,1)S(1)} %collective-permute-done.rows_ref), channel_id=1, source_target_pairs={{0,8},{8,0},{16,24},{24,16},{1,9},{9,1},{17,25},{25,17},{2,10},{10... | collective-permute-start | bytes 1572872 | tf_op jit(solution)/shard_map/ppermute | solution.py:306
  40.1 1.3 %lags.4 = (bf16[9,64,4096]{2,1,0:T(8,128)(2,1)S(1)}, f32[64,128]{1,0:T(8,128)S(1)}) custom-call(bf16[64,4096]{1,0:T(8,128)(2,1)S(1)} %collective-permute-done.rows_ref), custom_call_target="tpu_custom_call" | custom-call | flops 10485760 | bytes 6291456 | tf_op jit(solution)/shard_map/lags/pallas_call | solution.py:144
  41.4 3.4 %collective-permute-done.6.refs_4_ = bf16[4,8,4096]{2,1,0:T(8,128)(2,1)S(1)} collective-permute-done((bf16[4,8,4096]{2,1,0:T(8,128)(2,1)S(1)}, bf16[4,8,4096]{2,1,0:T(8,128)(2,1)S(1)}, u32[]{:S(2)}, u32[]{:S(2)}) %collective-permute-start.6) | collective-permute-done | bytes 262176 | tf_op jit(solution)/shard_map/ppermute | solution.py:298
  44.8 3.2 %collective-permute-start.9 = (bf16[4,8,4096]{2,1,0:T(8,128)(2,1)S(1)}, bf16[4,8,4096]{2,1,0:T(8,128)(2,1)S(1)}, u32[]{:S(2)}, u32[]{:S(2)}) collective-permute-start(bf16[4,8,4096]{2,1,0:T(8,128)(2,1)S(1)} %collective-permute-done.8.refs_5_), channel_id=1, source_target_pairs={{0,224},{32,0},{64,32},{96,64},{128,96},{160,128},{192,160},{224,1... | collective-permute-start | bytes 786440 | tf_op jit(solution)/shard_map/ppermute | solution.py:298
  48.1 1.3 %lags.6 = (bf16[9,64,4096]{2,1,0:T(8,128)(2,1)S(1)}, f32[64,128]{1,0:T(8,128)S(1)}) custom-call(bf16[64,4096]{1,0:T(8,128)(2,1)S(1)} %collective-permute-done.10.rows_ref), custom_call_target="tpu_custom_call" | custom-call | flops 10485760 | bytes 6291456 | tf_op jit(solution)/shard_map/lags/pallas_call | solution.py:144
  49.3 4.2 %collective-permute-done.7.refs_6_ = bf16[4,8,4096]{2,1,0:T(8,128)(2,1)S(1)} collective-permute-done((bf16[4,8,4096]{2,1,0:T(8,128)(2,1)S(1)}, bf16[4,8,4096]{2,1,0:T(8,128)(2,1)S(1)}, u32[]{:S(2)}, u32[]{:S(2)}) %collective-permute-start.7) | collective-permute-done | bytes 262176 | tf_op jit(solution)/shard_map/ppermute | solution.py:298
  53.7 3.3 %collective-permute-start.12 = (bf16[2,8,4096]{2,1,0:T(8,128)(2,1)S(1)}, bf16[2,8,4096]{2,1,0:T(8,128)(2,1)S(1)}, u32[]{:S(2)}, u32[]{:S(2)}) collective-permute-start(bf16[2,8,4096]{2,1,0:T(8,128)(2,1)S(1)} %slice.7), channel_id=1, source_target_pairs={{0,224},{32,0},{64,32},{96,64},{128,96},{160,128},{192,160},{224,1... | collective-permute-start | bytes 393224 | tf_op jit(solution)/shard_map/ppermute | solution.py:298
  57.0 1.3 %lags.5 = (bf16[9,64,4096]{2,1,0:T(8,128)(2,1)S(1)}, f32[64,128]{1,0:T(8,128)S(1)}) custom-call(bf16[64,4096]{1,0:T(8,128)(2,1)S(1)} %collective-permute-done.5.rows_ref), custom_call_target="tpu_custom_call" | custom-call | flops 10485760 | bytes 6291456 | tf_op jit(solution)/shard_map/lags/pallas_call | solution.py:144
  58.2 1.6 %collective-permute-done.11.refs_8_ = bf16[2,8,4096]{2,1,0:T(8,128)(2,1)S(1)} collective-permute-done((bf16[2,8,4096]{2,1,0:T(8,128)(2,1)S(1)}, bf16[2,8,4096]{2,1,0:T(8,128)(2,1)S(1)}, u32[]{:S(2)}, u32[]{:S(2)}) %collective-permute-start.11) | collective-permute-done | bytes 131104 | tf_op jit(solution)/shard_map/ppermute | solution.py:298
  59.8 1.2 %columns.1 = (bf16[32,8,4096]{2,1,0:T(8,128)(2,1)S(1)}, f32[8,256]{1,0:T(8,128)S(1)}) custom-call(s32[5]{0:T(128)S(1)} %stack.20.place.refs_0_, bf16[4,8,4096]{2,1,0:T(8,128)(2,1)S(1)} %constant_dynamic-update-slice_fusion.refs_1_, bf16[4,8,4096]{2,1,0:T(8,128)(2,1)S(1)} %collective-permute-done.3.refs_2_, ...), custom_call_target="tpu_custom_call" | custom-call | flops 8388608 | bytes 4194304 | tf_op jit(solution)/shard_map/columns/pallas_call | solution.py:196
  61.0 1.4 %weigh.6 = f32[9,64,256]{2,1,0:T(8,128)S(1)} custom-call(bf16[9,64,4096]{2,1,0:T(8,128)(2,1)S(1)} %get-tuple-element.35.refs_0_, f32[64,128]{1,0:T(8,128)S(1)} %get-tuple-element.36.refs_1_, bf16[32,8,4096]{2,1,0:T(8,128)(2,1)S(1)} %get-tuple-element.47.refs_2_, f32[8,256]{1,0:T(8,128)S(1)} %get-tuple-element.48.refs_3_), custom_call_target="tpu_custom_call" | custom-call | flops 1207959552 | bytes 589824 | tf_op jit(solution)/shard_map/weigh/pallas_call | solution.py:231
  62.5 3.9 %collective-permute-start.15 = (f16[9,64,256]{2,1,0:T(8,128)(2,1)S(1)}, f16[9,64,256]{2,1,0:T(8,128)(2,1)S(1)}, u32[]{:S(2)}, u32[]{:S(2)}) collective-permute-start(f16[9,64,256]{2,1,0:T(8,128)(2,1)S(1)} %convert_element_type.19), channel_id=1, source_target_pairs={{0,12},{4,8},{8,4},{12,0},{16,28},{20,24},{24,20},{28,16},{1,13},{... | collective-permute-start | bytes 884744 | tf_op jit(solution)/shard_map/ppermute | solution.py:310
  66.4 1.4 %weigh.7 = f32[9,64,256]{2,1,0:T(8,128)S(1)} custom-call(bf16[9,64,4096]{2,1,0:T(8,128)(2,1)S(1)} %get-tuple-element.39.refs_0_, f32[64,128]{1,0:T(8,128)S(1)} %get-tuple-element.40.refs_1_, bf16[32,8,4096]{2,1,0:T(8,128)(2,1)S(1)} %get-tuple-element.47.refs_2_, f32[8,256]{1,0:T(8,128)S(1)} %get-tuple-element.48.refs_3_), custom_call_target="tpu_custom_call" | custom-call | flops 1207959552 | bytes 589824 | tf_op jit(solution)/shard_map/weigh/pallas_call | solution.py:231
  68.6 1.4 %weigh.5 = f32[9,64,256]{2,1,0:T(8,128)S(1)} custom-call(bf16[9,64,4096]{2,1,0:T(8,128)(2,1)S(1)} %get-tuple-element.30.refs_0_, f32[64,128]{1,0:T(8,128)S(1)} %get-tuple-element.31.refs_1_, bf16[32,8,4096]{2,1,0:T(8,128)(2,1)S(1)} %get-tuple-element.47.refs_2_, f32[8,256]{1,0:T(8,128)S(1)} %get-tuple-element.48.refs_3_), custom_call_target="tpu_custom_call" | custom-call | flops 1207959552 | bytes 589824 | tf_op jit(solution)/shard_map/weigh/pallas_call | solution.py:231
  70.1 0.9 %collective-permute-start.13 = (f16[9,64,256]{2,1,0:T(8,128)(2,1)S(1)}, f16[9,64,256]{2,1,0:T(8,128)(2,1)S(1)}, u32[]{:S(2)}, u32[]{:S(2)}) collective-permute-start(f16[9,64,256]{2,1,0:T(8,128)(2,1)S(1)} %convert_element_type.18), channel_id=1, source_target_pairs={{0,4},{4,0},{1,5},{5,1},{2,6},{6,2},{3,7},{7,3},{8,12},{12,8},{9,1... | collective-permute-start | bytes 884744 | tf_op jit(solution)/shard_map/ppermute | solution.py:302
  71.0 1.3 %lags.7 = (bf16[9,64,4096]{2,1,0:T(8,128)(2,1)S(1)}, f32[64,128]{1,0:T(8,128)S(1)}) custom-call(bf16[64,4096]{1,0:T(8,128)(2,1)S(1)} %get-tuple-element.44.rows_ref), custom_call_target="tpu_custom_call" | custom-call | flops 10485760 | bytes 6291456 | tf_op jit(solution)/shard_map/lags/pallas_call | solution.py:144
  72.3 1.4 %weigh.4.refs_1_ = f32[9,64,256]{2,1,0:T(8,128)S(1)} custom-call(bf16[9,64,4096]{2,1,0:T(8,128)(2,1)S(1)} %get-tuple-element.45.refs_0_, f32[64,128]{1,0:T(8,128)S(1)} %get-tuple-element.46.refs_1_, bf16[32,8,4096]{2,1,0:T(8,128)(2,1)S(1)} %get-tuple-element.47.refs_2_, f32[8,256]{1,0:T(8,128)S(1)} %get-tuple-element.48.refs_3_), custom_call_target="tpu_custom_call" | custom-call | flops 1207959552 | bytes 589824 | tf_op jit(solution)/shard_map/weigh/pallas_call | solution.py:231
  73.7 0.7 collective-permute-done.15
  74.5 2.9 %collective-permute-done.14 = f16[9,64,256]{2,1,0:T(8,128)(2,1)S(1)} collective-permute-done((f16[9,64,256]{2,1,0:T(8,128)(2,1)S(1)}, f16[9,64,256]{2,1,0:T(8,128)(2,1)S(1)}, u32[]{:S(2)}, u32[]{:S(2)}) %collective-permute-start.14) | collective-permute-done | bytes 294944 | tf_op jit(solution)/shard_map/ppermute | solution.py:306
  77.5 1.8 %join.2.refs_3_ = f32[9,64,1024]{2,1,0:T(8,128)} custom-call(s32[5]{0:T(128)S(1)} %stack.20.place.refs_0_, f32[9,64,256]{2,1,0:T(8,128)S(1)} %convert_element_type.22.refs_1_, f32[9,64,256]{2,1,0:T(8,128)S(1)} %convert_element_type.21.refs_2_), custom_call_target="tpu_custom_call" | custom-call | tf_op jit(solution)/shard_map/join/pallas_call | solution.py:281
  79.4 1.8 %join.3 = f32[9,64,1024]{2,1,0:T(8,128)} custom-call(s32[5]{0:T(128)S(1)} %stack.20.place.refs_0_, f32[9,64,256]{2,1,0:T(8,128)S(1)} %weigh.4.refs_1_, f32[9,64,256]{2,1,0:T(8,128)S(1)} %convert_element_type.23.refs_2_, f32[9,64,1024]{2,1,0:T(8,128)} %join.2.refs_3_), custom_call_target="tpu_custom_call", output_to_operand_aliasing={{}: (3, {})} | custom-call | tf_op jit(solution)/shard_map/join/pallas_call | solution.py:281
  (27 shorter events, 2.1 us)
Async XLA Ops:
  8.2 0.7 copy-start
  10.0 15.6 %collective-permute-start.1 = (bf16[2,8,4096]{2,1,0:T(8,128)(2,1)S(1)}, bf16[2,8,4096]{2,1,0:T(8,128)(2,1)S(1)}, u32[]{:S(2)}, u32[]{:S(2)}) collective-permute-start(bf16[2,8,4096]{2,1,0:T(8,128)(2,1)S(1)} %pieces.1), channel_id=1, source_target_pairs={{0,176},{1,208},{2,240},{3,16},{8,184},{9,216},{10,248},{11,24},{1... | collective-permute-start | bytes 393224 | tf_op jit(solution)/shard_map/ppermute | solution.py:322
  18.4 8.5 %collective-permute-start.2 = (bf16[2,8,4096]{2,1,0:T(8,128)(2,1)S(1)}, bf16[2,8,4096]{2,1,0:T(8,128)(2,1)S(1)}, u32[]{:S(2)}, u32[]{:S(2)}) collective-permute-start(bf16[2,8,4096]{2,1,0:T(8,128)(2,1)S(1)} %pieces.1), channel_id=1, source_target_pairs={{0,160},{1,192},{2,224},{3,0},{8,168},{9,200},{10,232},{11,8},{16,... | collective-permute-start | bytes 393224 | tf_op jit(solution)/shard_map/ppermute | solution.py:322
  22.6 16.1 %collective-permute-start = (bf16[64,4096]{1,0:T(8,128)(2,1)S(1)}, bf16[64,4096]{1,0:T(8,128)(2,1)S(1)}, u32[]{:S(2)}, u32[]{:S(2)}) collective-permute-start(bf16[64,4096]{1,0:T(8,128)(2,1)S(1)} %get-tuple-element.44.rows_ref), channel_id=1, source_target_pairs={{0,4},{4,0},{1,5},{5,1},{2,6},{6,2},{3,7},{7,3},{8,12},{12,8},{9,1... | collective-permute-start | bytes 1572872 | tf_op jit(solution)/shard_map/ppermute | solution.py:302
  26.9 8.6 %collective-permute-start.3 = (bf16[4,8,4096]{2,1,0:T(8,128)(2,1)S(1)}, bf16[4,8,4096]{2,1,0:T(8,128)(2,1)S(1)}, u32[]{:S(2)}, u32[]{:S(2)}) collective-permute-start(bf16[4,8,4096]{2,1,0:T(8,128)(2,1)S(1)} %constant_dynamic-update-slice_fusion.refs_1_), channel_id=1, source_target_pairs={{0,32},{32,64},{64,96},{96,128},{128,160},{160,192},{192,224},{224... | collective-permute-start | bytes 786440 | tf_op jit(solution)/shard_map/ppermute | solution.py:298
  27.0 8.5 %collective-permute-start.4 = (bf16[4,8,4096]{2,1,0:T(8,128)(2,1)S(1)}, bf16[4,8,4096]{2,1,0:T(8,128)(2,1)S(1)}, u32[]{:S(2)}, u32[]{:S(2)}) collective-permute-start(bf16[4,8,4096]{2,1,0:T(8,128)(2,1)S(1)} %constant_dynamic-update-slice_fusion.refs_1_), channel_id=1, source_target_pairs={{0,224},{32,0},{64,32},{96,64},{128,96},{160,128},{192,160},{224,1... | collective-permute-start | bytes 786440 | tf_op jit(solution)/shard_map/ppermute | solution.py:298
  30.2 17.9 %collective-permute-start.10 = (bf16[64,4096]{1,0:T(8,128)(2,1)S(1)}, bf16[64,4096]{1,0:T(8,128)(2,1)S(1)}, u32[]{:S(2)}, u32[]{:S(2)}) collective-permute-start(bf16[64,4096]{1,0:T(8,128)(2,1)S(1)} %get-tuple-element.44.rows_ref), channel_id=1, source_target_pairs={{0,8},{8,0},{16,24},{24,16},{1,9},{9,1},{17,25},{25,17},{2,10},{10... | collective-permute-start | bytes 1572872 | tf_op jit(solution)/shard_map/ppermute | solution.py:306
  35.5 9.4 %collective-permute-start.6 = (bf16[4,8,4096]{2,1,0:T(8,128)(2,1)S(1)}, bf16[4,8,4096]{2,1,0:T(8,128)(2,1)S(1)}, u32[]{:S(2)}, u32[]{:S(2)}) collective-permute-start(bf16[4,8,4096]{2,1,0:T(8,128)(2,1)S(1)} %collective-permute-done.3.refs_2_), channel_id=1, source_target_pairs={{0,32},{32,64},{64,96},{96,128},{128,160},{160,192},{192,224},{224... | collective-permute-start | bytes 786440 | tf_op jit(solution)/shard_map/ppermute | solution.py:298
  35.5 9.4 %collective-permute-start.8 = (bf16[4,8,4096]{2,1,0:T(8,128)(2,1)S(1)}, bf16[4,8,4096]{2,1,0:T(8,128)(2,1)S(1)}, u32[]{:S(2)}, u32[]{:S(2)}) collective-permute-start(bf16[4,8,4096]{2,1,0:T(8,128)(2,1)S(1)} %collective-permute-done.4.refs_3_), channel_id=1, source_target_pairs={{0,224},{32,0},{64,32},{96,64},{128,96},{160,128},{192,160},{224,1... | collective-permute-start | bytes 786440 | tf_op jit(solution)/shard_map/ppermute | solution.py:298
  38.7 18.3 %collective-permute-start.5 = (bf16[64,4096]{1,0:T(8,128)(2,1)S(1)}, bf16[64,4096]{1,0:T(8,128)(2,1)S(1)}, u32[]{:S(2)}, u32[]{:S(2)}) collective-permute-start(bf16[64,4096]{1,0:T(8,128)(2,1)S(1)} %collective-permute-done.rows_ref), channel_id=1, source_target_pairs={{0,8},{8,0},{16,24},{24,16},{1,9},{9,1},{17,25},{25,17},{2,10},{10... | collective-permute-start | bytes 1572872 | tf_op jit(solution)/shard_map/ppermute | solution.py:306
  44.8 8.7 %collective-permute-start.7 = (bf16[4,8,4096]{2,1,0:T(8,128)(2,1)S(1)}, bf16[4,8,4096]{2,1,0:T(8,128)(2,1)S(1)}, u32[]{:S(2)}, u32[]{:S(2)}) collective-permute-start(bf16[4,8,4096]{2,1,0:T(8,128)(2,1)S(1)} %collective-permute-done.6.refs_4_), channel_id=1, source_target_pairs={{0,32},{32,64},{64,96},{96,128},{128,160},{160,192},{192,224},{224... | collective-permute-start | bytes 786440 | tf_op jit(solution)/shard_map/ppermute | solution.py:298
  44.8 8.8 %collective-permute-start.9 = (bf16[4,8,4096]{2,1,0:T(8,128)(2,1)S(1)}, bf16[4,8,4096]{2,1,0:T(8,128)(2,1)S(1)}, u32[]{:S(2)}, u32[]{:S(2)}) collective-permute-start(bf16[4,8,4096]{2,1,0:T(8,128)(2,1)S(1)} %collective-permute-done.8.refs_5_), channel_id=1, source_target_pairs={{0,224},{32,0},{64,32},{96,64},{128,96},{160,128},{192,160},{224,1... | collective-permute-start | bytes 786440 | tf_op jit(solution)/shard_map/ppermute | solution.py:298
  53.6 6.3 %collective-permute-start.11 = (bf16[2,8,4096]{2,1,0:T(8,128)(2,1)S(1)}, bf16[2,8,4096]{2,1,0:T(8,128)(2,1)S(1)}, u32[]{:S(2)}, u32[]{:S(2)}) collective-permute-start(bf16[2,8,4096]{2,1,0:T(8,128)(2,1)S(1)} %slice.6), channel_id=1, source_target_pairs={{0,32},{32,64},{64,96},{96,128},{128,160},{160,192},{192,224},{224... | collective-permute-start | bytes 393224 | tf_op jit(solution)/shard_map/ppermute | solution.py:298
  53.7 6.1 %collective-permute-start.12 = (bf16[2,8,4096]{2,1,0:T(8,128)(2,1)S(1)}, bf16[2,8,4096]{2,1,0:T(8,128)(2,1)S(1)}, u32[]{:S(2)}, u32[]{:S(2)}) collective-permute-start(bf16[2,8,4096]{2,1,0:T(8,128)(2,1)S(1)} %slice.7), channel_id=1, source_target_pairs={{0,224},{32,0},{64,32},{96,64},{128,96},{160,128},{192,160},{224,1... | collective-permute-start | bytes 393224 | tf_op jit(solution)/shard_map/ppermute | solution.py:298
  62.5 11.9 %collective-permute-start.15 = (f16[9,64,256]{2,1,0:T(8,128)(2,1)S(1)}, f16[9,64,256]{2,1,0:T(8,128)(2,1)S(1)}, u32[]{:S(2)}, u32[]{:S(2)}) collective-permute-start(f16[9,64,256]{2,1,0:T(8,128)(2,1)S(1)} %convert_element_type.19), channel_id=1, source_target_pairs={{0,12},{4,8},{8,4},{12,0},{16,28},{20,24},{24,20},{28,16},{1,13},{... | collective-permute-start | bytes 884744 | tf_op jit(solution)/shard_map/ppermute | solution.py:310
  67.9 9.5 %collective-permute-start.14 = (f16[9,64,256]{2,1,0:T(8,128)(2,1)S(1)}, f16[9,64,256]{2,1,0:T(8,128)(2,1)S(1)}, u32[]{:S(2)}, u32[]{:S(2)}) collective-permute-start(f16[9,64,256]{2,1,0:T(8,128)(2,1)S(1)} %convert_element_type.20), channel_id=1, source_target_pairs={{0,8},{8,0},{16,24},{24,16},{1,9},{9,1},{17,25},{25,17},{2,10},{10... | collective-permute-start | bytes 884744 | tf_op jit(solution)/shard_map/ppermute | solution.py:306
  70.1 9.3 %collective-permute-start.13 = (f16[9,64,256]{2,1,0:T(8,128)(2,1)S(1)}, f16[9,64,256]{2,1,0:T(8,128)(2,1)S(1)}, u32[]{:S(2)}, u32[]{:S(2)}) collective-permute-start(f16[9,64,256]{2,1,0:T(8,128)(2,1)S(1)} %convert_element_type.18), channel_id=1, source_target_pairs={{0,4},{4,0},{1,5},{5,1},{2,6},{6,2},{3,7},{7,3},{8,12},{12,8},{9,1... | collective-permute-start | bytes 884744 | tf_op jit(solution)/shard_map/ppermute | solution.py:302

commit v12 on v11

--- a/solution.py
+++ b/solution.py
@@ -165,9 +165,9 @@
         emit(lag, -0.5 * jnp.log(1.0 - ratio * ratio))
 
 
-def columns_kernel(steps, place, *refs):
+def columns_kernel(steps, place, lagged, energy, *refs):
     units = refs[: len(steps)]
-    columns, scale = refs[len(steps) :]
+    columns, scale, out = refs[len(steps) :]
     z = place[1]
     slab = place[2]
     for ref, moves in zip(units, steps):
@@ -176,18 +176,22 @@
             e = (up < 4).astype(jnp.int32)
             giver = (3 - jnp.where(up < 4, up, 7 - up)) ^ slab
             columns[e * 16 + (part >> 1) * 8 + giver * 2 + (part & 1)] = ref[k]
-    width = columns.shape[0] * columns.shape[1]
-    for g in range(width // 128):
-        block = columns[g * 16 : (g + 1) * 16].astype(jnp.float32).reshape(128, -1)
+    lags, count, bins = lagged.shape
+    left = lagged[...].reshape(lags * count, bins)
+    right = columns[...].reshape(-1, bins)
+    moments = lax.dot_general(left, right, NT, preferred_element_type=jnp.float32)
+    for g in range(right.shape[0] // 128):
+        block = right[g * 128 : (g + 1) * 128].astype(jnp.float32)
         total = jnp.sum(block * block, axis=1, keepdims=True)
         root = 0.8 / jnp.sqrt(total + 1e-05)
         root = jnp.transpose(jnp.broadcast_to(root, (128, 128)))
         scale[:, g * 128 : (g + 1) * 128] = root[0:8]
-
-
-def run_columns(place, units, steps):
+    emit(moments, energy, scale, SCALE, out)
+
+
+def run_columns(place, rows, units, steps):
     slots = sum(len(moves) for moves in steps)
-    bins = units[0].shape[2]
+    lags, count, bins = rows[0].shape
 
     def body(*refs):
         columns_kernel(steps, *refs)
@@ -195,16 +199,26 @@
     vmem = pl.BlockSpec(memory_space=pltpu.VMEM)
     return pl.pallas_call(
         body,
-        in_specs=[pl.BlockSpec(memory_space=pltpu.SMEM)] + [vmem] * len(units),
-        out_specs=[vmem, vmem],
+        in_specs=[pl.BlockSpec(memory_space=pltpu.SMEM)] + [vmem] * (2 + len(units)),
+        out_specs=[vmem] * 3,
         out_shape=[
             jax.ShapeDtypeStruct((slots, 8, bins), jnp.bfloat16),
             jax.ShapeDtypeStruct((8, slots * 8), jnp.float32),
-        ],
-        compiler_params=pltpu.CompilerParams(vmem_limit_bytes=8 * MB),
-        cost_estimate=pl.CostEstimate(flops=8 * MB, bytes_accessed=4 * MB, transcendentals=0),
+            jax.ShapeDtypeStruct((lags, count, slots * 8), jnp.float32),
+        ],
+        compiler_params=pltpu.CompilerParams(vmem_limit_bytes=8 * MB),
+        cost_estimate=pl.CostEstimate(flops=1 << 30, bytes_accessed=4 * MB, transcendentals=0),
         name="columns",
-    )(place, *units)
+    )(place, *rows, *units)
+
+
+def emit(moments, energy, scale, factor, out):
+    lags, count = out.shape[:2]
+    norms = (1.0 / jnp.sqrt(energy[:, 0:1] + 1e-05)) * scale[0:1, :]
+    for lag in range(lags):
+        ratio = moments[lag * count : (lag + 1) * count] * norms
+        value = -0.5 * jnp.log(1.0 - ratio * ratio)
+        out[lag] = value if factor == 1 else value * factor
 
 
 def weigh_kernel(factor, lagged, energy, columns, scale, out):
@@ -212,11 +226,7 @@
     left = lagged[...].reshape(lags * count, bins)
     right = columns[...].reshape(-1, bins)
     moments = lax.dot_general(left, right, NT, preferred_element_type=jnp.float32)
-    norms = (1.0 / jnp.sqrt(energy[:, 0:1] + 1e-05)) * scale[0:1, :]
-    for lag in range(lags):
-        ratio = moments[lag * count : (lag + 1) * count] * norms
-        value = -0.5 * jnp.log(1.0 - ratio * ratio)
-        out[lag] = value if factor == 1 else value * factor
+    emit(moments, energy, scale, factor, out)
 
 
 def run_weigh(rows, columns, scale, factor):
@@ -353,8 +363,8 @@
         steps += [[(part, -step) for part in order], [(part, step) for part in order]]
     steps += [[(part, 4) for part in order[0:2]], [(part, 4) for part in order[2:4]]]
     far_xy = run_lags(after(row_xy, *third))
-    columns, scale = run_columns(after(place, far_xy), units, steps)
-    send_xy = run_weigh(far_xy, columns, scale, SCALE).astype(SENT)
+    columns, scale, send_xy = run_columns(place, far_xy, units, steps)
+    send_xy = send_xy.astype(SENT)
     send_x = run_weigh(far_x, columns, after(scale, send_xy), SCALE).astype(SENT)
     send_y = run_weigh(far_y, columns, scale, SCALE).astype(SENT)
     came_xy = cross_xy(send_xy)

time: 81.5 us -> 81 us (level)
    pallas_call x4 -> x3, Pallas kernels: 5.74 us -> 4.29 us  [run_weigh(): pl.pallas_call(body, in_specs=[vmem] * 4, out_specs=vmem, out_shape=jax.S...]
    pallas_call x1, Pallas kernels: 1.21 us -> 2.22 us  [run_columns(): pl.pallas_call(body, in_specs=[pl.BlockSpec(memory_space=pltpu.SMEM)] + [...]
where the time goes in v12:
time: 81 us; the launch traced here: 80.9 us
  starting transfers between devices  34.3 us (42%)
  Pallas kernels  19 us (23%)
  waiting for transfers between devices  18.1 us (22%)
  blocking collectives  7.47 us (9%)
  between operations  0.99 us (1%)
    ppermute x8, starting transfers between devices, around(): lax.ppermute(value, axis, [(i, (i + step) % size) for i in range(size)])  13.2 us
    ppermute x8, waiting for transfers between devices, around(): lax.ppermute(value, axis, [(i, (i + step) % size) for i in range(size)])  13 us
    ppermute x2, starting transfers between devices, spread(): return lax.ppermute(value, ('z', 'x', 'yl', 'core'), pairs)  9.94 us
    all_gather x1, blocking collectives, shards(): parts = lax.all_gather(raw, ('yl', 'core'), axis=0, tiled=False)  7.47 us
    pallas_call x4, Pallas kernels, run_lags(): pl.pallas_call(lag_kernel, in_specs=[vmem], out_specs=[vmem, vmem], out_s...  5.05 us
    pallas_call x3, Pallas kernels, run_weigh(): pl.pallas_call(body, in_specs=[vmem] * 4, out_specs=vmem, out_shape=jax.S...  4.29 us
    ppermute x1, starting transfers between devices, cross_xy(): return lax.ppermute(value, ('x', 'yh'), [(i, i ^ 3) for i in range(8)])  3.85 us
    ppermute x2, starting transfers between devices, cross_y(): return lax.ppermute(value, 'yh', [(0, 1), (1, 0)])  3.84 us
  transfers between devices with their start and end apart: 16, of which 8 were waited for; matrix products, arithmetic and copies ran while one was open for 0% of the time, Pallas kernels for 17%

profile of v12, /device:TPU:2, one launch (start us, length us, event | category | flops | bytes accessed | tf_op | source)
XLA Modules:
  0.0 80.9 jit_solution(10495879095020476141)
XLA Ops:
  0.6 7.5 %all-gather = bf16[256,1024]{1,0:T(8,128)(2,1)S(1)} all-gather(bf16[64,1024]{1,0:T(8,128)(2,1)} %param.2), channel_id=2, replica_groups=mesh['z'=8,'x'=4,'yh'=2,'yl'=2,'core'=2] {'yl','core'}, dimensions={0}, use_global_device_ids=true | all-gather | bytes 655360 | tf_op jit(solution)/shard_map/all_gather | solution.py:346
  8.8 1.1 %pieces.1 = bf16[2,8,4096]{2,1,0:T(8,128)(2,1)S(1)} custom-call(s32[5]{0:T(128)S(1)} %stack.20.place.refs_0_, f32[1,65]{1,0:T(1,128)S(1)} %bitcast.8, bf16[4,64,1024]{2,1,0:T(8,128)(2,1)S(1)} %bitcast.6), custom_call_target="tpu_custom_call" | custom-call | tf_op jit(solution)/shard_map/pieces/pallas_call | solution.py:66
  10.0 8.4 %collective-permute-start.1 = (bf16[2,8,4096]{2,1,0:T(8,128)(2,1)S(1)}, bf16[2,8,4096]{2,1,0:T(8,128)(2,1)S(1)}, u32[]{:S(2)}, u32[]{:S(2)}) collective-permute-start(bf16[2,8,4096]{2,1,0:T(8,128)(2,1)S(1)} %pieces.1), channel_id=1, source_target_pairs={{0,176},{1,208},{2,240},{3,16},{8,184},{9,216},{10,248},{11,24},{1... | collective-permute-start | bytes 393224 | tf_op jit(solution)/shard_map/ppermute | solution.py:332
  18.4 1.5 %collective-permute-start.2 = (bf16[2,8,4096]{2,1,0:T(8,128)(2,1)S(1)}, bf16[2,8,4096]{2,1,0:T(8,128)(2,1)S(1)}, u32[]{:S(2)}, u32[]{:S(2)}) collective-permute-start(bf16[2,8,4096]{2,1,0:T(8,128)(2,1)S(1)} %pieces.1), channel_id=1, source_target_pairs={{0,160},{1,192},{2,224},{3,0},{8,168},{9,200},{10,232},{11,8},{16,... | collective-permute-start | bytes 393224 | tf_op jit(solution)/shard_map/ppermute | solution.py:332
  19.9 2.7 %rows.1 = (bf16[64,4096]{1,0:T(8,128)(2,1)S(1)}, bf16[64,1024]{1,0:T(8,128)(2,1)}) custom-call(s32[5]{0:T(128)S(1)} %stack.20.place.refs_0_, f32[1,65]{1,0:T(1,128)S(1)} %bitcast.9, bf16[4,64,1024]{2,1,0:T(8,128)(2,1)S(1)} %bitcast.7), custom_call_target="tpu_custom_call" | custom-call | flops 1073741824 | bytes 4194304 | tf_op jit(solution)/shard_map/rows/pallas_call | solution.py:103
  22.7 2.9 %collective-permute-start = (bf16[64,4096]{1,0:T(8,128)(2,1)S(1)}, bf16[64,4096]{1,0:T(8,128)(2,1)S(1)}, u32[]{:S(2)}, u32[]{:S(2)}) collective-permute-start(bf16[64,4096]{1,0:T(8,128)(2,1)S(1)} %get-tuple-element.43.rows_ref), channel_id=1, source_target_pairs={{0,4},{4,0},{1,5},{5,1},{2,6},{6,2},{3,7},{7,3},{8,12},{12,8},{9,1... | collective-permute-start | bytes 1572872 | tf_op jit(solution)/shard_map/ppermute | solution.py:312
  25.6 1.3 %collective-permute-done.2 = bf16[2,8,4096]{2,1,0:T(8,128)(2,1)S(1)} collective-permute-done((bf16[2,8,4096]{2,1,0:T(8,128)(2,1)S(1)}, bf16[2,8,4096]{2,1,0:T(8,128)(2,1)S(1)}, u32[]{:S(2)}, u32[]{:S(2)}) %collective-permute-start.2) | collective-permute-done | bytes 131104 | tf_op jit(solution)/shard_map/ppermute | solution.py:332
  27.0 3.2 %collective-permute-start.4 = (bf16[4,8,4096]{2,1,0:T(8,128)(2,1)S(1)}, bf16[4,8,4096]{2,1,0:T(8,128)(2,1)S(1)}, u32[]{:S(2)}, u32[]{:S(2)}) collective-permute-start(bf16[4,8,4096]{2,1,0:T(8,128)(2,1)S(1)} %constant_dynamic-update-slice_fusion.refs_3_), channel_id=1, source_target_pairs={{0,224},{32,0},{64,32},{96,64},{128,96},{160,128},{192,160},{224,1... | collective-permute-start | bytes 786440 | tf_op jit(solution)/shard_map/ppermute | solution.py:308
  30.2 1.4 %collective-permute-start.10 = (bf16[64,4096]{1,0:T(8,128)(2,1)S(1)}, bf16[64,4096]{1,0:T(8,128)(2,1)S(1)}, u32[]{:S(2)}, u32[]{:S(2)}) collective-permute-start(bf16[64,4096]{1,0:T(8,128)(2,1)S(1)} %get-tuple-element.43.rows_ref), channel_id=1, source_target_pairs={{0,8},{8,0},{16,24},{24,16},{1,9},{9,1},{17,25},{25,17},{2,10},{10... | collective-permute-start | bytes 1572872 | tf_op jit(solution)/shard_map/ppermute | solution.py:316
  31.6 3.8 %collective-permute-done.3.refs_4_ = bf16[4,8,4096]{2,1,0:T(8,128)(2,1)S(1)} collective-permute-done((bf16[4,8,4096]{2,1,0:T(8,128)(2,1)S(1)}, bf16[4,8,4096]{2,1,0:T(8,128)(2,1)S(1)}, u32[]{:S(2)}, u32[]{:S(2)}) %collective-permute-start.3) | collective-permute-done | bytes 262176 | tf_op jit(solution)/shard_map/ppermute | solution.py:308
  35.5 3.2 %collective-permute-start.8 = (bf16[4,8,4096]{2,1,0:T(8,128)(2,1)S(1)}, bf16[4,8,4096]{2,1,0:T(8,128)(2,1)S(1)}, u32[]{:S(2)}, u32[]{:S(2)}) collective-permute-start(bf16[4,8,4096]{2,1,0:T(8,128)(2,1)S(1)} %collective-permute-done.4.refs_5_), channel_id=1, source_target_pairs={{0,224},{32,0},{64,32},{96,64},{128,96},{160,128},{192,160},{224,1... | collective-permute-start | bytes 786440 | tf_op jit(solution)/shard_map/ppermute | solution.py:308
  38.7 1.4 %collective-permute-start.5 = (bf16[64,4096]{1,0:T(8,128)(2,1)S(1)}, bf16[64,4096]{1,0:T(8,128)(2,1)S(1)}, u32[]{:S(2)}, u32[]{:S(2)}) collective-permute-start(bf16[64,4096]{1,0:T(8,128)(2,1)S(1)} %collective-permute-done.rows_ref), channel_id=1, source_target_pairs={{0,8},{8,0},{16,24},{24,16},{1,9},{9,1},{17,25},{25,17},{2,10},{10... | collective-permute-start | bytes 1572872 | tf_op jit(solution)/shard_map/ppermute | solution.py:316
  40.1 1.3 %lags.4 = (bf16[9,64,4096]{2,1,0:T(8,128)(2,1)S(1)}, f32[64,128]{1,0:T(8,128)S(1)}) custom-call(bf16[64,4096]{1,0:T(8,128)(2,1)S(1)} %collective-permute-done.rows_ref), custom_call_target="tpu_custom_call" | custom-call | flops 10485760 | bytes 6291456 | tf_op jit(solution)/shard_map/lags/pallas_call | solution.py:144
  41.4 3.4 %collective-permute-done.6.refs_6_ = bf16[4,8,4096]{2,1,0:T(8,128)(2,1)S(1)} collective-permute-done((bf16[4,8,4096]{2,1,0:T(8,128)(2,1)S(1)}, bf16[4,8,4096]{2,1,0:T(8,128)(2,1)S(1)}, u32[]{:S(2)}, u32[]{:S(2)}) %collective-permute-start.6) | collective-permute-done | bytes 262176 | tf_op jit(solution)/shard_map/ppermute | solution.py:308
  44.8 3.2 %collective-permute-start.9 = (bf16[4,8,4096]{2,1,0:T(8,128)(2,1)S(1)}, bf16[4,8,4096]{2,1,0:T(8,128)(2,1)S(1)}, u32[]{:S(2)}, u32[]{:S(2)}) collective-permute-start(bf16[4,8,4096]{2,1,0:T(8,128)(2,1)S(1)} %collective-permute-done.8.refs_7_), channel_id=1, source_target_pairs={{0,224},{32,0},{64,32},{96,64},{128,96},{160,128},{192,160},{224,1... | collective-permute-start | bytes 786440 | tf_op jit(solution)/shard_map/ppermute | solution.py:308
  48.1 1.3 %lags.6 = (bf16[9,64,4096]{2,1,0:T(8,128)(2,1)S(1)}, f32[64,128]{1,0:T(8,128)S(1)}) custom-call(bf16[64,4096]{1,0:T(8,128)(2,1)S(1)} %collective-permute-done.10.rows_ref), custom_call_target="tpu_custom_call" | custom-call | flops 10485760 | bytes 6291456 | tf_op jit(solution)/shard_map/lags/pallas_call | solution.py:144
  49.3 4.2 %collective-permute-done.7.refs_8_ = bf16[4,8,4096]{2,1,0:T(8,128)(2,1)S(1)} collective-permute-done((bf16[4,8,4096]{2,1,0:T(8,128)(2,1)S(1)}, bf16[4,8,4096]{2,1,0:T(8,128)(2,1)S(1)}, u32[]{:S(2)}, u32[]{:S(2)}) %collective-permute-start.7) | collective-permute-done | bytes 262176 | tf_op jit(solution)/shard_map/ppermute | solution.py:308
  53.7 3.3 %collective-permute-start.12 = (bf16[2,8,4096]{2,1,0:T(8,128)(2,1)S(1)}, bf16[2,8,4096]{2,1,0:T(8,128)(2,1)S(1)}, u32[]{:S(2)}, u32[]{:S(2)}) collective-permute-start(bf16[2,8,4096]{2,1,0:T(8,128)(2,1)S(1)} %slice.7), channel_id=1, source_target_pairs={{0,224},{32,0},{64,32},{96,64},{128,96},{160,128},{192,160},{224,1... | collective-permute-start | bytes 393224 | tf_op jit(solution)/shard_map/ppermute | solution.py:308
  57.0 1.3 %lags.5 = (bf16[9,64,4096]{2,1,0:T(8,128)(2,1)S(1)}, f32[64,128]{1,0:T(8,128)S(1)}) custom-call(bf16[64,4096]{1,0:T(8,128)(2,1)S(1)} %collective-permute-done.5.rows_ref), custom_call_target="tpu_custom_call" | custom-call | flops 10485760 | bytes 6291456 | tf_op jit(solution)/shard_map/lags/pallas_call | solution.py:144
  58.2 1.6 %collective-permute-done.11.refs_10_ = bf16[2,8,4096]{2,1,0:T(8,128)(2,1)S(1)} collective-permute-done((bf16[2,8,4096]{2,1,0:T(8,128)(2,1)S(1)}, bf16[2,8,4096]{2,1,0:T(8,128)(2,1)S(1)}, u32[]{:S(2)}, u32[]{:S(2)}) %collective-permute-start.11) | collective-permute-done | bytes 131104 | tf_op jit(solution)/shard_map/ppermute | solution.py:308
  59.8 2.2 %columns.1 = (bf16[32,8,4096]{2,1,0:T(8,128)(2,1)S(1)}, f32[8,256]{1,0:T(8,128)S(1)}, f32[9,64,256]{2,1,0:T(8,128)S(1)}) custom-call(s32[5]{0:T(128)S(1)} %stack.20.place.refs_0_, bf16[9,64,4096]{2,1,0:T(8,128)(2,1)S(1)} %get-tuple-element.35.refs_1_, f32[64,128]{1,0:T(8,128)S(1)} %get-tuple-element.36.refs_2_, ...), custom_call_target="tpu_custom_call" | custom-call | flops 1073741824 | bytes 4194304 | tf_op jit(solution)/shard_map/columns/pallas_call | solution.py:200
  62.1 3.9 %collective-permute-start.15 = (f16[9,64,256]{2,1,0:T(8,128)(2,1)S(1)}, f16[9,64,256]{2,1,0:T(8,128)(2,1)S(1)}, u32[]{:S(2)}, u32[]{:S(2)}) collective-permute-start(f16[9,64,256]{2,1,0:T(8,128)(2,1)S(1)} %convert_element_type.19), channel_id=1, source_target_pairs={{0,12},{4,8},{8,4},{12,0},{16,28},{20,24},{24,20},{28,16},{1,13},{... | collective-permute-start | bytes 884744 | tf_op jit(solution)/shard_map/ppermute | solution.py:320
  65.9 1.4 %weigh.5 = f32[9,64,256]{2,1,0:T(8,128)S(1)} custom-call(bf16[9,64,4096]{2,1,0:T(8,128)(2,1)S(1)} %get-tuple-element.38.refs_0_, f32[64,128]{1,0:T(8,128)S(1)} %get-tuple-element.39.refs_1_, bf16[32,8,4096]{2,1,0:T(8,128)(2,1)S(1)} %get-tuple-element.46.refs_2_, f32[8,256]{1,0:T(8,128)S(1)} %get-tuple-element.48.refs_3_), custom_call_target="tpu_custom_call" | custom-call | flops 1207959552 | bytes 589824 | tf_op jit(solution)/shard_map/weigh/pallas_call | solution.py:241
  67.4 0.7 collective-permute-start.14
  68.1 1.4 %weigh.4 = f32[9,64,256]{2,1,0:T(8,128)S(1)} custom-call(bf16[9,64,4096]{2,1,0:T(8,128)(2,1)S(1)} %get-tuple-element.30.refs_0_, f32[64,128]{1,0:T(8,128)S(1)} %get-tuple-element.31.refs_1_, bf16[32,8,4096]{2,1,0:T(8,128)(2,1)S(1)} %get-tuple-element.46.refs_2_, f32[8,256]{1,0:T(8,128)S(1)} %get-tuple-element.48.refs_3_), custom_call_target="tpu_custom_call" | custom-call | flops 1207959552 | bytes 589824 | tf_op jit(solution)/shard_map/weigh/pallas_call | solution.py:241
  69.6 0.9 %collective-permute-start.13 = (f16[9,64,256]{2,1,0:T(8,128)(2,1)S(1)}, f16[9,64,256]{2,1,0:T(8,128)(2,1)S(1)}, u32[]{:S(2)}, u32[]{:S(2)}) collective-permute-start(f16[9,64,256]{2,1,0:T(8,128)(2,1)S(1)} %convert_element_type.18), channel_id=1, source_target_pairs={{0,4},{4,0},{1,5},{5,1},{2,6},{6,2},{3,7},{7,3},{8,12},{12,8},{9,1... | collective-permute-start | bytes 884744 | tf_op jit(solution)/shard_map/ppermute | solution.py:312
  70.5 1.3 %lags.7 = (bf16[9,64,4096]{2,1,0:T(8,128)(2,1)S(1)}, f32[64,128]{1,0:T(8,128)S(1)}) custom-call(bf16[64,4096]{1,0:T(8,128)(2,1)S(1)} %get-tuple-element.43.rows_ref), custom_call_target="tpu_custom_call" | custom-call | flops 10485760 | bytes 6291456 | tf_op jit(solution)/shard_map/lags/pallas_call | solution.py:144
  71.8 1.4 %weigh.3.refs_1_ = f32[9,64,256]{2,1,0:T(8,128)S(1)} custom-call(bf16[9,64,4096]{2,1,0:T(8,128)(2,1)S(1)} %get-tuple-element.44.refs_0_, f32[64,128]{1,0:T(8,128)S(1)} %get-tuple-element.45.refs_1_, bf16[32,8,4096]{2,1,0:T(8,128)(2,1)S(1)} %get-tuple-element.46.refs_2_, f32[8,256]{1,0:T(8,128)S(1)} %get-tuple-element.48.refs_3_), custom_call_target="tpu_custom_call" | custom-call | flops 1207959552 | bytes 589824 | tf_op jit(solution)/shard_map/weigh/pallas_call | solution.py:241
  73.3 0.7 collective-permute-done.15
  74.0 2.9 %collective-permute-done.14 = f16[9,64,256]{2,1,0:T(8,128)(2,1)S(1)} collective-permute-done((f16[9,64,256]{2,1,0:T(8,128)(2,1)S(1)}, f16[9,64,256]{2,1,0:T(8,128)(2,1)S(1)}, u32[]{:S(2)}, u32[]{:S(2)}) %collective-permute-start.14) | collective-permute-done | bytes 294944 | tf_op jit(solution)/shard_map/ppermute | solution.py:316
  77.0 1.8 %join.2.refs_3_ = f32[9,64,1024]{2,1,0:T(8,128)} custom-call(s32[5]{0:T(128)S(1)} %stack.20.place.refs_0_, f32[9,64,256]{2,1,0:T(8,128)S(1)} %convert_element_type.22.refs_1_, f32[9,64,256]{2,1,0:T(8,128)S(1)} %convert_element_type.21.refs_2_), custom_call_target="tpu_custom_call" | custom-call | tf_op jit(solution)/shard_map/join/pallas_call | solution.py:291
  79.0 1.8 %join.3 = f32[9,64,1024]{2,1,0:T(8,128)} custom-call(s32[5]{0:T(128)S(1)} %stack.20.place.refs_0_, f32[9,64,256]{2,1,0:T(8,128)S(1)} %weigh.3.refs_1_, f32[9,64,256]{2,1,0:T(8,128)S(1)} %convert_element_type.23.refs_2_, f32[9,64,1024]{2,1,0:T(8,128)} %join.2.refs_3_), custom_call_target="tpu_custom_call", output_to_operand_aliasing={{}: (3, {})} | custom-call | tf_op jit(solution)/shard_map/join/pallas_call | solution.py:291
  (26 shorter events, 1.4 us)
Async XLA Ops:
  8.2 0.7 copy-start
  10.0 15.6 %collective-permute-start.1 = (bf16[2,8,4096]{2,1,0:T(8,128)(2,1)S(1)}, bf16[2,8,4096]{2,1,0:T(8,128)(2,1)S(1)}, u32[]{:S(2)}, u32[]{:S(2)}) collective-permute-start(bf16[2,8,4096]{2,1,0:T(8,128)(2,1)S(1)} %pieces.1), channel_id=1, source_target_pairs={{0,176},{1,208},{2,240},{3,16},{8,184},{9,216},{10,248},{11,24},{1... | collective-permute-start | bytes 393224 | tf_op jit(solution)/shard_map/ppermute | solution.py:332
  18.4 8.5 %collective-permute-start.2 = (bf16[2,8,4096]{2,1,0:T(8,128)(2,1)S(1)}, bf16[2,8,4096]{2,1,0:T(8,128)(2,1)S(1)}, u32[]{:S(2)}, u32[]{:S(2)}) collective-permute-start(bf16[2,8,4096]{2,1,0:T(8,128)(2,1)S(1)} %pieces.1), channel_id=1, source_target_pairs={{0,160},{1,192},{2,224},{3,0},{8,168},{9,200},{10,232},{11,8},{16,... | collective-permute-start | bytes 393224 | tf_op jit(solution)/shard_map/ppermute | solution.py:332
  22.7 16.1 %collective-permute-start = (bf16[64,4096]{1,0:T(8,128)(2,1)S(1)}, bf16[64,4096]{1,0:T(8,128)(2,1)S(1)}, u32[]{:S(2)}, u32[]{:S(2)}) collective-permute-start(bf16[64,4096]{1,0:T(8,128)(2,1)S(1)} %get-tuple-element.43.rows_ref), channel_id=1, source_target_pairs={{0,4},{4,0},{1,5},{5,1},{2,6},{6,2},{3,7},{7,3},{8,12},{12,8},{9,1... | collective-permute-start | bytes 1572872 | tf_op jit(solution)/shard_map/ppermute | solution.py:312
  26.9 8.6 %collective-permute-start.3 = (bf16[4,8,4096]{2,1,0:T(8,128)(2,1)S(1)}, bf16[4,8,4096]{2,1,0:T(8,128)(2,1)S(1)}, u32[]{:S(2)}, u32[]{:S(2)}) collective-permute-start(bf16[4,8,4096]{2,1,0:T(8,128)(2,1)S(1)} %constant_dynamic-update-slice_fusion.refs_3_), channel_id=1, source_target_pairs={{0,32},{32,64},{64,96},{96,128},{128,160},{160,192},{192,224},{224... | collective-permute-start | bytes 786440 | tf_op jit(solution)/shard_map/ppermute | solution.py:308
  27.0 8.5 %collective-permute-start.4 = (bf16[4,8,4096]{2,1,0:T(8,128)(2,1)S(1)}, bf16[4,8,4096]{2,1,0:T(8,128)(2,1)S(1)}, u32[]{:S(2)}, u32[]{:S(2)}) collective-permute-start(bf16[4,8,4096]{2,1,0:T(8,128)(2,1)S(1)} %constant_dynamic-update-slice_fusion.refs_3_), channel_id=1, source_target_pairs={{0,224},{32,0},{64,32},{96,64},{128,96},{160,128},{192,160},{224,1... | collective-permute-start | bytes 786440 | tf_op jit(solution)/shard_map/ppermute | solution.py:308
  30.2 17.9 %collective-permute-start.10 = (bf16[64,4096]{1,0:T(8,128)(2,1)S(1)}, bf16[64,4096]{1,0:T(8,128)(2,1)S(1)}, u32[]{:S(2)}, u32[]{:S(2)}) collective-permute-start(bf16[64,4096]{1,0:T(8,128)(2,1)S(1)} %get-tuple-element.43.rows_ref), channel_id=1, source_target_pairs={{0,8},{8,0},{16,24},{24,16},{1,9},{9,1},{17,25},{25,17},{2,10},{10... | collective-permute-start | bytes 1572872 | tf_op jit(solution)/shard_map/ppermute | solution.py:316
  35.5 9.4 %collective-permute-start.6 = (bf16[4,8,4096]{2,1,0:T(8,128)(2,1)S(1)}, bf16[4,8,4096]{2,1,0:T(8,128)(2,1)S(1)}, u32[]{:S(2)}, u32[]{:S(2)}) collective-permute-start(bf16[4,8,4096]{2,1,0:T(8,128)(2,1)S(1)} %collective-permute-done.3.refs_4_), channel_id=1, source_target_pairs={{0,32},{32,64},{64,96},{96,128},{128,160},{160,192},{192,224},{224... | collective-permute-start | bytes 786440 | tf_op jit(solution)/shard_map/ppermute | solution.py:308
  35.5 9.4 %collective-permute-start.8 = (bf16[4,8,4096]{2,1,0:T(8,128)(2,1)S(1)}, bf16[4,8,4096]{2,1,0:T(8,128)(2,1)S(1)}, u32[]{:S(2)}, u32[]{:S(2)}) collective-permute-start(bf16[4,8,4096]{2,1,0:T(8,128)(2,1)S(1)} %collective-permute-done.4.refs_5_), channel_id=1, source_target_pairs={{0,224},{32,0},{64,32},{96,64},{128,96},{160,128},{192,160},{224,1... | collective-permute-start | bytes 786440 | tf_op jit(solution)/shard_map/ppermute | solution.py:308
  38.7 18.3 %collective-permute-start.5 = (bf16[64,4096]{1,0:T(8,128)(2,1)S(1)}, bf16[64,4096]{1,0:T(8,128)(2,1)S(1)}, u32[]{:S(2)}, u32[]{:S(2)}) collective-permute-start(bf16[64,4096]{1,0:T(8,128)(2,1)S(1)} %collective-permute-done.rows_ref), channel_id=1, source_target_pairs={{0,8},{8,0},{16,24},{24,16},{1,9},{9,1},{17,25},{25,17},{2,10},{10... | collective-permute-start | bytes 1572872 | tf_op jit(solution)/shard_map/ppermute | solution.py:316
  44.8 8.7 %collective-permute-start.7 = (bf16[4,8,4096]{2,1,0:T(8,128)(2,1)S(1)}, bf16[4,8,4096]{2,1,0:T(8,128)(2,1)S(1)}, u32[]{:S(2)}, u32[]{:S(2)}) collective-permute-start(bf16[4,8,4096]{2,1,0:T(8,128)(2,1)S(1)} %collective-permute-done.6.refs_6_), channel_id=1, source_target_pairs={{0,32},{32,64},{64,96},{96,128},{128,160},{160,192},{192,224},{224... | collective-permute-start | bytes 786440 | tf_op jit(solution)/shard_map/ppermute | solution.py:308
  44.8 8.8 %collective-permute-start.9 = (bf16[4,8,4096]{2,1,0:T(8,128)(2,1)S(1)}, bf16[4,8,4096]{2,1,0:T(8,128)(2,1)S(1)}, u32[]{:S(2)}, u32[]{:S(2)}) collective-permute-start(bf16[4,8,4096]{2,1,0:T(8,128)(2,1)S(1)} %collective-permute-done.8.refs_7_), channel_id=1, source_target_pairs={{0,224},{32,0},{64,32},{96,64},{128,96},{160,128},{192,160},{224,1... | collective-permute-start | bytes 786440 | tf_op jit(solution)/shard_map/ppermute | solution.py:308
  53.6 6.3 %collective-permute-start.11 = (bf16[2,8,4096]{2,1,0:T(8,128)(2,1)S(1)}, bf16[2,8,4096]{2,1,0:T(8,128)(2,1)S(1)}, u32[]{:S(2)}, u32[]{:S(2)}) collective-permute-start(bf16[2,8,4096]{2,1,0:T(8,128)(2,1)S(1)} %slice.6), channel_id=1, source_target_pairs={{0,32},{32,64},{64,96},{96,128},{128,160},{160,192},{192,224},{224... | collective-permute-start | bytes 393224 | tf_op jit(solution)/shard_map/ppermute | solution.py:308
  53.7 6.1 %collective-permute-start.12 = (bf16[2,8,4096]{2,1,0:T(8,128)(2,1)S(1)}, bf16[2,8,4096]{2,1,0:T(8,128)(2,1)S(1)}, u32[]{:S(2)}, u32[]{:S(2)}) collective-permute-start(bf16[2,8,4096]{2,1,0:T(8,128)(2,1)S(1)} %slice.7), channel_id=1, source_target_pairs={{0,224},{32,0},{64,32},{96,64},{128,96},{160,128},{192,160},{224,1... | collective-permute-start | bytes 393224 | tf_op jit(solution)/shard_map/ppermute | solution.py:308
  62.1 11.9 %collective-permute-start.15 = (f16[9,64,256]{2,1,0:T(8,128)(2,1)S(1)}, f16[9,64,256]{2,1,0:T(8,128)(2,1)S(1)}, u32[]{:S(2)}, u32[]{:S(2)}) collective-permute-start(f16[9,64,256]{2,1,0:T(8,128)(2,1)S(1)} %convert_element_type.19), channel_id=1, source_target_pairs={{0,12},{4,8},{8,4},{12,0},{16,28},{20,24},{24,20},{28,16},{1,13},{... | collective-permute-start | bytes 884744 | tf_op jit(solution)/shard_map/ppermute | solution.py:320
  67.4 9.5 %collective-permute-start.14 = (f16[9,64,256]{2,1,0:T(8,128)(2,1)S(1)}, f16[9,64,256]{2,1,0:T(8,128)(2,1)S(1)}, u32[]{:S(2)}, u32[]{:S(2)}) collective-permute-start(f16[9,64,256]{2,1,0:T(8,128)(2,1)S(1)} %convert_element_type.20), channel_id=1, source_target_pairs={{0,8},{8,0},{16,24},{24,16},{1,9},{9,1},{17,25},{25,17},{2,10},{10... | collective-permute-start | bytes 884744 | tf_op jit(solution)/shard_map/ppermute | solution.py:316
  69.6 9.3 %collective-permute-start.13 = (f16[9,64,256]{2,1,0:T(8,128)(2,1)S(1)}, f16[9,64,256]{2,1,0:T(8,128)(2,1)S(1)}, u32[]{:S(2)}, u32[]{:S(2)}) collective-permute-start(f16[9,64,256]{2,1,0:T(8,128)(2,1)S(1)} %convert_element_type.18), channel_id=1, source_target_pairs={{0,4},{4,0},{1,5},{5,1},{2,6},{6,2},{3,7},{7,3},{8,12},{12,8},{9,1... | collective-permute-start | bytes 884744 | tf_op jit(solution)/shard_map/ppermute | solution.py:312

commit v13 on v12

--- a/solution.py
+++ b/solution.py
@@ -351,13 +351,13 @@
     first = (around(base, "z", 1), around(base, "z", -1))
     second = (around(first[0], "z", 1), around(first[1], "z", -1))
     full, mine = run_row_filter(place, taps, after(parts, given))
+    row_x = cross_x(full)
     row_y = cross_y(full)
-    row_x = cross_x(full)
-    row_xy = cross_x(after(row_y, *first))
-    far_y = run_lags(after(row_y, *first))
-    third = (around(after(second[0], far_y), "z", 1), around(after(second[1], far_y), "z", -1))
-    far_x = run_lags(after(row_x, *second))
-    ready = after(third[0], far_x), after(third[1], far_x)
+    row_xy = cross_y(after(row_x, *first))
+    far_x = run_lags(after(row_x, *first))
+    third = (around(after(second[0], far_x), "z", 1), around(after(second[1], far_x), "z", -1))
+    far_y = run_lags(after(row_y, *second))
+    ready = after(third[0], far_y), after(third[1], far_y)
     units += [*first, *second, *third, around(ready[0][0:2], "z", 1), around(ready[1][2:4], "z", -1)]
     for step in (1, 2, 3):
         steps += [[(part, -step) for part in order], [(part, step) for part in order]]

time: 81 us -> 81 us (level)
  starting transfers between devices: 34.3 us -> 35.8 us
  waiting for transfers between devices: 18.1 us -> 16.7 us
    ppermute x8, waiting for transfers between devices: 13 us -> 10.1 us  [around(): lax.ppermute(value, axis, [(i, (i + step) % size) for i in range(size)])]
    ppermute x2 -> x3, starting transfers between devices: 3.84 us -> 6.75 us  [cross_y(): return lax.ppermute(value, 'yh', [(0, 1), (1, 0)])]
    ppermute x2, waiting for transfers between devices: 1.29 us -> 2.75 us  [spread(): return lax.ppermute(value, ('z', 'x', 'yl', 'core'), pairs)]
    ppermute x3 -> x2, starting transfers between devices: 3.56 us -> 2.12 us  [cross_x(): return lax.ppermute(value, 'x', [(0, 1), (1, 0), (2, 3), (3, 2)])]
    ppermute x3 -> x2, waiting for transfers between devices: 2.95 us -> 2.95 us  [cross_x(): return lax.ppermute(value, 'x', [(0, 1), (1, 0), (2, 3), (3, 2)])]
  transfers between devices with their start and end apart: 16 -> 16, of which waited for: 8 -> 9; matrix products, arithmetic and copies ran while one was open for 0% -> 0% of each run, Pallas kernels for 17% -> 17%
where the time goes in v13:
time: 81 us; the launch traced here: 80.9 us
  starting transfers between devices  35.8 us (44%)
  Pallas kernels  19 us (23%)
  waiting for transfers between devices  16.7 us (21%)
  blocking collectives  7.47 us (9%)
  between operations  0.99 us (1%)
    ppermute x8, starting transfers between devices, around(): lax.ppermute(value, axis, [(i, (i + step) % size) for i in range(size)])  13.2 us
    ppermute x8, waiting for transfers between devices, around(): lax.ppermute(value, axis, [(i, (i + step) % size) for i in range(size)])  10.1 us
    ppermute x2, starting transfers between devices, spread(): return lax.ppermute(value, ('z', 'x', 'yl', 'core'), pairs)  9.94 us
    all_gather x1, blocking collectives, shards(): parts = lax.all_gather(raw, ('yl', 'core'), axis=0, tiled=False)  7.47 us
    ppermute x3, starting transfers between devices, cross_y(): return lax.ppermute(value, 'yh', [(0, 1), (1, 0)])  6.75 us
    pallas_call x4, Pallas kernels, run_lags(): pl.pallas_call(lag_kernel, in_specs=[vmem], out_specs=[vmem, vmem], out_s...  5.05 us
    pallas_call x3, Pallas kernels, run_weigh(): pl.pallas_call(body, in_specs=[vmem] * 4, out_specs=vmem, out_shape=jax.S...  4.29 us
    ppermute x1, starting transfers between devices, cross_xy(): return lax.ppermute(value, ('x', 'yh'), [(i, i ^ 3) for i in range(8)])  3.85 us
  transfers between devices with their start and end apart: 16, of which 9 were waited for; matrix products, arithmetic and copies ran while one was open for 0% of the time, Pallas kernels for 17%

profile of v13, /device:TPU:2, one launch (start us, length us, event | category | flops | bytes accessed | tf_op | source)
XLA Modules:
  0.0 80.9 jit_solution(18245279329565391766)
XLA Ops:
  0.6 7.5 %all-gather = bf16[256,1024]{1,0:T(8,128)(2,1)S(1)} all-gather(bf16[64,1024]{1,0:T(8,128)(2,1)} %param.2), channel_id=2, replica_groups=mesh['z'=8,'x'=4,'yh'=2,'yl'=2,'core'=2] {'yl','core'}, dimensions={0}, use_global_device_ids=true | all-gather | bytes 655360 | tf_op jit(solution)/shard_map/all_gather | solution.py:346
  8.8 1.1 %pieces.1 = bf16[2,8,4096]{2,1,0:T(8,128)(2,1)S(1)} custom-call(s32[5]{0:T(128)S(1)} %stack.20.place.refs_0_, f32[1,65]{1,0:T(1,128)S(1)} %bitcast.8, bf16[4,64,1024]{2,1,0:T(8,128)(2,1)S(1)} %bitcast.6), custom_call_target="tpu_custom_call" | custom-call | tf_op jit(solution)/shard_map/pieces/pallas_call | solution.py:66
  10.0 8.4 %collective-permute-start.1 = (bf16[2,8,4096]{2,1,0:T(8,128)(2,1)S(1)}, bf16[2,8,4096]{2,1,0:T(8,128)(2,1)S(1)}, u32[]{:S(2)}, u32[]{:S(2)}) collective-permute-start(bf16[2,8,4096]{2,1,0:T(8,128)(2,1)S(1)} %pieces.1), channel_id=1, source_target_pairs={{0,176},{1,208},{2,240},{3,16},{8,184},{9,216},{10,248},{11,24},{1... | collective-permute-start | bytes 393224 | tf_op jit(solution)/shard_map/ppermute | solution.py:332
  18.4 1.5 %collective-permute-start.2 = (bf16[2,8,4096]{2,1,0:T(8,128)(2,1)S(1)}, bf16[2,8,4096]{2,1,0:T(8,128)(2,1)S(1)}, u32[]{:S(2)}, u32[]{:S(2)}) collective-permute-start(bf16[2,8,4096]{2,1,0:T(8,128)(2,1)S(1)} %pieces.1), channel_id=1, source_target_pairs={{0,160},{1,192},{2,224},{3,0},{8,168},{9,200},{10,232},{11,8},{16,... | collective-permute-start | bytes 393224 | tf_op jit(solution)/shard_map/ppermute | solution.py:332
  19.9 2.7 %rows.1 = (bf16[64,4096]{1,0:T(8,128)(2,1)S(1)}, bf16[64,1024]{1,0:T(8,128)(2,1)}) custom-call(s32[5]{0:T(128)S(1)} %stack.20.place.refs_0_, f32[1,65]{1,0:T(1,128)S(1)} %bitcast.9, bf16[4,64,1024]{2,1,0:T(8,128)(2,1)S(1)} %bitcast.7), custom_call_target="tpu_custom_call" | custom-call | flops 1073741824 | bytes 4194304 | tf_op jit(solution)/shard_map/rows/pallas_call | solution.py:103
  22.7 1.4 %collective-permute-start = (bf16[64,4096]{1,0:T(8,128)(2,1)S(1)}, bf16[64,4096]{1,0:T(8,128)(2,1)S(1)}, u32[]{:S(2)}, u32[]{:S(2)}) collective-permute-start(bf16[64,4096]{1,0:T(8,128)(2,1)S(1)} %get-tuple-element.43.rows_ref), channel_id=1, source_target_pairs={{0,8},{8,0},{16,24},{24,16},{1,9},{9,1},{17,25},{25,17},{2,10},{10... | collective-permute-start | bytes 1572872 | tf_op jit(solution)/shard_map/ppermute | solution.py:316
  24.1 0.8 %collective-permute-done.1 = bf16[2,8,4096]{2,1,0:T(8,128)(2,1)S(1)} collective-permute-done((bf16[2,8,4096]{2,1,0:T(8,128)(2,1)S(1)}, bf16[2,8,4096]{2,1,0:T(8,128)(2,1)S(1)}, u32[]{:S(2)}, u32[]{:S(2)}) %collective-permute-start.1) | collective-permute-done | bytes 131104 | tf_op jit(solution)/shard_map/ppermute | solution.py:332
  24.9 1.9 %collective-permute-done.2 = bf16[2,8,4096]{2,1,0:T(8,128)(2,1)S(1)} collective-permute-done((bf16[2,8,4096]{2,1,0:T(8,128)(2,1)S(1)}, bf16[2,8,4096]{2,1,0:T(8,128)(2,1)S(1)}, u32[]{:S(2)}, u32[]{:S(2)}) %collective-permute-start.2) | collective-permute-done | bytes 131104 | tf_op jit(solution)/shard_map/ppermute | solution.py:332
  27.0 3.2 %collective-permute-start.4 = (bf16[4,8,4096]{2,1,0:T(8,128)(2,1)S(1)}, bf16[4,8,4096]{2,1,0:T(8,128)(2,1)S(1)}, u32[]{:S(2)}, u32[]{:S(2)}) collective-permute-start(bf16[4,8,4096]{2,1,0:T(8,128)(2,1)S(1)} %constant_dynamic-update-slice_fusion.refs_3_), channel_id=1, source_target_pairs={{0,224},{32,0},{64,32},{96,64},{128,96},{160,128},{192,160},{224,1... | collective-permute-start | bytes 786440 | tf_op jit(solution)/shard_map/ppermute | solution.py:308
  30.2 2.9 %collective-permute-start.10 = (bf16[64,4096]{1,0:T(8,128)(2,1)S(1)}, bf16[64,4096]{1,0:T(8,128)(2,1)S(1)}, u32[]{:S(2)}, u32[]{:S(2)}) collective-permute-start(bf16[64,4096]{1,0:T(8,128)(2,1)S(1)} %get-tuple-element.43.rows_ref), channel_id=1, source_target_pairs={{0,4},{4,0},{1,5},{5,1},{2,6},{6,2},{3,7},{7,3},{8,12},{12,8},{9,1... | collective-permute-start | bytes 1572872 | tf_op jit(solution)/shard_map/ppermute | solution.py:312
  33.1 2.4 %collective-permute-done.3.refs_4_ = bf16[4,8,4096]{2,1,0:T(8,128)(2,1)S(1)} collective-permute-done((bf16[4,8,4096]{2,1,0:T(8,128)(2,1)S(1)}, bf16[4,8,4096]{2,1,0:T(8,128)(2,1)S(1)}, u32[]{:S(2)}, u32[]{:S(2)}) %collective-permute-start.3) | collective-permute-done | bytes 262176 | tf_op jit(solution)/shard_map/ppermute | solution.py:308
  35.5 3.2 %collective-permute-start.8 = (bf16[4,8,4096]{2,1,0:T(8,128)(2,1)S(1)}, bf16[4,8,4096]{2,1,0:T(8,128)(2,1)S(1)}, u32[]{:S(2)}, u32[]{:S(2)}) collective-permute-start(bf16[4,8,4096]{2,1,0:T(8,128)(2,1)S(1)} %collective-permute-done.4.refs_5_), channel_id=1, source_target_pairs={{0,224},{32,0},{64,32},{96,64},{128,96},{160,128},{192,160},{224,1... | collective-permute-start | bytes 786440 | tf_op jit(solution)/shard_map/ppermute | solution.py:308
  38.7 2.9 %collective-permute-start.5 = (bf16[64,4096]{1,0:T(8,128)(2,1)S(1)}, bf16[64,4096]{1,0:T(8,128)(2,1)S(1)}, u32[]{:S(2)}, u32[]{:S(2)}) collective-permute-start(bf16[64,4096]{1,0:T(8,128)(2,1)S(1)} %collective-permute-done.rows_ref), channel_id=1, source_target_pairs={{0,4},{4,0},{1,5},{5,1},{2,6},{6,2},{3,7},{7,3},{8,12},{12,8},{9,1... | collective-permute-start | bytes 1572872 | tf_op jit(solution)/shard_map/ppermute | solution.py:312
  41.6 1.3 %lags.4 = (bf16[9,64,4096]{2,1,0:T(8,128)(2,1)S(1)}, f32[64,128]{1,0:T(8,128)S(1)}) custom-call(bf16[64,4096]{1,0:T(8,128)(2,1)S(1)} %collective-permute-done.rows_ref), custom_call_target="tpu_custom_call" | custom-call | flops 10485760 | bytes 6291456 | tf_op jit(solution)/shard_map/lags/pallas_call | solution.py:144
  42.9 1.9 %collective-permute-done.6.refs_6_ = bf16[4,8,4096]{2,1,0:T(8,128)(2,1)S(1)} collective-permute-done((bf16[4,8,4096]{2,1,0:T(8,128)(2,1)S(1)}, bf16[4,8,4096]{2,1,0:T(8,128)(2,1)S(1)}, u32[]{:S(2)}, u32[]{:S(2)}) %collective-permute-start.6) | collective-permute-done | bytes 262176 | tf_op jit(solution)/shard_map/ppermute | solution.py:308
  44.8 3.2 %collective-permute-start.9 = (bf16[4,8,4096]{2,1,0:T(8,128)(2,1)S(1)}, bf16[4,8,4096]{2,1,0:T(8,128)(2,1)S(1)}, u32[]{:S(2)}, u32[]{:S(2)}) collective-permute-start(bf16[4,8,4096]{2,1,0:T(8,128)(2,1)S(1)} %collective-permute-done.8.refs_7_), channel_id=1, source_target_pairs={{0,224},{32,0},{64,32},{96,64},{128,96},{160,128},{192,160},{224,1... | collective-permute-start | bytes 786440 | tf_op jit(solution)/shard_map/ppermute | solution.py:308
  48.1 1.3 %lags.6 = (bf16[9,64,4096]{2,1,0:T(8,128)(2,1)S(1)}, f32[64,128]{1,0:T(8,128)S(1)}) custom-call(bf16[64,4096]{1,0:T(8,128)(2,1)S(1)} %collective-permute-done.10.rows_ref), custom_call_target="tpu_custom_call" | custom-call | flops 10485760 | bytes 6291456 | tf_op jit(solution)/shard_map/lags/pallas_call | solution.py:144
  49.3 4.2 %collective-permute-done.7.refs_8_ = bf16[4,8,4096]{2,1,0:T(8,128)(2,1)S(1)} collective-permute-done((bf16[4,8,4096]{2,1,0:T(8,128)(2,1)S(1)}, bf16[4,8,4096]{2,1,0:T(8,128)(2,1)S(1)}, u32[]{:S(2)}, u32[]{:S(2)}) %collective-permute-start.7) | collective-permute-done | bytes 262176 | tf_op jit(solution)/shard_map/ppermute | solution.py:308
  53.7 3.3 %collective-permute-start.12 = (bf16[2,8,4096]{2,1,0:T(8,128)(2,1)S(1)}, bf16[2,8,4096]{2,1,0:T(8,128)(2,1)S(1)}, u32[]{:S(2)}, u32[]{:S(2)}) collective-permute-start(bf16[2,8,4096]{2,1,0:T(8,128)(2,1)S(1)} %slice.7), channel_id=1, source_target_pairs={{0,224},{32,0},{64,32},{96,64},{128,96},{160,128},{192,160},{224,1... | collective-permute-start | bytes 393224 | tf_op jit(solution)/shard_map/ppermute | solution.py:308
  57.0 1.3 %lags.5 = (bf16[9,64,4096]{2,1,0:T(8,128)(2,1)S(1)}, f32[64,128]{1,0:T(8,128)S(1)}) custom-call(bf16[64,4096]{1,0:T(8,128)(2,1)S(1)} %collective-permute-done.5.rows_ref), custom_call_target="tpu_custom_call" | custom-call | flops 10485760 | bytes 6291456 | tf_op jit(solution)/shard_map/lags/pallas_call | solution.py:144
  58.2 1.6 %collective-permute-done.11.refs_10_ = bf16[2,8,4096]{2,1,0:T(8,128)(2,1)S(1)} collective-permute-done((bf16[2,8,4096]{2,1,0:T(8,128)(2,1)S(1)}, bf16[2,8,4096]{2,1,0:T(8,128)(2,1)S(1)}, u32[]{:S(2)}, u32[]{:S(2)}) %collective-permute-start.11) | collective-permute-done | bytes 131104 | tf_op jit(solution)/shard_map/ppermute | solution.py:308
  59.8 2.2 %columns.1 = (bf16[32,8,4096]{2,1,0:T(8,128)(2,1)S(1)}, f32[8,256]{1,0:T(8,128)S(1)}, f32[9,64,256]{2,1,0:T(8,128)S(1)}) custom-call(s32[5]{0:T(128)S(1)} %stack.20.place.refs_0_, bf16[9,64,4096]{2,1,0:T(8,128)(2,1)S(1)} %get-tuple-element.35.refs_1_, f32[64,128]{1,0:T(8,128)S(1)} %get-tuple-element.36.refs_2_, ...), custom_call_target="tpu_custom_call" | custom-call | flops 1073741824 | bytes 4194304 | tf_op jit(solution)/shard_map/columns/pallas_call | solution.py:200
  62.1 3.9 %collective-permute-start.15 = (f16[9,64,256]{2,1,0:T(8,128)(2,1)S(1)}, f16[9,64,256]{2,1,0:T(8,128)(2,1)S(1)}, u32[]{:S(2)}, u32[]{:S(2)}) collective-permute-start(f16[9,64,256]{2,1,0:T(8,128)(2,1)S(1)} %convert_element_type.19), channel_id=1, source_target_pairs={{0,12},{4,8},{8,4},{12,0},{16,28},{20,24},{24,20},{28,16},{1,13},{... | collective-permute-start | bytes 884744 | tf_op jit(solution)/shard_map/ppermute | solution.py:320
  65.9 1.4 %weigh.5 = f32[9,64,256]{2,1,0:T(8,128)S(1)} custom-call(bf16[9,64,4096]{2,1,0:T(8,128)(2,1)S(1)} %get-tuple-element.30.refs_0_, f32[64,128]{1,0:T(8,128)S(1)} %get-tuple-element.31.refs_1_, bf16[32,8,4096]{2,1,0:T(8,128)(2,1)S(1)} %get-tuple-element.46.refs_2_, f32[8,256]{1,0:T(8,128)S(1)} %get-tuple-element.48.refs_3_), custom_call_target="tpu_custom_call" | custom-call | flops 1207959552 | bytes 589824 | tf_op jit(solution)/shard_map/weigh/pallas_call | solution.py:241
  68.1 1.4 %weigh.4 = f32[9,64,256]{2,1,0:T(8,128)S(1)} custom-call(bf16[9,64,4096]{2,1,0:T(8,128)(2,1)S(1)} %get-tuple-element.38.refs_0_, f32[64,128]{1,0:T(8,128)S(1)} %get-tuple-element.39.refs_1_, bf16[32,8,4096]{2,1,0:T(8,128)(2,1)S(1)} %get-tuple-element.46.refs_2_, f32[8,256]{1,0:T(8,128)S(1)} %get-tuple-element.48.refs_3_), custom_call_target="tpu_custom_call" | custom-call | flops 1207959552 | bytes 589824 | tf_op jit(solution)/shard_map/weigh/pallas_call | solution.py:241
  69.6 0.9 %collective-permute-start.13 = (f16[9,64,256]{2,1,0:T(8,128)(2,1)S(1)}, f16[9,64,256]{2,1,0:T(8,128)(2,1)S(1)}, u32[]{:S(2)}, u32[]{:S(2)}) collective-permute-start(f16[9,64,256]{2,1,0:T(8,128)(2,1)S(1)} %convert_element_type.18), channel_id=1, source_target_pairs={{0,4},{4,0},{1,5},{5,1},{2,6},{6,2},{3,7},{7,3},{8,12},{12,8},{9,1... | collective-permute-start | bytes 884744 | tf_op jit(solution)/shard_map/ppermute | solution.py:312
  70.5 1.3 %lags.7 = (bf16[9,64,4096]{2,1,0:T(8,128)(2,1)S(1)}, f32[64,128]{1,0:T(8,128)S(1)}) custom-call(bf16[64,4096]{1,0:T(8,128)(2,1)S(1)} %get-tuple-element.43.rows_ref), custom_call_target="tpu_custom_call" | custom-call | flops 10485760 | bytes 6291456 | tf_op jit(solution)/shard_map/lags/pallas_call | solution.py:144
  71.8 1.4 %weigh.3.refs_1_ = f32[9,64,256]{2,1,0:T(8,128)S(1)} custom-call(bf16[9,64,4096]{2,1,0:T(8,128)(2,1)S(1)} %get-tuple-element.44.refs_0_, f32[64,128]{1,0:T(8,128)S(1)} %get-tuple-element.45.refs_1_, bf16[32,8,4096]{2,1,0:T(8,128)(2,1)S(1)} %get-tuple-element.46.refs_2_, f32[8,256]{1,0:T(8,128)S(1)} %get-tuple-element.48.refs_3_), custom_call_target="tpu_custom_call" | custom-call | flops 1207959552 | bytes 589824 | tf_op jit(solution)/shard_map/weigh/pallas_call | solution.py:241
  73.3 0.7 collective-permute-done.15
  74.0 2.9 %collective-permute-done.14 = f16[9,64,256]{2,1,0:T(8,128)(2,1)S(1)} collective-permute-done((f16[9,64,256]{2,1,0:T(8,128)(2,1)S(1)}, f16[9,64,256]{2,1,0:T(8,128)(2,1)S(1)}, u32[]{:S(2)}, u32[]{:S(2)}) %collective-permute-start.14) | collective-permute-done | bytes 294944 | tf_op jit(solution)/shard_map/ppermute | solution.py:316
  77.0 1.8 %join.2.refs_3_ = f32[9,64,1024]{2,1,0:T(8,128)} custom-call(s32[5]{0:T(128)S(1)} %stack.20.place.refs_0_, f32[9,64,256]{2,1,0:T(8,128)S(1)} %convert_element_type.22.refs_1_, f32[9,64,256]{2,1,0:T(8,128)S(1)} %convert_element_type.21.refs_2_), custom_call_target="tpu_custom_call" | custom-call | tf_op jit(solution)/shard_map/join/pallas_call | solution.py:291
  79.0 1.8 %join.3 = f32[9,64,1024]{2,1,0:T(8,128)} custom-call(s32[5]{0:T(128)S(1)} %stack.20.place.refs_0_, f32[9,64,256]{2,1,0:T(8,128)S(1)} %weigh.3.refs_1_, f32[9,64,256]{2,1,0:T(8,128)S(1)} %convert_element_type.23.refs_2_, f32[9,64,1024]{2,1,0:T(8,128)} %join.2.refs_3_), custom_call_target="tpu_custom_call", output_to_operand_aliasing={{}: (3, {})} | custom-call | tf_op jit(solution)/shard_map/join/pallas_call | solution.py:291
  (26 shorter events, 2.1 us)
Async XLA Ops:
  8.2 0.7 copy-start
  10.0 14.9 %collective-permute-start.1 = (bf16[2,8,4096]{2,1,0:T(8,128)(2,1)S(1)}, bf16[2,8,4096]{2,1,0:T(8,128)(2,1)S(1)}, u32[]{:S(2)}, u32[]{:S(2)}) collective-permute-start(bf16[2,8,4096]{2,1,0:T(8,128)(2,1)S(1)} %pieces.1), channel_id=1, source_target_pairs={{0,176},{1,208},{2,240},{3,16},{8,184},{9,216},{10,248},{11,24},{1... | collective-permute-start | bytes 393224 | tf_op jit(solution)/shard_map/ppermute | solution.py:332
  18.4 8.5 %collective-permute-start.2 = (bf16[2,8,4096]{2,1,0:T(8,128)(2,1)S(1)}, bf16[2,8,4096]{2,1,0:T(8,128)(2,1)S(1)}, u32[]{:S(2)}, u32[]{:S(2)}) collective-permute-start(bf16[2,8,4096]{2,1,0:T(8,128)(2,1)S(1)} %pieces.1), channel_id=1, source_target_pairs={{0,160},{1,192},{2,224},{3,0},{8,168},{9,200},{10,232},{11,8},{16,... | collective-permute-start | bytes 393224 | tf_op jit(solution)/shard_map/ppermute | solution.py:332
  22.7 16.1 %collective-permute-start = (bf16[64,4096]{1,0:T(8,128)(2,1)S(1)}, bf16[64,4096]{1,0:T(8,128)(2,1)S(1)}, u32[]{:S(2)}, u32[]{:S(2)}) collective-permute-start(bf16[64,4096]{1,0:T(8,128)(2,1)S(1)} %get-tuple-element.43.rows_ref), channel_id=1, source_target_pairs={{0,8},{8,0},{16,24},{24,16},{1,9},{9,1},{17,25},{25,17},{2,10},{10... | collective-permute-start | bytes 1572872 | tf_op jit(solution)/shard_map/ppermute | solution.py:316
  26.9 8.6 %collective-permute-start.3 = (bf16[4,8,4096]{2,1,0:T(8,128)(2,1)S(1)}, bf16[4,8,4096]{2,1,0:T(8,128)(2,1)S(1)}, u32[]{:S(2)}, u32[]{:S(2)}) collective-permute-start(bf16[4,8,4096]{2,1,0:T(8,128)(2,1)S(1)} %constant_dynamic-update-slice_fusion.refs_3_), channel_id=1, source_target_pairs={{0,32},{32,64},{64,96},{96,128},{128,160},{160,192},{192,224},{224... | collective-permute-start | bytes 786440 | tf_op jit(solution)/shard_map/ppermute | solution.py:308
  27.0 8.5 %collective-permute-start.4 = (bf16[4,8,4096]{2,1,0:T(8,128)(2,1)S(1)}, bf16[4,8,4096]{2,1,0:T(8,128)(2,1)S(1)}, u32[]{:S(2)}, u32[]{:S(2)}) collective-permute-start(bf16[4,8,4096]{2,1,0:T(8,128)(2,1)S(1)} %constant_dynamic-update-slice_fusion.refs_3_), channel_id=1, source_target_pairs={{0,224},{32,0},{64,32},{96,64},{128,96},{160,128},{192,160},{224,1... | collective-permute-start | bytes 786440 | tf_op jit(solution)/shard_map/ppermute | solution.py:308
  30.2 17.9 %collective-permute-start.10 = (bf16[64,4096]{1,0:T(8,128)(2,1)S(1)}, bf16[64,4096]{1,0:T(8,128)(2,1)S(1)}, u32[]{:S(2)}, u32[]{:S(2)}) collective-permute-start(bf16[64,4096]{1,0:T(8,128)(2,1)S(1)} %get-tuple-element.43.rows_ref), channel_id=1, source_target_pairs={{0,4},{4,0},{1,5},{5,1},{2,6},{6,2},{3,7},{7,3},{8,12},{12,8},{9,1... | collective-permute-start | bytes 1572872 | tf_op jit(solution)/shard_map/ppermute | solution.py:312
  35.5 9.4 %collective-permute-start.6 = (bf16[4,8,4096]{2,1,0:T(8,128)(2,1)S(1)}, bf16[4,8,4096]{2,1,0:T(8,128)(2,1)S(1)}, u32[]{:S(2)}, u32[]{:S(2)}) collective-permute-start(bf16[4,8,4096]{2,1,0:T(8,128)(2,1)S(1)} %collective-permute-done.3.refs_4_), channel_id=1, source_target_pairs={{0,32},{32,64},{64,96},{96,128},{128,160},{160,192},{192,224},{224... | collective-permute-start | bytes 786440 | tf_op jit(solution)/shard_map/ppermute | solution.py:308
  35.5 9.4 %collective-permute-start.8 = (bf16[4,8,4096]{2,1,0:T(8,128)(2,1)S(1)}, bf16[4,8,4096]{2,1,0:T(8,128)(2,1)S(1)}, u32[]{:S(2)}, u32[]{:S(2)}) collective-permute-start(bf16[4,8,4096]{2,1,0:T(8,128)(2,1)S(1)} %collective-permute-done.4.refs_5_), channel_id=1, source_target_pairs={{0,224},{32,0},{64,32},{96,64},{128,96},{160,128},{192,160},{224,1... | collective-permute-start | bytes 786440 | tf_op jit(solution)/shard_map/ppermute | solution.py:308
  38.7 18.3 %collective-permute-start.5 = (bf16[64,4096]{1,0:T(8,128)(2,1)S(1)}, bf16[64,4096]{1,0:T(8,128)(2,1)S(1)}, u32[]{:S(2)}, u32[]{:S(2)}) collective-permute-start(bf16[64,4096]{1,0:T(8,128)(2,1)S(1)} %collective-permute-done.rows_ref), channel_id=1, source_target_pairs={{0,4},{4,0},{1,5},{5,1},{2,6},{6,2},{3,7},{7,3},{8,12},{12,8},{9,1... | collective-permute-start | bytes 1572872 | tf_op jit(solution)/shard_map/ppermute | solution.py:312
  44.8 8.7 %collective-permute-start.7 = (bf16[4,8,4096]{2,1,0:T(8,128)(2,1)S(1)}, bf16[4,8,4096]{2,1,0:T(8,128)(2,1)S(1)}, u32[]{:S(2)}, u32[]{:S(2)}) collective-permute-start(bf16[4,8,4096]{2,1,0:T(8,128)(2,1)S(1)} %collective-permute-done.6.refs_6_), channel_id=1, source_target_pairs={{0,32},{32,64},{64,96},{96,128},{128,160},{160,192},{192,224},{224... | collective-permute-start | bytes 786440 | tf_op jit(solution)/shard_map/ppermute | solution.py:308
  44.8 8.8 %collective-permute-start.9 = (bf16[4,8,4096]{2,1,0:T(8,128)(2,1)S(1)}, bf16[4,8,4096]{2,1,0:T(8,128)(2,1)S(1)}, u32[]{:S(2)}, u32[]{:S(2)}) collective-permute-start(bf16[4,8,4096]{2,1,0:T(8,128)(2,1)S(1)} %collective-permute-done.8.refs_7_), channel_id=1, source_target_pairs={{0,224},{32,0},{64,32},{96,64},{128,96},{160,128},{192,160},{224,1... | collective-permute-start | bytes 786440 | tf_op jit(solution)/shard_map/ppermute | solution.py:308
  53.6 6.3 %collective-permute-start.11 = (bf16[2,8,4096]{2,1,0:T(8,128)(2,1)S(1)}, bf16[2,8,4096]{2,1,0:T(8,128)(2,1)S(1)}, u32[]{:S(2)}, u32[]{:S(2)}) collective-permute-start(bf16[2,8,4096]{2,1,0:T(8,128)(2,1)S(1)} %slice.6), channel_id=1, source_target_pairs={{0,32},{32,64},{64,96},{96,128},{128,160},{160,192},{192,224},{224... | collective-permute-start | bytes 393224 | tf_op jit(solution)/shard_map/ppermute | solution.py:308
  53.7 6.1 %collective-permute-start.12 = (bf16[2,8,4096]{2,1,0:T(8,128)(2,1)S(1)}, bf16[2,8,4096]{2,1,0:T(8,128)(2,1)S(1)}, u32[]{:S(2)}, u32[]{:S(2)}) collective-permute-start(bf16[2,8,4096]{2,1,0:T(8,128)(2,1)S(1)} %slice.7), channel_id=1, source_target_pairs={{0,224},{32,0},{64,32},{96,64},{128,96},{160,128},{192,160},{224,1... | collective-permute-start | bytes 393224 | tf_op jit(solution)/shard_map/ppermute | solution.py:308
  62.1 11.9 %collective-permute-start.15 = (f16[9,64,256]{2,1,0:T(8,128)(2,1)S(1)}, f16[9,64,256]{2,1,0:T(8,128)(2,1)S(1)}, u32[]{:S(2)}, u32[]{:S(2)}) collective-permute-start(f16[9,64,256]{2,1,0:T(8,128)(2,1)S(1)} %convert_element_type.19), channel_id=1, source_target_pairs={{0,12},{4,8},{8,4},{12,0},{16,28},{20,24},{24,20},{28,16},{1,13},{... | collective-permute-start | bytes 884744 | tf_op jit(solution)/shard_map/ppermute | solution.py:320
  67.4 9.5 %collective-permute-start.14 = (f16[9,64,256]{2,1,0:T(8,128)(2,1)S(1)}, f16[9,64,256]{2,1,0:T(8,128)(2,1)S(1)}, u32[]{:S(2)}, u32[]{:S(2)}) collective-permute-start(f16[9,64,256]{2,1,0:T(8,128)(2,1)S(1)} %convert_element_type.20), channel_id=1, source_target_pairs={{0,8},{8,0},{16,24},{24,16},{1,9},{9,1},{17,25},{25,17},{2,10},{10... | collective-permute-start | bytes 884744 | tf_op jit(solution)/shard_map/ppermute | solution.py:316
  69.6 9.3 %collective-permute-start.13 = (f16[9,64,256]{2,1,0:T(8,128)(2,1)S(1)}, f16[9,64,256]{2,1,0:T(8,128)(2,1)S(1)}, u32[]{:S(2)}, u32[]{:S(2)}) collective-permute-start(f16[9,64,256]{2,1,0:T(8,128)(2,1)S(1)} %convert_element_type.18), channel_id=1, source_target_pairs={{0,4},{4,0},{1,5},{5,1},{2,6},{6,2},{3,7},{7,3},{8,12},{12,8},{9,1... | collective-permute-start | bytes 884744 | tf_op jit(solution)/shard_map/ppermute | solution.py:312

commit v14 on v12

--- a/solution.py
+++ b/solution.py
@@ -260,20 +260,19 @@
     lags, rows, width = same.shape
     lane = lax.broadcasted_iota(jnp.int32, (rows, 128), 1) < 64
     copies = []
-    for group in range(0, lags, 3):
+    for lag in range(lags):
         for half in range(width // 128):
             span = slice(half * 128, (half + 1) * 128)
-            for lag in range(group, group + 3):
-                here = same[lag, :, span] * (1.0 / SCALE) if flip else same[lag, :, span]
-                there = cross[lag, :, span] * (1.0 / SCALE)
-                one = jnp.where(low, here, there)
-                two = jnp.where(low, there, here)
-                tiles[half * 2, lag] = jnp.where(lane, one, pltpu.roll(two, 64, axis=1))
-                tiles[half * 2 + 1, lag] = jnp.where(lane, pltpu.roll(one, 64, axis=1), two)
+            here = same[lag, :, span] * (1.0 / SCALE) if flip else same[lag, :, span]
+            there = cross[lag, :, span] * (1.0 / SCALE)
+            one = jnp.where(low, here, there)
+            two = jnp.where(low, there, here)
+            tiles[half * 2, lag] = jnp.where(lane, one, pltpu.roll(two, 64, axis=1))
+            tiles[half * 2 + 1, lag] = jnp.where(lane, pltpu.roll(one, 64, axis=1), two)
             for k, to_x in enumerate((here_x, here_x ^ 2)):
                 at = pl.multiple_of((half * 4 + to_x) * 128, 128)
-                source = tiles.at[half * 2 + k, pl.ds(group, 3)]
-                target = out.at[pl.ds(group, 3), :, pl.ds(at, 128)]
+                source = tiles.at[half * 2 + k, lag]
+                target = out.at[lag, :, pl.ds(at, 128)]
                 copies.append(pltpu.make_async_copy(source, target, sems.at[len(copies)]))
                 copies[-1].start()
     for copy in copies:
@@ -296,7 +295,7 @@
         input_output_aliases={3: 0} if base else {},
         scratch_shapes=[
             pltpu.VMEM((width // 64, lags, rows, 128), jnp.float32),
-            pltpu.SemaphoreType.DMA((width // 64 * (lags // 3),)),
+            pltpu.SemaphoreType.DMA((width // 64 * lags,)),
         ],
         compiler_params=pltpu.CompilerParams(vmem_limit_bytes=8 * MB),
         name="join",

time: 81 us -> 81.3 us (level)
  transfers between devices with their start and end apart: 16 -> 16, of which waited for: 8 -> 7; matrix products, arithmetic and copies ran while one was open for 0% -> 0% of each run, Pallas kernels for 17% -> 17%
where the time goes in v14:
time: 81.3 us; the launch traced here: 81.2 us
  starting transfers between devices  34.3 us (42%)
  Pallas kernels  19.3 us (24%)
  waiting for transfers between devices  18 us (22%)
  blocking collectives  7.47 us (9%)
  between operations  1 us (1%)
    ppermute x8, starting transfers between devices, around(): lax.ppermute(value, axis, [(i, (i + step) % size) for i in range(size)])  13.2 us
    ppermute x8, waiting for transfers between devices, around(): lax.ppermute(value, axis, [(i, (i + step) % size) for i in range(size)])  13 us
    ppermute x2, starting transfers between devices, spread(): return lax.ppermute(value, ('z', 'x', 'yl', 'core'), pairs)  9.94 us
    all_gather x1, blocking collectives, shards(): parts = lax.all_gather(raw, ('yl', 'core'), axis=0, tiled=False)  7.47 us
    pallas_call x4, Pallas kernels, run_lags(): pl.pallas_call(lag_kernel, in_specs=[vmem], out_specs=[vmem, vmem], out_s...  5.05 us
    pallas_call x3, Pallas kernels, run_weigh(): pl.pallas_call(body, in_specs=[vmem] * 4, out_specs=vmem, out_shape=jax.S...  4.29 us
    pallas_call x2, Pallas kernels, run_join(): pl.pallas_call(body, in_specs=[pl.BlockSpec(memory_space=pltpu.SMEM), vme...  3.87 us
    ppermute x1, starting transfers between devices, cross_xy(): return lax.ppermute(value, ('x', 'yh'), [(i, i ^ 3) for i in range(8)])  3.85 us
  transfers between devices with their start and end apart: 16, of which 7 were waited for; matrix products, arithmetic and copies ran while one was open for 0% of the time, Pallas kernels for 17%

profile of v14, /device:TPU:2, one launch (start us, length us, event | category | flops | bytes accessed | tf_op | source)
XLA Modules:
  0.0 81.2 jit_solution(6814818814412722064)
XLA Ops:
  0.6 7.5 %all-gather = bf16[256,1024]{1,0:T(8,128)(2,1)S(1)} all-gather(bf16[64,1024]{1,0:T(8,128)(2,1)} %param.2), channel_id=2, replica_groups=mesh['z'=8,'x'=4,'yh'=2,'yl'=2,'core'=2] {'yl','core'}, dimensions={0}, use_global_device_ids=true | all-gather | bytes 655360 | tf_op jit(solution)/shard_map/all_gather | solution.py:345
  8.8 1.1 %pieces.1 = bf16[2,8,4096]{2,1,0:T(8,128)(2,1)S(1)} custom-call(s32[5]{0:T(128)S(1)} %stack.20.place.refs_0_, f32[1,65]{1,0:T(1,128)S(1)} %bitcast.8, bf16[4,64,1024]{2,1,0:T(8,128)(2,1)S(1)} %bitcast.6), custom_call_target="tpu_custom_call" | custom-call | tf_op jit(solution)/shard_map/pieces/pallas_call | solution.py:66
  10.0 8.4 %collective-permute-start.1 = (bf16[2,8,4096]{2,1,0:T(8,128)(2,1)S(1)}, bf16[2,8,4096]{2,1,0:T(8,128)(2,1)S(1)}, u32[]{:S(2)}, u32[]{:S(2)}) collective-permute-start(bf16[2,8,4096]{2,1,0:T(8,128)(2,1)S(1)} %pieces.1), channel_id=1, source_target_pairs={{0,176},{1,208},{2,240},{3,16},{8,184},{9,216},{10,248},{11,24},{1... | collective-permute-start | bytes 393224 | tf_op jit(solution)/shard_map/ppermute | solution.py:331
  18.4 1.5 %collective-permute-start.2 = (bf16[2,8,4096]{2,1,0:T(8,128)(2,1)S(1)}, bf16[2,8,4096]{2,1,0:T(8,128)(2,1)S(1)}, u32[]{:S(2)}, u32[]{:S(2)}) collective-permute-start(bf16[2,8,4096]{2,1,0:T(8,128)(2,1)S(1)} %pieces.1), channel_id=1, source_target_pairs={{0,160},{1,192},{2,224},{3,0},{8,168},{9,200},{10,232},{11,8},{16,... | collective-permute-start | bytes 393224 | tf_op jit(solution)/shard_map/ppermute | solution.py:331
  19.9 2.7 %rows.1 = (bf16[64,4096]{1,0:T(8,128)(2,1)S(1)}, bf16[64,1024]{1,0:T(8,128)(2,1)}) custom-call(s32[5]{0:T(128)S(1)} %stack.20.place.refs_0_, f32[1,65]{1,0:T(1,128)S(1)} %bitcast.9, bf16[4,64,1024]{2,1,0:T(8,128)(2,1)S(1)} %bitcast.7), custom_call_target="tpu_custom_call" | custom-call | flops 1073741824 | bytes 4194304 | tf_op jit(solution)/shard_map/rows/pallas_call | solution.py:103
  22.7 2.9 %collective-permute-start = (bf16[64,4096]{1,0:T(8,128)(2,1)S(1)}, bf16[64,4096]{1,0:T(8,128)(2,1)S(1)}, u32[]{:S(2)}, u32[]{:S(2)}) collective-permute-start(bf16[64,4096]{1,0:T(8,128)(2,1)S(1)} %get-tuple-element.43.rows_ref), channel_id=1, source_target_pairs={{0,4},{4,0},{1,5},{5,1},{2,6},{6,2},{3,7},{7,3},{8,12},{12,8},{9,1... | collective-permute-start | bytes 1572872 | tf_op jit(solution)/shard_map/ppermute | solution.py:311
  25.6 1.3 %collective-permute-done.2 = bf16[2,8,4096]{2,1,0:T(8,128)(2,1)S(1)} collective-permute-done((bf16[2,8,4096]{2,1,0:T(8,128)(2,1)S(1)}, bf16[2,8,4096]{2,1,0:T(8,128)(2,1)S(1)}, u32[]{:S(2)}, u32[]{:S(2)}) %collective-permute-start.2) | collective-permute-done | bytes 131104 | tf_op jit(solution)/shard_map/ppermute | solution.py:331
  27.0 3.2 %collective-permute-start.4 = (bf16[4,8,4096]{2,1,0:T(8,128)(2,1)S(1)}, bf16[4,8,4096]{2,1,0:T(8,128)(2,1)S(1)}, u32[]{:S(2)}, u32[]{:S(2)}) collective-permute-start(bf16[4,8,4096]{2,1,0:T(8,128)(2,1)S(1)} %constant_dynamic-update-slice_fusion.refs_3_), channel_id=1, source_target_pairs={{0,224},{32,0},{64,32},{96,64},{128,96},{160,128},{192,160},{224,1... | collective-permute-start | bytes 786440 | tf_op jit(solution)/shard_map/ppermute | solution.py:307
  30.2 1.4 %collective-permute-start.10 = (bf16[64,4096]{1,0:T(8,128)(2,1)S(1)}, bf16[64,4096]{1,0:T(8,128)(2,1)S(1)}, u32[]{:S(2)}, u32[]{:S(2)}) collective-permute-start(bf16[64,4096]{1,0:T(8,128)(2,1)S(1)} %get-tuple-element.43.rows_ref), channel_id=1, source_target_pairs={{0,8},{8,0},{16,24},{24,16},{1,9},{9,1},{17,25},{25,17},{2,10},{10... | collective-permute-start | bytes 1572872 | tf_op jit(solution)/shard_map/ppermute | solution.py:315
  31.6 3.8 %collective-permute-done.3.refs_4_ = bf16[4,8,4096]{2,1,0:T(8,128)(2,1)S(1)} collective-permute-done((bf16[4,8,4096]{2,1,0:T(8,128)(2,1)S(1)}, bf16[4,8,4096]{2,1,0:T(8,128)(2,1)S(1)}, u32[]{:S(2)}, u32[]{:S(2)}) %collective-permute-start.3) | collective-permute-done | bytes 262176 | tf_op jit(solution)/shard_map/ppermute | solution.py:307
  35.5 3.2 %collective-permute-start.8 = (bf16[4,8,4096]{2,1,0:T(8,128)(2,1)S(1)}, bf16[4,8,4096]{2,1,0:T(8,128)(2,1)S(1)}, u32[]{:S(2)}, u32[]{:S(2)}) collective-permute-start(bf16[4,8,4096]{2,1,0:T(8,128)(2,1)S(1)} %collective-permute-done.4.refs_5_), channel_id=1, source_target_pairs={{0,224},{32,0},{64,32},{96,64},{128,96},{160,128},{192,160},{224,1... | collective-permute-start | bytes 786440 | tf_op jit(solution)/shard_map/ppermute | solution.py:307
  38.7 1.4 %collective-permute-start.5 = (bf16[64,4096]{1,0:T(8,128)(2,1)S(1)}, bf16[64,4096]{1,0:T(8,128)(2,1)S(1)}, u32[]{:S(2)}, u32[]{:S(2)}) collective-permute-start(bf16[64,4096]{1,0:T(8,128)(2,1)S(1)} %collective-permute-done.rows_ref), channel_id=1, source_target_pairs={{0,8},{8,0},{16,24},{24,16},{1,9},{9,1},{17,25},{25,17},{2,10},{10... | collective-permute-start | bytes 1572872 | tf_op jit(solution)/shard_map/ppermute | solution.py:315
  40.1 1.3 %lags.4 = (bf16[9,64,4096]{2,1,0:T(8,128)(2,1)S(1)}, f32[64,128]{1,0:T(8,128)S(1)}) custom-call(bf16[64,4096]{1,0:T(8,128)(2,1)S(1)} %collective-permute-done.rows_ref), custom_call_target="tpu_custom_call" | custom-call | flops 10485760 | bytes 6291456 | tf_op jit(solution)/shard_map/lags/pallas_call | solution.py:144
  41.4 3.4 %collective-permute-done.6.refs_6_ = bf16[4,8,4096]{2,1,0:T(8,128)(2,1)S(1)} collective-permute-done((bf16[4,8,4096]{2,1,0:T(8,128)(2,1)S(1)}, bf16[4,8,4096]{2,1,0:T(8,128)(2,1)S(1)}, u32[]{:S(2)}, u32[]{:S(2)}) %collective-permute-start.6) | collective-permute-done | bytes 262176 | tf_op jit(solution)/shard_map/ppermute | solution.py:307
  44.8 3.2 %collective-permute-start.9 = (bf16[4,8,4096]{2,1,0:T(8,128)(2,1)S(1)}, bf16[4,8,4096]{2,1,0:T(8,128)(2,1)S(1)}, u32[]{:S(2)}, u32[]{:S(2)}) collective-permute-start(bf16[4,8,4096]{2,1,0:T(8,128)(2,1)S(1)} %collective-permute-done.8.refs_7_), channel_id=1, source_target_pairs={{0,224},{32,0},{64,32},{96,64},{128,96},{160,128},{192,160},{224,1... | collective-permute-start | bytes 786440 | tf_op jit(solution)/shard_map/ppermute | solution.py:307
  48.1 1.3 %lags.6 = (bf16[9,64,4096]{2,1,0:T(8,128)(2,1)S(1)}, f32[64,128]{1,0:T(8,128)S(1)}) custom-call(bf16[64,4096]{1,0:T(8,128)(2,1)S(1)} %collective-permute-done.10.rows_ref), custom_call_target="tpu_custom_call" | custom-call | flops 10485760 | bytes 6291456 | tf_op jit(solution)/shard_map/lags/pallas_call | solution.py:144
  49.3 4.2 %collective-permute-done.7.refs_8_ = bf16[4,8,4096]{2,1,0:T(8,128)(2,1)S(1)} collective-permute-done((bf16[4,8,4096]{2,1,0:T(8,128)(2,1)S(1)}, bf16[4,8,4096]{2,1,0:T(8,128)(2,1)S(1)}, u32[]{:S(2)}, u32[]{:S(2)}) %collective-permute-start.7) | collective-permute-done | bytes 262176 | tf_op jit(solution)/shard_map/ppermute | solution.py:307
  53.7 3.3 %collective-permute-start.12 = (bf16[2,8,4096]{2,1,0:T(8,128)(2,1)S(1)}, bf16[2,8,4096]{2,1,0:T(8,128)(2,1)S(1)}, u32[]{:S(2)}, u32[]{:S(2)}) collective-permute-start(bf16[2,8,4096]{2,1,0:T(8,128)(2,1)S(1)} %slice.7), channel_id=1, source_target_pairs={{0,224},{32,0},{64,32},{96,64},{128,96},{160,128},{192,160},{224,1... | collective-permute-start | bytes 393224 | tf_op jit(solution)/shard_map/ppermute | solution.py:307
  57.0 1.3 %lags.5 = (bf16[9,64,4096]{2,1,0:T(8,128)(2,1)S(1)}, f32[64,128]{1,0:T(8,128)S(1)}) custom-call(bf16[64,4096]{1,0:T(8,128)(2,1)S(1)} %collective-permute-done.5.rows_ref), custom_call_target="tpu_custom_call" | custom-call | flops 10485760 | bytes 6291456 | tf_op jit(solution)/shard_map/lags/pallas_call | solution.py:144
  58.2 1.6 %collective-permute-done.11.refs_10_ = bf16[2,8,4096]{2,1,0:T(8,128)(2,1)S(1)} collective-permute-done((bf16[2,8,4096]{2,1,0:T(8,128)(2,1)S(1)}, bf16[2,8,4096]{2,1,0:T(8,128)(2,1)S(1)}, u32[]{:S(2)}, u32[]{:S(2)}) %collective-permute-start.11) | collective-permute-done | bytes 131104 | tf_op jit(solution)/shard_map/ppermute | solution.py:307
  59.8 2.2 %columns.1 = (bf16[32,8,4096]{2,1,0:T(8,128)(2,1)S(1)}, f32[8,256]{1,0:T(8,128)S(1)}, f32[9,64,256]{2,1,0:T(8,128)S(1)}) custom-call(s32[5]{0:T(128)S(1)} %stack.20.place.refs_0_, bf16[9,64,4096]{2,1,0:T(8,128)(2,1)S(1)} %get-tuple-element.35.refs_1_, f32[64,128]{1,0:T(8,128)S(1)} %get-tuple-element.36.refs_2_, ...), custom_call_target="tpu_custom_call" | custom-call | flops 1073741824 | bytes 4194304 | tf_op jit(solution)/shard_map/columns/pallas_call | solution.py:200
  62.1 3.9 %collective-permute-start.15 = (f16[9,64,256]{2,1,0:T(8,128)(2,1)S(1)}, f16[9,64,256]{2,1,0:T(8,128)(2,1)S(1)}, u32[]{:S(2)}, u32[]{:S(2)}) collective-permute-start(f16[9,64,256]{2,1,0:T(8,128)(2,1)S(1)} %convert_element_type.19), channel_id=1, source_target_pairs={{0,12},{4,8},{8,4},{12,0},{16,28},{20,24},{24,20},{28,16},{1,13},{... | collective-permute-start | bytes 884744 | tf_op jit(solution)/shard_map/ppermute | solution.py:319
  65.9 1.4 %weigh.5 = f32[9,64,256]{2,1,0:T(8,128)S(1)} custom-call(bf16[9,64,4096]{2,1,0:T(8,128)(2,1)S(1)} %get-tuple-element.38.refs_0_, f32[64,128]{1,0:T(8,128)S(1)} %get-tuple-element.39.refs_1_, bf16[32,8,4096]{2,1,0:T(8,128)(2,1)S(1)} %get-tuple-element.46.refs_2_, f32[8,256]{1,0:T(8,128)S(1)} %get-tuple-element.48.refs_3_), custom_call_target="tpu_custom_call" | custom-call | flops 1207959552 | bytes 589824 | tf_op jit(solution)/shard_map/weigh/pallas_call | solution.py:241
  67.4 0.7 collective-permute-start.14
  68.1 1.4 %weigh.4 = f32[9,64,256]{2,1,0:T(8,128)S(1)} custom-call(bf16[9,64,4096]{2,1,0:T(8,128)(2,1)S(1)} %get-tuple-element.30.refs_0_, f32[64,128]{1,0:T(8,128)S(1)} %get-tuple-element.31.refs_1_, bf16[32,8,4096]{2,1,0:T(8,128)(2,1)S(1)} %get-tuple-element.46.refs_2_, f32[8,256]{1,0:T(8,128)S(1)} %get-tuple-element.48.refs_3_), custom_call_target="tpu_custom_call" | custom-call | flops 1207959552 | bytes 589824 | tf_op jit(solution)/shard_map/weigh/pallas_call | solution.py:241
  69.6 0.9 %collective-permute-start.13 = (f16[9,64,256]{2,1,0:T(8,128)(2,1)S(1)}, f16[9,64,256]{2,1,0:T(8,128)(2,1)S(1)}, u32[]{:S(2)}, u32[]{:S(2)}) collective-permute-start(f16[9,64,256]{2,1,0:T(8,128)(2,1)S(1)} %convert_element_type.18), channel_id=1, source_target_pairs={{0,4},{4,0},{1,5},{5,1},{2,6},{6,2},{3,7},{7,3},{8,12},{12,8},{9,1... | collective-permute-start | bytes 884744 | tf_op jit(solution)/shard_map/ppermute | solution.py:311
  70.5 1.3 %lags.7 = (bf16[9,64,4096]{2,1,0:T(8,128)(2,1)S(1)}, f32[64,128]{1,0:T(8,128)S(1)}) custom-call(bf16[64,4096]{1,0:T(8,128)(2,1)S(1)} %get-tuple-element.43.rows_ref), custom_call_target="tpu_custom_call" | custom-call | flops 10485760 | bytes 6291456 | tf_op jit(solution)/shard_map/lags/pallas_call | solution.py:144
  71.8 1.4 %weigh.3.refs_1_ = f32[9,64,256]{2,1,0:T(8,128)S(1)} custom-call(bf16[9,64,4096]{2,1,0:T(8,128)(2,1)S(1)} %get-tuple-element.44.refs_0_, f32[64,128]{1,0:T(8,128)S(1)} %get-tuple-element.45.refs_1_, bf16[32,8,4096]{2,1,0:T(8,128)(2,1)S(1)} %get-tuple-element.46.refs_2_, f32[8,256]{1,0:T(8,128)S(1)} %get-tuple-element.48.refs_3_), custom_call_target="tpu_custom_call" | custom-call | flops 1207959552 | bytes 589824 | tf_op jit(solution)/shard_map/weigh/pallas_call | solution.py:241
  73.3 0.7 collective-permute-done.15
  74.0 2.9 %collective-permute-done.14 = f16[9,64,256]{2,1,0:T(8,128)(2,1)S(1)} collective-permute-done((f16[9,64,256]{2,1,0:T(8,128)(2,1)S(1)}, f16[9,64,256]{2,1,0:T(8,128)(2,1)S(1)}, u32[]{:S(2)}, u32[]{:S(2)}) %collective-permute-start.14) | collective-permute-done | bytes 294944 | tf_op jit(solution)/shard_map/ppermute | solution.py:315
  77.0 1.9 %join.2.refs_3_ = f32[9,64,1024]{2,1,0:T(8,128)} custom-call(s32[5]{0:T(128)S(1)} %stack.20.place.refs_0_, f32[9,64,256]{2,1,0:T(8,128)S(1)} %convert_element_type.22.refs_1_, f32[9,64,256]{2,1,0:T(8,128)S(1)} %convert_element_type.21.refs_2_), custom_call_target="tpu_custom_call" | custom-call | tf_op jit(solution)/shard_map/join/pallas_call | solution.py:290
  79.0 1.9 %join.3 = f32[9,64,1024]{2,1,0:T(8,128)} custom-call(s32[5]{0:T(128)S(1)} %stack.20.place.refs_0_, f32[9,64,256]{2,1,0:T(8,128)S(1)} %weigh.3.refs_1_, f32[9,64,256]{2,1,0:T(8,128)S(1)} %convert_element_type.23.refs_2_, f32[9,64,1024]{2,1,0:T(8,128)} %join.2.refs_3_), custom_call_target="tpu_custom_call", output_to_operand_aliasing={{}: (3, {})} | custom-call | tf_op jit(solution)/shard_map/join/pallas_call | solution.py:290
  (26 shorter events, 1.3 us)
Async XLA Ops:
  8.2 0.7 copy-start
  10.0 15.6 %collective-permute-start.1 = (bf16[2,8,4096]{2,1,0:T(8,128)(2,1)S(1)}, bf16[2,8,4096]{2,1,0:T(8,128)(2,1)S(1)}, u32[]{:S(2)}, u32[]{:S(2)}) collective-permute-start(bf16[2,8,4096]{2,1,0:T(8,128)(2,1)S(1)} %pieces.1), channel_id=1, source_target_pairs={{0,176},{1,208},{2,240},{3,16},{8,184},{9,216},{10,248},{11,24},{1... | collective-permute-start | bytes 393224 | tf_op jit(solution)/shard_map/ppermute | solution.py:331
  18.4 8.5 %collective-permute-start.2 = (bf16[2,8,4096]{2,1,0:T(8,128)(2,1)S(1)}, bf16[2,8,4096]{2,1,0:T(8,128)(2,1)S(1)}, u32[]{:S(2)}, u32[]{:S(2)}) collective-permute-start(bf16[2,8,4096]{2,1,0:T(8,128)(2,1)S(1)} %pieces.1), channel_id=1, source_target_pairs={{0,160},{1,192},{2,224},{3,0},{8,168},{9,200},{10,232},{11,8},{16,... | collective-permute-start | bytes 393224 | tf_op jit(solution)/shard_map/ppermute | solution.py:331
  22.7 16.1 %collective-permute-start = (bf16[64,4096]{1,0:T(8,128)(2,1)S(1)}, bf16[64,4096]{1,0:T(8,128)(2,1)S(1)}, u32[]{:S(2)}, u32[]{:S(2)}) collective-permute-start(bf16[64,4096]{1,0:T(8,128)(2,1)S(1)} %get-tuple-element.43.rows_ref), channel_id=1, source_target_pairs={{0,4},{4,0},{1,5},{5,1},{2,6},{6,2},{3,7},{7,3},{8,12},{12,8},{9,1... | collective-permute-start | bytes 1572872 | tf_op jit(solution)/shard_map/ppermute | solution.py:311
  26.9 8.6 %collective-permute-start.3 = (bf16[4,8,4096]{2,1,0:T(8,128)(2,1)S(1)}, bf16[4,8,4096]{2,1,0:T(8,128)(2,1)S(1)}, u32[]{:S(2)}, u32[]{:S(2)}) collective-permute-start(bf16[4,8,4096]{2,1,0:T(8,128)(2,1)S(1)} %constant_dynamic-update-slice_fusion.refs_3_), channel_id=1, source_target_pairs={{0,32},{32,64},{64,96},{96,128},{128,160},{160,192},{192,224},{224... | collective-permute-start | bytes 786440 | tf_op jit(solution)/shard_map/ppermute | solution.py:307
  27.0 8.5 %collective-permute-start.4 = (bf16[4,8,4096]{2,1,0:T(8,128)(2,1)S(1)}, bf16[4,8,4096]{2,1,0:T(8,128)(2,1)S(1)}, u32[]{:S(2)}, u32[]{:S(2)}) collective-permute-start(bf16[4,8,4096]{2,1,0:T(8,128)(2,1)S(1)} %constant_dynamic-update-slice_fusion.refs_3_), channel_id=1, source_target_pairs={{0,224},{32,0},{64,32},{96,64},{128,96},{160,128},{192,160},{224,1... | collective-permute-start | bytes 786440 | tf_op jit(solution)/shard_map/ppermute | solution.py:307
  30.2 17.9 %collective-permute-start.10 = (bf16[64,4096]{1,0:T(8,128)(2,1)S(1)}, bf16[64,4096]{1,0:T(8,128)(2,1)S(1)}, u32[]{:S(2)}, u32[]{:S(2)}) collective-permute-start(bf16[64,4096]{1,0:T(8,128)(2,1)S(1)} %get-tuple-element.43.rows_ref), channel_id=1, source_target_pairs={{0,8},{8,0},{16,24},{24,16},{1,9},{9,1},{17,25},{25,17},{2,10},{10... | collective-permute-start | bytes 1572872 | tf_op jit(solution)/shard_map/ppermute | solution.py:315
  35.5 9.4 %collective-permute-start.6 = (bf16[4,8,4096]{2,1,0:T(8,128)(2,1)S(1)}, bf16[4,8,4096]{2,1,0:T(8,128)(2,1)S(1)}, u32[]{:S(2)}, u32[]{:S(2)}) collective-permute-start(bf16[4,8,4096]{2,1,0:T(8,128)(2,1)S(1)} %collective-permute-done.3.refs_4_), channel_id=1, source_target_pairs={{0,32},{32,64},{64,96},{96,128},{128,160},{160,192},{192,224},{224... | collective-permute-start | bytes 786440 | tf_op jit(solution)/shard_map/ppermute | solution.py:307
  35.5 9.4 %collective-permute-start.8 = (bf16[4,8,4096]{2,1,0:T(8,128)(2,1)S(1)}, bf16[4,8,4096]{2,1,0:T(8,128)(2,1)S(1)}, u32[]{:S(2)}, u32[]{:S(2)}) collective-permute-start(bf16[4,8,4096]{2,1,0:T(8,128)(2,1)S(1)} %collective-permute-done.4.refs_5_), channel_id=1, source_target_pairs={{0,224},{32,0},{64,32},{96,64},{128,96},{160,128},{192,160},{224,1... | collective-permute-start | bytes 786440 | tf_op jit(solution)/shard_map/ppermute | solution.py:307
  38.7 18.3 %collective-permute-start.5 = (bf16[64,4096]{1,0:T(8,128)(2,1)S(1)}, bf16[64,4096]{1,0:T(8,128)(2,1)S(1)}, u32[]{:S(2)}, u32[]{:S(2)}) collective-permute-start(bf16[64,4096]{1,0:T(8,128)(2,1)S(1)} %collective-permute-done.rows_ref), channel_id=1, source_target_pairs={{0,8},{8,0},{16,24},{24,16},{1,9},{9,1},{17,25},{25,17},{2,10},{10... | collective-permute-start | bytes 1572872 | tf_op jit(solution)/shard_map/ppermute | solution.py:315
  44.8 8.7 %collective-permute-start.7 = (bf16[4,8,4096]{2,1,0:T(8,128)(2,1)S(1)}, bf16[4,8,4096]{2,1,0:T(8,128)(2,1)S(1)}, u32[]{:S(2)}, u32[]{:S(2)}) collective-permute-start(bf16[4,8,4096]{2,1,0:T(8,128)(2,1)S(1)} %collective-permute-done.6.refs_6_), channel_id=1, source_target_pairs={{0,32},{32,64},{64,96},{96,128},{128,160},{160,192},{192,224},{224... | collective-permute-start | bytes 786440 | tf_op jit(solution)/shard_map/ppermute | solution.py:307
  44.8 8.8 %collective-permute-start.9 = (bf16[4,8,4096]{2,1,0:T(8,128)(2,1)S(1)}, bf16[4,8,4096]{2,1,0:T(8,128)(2,1)S(1)}, u32[]{:S(2)}, u32[]{:S(2)}) collective-permute-start(bf16[4,8,4096]{2,1,0:T(8,128)(2,1)S(1)} %collective-permute-done.8.refs_7_), channel_id=1, source_target_pairs={{0,224},{32,0},{64,32},{96,64},{128,96},{160,128},{192,160},{224,1... | collective-permute-start | bytes 786440 | tf_op jit(solution)/shard_map/ppermute | solution.py:307
  53.6 6.3 %collective-permute-start.11 = (bf16[2,8,4096]{2,1,0:T(8,128)(2,1)S(1)}, bf16[2,8,4096]{2,1,0:T(8,128)(2,1)S(1)}, u32[]{:S(2)}, u32[]{:S(2)}) collective-permute-start(bf16[2,8,4096]{2,1,0:T(8,128)(2,1)S(1)} %slice.6), channel_id=1, source_target_pairs={{0,32},{32,64},{64,96},{96,128},{128,160},{160,192},{192,224},{224... | collective-permute-start | bytes 393224 | tf_op jit(solution)/shard_map/ppermute | solution.py:307
  53.7 6.1 %collective-permute-start.12 = (bf16[2,8,4096]{2,1,0:T(8,128)(2,1)S(1)}, bf16[2,8,4096]{2,1,0:T(8,128)(2,1)S(1)}, u32[]{:S(2)}, u32[]{:S(2)}) collective-permute-start(bf16[2,8,4096]{2,1,0:T(8,128)(2,1)S(1)} %slice.7), channel_id=1, source_target_pairs={{0,224},{32,0},{64,32},{96,64},{128,96},{160,128},{192,160},{224,1... | collective-permute-start | bytes 393224 | tf_op jit(solution)/shard_map/ppermute | solution.py:307
  62.1 11.9 %collective-permute-start.15 = (f16[9,64,256]{2,1,0:T(8,128)(2,1)S(1)}, f16[9,64,256]{2,1,0:T(8,128)(2,1)S(1)}, u32[]{:S(2)}, u32[]{:S(2)}) collective-permute-start(f16[9,64,256]{2,1,0:T(8,128)(2,1)S(1)} %convert_element_type.19), channel_id=1, source_target_pairs={{0,12},{4,8},{8,4},{12,0},{16,28},{20,24},{24,20},{28,16},{1,13},{... | collective-permute-start | bytes 884744 | tf_op jit(solution)/shard_map/ppermute | solution.py:319
  67.4 9.5 %collective-permute-start.14 = (f16[9,64,256]{2,1,0:T(8,128)(2,1)S(1)}, f16[9,64,256]{2,1,0:T(8,128)(2,1)S(1)}, u32[]{:S(2)}, u32[]{:S(2)}) collective-permute-start(f16[9,64,256]{2,1,0:T(8,128)(2,1)S(1)} %convert_element_type.20), channel_id=1, source_target_pairs={{0,8},{8,0},{16,24},{24,16},{1,9},{9,1},{17,25},{25,17},{2,10},{10... | collective-permute-start | bytes 884744 | tf_op jit(solution)/shard_map/ppermute | solution.py:315
  69.6 9.4 %collective-permute-start.13 = (f16[9,64,256]{2,1,0:T(8,128)(2,1)S(1)}, f16[9,64,256]{2,1,0:T(8,128)(2,1)S(1)}, u32[]{:S(2)}, u32[]{:S(2)}) collective-permute-start(f16[9,64,256]{2,1,0:T(8,128)(2,1)S(1)} %convert_element_type.18), channel_id=1, source_target_pairs={{0,4},{4,0},{1,5},{5,1},{2,6},{6,2},{3,7},{7,3},{8,12},{12,8},{9,1... | collective-permute-start | bytes 884744 | tf_op jit(solution)/shard_map/ppermute | solution.py:311

commit v15 on v13

--- a/solution.py
+++ b/solution.py
@@ -351,12 +351,12 @@
     first = (around(base, "z", 1), around(base, "z", -1))
     second = (around(first[0], "z", 1), around(first[1], "z", -1))
     full, mine = run_row_filter(place, taps, after(parts, given))
+    row_y = cross_y(full)
     row_x = cross_x(full)
-    row_y = cross_y(full)
-    row_xy = cross_y(after(row_x, *first))
-    far_x = run_lags(after(row_x, *first))
-    third = (around(after(second[0], far_x), "z", 1), around(after(second[1], far_x), "z", -1))
+    row_xy = cross_x(after(row_y, first[0]))
     far_y = run_lags(after(row_y, *second))
+    third = (around(second[0], "z", 1), around(second[1], "z", -1))
+    far_x = run_lags(after(row_x, *third))
     ready = after(third[0], far_y), after(third[1], far_y)
     units += [*first, *second, *third, around(ready[0][0:2], "z", 1), around(ready[1][2:4], "z", -1)]
     for step in (1, 2, 3):

time: 81 us -> 88.4 us (1.091)
  waiting for transfers between devices: 16.7 us -> 26.3 us
  starting transfers between devices: 35.8 us -> 32.9 us
    ppermute x2 -> x3, waiting for transfers between devices: 2.95 us -> 9.64 us  [cross_x(): return lax.ppermute(value, 'x', [(0, 1), (1, 0), (2, 3), (3, 2)])]
    ppermute x8, waiting for transfers between devices: 10.1 us -> 13.9 us  [around(): lax.ppermute(value, axis, [(i, (i + step) % size) for i in range(size)])]
    ppermute x3 -> x2, starting transfers between devices: 6.75 us -> 3.61 us  [cross_y(): return lax.ppermute(value, 'yh', [(0, 1), (1, 0)])]
    ppermute x2, waiting for transfers between devices: 2.75 us -> 1.29 us  [spread(): return lax.ppermute(value, ('z', 'x', 'yl', 'core'), pairs)]
    ppermute x2 -> x3, starting transfers between devices: 2.12 us -> 2.72 us  [cross_x(): return lax.ppermute(value, 'x', [(0, 1), (1, 0), (2, 3), (3, 2)])]
  transfers between devices with their start and end apart: 16 -> 16, of which waited for: 9 -> 9; matrix products, arithmetic and copies ran while one was open for 0% -> 0% of each run, Pallas kernels for 17% -> 16%
where the time goes in v15:
time: 88.4 us; the launch traced here: 87.7 us
  starting transfers between devices  32.9 us (37%)
  waiting for transfers between devices  26.3 us (30%)
  Pallas kernels  19 us (21%)
  blocking collectives  7.47 us (8%)
  between operations  0.98 us (1%)
    ppermute x8, waiting for transfers between devices, around(): lax.ppermute(value, axis, [(i, (i + step) % size) for i in range(size)])  13.9 us
    ppermute x8, starting transfers between devices, around(): lax.ppermute(value, axis, [(i, (i + step) % size) for i in range(size)])  12.8 us
    ppermute x2, starting transfers between devices, spread(): return lax.ppermute(value, ('z', 'x', 'yl', 'core'), pairs)  9.94 us
    ppermute x3, waiting for transfers between devices, cross_x(): return lax.ppermute(value, 'x', [(0, 1), (1, 0), (2, 3), (3, 2)])  9.64 us
    all_gather x1, blocking collectives, shards(): parts = lax.all_gather(raw, ('yl', 'core'), axis=0, tiled=False)  7.47 us
    pallas_call x4, Pallas kernels, run_lags(): pl.pallas_call(lag_kernel, in_specs=[vmem], out_specs=[vmem, vmem], out_s...  5.06 us
    pallas_call x3, Pallas kernels, run_weigh(): pl.pallas_call(body, in_specs=[vmem] * 4, out_specs=vmem, out_shape=jax.S...  4.29 us
    ppermute x1, starting transfers between devices, cross_xy(): return lax.ppermute(value, ('x', 'yh'), [(i, i ^ 3) for i in range(8)])  3.87 us
  transfers between devices with their start and end apart: 16, of which 9 were waited for; matrix products, arithmetic and copies ran while one was open for 0% of the time, Pallas kernels for 16%

profile of v15, /device:TPU:2, one launch (start us, length us, event | category | flops | bytes accessed | tf_op | source)
XLA Modules:
  0.0 87.7 jit_solution(16539240775097928791)
XLA Ops:
  0.6 7.5 %all-gather = bf16[256,1024]{1,0:T(8,128)(2,1)S(1)} all-gather(bf16[64,1024]{1,0:T(8,128)(2,1)} %param.2), channel_id=2, replica_groups=mesh['z'=8,'x'=4,'yh'=2,'yl'=2,'core'=2] {'yl','core'}, dimensions={0}, use_global_device_ids=true | all-gather | bytes 655360 | tf_op jit(solution)/shard_map/all_gather | solution.py:346
  8.2 0.7 copy-done
  8.8 1.1 %pieces.1 = bf16[2,8,4096]{2,1,0:T(8,128)(2,1)S(1)} custom-call(s32[5]{0:T(128)S(1)} %stack.20.place.refs_0_, f32[1,65]{1,0:T(1,128)S(1)} %bitcast.8, bf16[4,64,1024]{2,1,0:T(8,128)(2,1)S(1)} %bitcast.6), custom_call_target="tpu_custom_call" | custom-call | tf_op jit(solution)/shard_map/pieces/pallas_call | solution.py:66
  10.0 8.4 %collective-permute-start.1 = (bf16[2,8,4096]{2,1,0:T(8,128)(2,1)S(1)}, bf16[2,8,4096]{2,1,0:T(8,128)(2,1)S(1)}, u32[]{:S(2)}, u32[]{:S(2)}) collective-permute-start(bf16[2,8,4096]{2,1,0:T(8,128)(2,1)S(1)} %pieces.1), channel_id=1, source_target_pairs={{0,176},{1,208},{2,240},{3,16},{8,184},{9,216},{10,248},{11,24},{1... | collective-permute-start | bytes 393224 | tf_op jit(solution)/shard_map/ppermute | solution.py:332
  18.4 1.5 %collective-permute-start.2 = (bf16[2,8,4096]{2,1,0:T(8,128)(2,1)S(1)}, bf16[2,8,4096]{2,1,0:T(8,128)(2,1)S(1)}, u32[]{:S(2)}, u32[]{:S(2)}) collective-permute-start(bf16[2,8,4096]{2,1,0:T(8,128)(2,1)S(1)} %pieces.1), channel_id=1, source_target_pairs={{0,160},{1,192},{2,224},{3,0},{8,168},{9,200},{10,232},{11,8},{16,... | collective-permute-start | bytes 393224 | tf_op jit(solution)/shard_map/ppermute | solution.py:332
  19.9 2.7 %rows.1 = (bf16[64,4096]{1,0:T(8,128)(2,1)S(1)}, bf16[64,1024]{1,0:T(8,128)(2,1)}) custom-call(s32[5]{0:T(128)S(1)} %stack.20.place.refs_0_, f32[1,65]{1,0:T(1,128)S(1)} %bitcast.9, bf16[4,64,1024]{2,1,0:T(8,128)(2,1)S(1)} %bitcast.7), custom_call_target="tpu_custom_call" | custom-call | flops 1073741824 | bytes 4194304 | tf_op jit(solution)/shard_map/rows/pallas_call | solution.py:103
  22.7 2.9 %collective-permute-start = (bf16[64,4096]{1,0:T(8,128)(2,1)S(1)}, bf16[64,4096]{1,0:T(8,128)(2,1)S(1)}, u32[]{:S(2)}, u32[]{:S(2)}) collective-permute-start(bf16[64,4096]{1,0:T(8,128)(2,1)S(1)} %get-tuple-element.38.rows_ref), channel_id=1, source_target_pairs={{0,4},{4,0},{1,5},{5,1},{2,6},{6,2},{3,7},{7,3},{8,12},{12,8},{9,1... | collective-permute-start | bytes 1572872 | tf_op jit(solution)/shard_map/ppermute | solution.py:312
  25.6 1.3 %collective-permute-done.2 = bf16[2,8,4096]{2,1,0:T(8,128)(2,1)S(1)} collective-permute-done((bf16[2,8,4096]{2,1,0:T(8,128)(2,1)S(1)}, bf16[2,8,4096]{2,1,0:T(8,128)(2,1)S(1)}, u32[]{:S(2)}, u32[]{:S(2)}) %collective-permute-start.2) | collective-permute-done | bytes 131104 | tf_op jit(solution)/shard_map/ppermute | solution.py:332
  27.1 1.8 %collective-permute-start.3 = (bf16[4,8,4096]{2,1,0:T(8,128)(2,1)S(1)}, bf16[4,8,4096]{2,1,0:T(8,128)(2,1)S(1)}, u32[]{:S(2)}, u32[]{:S(2)}) collective-permute-start(bf16[4,8,4096]{2,1,0:T(8,128)(2,1)S(1)} %constant_dynamic-update-slice_fusion.refs_3_), channel_id=1, source_target_pairs={{0,32},{32,64},{64,96},{96,128},{128,160},{160,192},{192,224},{224... | collective-permute-start | bytes 786440 | tf_op jit(solution)/shard_map/ppermute | solution.py:308
  29.0 5.3 %collective-permute-done.7.refs_5_ = bf16[4,8,4096]{2,1,0:T(8,128)(2,1)S(1)} collective-permute-done((bf16[4,8,4096]{2,1,0:T(8,128)(2,1)S(1)}, bf16[4,8,4096]{2,1,0:T(8,128)(2,1)S(1)}, u32[]{:S(2)}, u32[]{:S(2)}) %collective-permute-start.7) | collective-permute-done | bytes 262176 | tf_op jit(solution)/shard_map/ppermute | solution.py:308
  34.2 3.0 %collective-permute-start.8 = (bf16[4,8,4096]{2,1,0:T(8,128)(2,1)S(1)}, bf16[4,8,4096]{2,1,0:T(8,128)(2,1)S(1)}, u32[]{:S(2)}, u32[]{:S(2)}) collective-permute-start(bf16[4,8,4096]{2,1,0:T(8,128)(2,1)S(1)} %collective-permute-done.7.refs_5_), channel_id=1, source_target_pairs={{0,224},{32,0},{64,32},{96,64},{128,96},{160,128},{192,160},{224,1... | collective-permute-start | bytes 786440 | tf_op jit(solution)/shard_map/ppermute | solution.py:308
  37.7 1.5 %collective-permute-start.13 = (bf16[64,4096]{1,0:T(8,128)(2,1)S(1)}, bf16[64,4096]{1,0:T(8,128)(2,1)S(1)}, u32[]{:S(2)}, u32[]{:S(2)}) collective-permute-start(bf16[64,4096]{1,0:T(8,128)(2,1)S(1)} %get-tuple-element.38.rows_ref), channel_id=1, source_target_pairs={{0,8},{8,0},{16,24},{24,16},{1,9},{9,1},{17,25},{25,17},{2,10},{10... | collective-permute-start | bytes 1572872 | tf_op jit(solution)/shard_map/ppermute | solution.py:316
  39.7 3.9 %collective-permute-done.8.refs_7_ = bf16[4,8,4096]{2,1,0:T(8,128)(2,1)S(1)} collective-permute-done((bf16[4,8,4096]{2,1,0:T(8,128)(2,1)S(1)}, bf16[4,8,4096]{2,1,0:T(8,128)(2,1)S(1)}, u32[]{:S(2)}, u32[]{:S(2)}) %collective-permute-start.8) | collective-permute-done | bytes 262176 | tf_op jit(solution)/shard_map/ppermute | solution.py:308
  43.6 3.7 %collective-permute-start.9 = (bf16[4,8,4096]{2,1,0:T(8,128)(2,1)S(1)}, bf16[4,8,4096]{2,1,0:T(8,128)(2,1)S(1)}, u32[]{:S(2)}, u32[]{:S(2)}) collective-permute-start(bf16[4,8,4096]{2,1,0:T(8,128)(2,1)S(1)} %collective-permute-done.8.refs_7_), channel_id=1, source_target_pairs={{0,224},{32,0},{64,32},{96,64},{128,96},{160,128},{192,160},{224,1... | collective-permute-start | bytes 786440 | tf_op jit(solution)/shard_map/ppermute | solution.py:308
  47.5 1.3 %lags.5 = (bf16[9,64,4096]{2,1,0:T(8,128)(2,1)S(1)}, f32[64,128]{1,0:T(8,128)S(1)}) custom-call(bf16[64,4096]{1,0:T(8,128)(2,1)S(1)} %collective-permute-done.rows_ref), custom_call_target="tpu_custom_call" | custom-call | flops 10485760 | bytes 6291456 | tf_op jit(solution)/shard_map/lags/pallas_call | solution.py:144
  48.8 4.1 %collective-permute-done.9.refs_9_ = bf16[4,8,4096]{2,1,0:T(8,128)(2,1)S(1)} collective-permute-done((bf16[4,8,4096]{2,1,0:T(8,128)(2,1)S(1)}, bf16[4,8,4096]{2,1,0:T(8,128)(2,1)S(1)}, u32[]{:S(2)}, u32[]{:S(2)}) %collective-permute-start.9) | collective-permute-done | bytes 262176 | tf_op jit(solution)/shard_map/ppermute | solution.py:308
  52.9 3.8 %collective-permute-start.11 = (bf16[2,8,4096]{2,1,0:T(8,128)(2,1)S(1)}, bf16[2,8,4096]{2,1,0:T(8,128)(2,1)S(1)}, u32[]{:S(2)}, u32[]{:S(2)}) collective-permute-start(bf16[2,8,4096]{2,1,0:T(8,128)(2,1)S(1)} %slice.7), channel_id=1, source_target_pairs={{0,224},{32,0},{64,32},{96,64},{128,96},{160,128},{192,160},{224,1... | collective-permute-start | bytes 393224 | tf_op jit(solution)/shard_map/ppermute | solution.py:308
  56.9 1.3 %lags.7 = (bf16[9,64,4096]{2,1,0:T(8,128)(2,1)S(1)}, f32[64,128]{1,0:T(8,128)S(1)}) custom-call(bf16[64,4096]{1,0:T(8,128)(2,1)S(1)} %collective-permute-done.13.rows_ref), custom_call_target="tpu_custom_call" | custom-call | flops 10485760 | bytes 6291456 | tf_op jit(solution)/shard_map/lags/pallas_call | solution.py:144
  58.2 4.9 %collective-permute-done.4.rows_ref = bf16[64,4096]{1,0:T(8,128)(2,1)S(1)} collective-permute-done((bf16[64,4096]{1,0:T(8,128)(2,1)S(1)}, bf16[64,4096]{1,0:T(8,128)(2,1)S(1)}, u32[]{:S(2)}, u32[]{:S(2)}) %collective-permute-start.4) | collective-permute-done | bytes 524320 | tf_op jit(solution)/shard_map/ppermute | solution.py:316
  63.1 1.3 %lags.4 = (bf16[9,64,4096]{2,1,0:T(8,128)(2,1)S(1)}, f32[64,128]{1,0:T(8,128)S(1)}) custom-call(bf16[64,4096]{1,0:T(8,128)(2,1)S(1)} %collective-permute-done.4.rows_ref), custom_call_target="tpu_custom_call" | custom-call | flops 10485760 | bytes 6291456 | tf_op jit(solution)/shard_map/lags/pallas_call | solution.py:144
  64.4 2.2 %columns.1 = (bf16[32,8,4096]{2,1,0:T(8,128)(2,1)S(1)}, f32[8,256]{1,0:T(8,128)S(1)}, f32[9,64,256]{2,1,0:T(8,128)S(1)}) custom-call(s32[5]{0:T(128)S(1)} %stack.20.place.refs_0_, bf16[9,64,4096]{2,1,0:T(8,128)(2,1)S(1)} %get-tuple-element.30.refs_1_, f32[64,128]{1,0:T(8,128)S(1)} %get-tuple-element.31.refs_2_, ...), custom_call_target="tpu_custom_call" | custom-call | flops 1073741824 | bytes 4194304 | tf_op jit(solution)/shard_map/columns/pallas_call | solution.py:200
  66.7 3.9 %collective-permute-start.15 = (f16[9,64,256]{2,1,0:T(8,128)(2,1)S(1)}, f16[9,64,256]{2,1,0:T(8,128)(2,1)S(1)}, u32[]{:S(2)}, u32[]{:S(2)}) collective-permute-start(f16[9,64,256]{2,1,0:T(8,128)(2,1)S(1)} %convert_element_type.19), channel_id=1, source_target_pairs={{0,12},{4,8},{8,4},{12,0},{16,28},{20,24},{24,20},{28,16},{1,13},{... | collective-permute-start | bytes 884744 | tf_op jit(solution)/shard_map/ppermute | solution.py:320
  70.6 1.4 %weigh.5 = f32[9,64,256]{2,1,0:T(8,128)S(1)} custom-call(bf16[9,64,4096]{2,1,0:T(8,128)(2,1)S(1)} %get-tuple-element.43.refs_0_, f32[64,128]{1,0:T(8,128)S(1)} %get-tuple-element.44.refs_1_, bf16[32,8,4096]{2,1,0:T(8,128)(2,1)S(1)} %get-tuple-element.41.refs_2_, f32[8,256]{1,0:T(8,128)S(1)} %get-tuple-element.46.refs_3_), custom_call_target="tpu_custom_call" | custom-call | flops 1207959552 | bytes 589824 | tf_op jit(solution)/shard_map/weigh/pallas_call | solution.py:241
  72.1 0.7 collective-permute-start.14
  72.7 1.4 %weigh.4 = f32[9,64,256]{2,1,0:T(8,128)S(1)} custom-call(bf16[9,64,4096]{2,1,0:T(8,128)(2,1)S(1)} %get-tuple-element.33.refs_0_, f32[64,128]{1,0:T(8,128)S(1)} %get-tuple-element.34.refs_1_, bf16[32,8,4096]{2,1,0:T(8,128)(2,1)S(1)} %get-tuple-element.41.refs_2_, f32[8,256]{1,0:T(8,128)S(1)} %get-tuple-element.46.refs_3_), custom_call_target="tpu_custom_call" | custom-call | flops 1207959552 | bytes 589824 | tf_op jit(solution)/shard_map/weigh/pallas_call | solution.py:241
  74.2 0.7 collective-permute-start.12
  74.9 1.3 %lags.6 = (bf16[9,64,4096]{2,1,0:T(8,128)(2,1)S(1)}, f32[64,128]{1,0:T(8,128)S(1)}) custom-call(bf16[64,4096]{1,0:T(8,128)(2,1)S(1)} %get-tuple-element.38.rows_ref), custom_call_target="tpu_custom_call" | custom-call | flops 10485760 | bytes 6291456 | tf_op jit(solution)/shard_map/lags/pallas_call | solution.py:144
  76.2 1.4 %weigh.3.refs_1_ = f32[9,64,256]{2,1,0:T(8,128)S(1)} custom-call(bf16[9,64,4096]{2,1,0:T(8,128)(2,1)S(1)} %get-tuple-element.39.refs_0_, f32[64,128]{1,0:T(8,128)S(1)} %get-tuple-element.40.refs_1_, bf16[32,8,4096]{2,1,0:T(8,128)(2,1)S(1)} %get-tuple-element.41.refs_2_, f32[8,256]{1,0:T(8,128)S(1)} %get-tuple-element.46.refs_3_), custom_call_target="tpu_custom_call" | custom-call | flops 1207959552 | bytes 589824 | tf_op jit(solution)/shard_map/weigh/pallas_call | solution.py:241
  77.6 1.5 %collective-permute-done.15 = f16[9,64,256]{2,1,0:T(8,128)(2,1)S(1)} collective-permute-done((f16[9,64,256]{2,1,0:T(8,128)(2,1)S(1)}, f16[9,64,256]{2,1,0:T(8,128)(2,1)S(1)}, u32[]{:S(2)}, u32[]{:S(2)}) %collective-permute-start.15) | collective-permute-done | bytes 294944 | tf_op jit(solution)/shard_map/ppermute | solution.py:320
  79.2 4.7 %collective-permute-done.14 = f16[9,64,256]{2,1,0:T(8,128)(2,1)S(1)} collective-permute-done((f16[9,64,256]{2,1,0:T(8,128)(2,1)S(1)}, f16[9,64,256]{2,1,0:T(8,128)(2,1)S(1)}, u32[]{:S(2)}, u32[]{:S(2)}) %collective-permute-start.14) | collective-permute-done | bytes 294944 | tf_op jit(solution)/shard_map/ppermute | solution.py:316
  84.0 1.8 %join.2.refs_3_ = f32[9,64,1024]{2,1,0:T(8,128)} custom-call(s32[5]{0:T(128)S(1)} %stack.20.place.refs_0_, f32[9,64,256]{2,1,0:T(8,128)S(1)} %convert_element_type.22.refs_1_, f32[9,64,256]{2,1,0:T(8,128)S(1)} %convert_element_type.21.refs_2_), custom_call_target="tpu_custom_call" | custom-call | tf_op jit(solution)/shard_map/join/pallas_call | solution.py:291
  85.8 1.8 %join.3 = f32[9,64,1024]{2,1,0:T(8,128)} custom-call(s32[5]{0:T(128)S(1)} %stack.20.place.refs_0_, f32[9,64,256]{2,1,0:T(8,128)S(1)} %weigh.3.refs_1_, f32[9,64,256]{2,1,0:T(8,128)S(1)} %convert_element_type.23.refs_2_, f32[9,64,1024]{2,1,0:T(8,128)} %join.2.refs_3_), custom_call_target="tpu_custom_call", output_to_operand_aliasing={{}: (3, {})} | custom-call | tf_op jit(solution)/shard_map/join/pallas_call | solution.py:291
  (26 shorter events, 2.2 us)
Async XLA Ops:
  8.2 0.7 copy-start
  10.0 15.6 %collective-permute-start.1 = (bf16[2,8,4096]{2,1,0:T(8,128)(2,1)S(1)}, bf16[2,8,4096]{2,1,0:T(8,128)(2,1)S(1)}, u32[]{:S(2)}, u32[]{:S(2)}) collective-permute-start(bf16[2,8,4096]{2,1,0:T(8,128)(2,1)S(1)} %pieces.1), channel_id=1, source_target_pairs={{0,176},{1,208},{2,240},{3,16},{8,184},{9,216},{10,248},{11,24},{1... | collective-permute-start | bytes 393224 | tf_op jit(solution)/shard_map/ppermute | solution.py:332
  18.4 8.5 %collective-permute-start.2 = (bf16[2,8,4096]{2,1,0:T(8,128)(2,1)S(1)}, bf16[2,8,4096]{2,1,0:T(8,128)(2,1)S(1)}, u32[]{:S(2)}, u32[]{:S(2)}) collective-permute-start(bf16[2,8,4096]{2,1,0:T(8,128)(2,1)S(1)} %pieces.1), channel_id=1, source_target_pairs={{0,160},{1,192},{2,224},{3,0},{8,168},{9,200},{10,232},{11,8},{16,... | collective-permute-start | bytes 393224 | tf_op jit(solution)/shard_map/ppermute | solution.py:332
  22.7 16.5 %collective-permute-start = (bf16[64,4096]{1,0:T(8,128)(2,1)S(1)}, bf16[64,4096]{1,0:T(8,128)(2,1)S(1)}, u32[]{:S(2)}, u32[]{:S(2)}) collective-permute-start(bf16[64,4096]{1,0:T(8,128)(2,1)S(1)} %get-tuple-element.38.rows_ref), channel_id=1, source_target_pairs={{0,4},{4,0},{1,5},{5,1},{2,6},{6,2},{3,7},{7,3},{8,12},{12,8},{9,1... | collective-permute-start | bytes 1572872 | tf_op jit(solution)/shard_map/ppermute | solution.py:312
  26.9 7.4 %collective-permute-start.7 = (bf16[4,8,4096]{2,1,0:T(8,128)(2,1)S(1)}, bf16[4,8,4096]{2,1,0:T(8,128)(2,1)S(1)}, u32[]{:S(2)}, u32[]{:S(2)}) collective-permute-start(bf16[4,8,4096]{2,1,0:T(8,128)(2,1)S(1)} %constant_dynamic-update-slice_fusion.refs_3_), channel_id=1, source_target_pairs={{0,224},{32,0},{64,32},{96,64},{128,96},{160,128},{192,160},{224,1... | collective-permute-start | bytes 786440 | tf_op jit(solution)/shard_map/ppermute | solution.py:308
  27.1 10.5 %collective-permute-start.3 = (bf16[4,8,4096]{2,1,0:T(8,128)(2,1)S(1)}, bf16[4,8,4096]{2,1,0:T(8,128)(2,1)S(1)}, u32[]{:S(2)}, u32[]{:S(2)}) collective-permute-start(bf16[4,8,4096]{2,1,0:T(8,128)(2,1)S(1)} %constant_dynamic-update-slice_fusion.refs_3_), channel_id=1, source_target_pairs={{0,32},{32,64},{64,96},{96,128},{128,160},{160,192},{192,224},{224... | collective-permute-start | bytes 786440 | tf_op jit(solution)/shard_map/ppermute | solution.py:308
  34.2 9.4 %collective-permute-start.8 = (bf16[4,8,4096]{2,1,0:T(8,128)(2,1)S(1)}, bf16[4,8,4096]{2,1,0:T(8,128)(2,1)S(1)}, u32[]{:S(2)}, u32[]{:S(2)}) collective-permute-start(bf16[4,8,4096]{2,1,0:T(8,128)(2,1)S(1)} %collective-permute-done.7.refs_5_), channel_id=1, source_target_pairs={{0,224},{32,0},{64,32},{96,64},{128,96},{160,128},{192,160},{224,1... | collective-permute-start | bytes 786440 | tf_op jit(solution)/shard_map/ppermute | solution.py:308
  37.7 9.8 %collective-permute-start.5 = (bf16[4,8,4096]{2,1,0:T(8,128)(2,1)S(1)}, bf16[4,8,4096]{2,1,0:T(8,128)(2,1)S(1)}, u32[]{:S(2)}, u32[]{:S(2)}) collective-permute-start(bf16[4,8,4096]{2,1,0:T(8,128)(2,1)S(1)} %collective-permute-done.3.refs_4_), channel_id=1, source_target_pairs={{0,32},{32,64},{64,96},{96,128},{128,160},{160,192},{192,224},{224... | collective-permute-start | bytes 786440 | tf_op jit(solution)/shard_map/ppermute | solution.py:308
  37.7 19.3 %collective-permute-start.13 = (bf16[64,4096]{1,0:T(8,128)(2,1)S(1)}, bf16[64,4096]{1,0:T(8,128)(2,1)S(1)}, u32[]{:S(2)}, u32[]{:S(2)}) collective-permute-start(bf16[64,4096]{1,0:T(8,128)(2,1)S(1)} %get-tuple-element.38.rows_ref), channel_id=1, source_target_pairs={{0,8},{8,0},{16,24},{24,16},{1,9},{9,1},{17,25},{25,17},{2,10},{10... | collective-permute-start | bytes 1572872 | tf_op jit(solution)/shard_map/ppermute | solution.py:316
  39.2 24.0 %collective-permute-start.4 = (bf16[64,4096]{1,0:T(8,128)(2,1)S(1)}, bf16[64,4096]{1,0:T(8,128)(2,1)S(1)}, u32[]{:S(2)}, u32[]{:S(2)}) collective-permute-start(bf16[64,4096]{1,0:T(8,128)(2,1)S(1)} %collective-permute-done.rows_ref), channel_id=1, source_target_pairs={{0,8},{8,0},{16,24},{24,16},{1,9},{9,1},{17,25},{25,17},{2,10},{10... | collective-permute-start | bytes 1572872 | tf_op jit(solution)/shard_map/ppermute | solution.py:316
  43.6 9.2 %collective-permute-start.9 = (bf16[4,8,4096]{2,1,0:T(8,128)(2,1)S(1)}, bf16[4,8,4096]{2,1,0:T(8,128)(2,1)S(1)}, u32[]{:S(2)}, u32[]{:S(2)}) collective-permute-start(bf16[4,8,4096]{2,1,0:T(8,128)(2,1)S(1)} %collective-permute-done.8.refs_7_), channel_id=1, source_target_pairs={{0,224},{32,0},{64,32},{96,64},{128,96},{160,128},{192,160},{224,1... | collective-permute-start | bytes 786440 | tf_op jit(solution)/shard_map/ppermute | solution.py:308
  47.5 9.2 %collective-permute-start.6 = (bf16[4,8,4096]{2,1,0:T(8,128)(2,1)S(1)}, bf16[4,8,4096]{2,1,0:T(8,128)(2,1)S(1)}, u32[]{:S(2)}, u32[]{:S(2)}) collective-permute-start(bf16[4,8,4096]{2,1,0:T(8,128)(2,1)S(1)} %collective-permute-done.5.refs_6_), channel_id=1, source_target_pairs={{0,32},{32,64},{64,96},{96,128},{128,160},{160,192},{192,224},{224... | collective-permute-start | bytes 786440 | tf_op jit(solution)/shard_map/ppermute | solution.py:308
  52.9 11.5 %collective-permute-start.11 = (bf16[2,8,4096]{2,1,0:T(8,128)(2,1)S(1)}, bf16[2,8,4096]{2,1,0:T(8,128)(2,1)S(1)}, u32[]{:S(2)}, u32[]{:S(2)}) collective-permute-start(bf16[2,8,4096]{2,1,0:T(8,128)(2,1)S(1)} %slice.7), channel_id=1, source_target_pairs={{0,224},{32,0},{64,32},{96,64},{128,96},{160,128},{192,160},{224,1... | collective-permute-start | bytes 393224 | tf_op jit(solution)/shard_map/ppermute | solution.py:308
  56.7 7.7 %collective-permute-start.10 = (bf16[2,8,4096]{2,1,0:T(8,128)(2,1)S(1)}, bf16[2,8,4096]{2,1,0:T(8,128)(2,1)S(1)}, u32[]{:S(2)}, u32[]{:S(2)}) collective-permute-start(bf16[2,8,4096]{2,1,0:T(8,128)(2,1)S(1)} %slice.6), channel_id=1, source_target_pairs={{0,32},{32,64},{64,96},{96,128},{128,160},{160,192},{192,224},{224... | collective-permute-start | bytes 393224 | tf_op jit(solution)/shard_map/ppermute | solution.py:308
  66.7 12.4 %collective-permute-start.15 = (f16[9,64,256]{2,1,0:T(8,128)(2,1)S(1)}, f16[9,64,256]{2,1,0:T(8,128)(2,1)S(1)}, u32[]{:S(2)}, u32[]{:S(2)}) collective-permute-start(f16[9,64,256]{2,1,0:T(8,128)(2,1)S(1)} %convert_element_type.19), channel_id=1, source_target_pairs={{0,12},{4,8},{8,4},{12,0},{16,28},{20,24},{24,20},{28,16},{1,13},{... | collective-permute-start | bytes 884744 | tf_op jit(solution)/shard_map/ppermute | solution.py:320
  72.1 11.8 %collective-permute-start.14 = (f16[9,64,256]{2,1,0:T(8,128)(2,1)S(1)}, f16[9,64,256]{2,1,0:T(8,128)(2,1)S(1)}, u32[]{:S(2)}, u32[]{:S(2)}) collective-permute-start(f16[9,64,256]{2,1,0:T(8,128)(2,1)S(1)} %convert_element_type.20), channel_id=1, source_target_pairs={{0,8},{8,0},{16,24},{24,16},{1,9},{9,1},{17,25},{25,17},{2,10},{10... | collective-permute-start | bytes 884744 | tf_op jit(solution)/shard_map/ppermute | solution.py:316
  74.2 11.5 %collective-permute-start.12 = (f16[9,64,256]{2,1,0:T(8,128)(2,1)S(1)}, f16[9,64,256]{2,1,0:T(8,128)(2,1)S(1)}, u32[]{:S(2)}, u32[]{:S(2)}) collective-permute-start(f16[9,64,256]{2,1,0:T(8,128)(2,1)S(1)} %convert_element_type.18), channel_id=1, source_target_pairs={{0,4},{4,0},{1,5},{5,1},{2,6},{6,2},{3,7},{7,3},{8,12},{12,8},{9,1... | collective-permute-start | bytes 884744 | tf_op jit(solution)/shard_map/ppermute | solution.py:312
